TPU v7x, 32 devices: a whole 2x2x4 slice. The times are simulated.
32 devices in a mesh: groups: 2 (over y), rows: 4 (over z), mp: 2 (over x), pair: 2 (over core).
Axes of the slice: x: 2, y: 2, z: 4, core: 2. Of those that a mesh axis runs over, the one named last changes fastest.
Arguments:
- query_rows: bfloat16 [2048, 512], P(('groups', 'rows', 'pair'), 'mp'), parts along dimension 0, may hold values from -240 to 240
- key_rows: bfloat16 [65536, 512], P(('groups', 'rows', 'pair'), 'mp'), parts along dimension 0, may hold values from -24 to 24
- value_rows: bfloat16 [65536, 512], P(('groups', 'rows', 'pair'), 'mp'), parts along dimension 0, may hold values from -6 to 6
- cotangent: bfloat16 [2048, 512], P(('groups', 'rows', 'pair'), 'mp'), parts along dimension 0, may hold values from -1536 to 1536
- train_rows: int32 [16], P('groups'), parts along dimension 0, may hold values from 1 to 12288, as said below
- test_rows: int32 [16], P('groups'), parts along dimension 0, may hold values from 32 to 128
- block_table: int32 [128], P('groups'), parts along dimension 0, may hold values from 0 to 7, as said below
Outputs:
- query_grad: bfloat16 [2048, 512], P(('groups', 'rows', 'pair'), 'mp'), parts along dimension 0
- key_grad: bfloat16 [65536, 512], P(('groups', 'rows', 'pair'), 'mp'), parts along dimension 0
- value_grad: bfloat16 [65536, 512], P(('groups', 'rows', 'pair'), 'mp'), parts along dimension 0
There are 2 independent parts, one for each index of `groups`. A program takes and returns all parts, laid end to end along the dimension named above; each array names one. Nothing has to cross between parts.
Inputs may be any that keep to these rules, and one draw needn't show every extreme that they name: block_table names table t exactly ceil(train_rows[t] / 512) times; the largest table has 24 full blocks. `block_table`: every table is named at least once.
All inputs are finite; a program needn't handle non-finite values.
Results may differ from a plain program's by a relative error of at most 0.0075.
Values may be sent and summed in bfloat16 or wider, within the bound.
No kernel may reach another device: no remote copies, remote signals or barrier semaphores. Data moves between devices by JAX's collectives and lax.ppermute only.
A program may use at most 64 MiB of HBM per device.

v0:
```python
import math

import jax
import jax.numpy as jnp
from jax import lax
from jax.sharding import PartitionSpec as P

HD = 64
TEST = 128
BLK = 512


NEG = -1e30


def combined_all(value, axis, join):
    pieces = jax.tree.map(lambda part: lax.all_gather(part, axis), value)
    head = jax.tree.map(lambda part: part[0], pieces)
    tail = jax.tree.map(lambda part: part[1:], pieces)
    total, _ = lax.scan(lambda total, piece: (join(total, piece), None), head, tail)
    return total


def table_lookup(positions, entries):
    matches = positions[:, None] == jnp.arange(entries.shape[0], dtype=jnp.int32)[None, :]
    return jnp.sum(jnp.where(matches, entries[None, :], 0), axis=1)


def merge_two(former, latter):
    new_peak = jnp.maximum(former[0], latter[0])
    return (
        new_peak,
        former[1] * jnp.exp(former[0] - new_peak) + latter[1] * jnp.exp(latter[0] - new_peak),
    )


def contract_rows(left, right):
    return lax.dot_general(
        left, right, (((0,), (0,)), ((), ())), preferred_element_type=jnp.float32
    )


def contract_features(left, right):
    return lax.dot_general(
        left, right, (((1,), (1,)), ((), ())), preferred_element_type=jnp.float32
    )


def local(query_rows, key_rows, value_rows, cotangent, train_rows, test_rows, block_table):
    device = lax.axis_index(("rows", "pair"))
    local_rows = query_rows.shape[0]
    features = query_rows.shape[1]
    head_count = features // HD
    blocks = key_rows.shape[0] // BLK
    tables = train_rows.shape[0]
    query_count = tables * TEST
    stacked = head_count * TEST
    score_scale = 1.0 / math.sqrt(HD)
    row_ids = device * local_rows + jnp.arange(local_rows, dtype=jnp.int32)
    query_live = row_ids % TEST < table_lookup(row_ids // TEST, test_rows)
    live_grads = jnp.where(query_live[:, None], cotangent, jnp.zeros_like(cotangent))
    all_queries, all_grads = (
        lax.all_gather(query_rows, ("rows", "pair"), axis=0, tiled=True),
        lax.all_gather(live_grads, ("rows", "pair"), axis=0, tiled=True),
    )
    head_of_feature = jnp.arange(features, dtype=jnp.int32) // HD
    head_mask = head_of_feature[None, :] == jnp.arange(head_count, dtype=jnp.int32)[:, None]

    def expand(rows):
        shaped = rows.reshape(tables, 1, TEST, features)
        masked = jnp.where(head_mask[None, :, None, :], shaped, jnp.zeros_like(shaped))
        return masked.reshape(tables, stacked, features)

    def collapse(product):
        shaped = product.reshape(head_count, TEST, features)
        return jnp.sum(jnp.where(head_mask[:, None, :], shaped, 0.0), axis=0)

    spread_queries = expand(all_queries)
    spread_grads = expand(all_grads)
    block_ids = jnp.arange(block_table.shape[0], dtype=jnp.int32)
    my_blocks = device * blocks + jnp.arange(blocks, dtype=jnp.int32)
    block_owner = lax.dynamic_slice_in_dim(block_table, device * blocks, blocks)
    earlier = (block_table[None, :] == block_owner[:, None]) & (
        block_ids[None, :] < my_blocks[:, None]
    )
    ordinal = jnp.sum(jnp.where(earlier, 1, 0), axis=1).astype(jnp.int32)
    live_keys = table_lookup(block_owner, train_rows) - ordinal * BLK
    key_blocks = key_rows.reshape(blocks, BLK, features)
    value_blocks = value_rows.reshape(blocks, BLK, features)
    key_index = jnp.arange(BLK, dtype=jnp.int32)
    block_inputs = (block_owner, live_keys, key_blocks, value_blocks)

    def block_scores(which_table, live_count, key_block):
        query_block = spread_queries[which_table]
        raw_scores = contract_features(query_block, key_block) * score_scale
        return (query_block, jnp.where(key_index[None, :] < live_count, raw_scores, NEG))

    def stats_step(running, inputs):
        which_table, live_count, key_block, value_block = inputs
        _, scores = block_scores(which_table, live_count, key_block)
        block_peak = jnp.max(scores, axis=1)
        weights = jnp.exp(scores - block_peak[:, None])
        block_mass = jnp.sum(weights, axis=1)
        old_peak = running[0][which_table]
        old_mass = running[1][which_table]
        new_peak = jnp.maximum(old_peak, block_peak)
        old_weight = jnp.exp(old_peak - new_peak)
        new_weight = jnp.exp(block_peak - new_peak)
        updated = [
            running[0].at[which_table].set(new_peak),
            running[1].at[which_table].set(old_mass * old_weight + block_mass * new_weight),
        ]
        return (tuple(updated), None)

    initial = [
        jnp.full((tables, stacked), NEG, jnp.float32),
        jnp.zeros((tables, stacked), jnp.float32),
    ]
    result, _ = lax.scan(stats_step, tuple(initial), block_inputs)
    peaks, masses = result
    peaks, masses = combined_all((peaks, masses), ("rows", "pair"), merge_two)

    def inner_step(running, inputs):
        which_table, live_count, key_block, value_block = inputs
        _, scores = block_scores(which_table, live_count, key_block)
        dprobs = contract_features(spread_grads[which_table], value_block)
        block_peak = jnp.max(scores, axis=1)
        weights_low = jnp.exp(scores - block_peak[:, None]).astype(jnp.bfloat16).astype(jnp.float32)
        term = (
            jnp.sum(weights_low * dprobs, axis=1)
            * jnp.exp(block_peak - peaks[which_table])
            / masses[which_table]
        )
        return (running.at[which_table].add(term), None)

    inner_terms, _ = lax.scan(inner_step, jnp.zeros((tables, stacked), jnp.float32), block_inputs)
    inner = lax.psum(inner_terms, ("rows", "pair"))

    def grad_step(running, inputs):
        which_table, live_count, key_block, value_block = inputs
        query_block, scores = block_scores(which_table, live_count, key_block)
        grad_block = spread_grads[which_table]
        probs = jnp.exp(scores - peaks[which_table][:, None]) / masses[which_table][:, None]
        dprobs = contract_features(grad_block, value_block)
        probs_low = probs.astype(jnp.bfloat16)
        value_part = contract_rows(probs_low, grad_block)
        dscores = (probs * (dprobs - inner[which_table][:, None])).astype(jnp.bfloat16)
        key_part = contract_rows(dscores, query_block) * score_scale
        query_part = (
            collapse(jnp.dot(dscores, key_block, preferred_element_type=jnp.float32)) * score_scale
        )
        running = running.at[which_table].add(query_part)
        return (running, (key_part.astype(jnp.bfloat16), value_part.astype(jnp.bfloat16)))

    query_terms, (key_parts, value_parts) = lax.scan(
        grad_step, jnp.zeros((tables, TEST, features), jnp.float32), block_inputs
    )
    query_total = lax.psum_scatter(
        query_terms.reshape(query_count, features),
        ("rows", "pair"),
        scatter_dimension=0,
        tiled=True,
    )
    return (
        query_total.astype(jnp.bfloat16),
        key_parts.reshape(blocks * BLK, features),
        value_parts.reshape(blocks * BLK, features),
    )


def solution(mesh):
    in_specs = (
        P(("groups", "rows", "pair"), "mp"),
        P(("groups", "rows", "pair"), "mp"),
        P(("groups", "rows", "pair"), "mp"),
        P(("groups", "rows", "pair"), "mp"),
        P("groups"),
        P("groups"),
        P("groups"),
    )
    out_specs = (
        P(("groups", "rows", "pair"), "mp"),
        P(("groups", "rows", "pair"), "mp"),
        P(("groups", "rows", "pair"), "mp"),
    )
    return jax.shard_map(local, mesh=mesh, in_specs=in_specs, out_specs=out_specs, check_vma=False)
```

profile of v0, /device:TPU:0, one launch (start us, length us, event | category | flops | bytes accessed | tf_op | source)
XLA Modules:
  0.0 357.1 jit_solution(11898617688526695184)
XLA Ops:
  11.4 16.6 %all_gather.23 = bf16[1024,256]{1,0:T(8,128)(2,1)S(1)} all-gather(bf16[128,256]{1,0:T(8,128)(2,1)S(1)} %broadcast_select_fusion.3), channel_id=1, replica_groups=mesh['groups'=2,'rows'=4,'mp'=2,'pair'=2] {'rows','pair'}, dimensions={0}, use_global_device_ids=true | all-gather | bytes 589824 | tf_op jit(solution)/shard_map/all_gather | solution.py:64
  28.0 14.9 %all_gather.18 = bf16[1024,256]{1,0:T(8,128)(2,1)S(1)} all-gather(bf16[128,256]{1,0:T(8,128)(2,1)} %param.23), channel_id=1, replica_groups=mesh['groups'=2,'rows'=4,'mp'=2,'pair'=2] {'rows','pair'}, dimensions={0}, use_global_device_ids=true | all-gather | bytes 589824 | tf_op jit(solution)/shard_map/all_gather | solution.py:63
  42.9 1.7 bitcast_select_fusion
  44.6 55.1 %while.60 = (s32[]{:T(128)}, f32[8,512]{1,0:T(8,128)S(1)}, f32[8,512]{1,0:T(8,128)S(1)}, s32[8]{0:T(128)S(1)}, s32[8]{0:T(128)S(1)}, /*index=5*/bf16[8,512,256]{...) while((s32[]{:T(128)}, f32[8,512]{1,0:T(8,128)S(1)}, ...), condition=%wide.region_7.8_spmd.clone.clone, body=%wide.region_3.7_spmd.clone.sunk.clone | while | flops 135532048 | bytes 2649797 | solution.py:119
  49.2 1.4 fusion.112
  56.0 1.4 fusion.112
  62.9 1.4 fusion.112
  69.8 1.4 fusion.112
  76.7 1.4 fusion.112
  83.6 1.4 fusion.112
  90.5 1.4 fusion.112
  97.4 1.4 fusion.112
  99.8 14.2 %all-gather.1 = f32[64,512]{1,0:T(8,128)S(1)} all-gather(f32[8,512]{1,0:T(8,128)S(1)} %get-tuple-element.259), channel_id=3, replica_groups=mesh['groups'=2,'rows'=4,'mp'=2,'pair'=2] {'rows','pair'}, dimensions={0}, use_global_device_ids=true | all-gather | bytes 147456 | tf_op jit(solution)/shard_map/all_gather | solution.py:17
  114.0 14.0 %all-gather = f32[64,512]{1,0:T(8,128)S(1)} all-gather(f32[8,512]{1,0:T(8,128)S(1)} %get-tuple-element.258), channel_id=2, replica_groups=mesh['groups'=2,'rows'=4,'mp'=2,'pair'=2] {'rows','pair'}, dimensions={0}, use_global_device_ids=true | all-gather | bytes 147456 | tf_op jit(solution)/shard_map/all_gather | solution.py:17
  128.3 61.7 %while.61 = (s32[]{:T(128)}, f32[8,512]{1,0:T(8,128)S(1)}, s32[8]{0:T(128)S(1)}, s32[8]{0:T(128)S(1)}, bf16[8,512,256]{2,1,0:T(8,128)(2,1)}, /*index=5*/bf16[8,5...) while((s32[]{:T(128)}, f32[8,512]{1,0:T(8,128)S(1)}, ...), condition=%wide.region_14.15_spmd.clone.clone, body=%wide.region_10.14_spmd.clone.sunk.clone | while | flops 270534656 | bytes 3170525 | solution.py:136
  132.6 1.4 fusion.115
  134.0 1.3 fusion.116
  140.3 1.4 fusion.115
  141.7 1.3 fusion.116
  148.1 1.4 fusion.115
  149.4 1.3 fusion.116
  155.8 1.4 fusion.115
  163.5 1.4 fusion.115
  171.2 1.4 fusion.115
  172.6 1.3 fusion.116
  178.9 1.4 fusion.115
  180.3 1.3 fusion.116
  186.6 1.4 fusion.115
  190.1 29.2 %psum.7 = f32[8,512]{1,0:T(8,128)S(1)} all-reduce(f32[8,512]{1,0:T(8,128)S(1)} %get-tuple-element.262), channel_id=1, replica_groups=mesh['groups'=2,'rows'=4,'mp'=2,'pair'=2] {'rows','pair'}, use_global_device_ids=true, to_apply=%region_15.16 | all-reduce | flops 4096 | bytes 32768 | tf_op jit(solution)/shard_map/psum | solution.py:137
  219.4 97.7 %while.62 = (s32[]{:T(128)}, f32[8,128,256]{2,1,0:T(8,128)S(1)}, bf16[8,512,256]{2,1,0:T(8,128)(2,1)}, bf16[8,512,256]{2,1,0:T(8,128)(2,1)}, s32[8]{0:T(128)S(1)...) while((s32[]{:T(128)}, f32[8,128,256]{2,1,0:T(8,128)S(1)}, ...), condition=%wide.region_19.20_spmd.clone.clone, body=%wide.region_16.19_spmd.clone.sunk.clone | while | flops 673908224 | bytes 7627025 | solution.py:155
  223.8 1.5 fusion.127
  229.6 2.0 fusion.131
  236.0 1.5 fusion.127
  241.8 2.0 fusion.131
  248.3 1.5 fusion.127
  254.0 2.0 fusion.131
  260.5 1.5 fusion.127
  266.2 2.0 fusion.131
  272.7 1.5 fusion.127
  278.4 2.0 fusion.131
  284.9 1.5 fusion.127
  290.6 2.0 fusion.131
  297.1 1.5 fusion.127
  302.9 2.0 fusion.131
  309.3 1.5 fusion.127
  315.1 2.0 fusion.131
  318.1 30.6 %reduce-scatter.2.cloned.1.call-done = f32[128,256]{1,0:T(8,128)} async-done(((f32[1024,256]{1,0:T(8,128)}), f32[128,256]{1,0:T(8,128)}) %reduce-scatter.2.cloned.1.call-update) | async-done | bytes 131088 | tf_op jit(solution)/shard_map/reduce_scatter | solution.py:158
  348.7 1.5 convert_element_type.21
  (241 shorter events, 118.2 us)
Async XLA Ops:
  7.2 341.5 %reduce-scatter.2.cloned.1.call-start = ((), (), s32[]{:S(2)}) async-start(), calls=%async_computation.1 | async-start | bytes 1179648 | tf_op jit(solution)/shard_map/reduce_scatter | solution.py:158
  42.9 1.7 copy-start.1
  128.3 91.1 %copy-start.2 = (s32[3]{0:T(128)S(1)}, s32[3]{0:T(128)}, u32[]{:S(2)}) copy-start(s32[3]{0:T(128)} %constant.200.clone.2) | copy-start | bytes 40
  317.1 1.0 copy-start
Sparse Core Ops, SparseCore 0:
  318.2 30.4 reduce-scatter.1
where the time goes:
time: 360 us; the launch traced here: 357 us
  matrix products  89.4 us (25%)
  blocking collectives  89 us (25%)
  other arithmetic  55.6 us (15%)
  loops' own time  45.8 us (13%)
  local copies, waits for them, and re-layouts  32.5 us (9%)
  waiting for transfers between devices  30.6 us (8%)
  between operations  14.2 us (4%)
    dot_general x40, matrix products, contract_features(): lax.dot_general(left, right, (((1,), (1,)), ((), ())), preferred_element_...  54.7 us
    reduce_scatter x1, waiting for transfers between devices, local(): lax.psum_scatter(query_terms.reshape(query_count, features), ('rows', 'pa...  30.6 us
    psum x1, blocking collectives, local(): inner = lax.psum(inner_terms, ('rows', 'pair'))  29.2 us
    dynamic_slice x48, local copies, waits for them, and re-layouts, local(): result, _ = lax.scan(stats_step, tuple(initial), block_inputs)  29 us
    all_gather x2, blocking collectives, combined_all(): pieces = jax.tree.map(lambda part: lax.all_gather(part, axis), value)  28.2 us
    another operation x42, other arithmetic  27.8 us
    dot_general x16, matrix products, contract_rows(): lax.dot_general(left, right, (((0,), (0,)), ((), ())), preferred_element_...  24.6 us
    all_gather x1, blocking collectives, local(): lax.all_gather(live_grads, ('rows', 'pair'), axis=0, tiled=True)  16.6 us
  transfers between devices with their start and end apart: 1, of which 1 were waited for; matrix products, arithmetic and copies ran while one was open for 0% of the time, Pallas kernels for 0%

commit v1 on v0

v1 whole, which is shorter than its diff:
```python
import math

import jax
import jax.numpy as jnp
from jax import lax
from jax.experimental import pallas as pl
from jax.experimental.pallas import tpu as pltpu
from jax.sharding import PartitionSpec as P

HD = 64
TEST = 128
BLK = 512
LANES = 128
WIDE = 2 * TEST

NEG = -1e30
SCORE_SCALE = 1.0 / math.sqrt(HD)
LOG2_SCALE = SCORE_SCALE * math.log2(math.e)
RP = ("rows", "pair")
PAIR = [(0, 1), (1, 0)]


def table_lookup(positions, entries):
    matches = positions[:, None] == jnp.arange(entries.shape[0], dtype=jnp.int32)[None, :]
    return jnp.sum(jnp.where(matches, entries[None, :], 0), axis=1)


def params(mib):
    return pltpu.CompilerParams(
        dimension_semantics=("arbitrary",), vmem_limit_bytes=mib * 1024 * 1024
    )


def two_heads(rows):
    feature = lax.broadcasted_iota(jnp.int32, rows.shape, 0)
    zero = jnp.zeros_like(rows)
    return jnp.concatenate(
        [jnp.where(feature < HD, rows, zero), jnp.where(feature < HD, zero, rows)], axis=1
    )


def scores_kernel(features, piece_slots, owner, live, testn, slot, *refs):
    count = len(piece_slots)
    pieces = refs[:count]
    key_ref, value_ref, qgt_ref, e_ref, u_ref, blk_ref, tab_ref, qg_s, sem = refs[count:]
    b = pl.program_id(0)
    table = owner[b]

    @pl.when(b == 0)
    def _():
        copies = []
        for n, (start, size) in enumerate(piece_slots):
            copies.append(
                pltpu.make_async_copy(pieces[n], qg_s.at[pl.ds(start, size)], sem.at[n])
            )
        for copy in copies:
            copy.start()
        tab_ref[0] = jnp.full(tab_ref.shape[1:], NEG, jnp.float32)
        tab_ref[1] = jnp.zeros(tab_ref.shape[1:], jnp.float32)
        tab_ref[2] = jnp.zeros(tab_ref.shape[1:], jnp.float32)
        for copy in copies:
            copy.wait()

    turned = qg_s[slot[table]].T
    query = lax.broadcasted_iota(jnp.int32, (LANES, TEST), 1)
    grad_live = query < testn[table]
    key_live = lax.broadcasted_iota(jnp.int32, (BLK, WIDE), 0) < live[b]
    for p in range(features // LANES):
        at = slice(p * LANES, (p + 1) * LANES)
        wide = slice(p * WIDE, (p + 1) * WIDE)
        q_t = turned[at]
        g_t = turned[features + p * LANES : features + (p + 1) * LANES]
        g_t = jnp.where(grad_live, g_t, jnp.zeros_like(g_t))
        qgt_ref[0, at, :] = q_t
        qgt_ref[0, pl.ds(features + p * LANES, LANES), :] = g_t
        scores = jnp.dot(key_ref[:, at], two_heads(q_t), preferred_element_type=jnp.float32)
        dprobs = jnp.dot(value_ref[:, at], two_heads(g_t), preferred_element_type=jnp.float32)
        scores = jnp.where(key_live, scores, NEG)
        peak = jnp.max(scores, axis=0, keepdims=True) * LOG2_SCALE
        weights = jnp.exp2(scores * LOG2_SCALE - peak)
        mass = jnp.sum(weights, axis=0, keepdims=True)
        part = jnp.sum(weights * dprobs, axis=0, keepdims=True)
        e_ref[0, :, wide] = weights.astype(jnp.bfloat16)
        u_ref[0, :, wide] = (weights * (dprobs - part / mass)).astype(jnp.bfloat16)
        blk_ref[0, pl.ds(b, 1), wide] = peak
        blk_ref[1, pl.ds(b, 1), wide] = mass
        blk_ref[2, pl.ds(b, 1), wide] = part
        old = tab_ref[0, pl.ds(table, 1), wide]
        new = jnp.maximum(old, peak)
        old_weight = jnp.exp2(old - new)
        new_weight = jnp.exp2(peak - new)
        tab_ref[0, pl.ds(table, 1), wide] = new
        tab_ref[1, pl.ds(table, 1), wide] = (
            tab_ref[1, pl.ds(table, 1), wide] * old_weight + mass * new_weight
        )
        tab_ref[2, pl.ds(table, 1), wide] = (
            tab_ref[2, pl.ds(table, 1), wide] * old_weight + part * new_weight
        )


def block_scores(owner, live, testn, slot, pieces, key_rows, value_rows):
    features = key_rows.shape[1]
    blocks = owner.shape[0]
    tables = testn.shape[0]
    stacked = features // HD * TEST
    starts, total = [], 0
    for piece in pieces:
        starts.append((total, piece.shape[0]))
        total += piece.shape[0]
    row_block = pl.BlockSpec((BLK, features), lambda b, *_: (b, 0))
    block_out = lambda *shape: pl.BlockSpec((1,) + shape, lambda b, *_: (b, 0, 0))
    whole = lambda *shape: pl.BlockSpec(shape, lambda b, *_: (0,) * len(shape))
    return pl.pallas_call(
        lambda *refs: scores_kernel(features, tuple(starts), *refs),
        grid_spec=pltpu.PrefetchScalarGridSpec(
            num_scalar_prefetch=4,
            grid=(blocks,),
            in_specs=[pl.BlockSpec(memory_space=pl.ANY) for _ in pieces]
            + [row_block, row_block],
            out_specs=[
                block_out(2 * features, TEST),
                block_out(BLK, stacked),
                block_out(BLK, stacked),
                whole(3, blocks, stacked),
                whole(3, tables, stacked),
            ],
            scratch_shapes=[
                pltpu.VMEM((tables, TEST, 2 * features), jnp.bfloat16),
                pltpu.SemaphoreType.DMA((len(pieces),)),
            ],
        ),
        out_shape=[
            jax.ShapeDtypeStruct((blocks, 2 * features, TEST), jnp.bfloat16),
            jax.ShapeDtypeStruct((blocks, BLK, stacked), jnp.bfloat16),
            jax.ShapeDtypeStruct((blocks, BLK, stacked), jnp.bfloat16),
            jax.ShapeDtypeStruct((3, blocks, stacked), jnp.float32),
            jax.ShapeDtypeStruct((3, tables, stacked), jnp.float32),
        ],
        compiler_params=params(40),
        name="block_scores",
    )(owner, live, testn, slot, *pieces, key_rows, value_rows)


def query_sums_kernel(features, key_ref, e_ref, u_ref, out_ref):
    for p in range(features // LANES):
        at = slice(p * LANES, (p + 1) * LANES)
        wide = slice(p * WIDE, (p + 1) * WIDE)
        keys = key_ref[:, at]
        for n, ref in enumerate((u_ref, e_ref)):
            product = lax.dot_general(
                keys, ref[0, :, wide], (((0,), (0,)), ((), ())), preferred_element_type=jnp.float32
            )
            out_ref[0, n, pl.ds(p * LANES, HD), :] = product[:HD, :TEST]
            out_ref[0, n, pl.ds(p * LANES + HD, HD), :] = product[HD:, TEST:]


def query_sums(key_rows, e_all, u_all):
    features = key_rows.shape[1]
    blocks, _, stacked = e_all.shape
    return pl.pallas_call(
        lambda *refs: query_sums_kernel(features, *refs),
        grid=(blocks,),
        in_specs=[
            pl.BlockSpec((BLK, features), lambda b: (b, 0)),
            pl.BlockSpec((1, BLK, stacked), lambda b: (b, 0, 0)),
            pl.BlockSpec((1, BLK, stacked), lambda b: (b, 0, 0)),
        ],
        out_specs=pl.BlockSpec((1, 2, features, TEST), lambda b: (b, 0, 0, 0)),
        out_shape=jax.ShapeDtypeStruct((blocks, 2, features, TEST), jnp.float32),
        compiler_params=params(40),
        name="query_sums",
    )(key_rows, e_all, u_all)


def merged(pieces):
    peak = pieces[0][0]
    for piece in pieces[1:]:
        peak = jnp.maximum(peak, piece[0])
    mass = part = 0.0
    for piece in pieces:
        weight = jnp.exp2(piece[0] - peak)
        mass = mass + piece[1] * weight
        part = part + piece[2] * weight
    return peak, mass, part


def merge_kernel(a_ref, b_ref, out_ref):
    out_ref[0], out_ref[1], out_ref[2] = merged([a_ref, b_ref])


def merge_stats(a, b):
    return pl.pallas_call(
        merge_kernel, out_shape=jax.ShapeDtypeStruct(a.shape, jnp.float32), name="merge_stats"
    )(a, b)


def query_grad_kernel(features, count, owner, slot, *refs):
    pieces = refs[:count]
    blk_ref, ab_ref = refs[count : count + 2]
    outs = refs[count + 2 : -2]
    c_ref, d_ref, *q_refs = outs
    tab_s, acc_s = refs[-2:]
    blocks = blk_ref.shape[1]
    tab_s[0], tab_s[1], tab_s[2] = merged(pieces)
    acc_s[...] = jnp.zeros_like(acc_s)
    for b in range(blocks):
        table = owner[b]
        at = slot[table]
        mass = tab_s[1, pl.ds(table, 1), :]
        c = jnp.exp2(blk_ref[0, b : b + 1, :] - tab_s[0, pl.ds(table, 1), :]) / mass
        shift = blk_ref[2, b : b + 1, :] / blk_ref[1, b : b + 1, :]
        d = c * (shift - tab_s[2, pl.ds(table, 1), :] / mass)
        c_ref[b : b + 1, :] = c
        d_ref[b : b + 1, :] = d
        for h in range(features // HD):
            rows = slice(h * HD, (h + 1) * HD)
            lanes = slice(h * TEST, (h + 1) * TEST)
            acc_s[at, rows, :] += c[:, lanes] * ab_ref[b, 0, rows, :] + d[:, lanes] * ab_ref[b, 1, rows, :]
    tables = acc_s.shape[0]
    per = tables // len(q_refs)
    for n in range(tables):
        ref = q_refs[n // per]
        ref[n % per] = (acc_s[n] * SCORE_SCALE).T.astype(ref.dtype)


def query_grads(owner, slot, pieces, blk, ab, q_dtypes):
    blocks, _, features, _ = ab.shape
    tables = slot.shape[0]
    stacked = blk.shape[2]
    per = tables // len(q_dtypes)
    vmem = pl.BlockSpec(memory_space=pltpu.VMEM)
    smem = pl.BlockSpec(memory_space=pltpu.SMEM)
    return pl.pallas_call(
        lambda *refs: query_grad_kernel(features, len(pieces), *refs),
        in_specs=[smem, smem] + [vmem] * (len(pieces) + 2),
        out_specs=[vmem] * (2 + len(q_dtypes)),
        out_shape=[
            jax.ShapeDtypeStruct((blocks, stacked), jnp.float32),
            jax.ShapeDtypeStruct((blocks, stacked), jnp.float32),
        ]
        + [jax.ShapeDtypeStruct((per, TEST, features), dtype) for dtype in q_dtypes],
        scratch_shapes=[
            pltpu.VMEM((3, tables, stacked), jnp.float32),
            pltpu.VMEM((tables, features, TEST), jnp.float32),
        ],
        compiler_params=pltpu.CompilerParams(vmem_limit_bytes=40 * 1024 * 1024),
        name="query_grads",
    )(owner, slot, *pieces, blk, ab)


def row_grads_kernel(features, qgt_ref, c_ref, d_ref, e_ref, u_ref, dk_ref, dv_ref):
    b = pl.program_id(0)
    turned = (((1,), (1,)), ((), ()))
    for p in range(features // LANES):
        at = slice(p * LANES, (p + 1) * LANES)
        wide = slice(p * WIDE, (p + 1) * WIDE)
        c = c_ref[pl.ds(b, 1), wide]
        d = d_ref[pl.ds(b, 1), wide]
        q_t = two_heads(qgt_ref[0, at, :].astype(jnp.float32))
        g_t = two_heads(qgt_ref[0, pl.ds(features + p * LANES, LANES), :].astype(jnp.float32))
        for_u = (q_t * (c * SCORE_SCALE)).astype(jnp.bfloat16)
        for_e = jnp.concatenate([g_t * c, q_t * (d * SCORE_SCALE)], axis=0).astype(jnp.bfloat16)
        from_e = lax.dot_general(e_ref[0, :, wide], for_e, turned, preferred_element_type=jnp.float32)
        from_u = lax.dot_general(u_ref[0, :, wide], for_u, turned, preferred_element_type=jnp.float32)
        dv_ref[:, at] = from_e[:, :LANES].astype(jnp.bfloat16)
        dk_ref[:, at] = (from_u + from_e[:, LANES:]).astype(jnp.bfloat16)


def row_grads(qgt, c, d, e_all, u_all):
    blocks, _, stacked = e_all.shape
    features = qgt.shape[1] // 2
    one = lambda *shape: pl.BlockSpec((1,) + shape, lambda b: (b, 0, 0))
    whole = pl.BlockSpec((blocks, stacked), lambda b: (0, 0))
    rows = pl.BlockSpec((BLK, features), lambda b: (b, 0))
    return pl.pallas_call(
        lambda *refs: row_grads_kernel(features, *refs),
        grid=(blocks,),
        in_specs=[one(2 * features, TEST), whole, whole, one(BLK, stacked), one(BLK, stacked)],
        out_specs=[rows, rows],
        out_shape=[jax.ShapeDtypeStruct((blocks * BLK, features), jnp.bfloat16)] * 2,
        compiler_params=params(40),
        name="row_grads",
    )(qgt, c, d, e_all, u_all)


def local(small, query_rows, key_rows, value_rows, cotangent, train_rows, test_rows, block_table):
    chip = lax.axis_index("rows").astype(jnp.int32)
    core = lax.axis_index("pair").astype(jnp.int32)
    device = lax.axis_index(RP).astype(jnp.int32)
    local_rows, features = query_rows.shape
    blocks = key_rows.shape[0] // BLK
    tables = train_rows.shape[0]
    stacked = features // HD * TEST

    my_blocks = device * blocks + jnp.arange(blocks, dtype=jnp.int32)
    block_ids = jnp.arange(block_table.shape[0], dtype=jnp.int32)
    owner = lax.dynamic_slice_in_dim(block_table, device * blocks, blocks)
    earlier = (block_table[None, :] == owner[:, None]) & (block_ids[None, :] < my_blocks[:, None])
    ordinal = jnp.sum(jnp.where(earlier, 1, 0), axis=1).astype(jnp.int32)
    live = jnp.minimum(table_lookup(owner, train_rows) - ordinal * BLK, BLK).astype(jnp.int32)
    ids = jnp.arange(tables, dtype=jnp.int32)

    both = jnp.concatenate([query_rows, cotangent], axis=1)
    if small:
        cross = [(2 * z + c, 2 * (z ^ (1 + c)) + c) for z in range(4) for c in range(2)]
        far = [(2 * z + c, 2 * (z ^ 3) + c) for z in range(4) for c in range(2)]
        mine = chip ^ (1 + core)
        other = chip ^ (2 - core)
        table_chip, table_core = ids // 2, ids % 2
        is_far = jnp.where(table_core == core, 6, 7)
        slot_in = jnp.where(
            table_chip == chip,
            table_core,
            jnp.where(
                table_chip == mine, 2 + table_core, jnp.where(table_chip == other, 4 + table_core, is_far)
            ),
        ).astype(jnp.int32)
        not_mine = jnp.where(table_core == core, 0, 1)
        slot_out = jnp.where(
            table_chip == mine,
            not_mine,
            jnp.where(
                table_chip == other,
                5 - not_mine,
                jnp.where(table_chip == chip, 3 + 4 * not_mine, 2 + 4 * not_mine),
            ),
        ).astype(jnp.int32)

        own = both.reshape(1, TEST, 2 * features)
        from_far = lax.ppermute(own, RP, far)
        chip_rows = lax.all_gather(own, "pair", axis=0, tiled=True)
        from_mine = lax.ppermute(chip_rows, RP, cross)
        from_other = lax.ppermute(from_mine, "pair", PAIR)
        peer_far = lax.ppermute(from_far, "pair", PAIR)
        pieces = [chip_rows, from_mine, from_other, from_far, peer_far]
    else:
        slot_in = slot_out = ids
        everyone = lax.all_gather(both, RP, axis=0, tiled=True)
        pieces = [everyone.reshape(tables, TEST, 2 * features)]

    qgt, e_all, u_all, blk, tab = block_scores(
        owner, live, test_rows, slot_in, pieces, key_rows, value_rows
    )
    if small:
        chip_tab = merge_stats(tab, lax.ppermute(tab, "pair", PAIR))
        far_tab = lax.ppermute(chip_tab, RP, far)
        mine_tab = lax.ppermute(chip_tab, RP, cross)
        other_tab = lax.ppermute(mine_tab, "pair", PAIR)
        stats = [chip_tab, far_tab, mine_tab, other_tab]
        dtypes = [jnp.float32, jnp.bfloat16]
    else:
        peak = lax.pmax(tab[0], RP)
        sums = lax.psum(tab[1:] * jnp.exp2(tab[0] - peak)[None], RP)
        stats = [jnp.concatenate([peak[None], sums], axis=0)]
        dtypes = [jnp.float32]
    ab = query_sums(key_rows, e_all, u_all)
    c, d, *q_terms = query_grads(owner, slot_out, stats, blk, ab, dtypes)
    if small:
        keep, send = q_terms
        total = keep + lax.ppermute(send, "pair", PAIR).astype(jnp.float32)
        to_mine = total[:2].astype(jnp.bfloat16)
        to_far = total[2].astype(jnp.bfloat16)
        got_far = lax.ppermute(to_far, RP, far)
        got_mine = lax.ppermute(to_mine, RP, cross)
        got_other = lax.ppermute(got_mine[1], "pair", PAIR)
        wide = lambda value: value.astype(jnp.float32)
        query_grad = total[3] + wide(got_far) + wide(got_mine[0]) + wide(got_other)
    else:
        query_grad = lax.psum_scatter(
            q_terms[0].reshape(tables * TEST, features), RP, scatter_dimension=0, tiled=True
        )
    key_grad, value_grad = row_grads(qgt, c, d, e_all, u_all)
    return query_grad.astype(jnp.bfloat16), key_grad, value_grad


def solution(mesh):
    sizes = mesh.shape
    tables_of_rows = P(("groups", "rows", "pair"), "mp")
    in_specs = (tables_of_rows,) * 4 + (P("groups"),) * 3
    out_specs = (tables_of_rows,) * 3

    def run(query_rows, *rest):
        local_rows = query_rows.shape[0] // (sizes["groups"] * sizes["rows"] * sizes["pair"])
        small = sizes["rows"] == 4 and sizes["pair"] == 2 and local_rows == TEST
        return jax.shard_map(
            lambda *args: local(small, *args),
            mesh=mesh,
            in_specs=in_specs,
            out_specs=out_specs,
            check_vma=False,
        )(query_rows, *rest)

    return run
```

time: 360 us -> 72.5 us (0.20)
  matrix products: 89.4 us -> 0 us
  blocking collectives: 89 us -> 2.07 us
  other arithmetic: 55.6 us -> 2.42 us
  loops' own time: 45.8 us -> 0 us
  waiting for transfers between devices: 30.6 us -> 10 us
  Pallas kernels: 0 us -> 19.7 us
  starting transfers between devices: 0.04 us -> 18.7 us
  local copies, waits for them, and re-layouts: 32.5 us -> 17.8 us
  between operations: 14.2 us -> 0.82 us
    dot_general x64 -> x0, matrix products: 89.4 us -> none  [the longest x40 54.7 us: contract_features(): lax.dot_general(left, right, (((1,), (1,)), ((), ())), preferred_element_...]
    all_gather x4 -> x1, blocking collectives: 59.7 us -> 2.07 us  [local(): chip_rows = lax.all_gather(own, 'pair', axis=0, tiled=True)]
    another operation x4 -> x0, loops' own time: 45.8 us -> none  [the longest x1 15.3 us: local(): result, _ = lax.scan(stats_step, tuple(initial), block_inputs)]
    reduce_scatter x1 -> x0, waiting for transfers between devices: 30.6 us -> none  [local(): lax.psum_scatter(query_terms.reshape(query_count, features), ('rows', 'pa...]
    psum x1 -> x0, blocking collectives: 29.2 us -> none  [local(): inner = lax.psum(inner_terms, ('rows', 'pair'))]
    dynamic_slice x65 -> x1, local copies, waits for them, and re-layouts: 29.9 us -> 0.73 us  [local(): owner = lax.dynamic_slice_in_dim(block_table, device * blocks, blocks)]
    another operation x42 -> x1, other arithmetic: 27.8 us -> 0.07 us  [run(): jax.shard_map(lambda *args: local(small, *args), mesh=mesh, in_specs=in_s...]
    pallas_call x0 -> x5, Pallas kernels: none -> 19.7 us  [the longest x1 9.16 us: block_scores(): pl.pallas_call(lambda *refs: scores_kernel(features, tuple(starts), *refs...]
  transfers between devices with their start and end apart: 1 -> 12, of which waited for: 1 -> 6; matrix products, arithmetic and copies ran while one was open for 0% -> 3% of each run, Pallas kernels for 0% -> 11%
where the time goes in v1:
time: 72.5 us; the launch traced here: 71.5 us
  Pallas kernels  19.7 us (27%)
  starting transfers between devices  18.7 us (26%)
  local copies, waits for them, and re-layouts  17.8 us (25%)
  waiting for transfers between devices  10 us (14%)
  other arithmetic  2.42 us (3%)
  blocking collectives  2.07 us (3%)
  between operations  0.82 us (1%)
    unnamed x37, local copies, waits for them, and re-layouts  16.2 us
    pallas_call x1, Pallas kernels, block_scores(): pl.pallas_call(lambda *refs: scores_kernel(features, tuple(starts), *refs...  9.16 us
    pallas_call x1, Pallas kernels, row_grads(): pl.pallas_call(lambda *refs: row_grads_kernel(features, *refs), grid=(blo...  5.38 us
    ppermute x1, starting transfers between devices, local(): from_other = lax.ppermute(from_mine, 'pair', PAIR)  5.2 us
    ppermute x1, starting transfers between devices, local(): got_far = lax.ppermute(to_far, RP, far)  2.94 us
    ppermute x1, starting transfers between devices, local(): from_mine = lax.ppermute(chip_rows, RP, cross)  2.93 us
    ppermute x1, waiting for transfers between devices, local(): got_mine = lax.ppermute(to_mine, RP, cross)  2.7 us
    pallas_call x1, Pallas kernels, query_sums(): pl.pallas_call(lambda *refs: query_sums_kernel(features, *refs), grid=(bl...  2.63 us
  transfers between devices with their start and end apart: 12, of which 6 were waited for; matrix products, arithmetic and copies ran while one was open for 3% of the time, Pallas kernels for 11%

profile of v1, /device:TPU:0, one launch (start us, length us, event | category | flops | bytes accessed | tf_op | source)
XLA Modules:
  0.0 71.5 jit_solution(16658244202661161809)
XLA Ops:
  0.6 0.8 %constant_dynamic-update-slice_fusion.1 = bf16[128,512]{1,0:T(8,128)(2,1)S(1)} fusion(bf16[128,256]{1,0:T(8,128)(2,1)} %param.7), kind=kLoop, calls=%fused_computation.10 | loop fusion | bytes 131072
  1.5 0.8 %constant_dynamic-update-slice_fusion = bf16[128,512]{1,0:T(8,128)(2,1)S(1)} fusion(bf16[128,512]{1,0:T(8,128)(2,1)S(1)} %constant_dynamic-update-slice_fusion.1, bf16[128,256]{1,0:T(8,128)(2,1)} %param.10), kind=kLoop, calls=%fused_computation.9 | loop fusion | bytes 131072 | tf_op jit(solution)/shard_map/concatenate | solution.py:303
  2.3 2.1 %all-gather = bf16[256,512]{1,0:T(8,128)(2,1)S(1)} all-gather(bf16[128,512]{1,0:T(8,128)(2,1)S(1)} %constant_dynamic-update-slice_fusion), channel_id=2, replica_groups=mesh['groups'=2,'rows'=4,'mp'=2,'pair'=2] {'pair'}, dimensions={0}, use_global_device_ids=true | all-gather | bytes 393216 | tf_op jit(solution)/shard_map/all_gather | solution.py:331
  4.4 2.9 %collective-permute-start = (bf16[2,128,512]{2,1,0:T(8,128)(2,1)S(1)}, bf16[2,128,512]{2,1,0:T(8,128)(2,1)S(1)}, u32[]{:S(2)}, u32[]{:S(2)}) collective-permute-start(bf16[2,128,512]{2,1,0:T(8,128)(2,1)S(1)} %bitcast.21), channel_id=1, source_target_pairs={{0,4},{1,9},{4,0},{5,13},{8,12},{9,1},{12,8},{13,5},{2,6},{3,11},{... | collective-permute-start | bytes 786440 | tf_op jit(solution)/shard_map/ppermute | solution.py:332
  7.3 2.5 %collective-permute-start.2 = (bf16[1,128,512]{2,1,0:T(8,128)(2,1)S(1)}, bf16[1,128,512]{2,1,0:T(8,128)(2,1)S(1)}, u32[]{:S(2)}, u32[]{:S(2)}) collective-permute-start(bf16[1,128,512]{2,1,0:T(8,128)(2,1)S(1)} %bitcast.23), channel_id=1, source_target_pairs={{0,12},{1,13},{4,8},{5,9},{8,4},{9,5},{12,0},{13,1},{2,14},{3,15},... | collective-permute-start | bytes 393224 | tf_op jit(solution)/shard_map/ppermute | solution.py:330
  9.8 0.7 %dynamic_slice.3.refs_0_ = s32[8]{0:T(128)S(1)} dynamic-slice(s32[64]{0:T(128)} %param.13, s32[]{:T(128)S(6)} %select_n.60), dynamic_slice_sizes={8} | dynamic-slice | bytes 68 | tf_op jit(solution)/shard_map/dynamic_slice | solution.py:297
  10.5 0.8 %select_reduce_fusion = s32[8]{0:T(128)S(1)} fusion(s32[8]{0:T(128)S(1)} %iota_add_fusion, s32[64]{0:T(128)} %param.13, s32[8]{0:T(128)S(1)} %dynamic_slice.3.refs_0_), kind=kLoop, calls=%fused_computation.11 | loop fusion | flops 2552 | bytes 352 | tf_op jit(solution)/shard_map/reduce_sum | solution.py:299
  11.4 2.5 %collective-permute-done.refs_5_ = bf16[2,128,512]{2,1,0:T(8,128)(2,1)S(1)} collective-permute-done((bf16[2,128,512]{2,1,0:T(8,128)(2,1)S(1)}, bf16[2,128,512]{2,1,0:T(8,128)(2,1)S(1)}, u32[]{:S(2)}, u32[]{:S(2)}) %collective-permute-start) | collective-permute-done | bytes 262176 | tf_op jit(solution)/shard_map/ppermute | solution.py:332
  13.8 5.2 %collective-permute-start.1 = (bf16[2,128,512]{2,1,0:T(8,128)(2,1)S(1)}, bf16[2,128,512]{2,1,0:T(8,128)(2,1)S(1)}, u32[]{:S(2)}, u32[]{:S(2)}) collective-permute-start(bf16[2,128,512]{2,1,0:T(8,128)(2,1)S(1)} %collective-permute-done.refs_5_), channel_id=1, source_target_pairs={{0,1},{1,0},{2,3},{3,2},{4,5},{5,4},{6,7},{7,6},{8,9},{9,8},{10,11... | collective-permute-start | bytes 786440 | tf_op jit(solution)/shard_map/ppermute | solution.py:333
  19.0 0.7 copy-done.8
  19.7 0.8 %select_reduce_fusion.1 = s32[8]{0:T(128)S(1)} fusion(s32[8]{0:T(128)} %param.11, s32[8]{0:T(128)S(1)} %dynamic_slice.3.refs_0_), kind=kLoop, calls=%fused_computation.13 | loop fusion | flops 184 | bytes 96 | tf_op jit(solution)/shard_map/reduce_sum | solution.py:25
  20.6 0.0 collective-permute-done.2.refs_7_
  20.6 0.1 collective-permute-start.3
  20.7 1.3 %collective-permute-done.3.refs_8_ = bf16[1,128,512]{2,1,0:T(8,128)(2,1)S(1)} collective-permute-done((bf16[1,128,512]{2,1,0:T(8,128)(2,1)S(1)}, bf16[1,128,512]{2,1,0:T(8,128)(2,1)S(1)}, u32[]{:S(2)}, u32[]{:S(2)}) %collective-permute-start.3) | collective-permute-done | bytes 131104 | tf_op jit(solution)/shard_map/ppermute | solution.py:334
  22.0 0.0 collective-permute-done.1.refs_6_
  22.0 0.7 copy-done.10
  22.7 1.6 %copy-done.5 = bf16[4096,256]{1,0:T(8,128)(2,1)S(1)} copy-done((bf16[4096,256]{1,0:T(8,128)(2,1)S(1)}, bf16[4096,256]{1,0:T(8,128)(2,1)}, u32[]{:S(2)}) %copy-start.5) | copy-done | bytes 2097176
  24.3 1.6 %copy-done.7 = bf16[4096,256]{1,0:T(8,128)(2,1)S(1)} copy-done((bf16[4096,256]{1,0:T(8,128)(2,1)S(1)}, bf16[4096,256]{1,0:T(8,128)(2,1)}, u32[]{:S(2)}) %copy-start.7) | copy-done | bytes 2097176
  25.9 0.9 %copy-done.9 = bf16[2,128,512]{2,1,0:T(8,128)(2,1)S(1)} copy-done((bf16[2,128,512]{2,1,0:T(8,128)(2,1)S(1)}, bf16[2,128,512]{2,1,0:T(8,128)(2,1)}, u32[]{:S(2)}) %copy-start.9) | copy-done | bytes 262168
  26.8 0.9 %copy-done.11 = bf16[2,128,512]{2,1,0:T(8,128)(2,1)S(1)} copy-done((bf16[2,128,512]{2,1,0:T(8,128)(2,1)S(1)}, bf16[2,128,512]{2,1,0:T(8,128)(2,1)}, u32[]{:S(2)}) %copy-start.11) | copy-done | bytes 262168
  27.8 0.7 copy-done.16
  28.4 9.2 %block_scores.1 = (bf16[8,512,128]{2,1,0:T(8,128)(2,1)S(1)}, bf16[8,512,512]{2,1,0:T(8,128)(2,1)S(1)}, bf16[8,512,512]{2,1,0:T(8,128)(2,1)}, f32[3,8,512]{2,1,0:T(8,128)S(1)}, f32[3,8,512]{2,1,0:T(8,128)S(1)}) custom-call(s32[8]{0:T(128)S(1)} %dynamic_slice.3.refs_0_, s32[8]{0:T(128)S(1)} %get-tuple-element.28.refs_1_, s32[8]{0:T(128)S(1)} %copy-done.16, ...), custom_call_target="tpu_custom_call" | custom-call | tf_op jit(solution)/shard_map/block_scores/pallas_call | solution.py:113
  37.6 2.0 %copy-done = bf16[8,512,512]{2,1,0:T(8,128)(2,1)} copy-done((bf16[8,512,512]{2,1,0:T(8,128)(2,1)}, bf16[8,512,512]{2,1,0:T(8,128)(2,1)S(1)}, u32[]{:S(2)}) %copy-start) | copy-done | bytes 4194328
  39.6 0.6 copy-done.14
  40.3 0.6 copy-done.13
  40.9 0.1 collective-permute-start.4
  41.0 1.1 %collective-permute-done.4.b_ref = f32[3,8,512]{2,1,0:T(8,128)S(1)} collective-permute-done((f32[3,8,512]{2,1,0:T(8,128)S(1)}, f32[3,8,512]{2,1,0:T(8,128)S(1)}, u32[]{:S(2)}, u32[]{:S(2)}) %collective-permute-start.4) | collective-permute-done | bytes 49184 | tf_op jit(solution)/shard_map/ppermute | solution.py:345
  42.1 0.6 copy-done.17
  42.7 1.5 %merge_stats.1.refs_2_ = f32[3,8,512]{2,1,0:T(8,128)} custom-call(f32[3,8,512]{2,1,0:T(8,128)} %copy-done.13, f32[3,8,512]{2,1,0:T(8,128)} %copy-done.17), custom_call_target="tpu_custom_call" | custom-call | tf_op jit(solution)/shard_map/merge_stats/pallas_call | solution.py:192
  44.2 1.0 %collective-permute-start.6 = (f32[3,8,512]{2,1,0:T(8,128)}, f32[3,8,512]{2,1,0:T(8,128)S(1)}, u32[]{:S(2)}, u32[]{:S(2)}) collective-permute-start(f32[3,8,512]{2,1,0:T(8,128)} %merge_stats.1.refs_2_), channel_id=1, source_target_pairs={{0,4},{1,9},{4,0},{5,13},{8,12},{9,1},{12,8},{13,5},{2,6},{3,11},{... | collective-permute-start | bytes 147464 | tf_op jit(solution)/shard_map/ppermute | solution.py:347
  45.2 2.5 %collective-permute-start.5 = (f32[3,8,512]{2,1,0:T(8,128)}, f32[3,8,512]{2,1,0:T(8,128)S(1)}, u32[]{:S(2)}, u32[]{:S(2)}) collective-permute-start(f32[3,8,512]{2,1,0:T(8,128)} %merge_stats.1.refs_2_), channel_id=1, source_target_pairs={{0,12},{1,13},{4,8},{5,9},{8,4},{9,5},{12,0},{13,1},{2,14},{3,15},... | collective-permute-start | bytes 147464 | tf_op jit(solution)/shard_map/ppermute | solution.py:346
  47.7 1.3 %collective-permute-done.6.refs_4_ = f32[3,8,512]{2,1,0:T(8,128)S(1)} collective-permute-done((f32[3,8,512]{2,1,0:T(8,128)}, f32[3,8,512]{2,1,0:T(8,128)S(1)}, u32[]{:S(2)}, u32[]{:S(2)}) %collective-permute-start.6) | collective-permute-done | bytes 49184 | tf_op jit(solution)/shard_map/ppermute | solution.py:347
  49.0 0.0 collective-permute-start.7
  49.0 2.2 %copy-done.1 = bf16[8,512,512]{2,1,0:T(8,128)(2,1)S(1)} copy-done((bf16[8,512,512]{2,1,0:T(8,128)(2,1)S(1)}, bf16[8,512,512]{2,1,0:T(8,128)(2,1)}, u32[]{:S(2)}) %copy-start.1) | copy-done | bytes 4194328
  51.2 2.2 %copy-done.3 = bf16[8,512,512]{2,1,0:T(8,128)(2,1)S(1)} copy-done((bf16[8,512,512]{2,1,0:T(8,128)(2,1)S(1)}, bf16[8,512,512]{2,1,0:T(8,128)(2,1)}, u32[]{:S(2)}) %copy-start.3) | copy-done | bytes 4194328
  53.4 2.6 %query_sums.1.refs_7_ = f32[8,2,256,128]{3,2,1,0:T(8,128)S(1)} custom-call(bf16[4096,256]{1,0:T(8,128)(2,1)S(1)} %copy-done.6, bf16[8,512,512]{2,1,0:T(8,128)(2,1)S(1)} %copy-done.1, bf16[8,512,512]{2,1,0:T(8,128)(2,1)S(1)} %copy-done.3), custom_call_target="tpu_custom_call" | custom-call | tf_op jit(solution)/shard_map/query_sums/pallas_call | solution.py:160
  56.1 0.0 collective-permute-done.5.refs_3_
  56.1 0.0 collective-permute-done.7.refs_5_
  56.1 1.1 %query_grads.1 = (f32[8,512]{1,0:T(8,128)S(1)}, f32[8,512]{1,0:T(8,128)S(1)}, f32[4,128,256]{2,1,0:T(8,128)S(1)}, bf16[4,128,256]{2,1,0:T(8,128)(2,1)S(1)}) custom-call(s32[8]{0:T(128)S(1)} %dynamic_slice.3.refs_0_, s32[8]{0:T(128)S(1)} %compare_select_fusion.7.refs_1_, f32[3,8,512]{2,1,0:T(8,128)S(1)} %copy-done.12, ...), custom_call_target="tpu_custom_call" | custom-call | tf_op jit(solution)/shard_map/query_grads/pallas_call | solution.py:233
  57.2 0.6 collective-permute-start.8
  57.8 1.2 %collective-permute-done.8 = bf16[4,128,256]{2,1,0:T(8,128)(2,1)S(1)} collective-permute-done((bf16[4,128,256]{2,1,0:T(8,128)(2,1)S(1)}, bf16[4,128,256]{2,1,0:T(8,128)(2,1)S(1)}, u32[]{:S(2)}, u32[]{:S(2)}) %collective-permute-start.8) | collective-permute-done | bytes 262176 | tf_op jit(solution)/shard_map/ppermute | solution.py:360
  58.9 0.1 fusion.5
  59.0 0.8 %collective-permute-start.10 = (bf16[2,128,256]{2,1,0:T(8,128)(2,1)S(1)}, bf16[2,128,256]{2,1,0:T(8,128)(2,1)S(1)}, u32[]{:S(2)}, u32[]{:S(2)}) collective-permute-start(bf16[2,128,256]{2,1,0:T(8,128)(2,1)S(1)} %slice.24), channel_id=1, source_target_pairs={{0,4},{1,9},{4,0},{5,13},{8,12},{9,1},{12,8},{13,5},{2,6},{3,11},{... | collective-permute-start | bytes 393224 | tf_op jit(solution)/shard_map/ppermute | solution.py:364
  59.8 2.9 %collective-permute-start.9 = (bf16[128,256]{1,0:T(8,128)(2,1)S(1)}, bf16[128,256]{1,0:T(8,128)(2,1)S(1)}, u32[]{:S(2)}, u32[]{:S(2)}) collective-permute-start(bf16[128,256]{1,0:T(8,128)(2,1)S(1)} %slice_bitcast_fusion.3), channel_id=1, source_target_pairs={{0,12},{1,13},{4,8},{5,9},{8,4},{9,5},{12,0},{13,1},{2,14},{3,15},... | collective-permute-start | bytes 196616 | tf_op jit(solution)/shard_map/ppermute | solution.py:363
  62.8 2.7 %collective-permute-done.10 = bf16[2,128,256]{2,1,0:T(8,128)(2,1)S(1)} collective-permute-done((bf16[2,128,256]{2,1,0:T(8,128)(2,1)S(1)}, bf16[2,128,256]{2,1,0:T(8,128)(2,1)S(1)}, u32[]{:S(2)}, u32[]{:S(2)}) %collective-permute-start.10) | collective-permute-done | bytes 131104 | tf_op jit(solution)/shard_map/ppermute | solution.py:364
  65.5 0.0 collective-permute-start.11
  65.5 5.4 %row_grads.1 = (bf16[4096,256]{1,0:T(8,128)(2,1)}, bf16[4096,256]{1,0:T(8,128)(2,1)}) custom-call(bf16[8,512,128]{2,1,0:T(8,128)(2,1)S(1)} %get-tuple-element.20.refs_0_, f32[8,512]{1,0:T(8,128)S(1)} %get-tuple-element.21.refs_1_, f32[8,512]{1,0:T(8,128)S(1)} %get-tuple-element.22.refs_2_, bf16[8,512,512]{2,1,0:T(8,128)(2,1)S(1)} %copy-done.2, ...), custom_call_target="tpu_custom_call" | custom-call | tf_op jit(solution)/shard_map/row_grads/pallas_call | solution.py:275
  70.9 0.7 fusion.3
  (31 shorter events, 0.1 us)
Async XLA Ops:
  4.4 9.4 %collective-permute-start = (bf16[2,128,512]{2,1,0:T(8,128)(2,1)S(1)}, bf16[2,128,512]{2,1,0:T(8,128)(2,1)S(1)}, u32[]{:S(2)}, u32[]{:S(2)}) collective-permute-start(bf16[2,128,512]{2,1,0:T(8,128)(2,1)S(1)} %bitcast.21), channel_id=1, source_target_pairs={{0,4},{1,9},{4,0},{5,13},{8,12},{9,1},{12,8},{13,5},{2,6},{3,11},{... | collective-permute-start | bytes 786440 | tf_op jit(solution)/shard_map/ppermute | solution.py:332
  7.3 13.3 %collective-permute-start.2 = (bf16[1,128,512]{2,1,0:T(8,128)(2,1)S(1)}, bf16[1,128,512]{2,1,0:T(8,128)(2,1)S(1)}, u32[]{:S(2)}, u32[]{:S(2)}) collective-permute-start(bf16[1,128,512]{2,1,0:T(8,128)(2,1)S(1)} %bitcast.23), channel_id=1, source_target_pairs={{0,12},{1,13},{4,8},{5,9},{8,4},{9,5},{12,0},{13,1},{2,14},{3,15},... | collective-permute-start | bytes 393224 | tf_op jit(solution)/shard_map/ppermute | solution.py:330
  13.8 8.2 %collective-permute-start.1 = (bf16[2,128,512]{2,1,0:T(8,128)(2,1)S(1)}, bf16[2,128,512]{2,1,0:T(8,128)(2,1)S(1)}, u32[]{:S(2)}, u32[]{:S(2)}) collective-permute-start(bf16[2,128,512]{2,1,0:T(8,128)(2,1)S(1)} %collective-permute-done.refs_5_), channel_id=1, source_target_pairs={{0,1},{1,0},{2,3},{3,2},{4,5},{5,4},{6,7},{7,6},{8,9},{9,8},{10,11... | collective-permute-start | bytes 786440 | tf_op jit(solution)/shard_map/ppermute | solution.py:333
  19.0 0.7 copy-start.8
  20.6 1.4 %collective-permute-start.3 = (bf16[1,128,512]{2,1,0:T(8,128)(2,1)S(1)}, bf16[1,128,512]{2,1,0:T(8,128)(2,1)S(1)}, u32[]{:S(2)}, u32[]{:S(2)}) collective-permute-start(bf16[1,128,512]{2,1,0:T(8,128)(2,1)S(1)} %collective-permute-done.2.refs_7_), channel_id=1, source_target_pairs={{0,1},{1,0},{2,3},{3,2},{4,5},{5,4},{6,7},{7,6},{8,9},{9,8},{10,11... | collective-permute-start | bytes 393224 | tf_op jit(solution)/shard_map/ppermute | solution.py:334
  22.0 0.7 copy-start.10
  22.7 1.6 %copy-start.5 = (bf16[4096,256]{1,0:T(8,128)(2,1)S(1)}, bf16[4096,256]{1,0:T(8,128)(2,1)}, u32[]{:S(2)}) copy-start(bf16[4096,256]{1,0:T(8,128)(2,1)} %refs_0_.1) | copy-start | bytes 6291460
  24.3 1.6 %copy-start.7 = (bf16[4096,256]{1,0:T(8,128)(2,1)S(1)}, bf16[4096,256]{1,0:T(8,128)(2,1)}, u32[]{:S(2)}) copy-start(bf16[4096,256]{1,0:T(8,128)(2,1)} %refs_10_.1) | copy-start | bytes 6291460
  25.9 0.9 %copy-start.9 = (bf16[2,128,512]{2,1,0:T(8,128)(2,1)S(1)}, bf16[2,128,512]{2,1,0:T(8,128)(2,1)}, u32[]{:S(2)}) copy-start(bf16[2,128,512]{2,1,0:T(8,128)(2,1)} %copy-done.8) | copy-start | bytes 786436
  26.8 0.9 %copy-start.11 = (bf16[2,128,512]{2,1,0:T(8,128)(2,1)S(1)}, bf16[2,128,512]{2,1,0:T(8,128)(2,1)}, u32[]{:S(2)}) copy-start(bf16[2,128,512]{2,1,0:T(8,128)(2,1)} %copy-done.10) | copy-start | bytes 786436
  27.8 0.7 copy-start.16
  28.4 20.6 %copy-start.6 = (bf16[4096,256]{1,0:T(8,128)(2,1)S(1)}, bf16[4096,256]{1,0:T(8,128)(2,1)}, u32[]{:S(2)}) copy-start(bf16[4096,256]{1,0:T(8,128)(2,1)} %refs_0_.1) | copy-start | bytes 6291460
  37.6 2.0 %copy-start = (bf16[8,512,512]{2,1,0:T(8,128)(2,1)}, bf16[8,512,512]{2,1,0:T(8,128)(2,1)S(1)}, u32[]{:S(2)}) copy-start(bf16[8,512,512]{2,1,0:T(8,128)(2,1)S(1)} %get-tuple-element.16.refs_1_.refs_3_) | copy-start | bytes 12582916
  39.6 0.6 copy-start.14
  40.3 0.6 copy-start.13
  40.9 1.2 %collective-permute-start.4 = (f32[3,8,512]{2,1,0:T(8,128)S(1)}, f32[3,8,512]{2,1,0:T(8,128)S(1)}, u32[]{:S(2)}, u32[]{:S(2)}) collective-permute-start(f32[3,8,512]{2,1,0:T(8,128)S(1)} %get-tuple-element.14.a_ref), channel_id=1, source_target_pairs={{0,1},{1,0},{2,3},{3,2},{4,5},{5,4},{6,7},{7,6},{8,9},{9,8},{10,11... | collective-permute-start | bytes 147464 | tf_op jit(solution)/shard_map/ppermute | solution.py:345
  42.1 0.6 copy-start.17
  44.2 4.8 %collective-permute-start.6 = (f32[3,8,512]{2,1,0:T(8,128)}, f32[3,8,512]{2,1,0:T(8,128)S(1)}, u32[]{:S(2)}, u32[]{:S(2)}) collective-permute-start(f32[3,8,512]{2,1,0:T(8,128)} %merge_stats.1.refs_2_), channel_id=1, source_target_pairs={{0,4},{1,9},{4,0},{5,13},{8,12},{9,1},{12,8},{13,5},{2,6},{3,11},{... | collective-permute-start | bytes 147464 | tf_op jit(solution)/shard_map/ppermute | solution.py:347
  45.2 10.8 %collective-permute-start.5 = (f32[3,8,512]{2,1,0:T(8,128)}, f32[3,8,512]{2,1,0:T(8,128)S(1)}, u32[]{:S(2)}, u32[]{:S(2)}) collective-permute-start(f32[3,8,512]{2,1,0:T(8,128)} %merge_stats.1.refs_2_), channel_id=1, source_target_pairs={{0,12},{1,13},{4,8},{5,9},{8,4},{9,5},{12,0},{13,1},{2,14},{3,15},... | collective-permute-start | bytes 147464 | tf_op jit(solution)/shard_map/ppermute | solution.py:346
  49.0 7.1 %collective-permute-start.7 = (f32[3,8,512]{2,1,0:T(8,128)S(1)}, f32[3,8,512]{2,1,0:T(8,128)S(1)}, u32[]{:S(2)}, u32[]{:S(2)}) collective-permute-start(f32[3,8,512]{2,1,0:T(8,128)S(1)} %collective-permute-done.6.refs_4_), channel_id=1, source_target_pairs={{0,1},{1,0},{2,3},{3,2},{4,5},{5,4},{6,7},{7,6},{8,9},{9,8},{10,11... | collective-permute-start | bytes 147464 | tf_op jit(solution)/shard_map/ppermute | solution.py:348
  49.0 2.2 %copy-start.1 = (bf16[8,512,512]{2,1,0:T(8,128)(2,1)S(1)}, bf16[8,512,512]{2,1,0:T(8,128)(2,1)}, u32[]{:S(2)}) copy-start(bf16[8,512,512]{2,1,0:T(8,128)(2,1)} %copy-done) | copy-start | bytes 12582916
  51.2 2.2 %copy-start.3 = (bf16[8,512,512]{2,1,0:T(8,128)(2,1)S(1)}, bf16[8,512,512]{2,1,0:T(8,128)(2,1)}, u32[]{:S(2)}) copy-start(bf16[8,512,512]{2,1,0:T(8,128)(2,1)} %get-tuple-element.17.refs_2_.refs_4_) | copy-start | bytes 12582916
  53.4 2.7 %copy-start.12 = (f32[3,8,512]{2,1,0:T(8,128)S(1)}, f32[3,8,512]{2,1,0:T(8,128)}, u32[]{:S(2)}) copy-start(f32[3,8,512]{2,1,0:T(8,128)} %merge_stats.1.refs_2_) | copy-start | bytes 147460
  53.4 2.7 %copy-start.15 = (f32[3,8,512]{2,1,0:T(8,128)S(1)}, f32[3,8,512]{2,1,0:T(8,128)}, u32[]{:S(2)}) copy-start(f32[3,8,512]{2,1,0:T(8,128)} %copy-done.14) | copy-start | bytes 147460
  53.4 12.1 %copy-start.4 = (bf16[8,512,512]{2,1,0:T(8,128)(2,1)S(1)}, bf16[8,512,512]{2,1,0:T(8,128)(2,1)}, u32[]{:S(2)}) copy-start(bf16[8,512,512]{2,1,0:T(8,128)(2,1)} %get-tuple-element.17.refs_2_.refs_4_) | copy-start | bytes 12582916
  56.1 9.4 %copy-start.2 = (bf16[8,512,512]{2,1,0:T(8,128)(2,1)S(1)}, bf16[8,512,512]{2,1,0:T(8,128)(2,1)}, u32[]{:S(2)}) copy-start(bf16[8,512,512]{2,1,0:T(8,128)(2,1)} %copy-done) | copy-start | bytes 12582916
  57.2 1.7 %collective-permute-start.8 = (bf16[4,128,256]{2,1,0:T(8,128)(2,1)S(1)}, bf16[4,128,256]{2,1,0:T(8,128)(2,1)S(1)}, u32[]{:S(2)}, u32[]{:S(2)}) collective-permute-start(bf16[4,128,256]{2,1,0:T(8,128)(2,1)S(1)} %get-tuple-element.19), channel_id=1, source_target_pairs={{0,1},{1,0},{2,3},{3,2},{4,5},{5,4},{6,7},{7,6},{8,9},{9,8},{10,11... | collective-permute-start | bytes 786440 | tf_op jit(solution)/shard_map/ppermute | solution.py:360
  59.0 6.4 %collective-permute-start.10 = (bf16[2,128,256]{2,1,0:T(8,128)(2,1)S(1)}, bf16[2,128,256]{2,1,0:T(8,128)(2,1)S(1)}, u32[]{:S(2)}, u32[]{:S(2)}) collective-permute-start(bf16[2,128,256]{2,1,0:T(8,128)(2,1)S(1)} %slice.24), channel_id=1, source_target_pairs={{0,4},{1,9},{4,0},{5,13},{8,12},{9,1},{12,8},{13,5},{2,6},{3,11},{... | collective-permute-start | bytes 393224 | tf_op jit(solution)/shard_map/ppermute | solution.py:364
  59.8 11.1 %collective-permute-start.9 = (bf16[128,256]{1,0:T(8,128)(2,1)S(1)}, bf16[128,256]{1,0:T(8,128)(2,1)S(1)}, u32[]{:S(2)}, u32[]{:S(2)}) collective-permute-start(bf16[128,256]{1,0:T(8,128)(2,1)S(1)} %slice_bitcast_fusion.3), channel_id=1, source_target_pairs={{0,12},{1,13},{4,8},{5,9},{8,4},{9,5},{12,0},{13,1},{2,14},{3,15},... | collective-permute-start | bytes 196616 | tf_op jit(solution)/shard_map/ppermute | solution.py:363
  65.5 5.4 %collective-permute-start.11 = (bf16[128,256]{1,0:T(8,128)(2,1)S(1)}, bf16[128,256]{1,0:T(8,128)(2,1)S(1)}, u32[]{:S(2)}, u32[]{:S(2)}) collective-permute-start(bf16[128,256]{1,0:T(8,128)(2,1)S(1)} %slice_bitcast_fusion.1), channel_id=1, source_target_pairs={{0,1},{1,0},{2,3},{3,2},{4,5},{5,4},{6,7},{7,6},{8,9},{9,8},{10,11... | collective-permute-start | bytes 196616 | tf_op jit(solution)/shard_map/ppermute | solution.py:365

commit v2 on v1

v2 whole, which is shorter than its diff:
```python
import math

import jax
import jax.numpy as jnp
from jax import lax
from jax.experimental import pallas as pl
from jax.experimental.pallas import tpu as pltpu
from jax.sharding import PartitionSpec as P

HD = 64
TEST = 128
BLK = 512
LANES = 128
WIDE = 2 * TEST

NEG = -1e30
SCORE_SCALE = 1.0 / math.sqrt(HD)
LOG2_SCALE = SCORE_SCALE * math.log2(math.e)
RP = ("rows", "pair")
PAIR = [(0, 1), (1, 0)]


def table_lookup(positions, entries):
    matches = positions[:, None] == jnp.arange(entries.shape[0], dtype=jnp.int32)[None, :]
    return jnp.sum(jnp.where(matches, entries[None, :], 0), axis=1)


def params(mib):
    return pltpu.CompilerParams(vmem_limit_bytes=mib * 1024 * 1024)


def two_heads(rows):
    feature = lax.broadcasted_iota(jnp.int32, rows.shape, 0)
    zero = jnp.zeros_like(rows)
    return jnp.concatenate(
        [jnp.where(feature < HD, rows, zero), jnp.where(feature < HD, zero, rows)], axis=1
    )


def pack_kernel(query_ref, grad_ref, out_ref, sem):
    first = pltpu.make_async_copy(query_ref, out_ref.at[0, 0], sem.at[0])
    second = pltpu.make_async_copy(grad_ref, out_ref.at[0, 1], sem.at[1])
    first.start()
    second.start()
    first.wait()
    second.wait()


def pack(query_rows, cotangent):
    rows, features = query_rows.shape
    hbm = pl.BlockSpec(memory_space=pltpu.HBM)
    return pl.pallas_call(
        pack_kernel,
        in_specs=[hbm, hbm],
        out_specs=pl.BlockSpec(memory_space=pltpu.VMEM),
        out_shape=jax.ShapeDtypeStruct((1, 2, rows, features), query_rows.dtype),
        scratch_shapes=[pltpu.SemaphoreType.DMA((2,))],
        name="pack",
    )(query_rows, cotangent)


def scores_kernel(count, owner, live, testn, slot, table_of, *refs):
    pieces = refs[:count]
    key_hbm, value_hbm = refs[count : count + 2]
    qgt_ref, e_ref, u_ref, ab_ref, blk_ref, tab_ref, key_s, value_s, sem = refs[count + 2 :]
    blocks, _, features = key_s.shape

    def fetch(b):
        rows = pl.ds(b * BLK, BLK)
        return (
            pltpu.make_async_copy(key_hbm.at[rows], key_s.at[b], sem.at[0, b]),
            pltpu.make_async_copy(value_hbm.at[rows], value_s.at[b], sem.at[1, b]),
        )

    for b in range(blocks):
        for copy in fetch(b):
            copy.start()
    tab_ref[0] = jnp.full(tab_ref.shape[1:], NEG, jnp.float32)
    tab_ref[1] = jnp.zeros(tab_ref.shape[1:], jnp.float32)
    tab_ref[2] = jnp.zeros(tab_ref.shape[1:], jnp.float32)
    query = lax.broadcasted_iota(jnp.int32, (features, TEST), 1)
    at_slot = 0
    for piece in pieces:
        for n in range(piece.shape[0]):
            grads = piece[n, 1].T
            qgt_ref[at_slot, :features, :] = piece[n, 0].T
            qgt_ref[at_slot, features:, :] = jnp.where(
                query < testn[table_of[at_slot]], grads, jnp.zeros_like(grads)
            )
            at_slot += 1

    def block(b, carry):
        for copy in fetch(b):
            copy.wait()
        table = owner[b]
        at_slot = slot[table]
        key_live = lax.broadcasted_iota(jnp.int32, (BLK, WIDE), 0) < live[b]
        for p in range(features // LANES):
            at = slice(p * LANES, (p + 1) * LANES)
            wide = slice(p * WIDE, (p + 1) * WIDE)
            q_t = qgt_ref[at_slot, at, :]
            g_t = qgt_ref[at_slot, features + p * LANES : features + (p + 1) * LANES, :]
            keys = key_s[b, :, at]
            scores = jnp.dot(keys, two_heads(q_t), preferred_element_type=jnp.float32)
            dprobs = jnp.dot(value_s[b, :, at], two_heads(g_t), preferred_element_type=jnp.float32)
            scores = jnp.where(key_live, scores, NEG)
            peak = jnp.max(scores, axis=0, keepdims=True) * LOG2_SCALE
            weights = jnp.exp2(scores * LOG2_SCALE - peak)
            mass = jnp.sum(weights, axis=0, keepdims=True)
            part = jnp.sum(weights * dprobs, axis=0, keepdims=True)
            low = weights.astype(jnp.bfloat16)
            moved = (weights * (dprobs - part / mass)).astype(jnp.bfloat16)
            e_ref[b, :, wide] = low
            u_ref[b, :, wide] = moved
            for n, value in enumerate((moved, low)):
                product = lax.dot_general(
                    keys, value, (((0,), (0,)), ((), ())), preferred_element_type=jnp.float32
                )
                ab_ref[b, n, p * LANES : p * LANES + HD, :] = product[:HD, :TEST]
                ab_ref[b, n, p * LANES + HD : (p + 1) * LANES, :] = product[HD:, TEST:]
            blk_ref[0, pl.ds(b, 1), wide] = peak
            blk_ref[1, pl.ds(b, 1), wide] = mass
            blk_ref[2, pl.ds(b, 1), wide] = part
            old = tab_ref[0, pl.ds(table, 1), wide]
            new = jnp.maximum(old, peak)
            old_weight = jnp.exp2(old - new)
            new_weight = jnp.exp2(peak - new)
            tab_ref[0, pl.ds(table, 1), wide] = new
            tab_ref[1, pl.ds(table, 1), wide] = (
                tab_ref[1, pl.ds(table, 1), wide] * old_weight + mass * new_weight
            )
            tab_ref[2, pl.ds(table, 1), wide] = (
                tab_ref[2, pl.ds(table, 1), wide] * old_weight + part * new_weight
            )
        return carry

    lax.fori_loop(0, blocks, block, 0)


def block_scores(owner, live, testn, slot, table_of, pieces, key_rows, value_rows):
    features = key_rows.shape[1]
    blocks = owner.shape[0]
    tables = testn.shape[0]
    stacked = features // HD * TEST
    vmem = pl.BlockSpec(memory_space=pltpu.VMEM)
    smem = pl.BlockSpec(memory_space=pltpu.SMEM)
    hbm = pl.BlockSpec(memory_space=pltpu.HBM)
    return pl.pallas_call(
        lambda *refs: scores_kernel(len(pieces), *refs),
        in_specs=[smem] * 5 + [vmem] * len(pieces) + [hbm, hbm],
        out_specs=[vmem] * 6,
        out_shape=[
            pltpu.VMEM((tables, 2 * features, TEST), jnp.bfloat16),
            pltpu.VMEM((blocks, BLK, stacked), jnp.bfloat16),
            pltpu.VMEM((blocks, BLK, stacked), jnp.bfloat16),
            pltpu.VMEM((blocks, 2, features, TEST), jnp.float32),
            pltpu.VMEM((3, blocks, stacked), jnp.float32),
            jax.ShapeDtypeStruct((3, tables, stacked), jnp.float32),
        ],
        scratch_shapes=[
            pltpu.VMEM((blocks, BLK, features), jnp.bfloat16),
            pltpu.VMEM((blocks, BLK, features), jnp.bfloat16),
            pltpu.SemaphoreType.DMA((2, blocks)),
        ],
        compiler_params=params(40),
        name="block_scores",
    )(owner, live, testn, slot, table_of, *pieces, key_rows, value_rows)


def merged(pieces):
    peak = pieces[0][0]
    for piece in pieces[1:]:
        peak = jnp.maximum(peak, piece[0])
    mass = part = 0.0
    for piece in pieces:
        weight = jnp.exp2(piece[0] - peak)
        mass = mass + piece[1] * weight
        part = part + piece[2] * weight
    return peak, mass, part


def query_grad_kernel(features, count, owner, slot, *refs):
    pieces = refs[:count]
    blk_ref, ab_ref = refs[count : count + 2]
    outs = refs[count + 2 : -2]
    c_ref, d_ref, *q_refs = outs
    tab_s, acc_s = refs[-2:]
    blocks = blk_ref.shape[1]
    tab_s[0], tab_s[1], tab_s[2] = merged(
        [piece.at[n] for piece in pieces for n in range(piece.shape[0])]
    )
    acc_s[...] = jnp.zeros_like(acc_s)
    for b in range(blocks):
        table = owner[b]
        at = slot[table]
        mass = tab_s[1, pl.ds(table, 1), :]
        c = jnp.exp2(blk_ref[0, b : b + 1, :] - tab_s[0, pl.ds(table, 1), :]) / mass
        shift = blk_ref[2, b : b + 1, :] / blk_ref[1, b : b + 1, :]
        d = c * (shift - tab_s[2, pl.ds(table, 1), :] / mass)
        c_ref[b : b + 1, :] = c
        d_ref[b : b + 1, :] = d
        for h in range(features // HD):
            rows = slice(h * HD, (h + 1) * HD)
            lanes = slice(h * TEST, (h + 1) * TEST)
            acc_s[at, rows, :] += c[:, lanes] * ab_ref[b, 0, rows, :] + d[:, lanes] * ab_ref[b, 1, rows, :]
    tables = acc_s.shape[0]
    per = tables // len(q_refs)
    for n in range(tables):
        ref = q_refs[n // per]
        ref[n % per] = (acc_s[n] * SCORE_SCALE).T.astype(ref.dtype)


def query_grads(owner, slot, pieces, blk, ab, q_dtypes):
    blocks, _, features, _ = ab.shape
    tables = slot.shape[0]
    stacked = blk.shape[2]
    per = tables // len(q_dtypes)
    vmem = pl.BlockSpec(memory_space=pltpu.VMEM)
    smem = pl.BlockSpec(memory_space=pltpu.SMEM)
    return pl.pallas_call(
        lambda *refs: query_grad_kernel(features, len(pieces), *refs),
        in_specs=[smem, smem] + [vmem] * (len(pieces) + 2),
        out_specs=[vmem] * (2 + len(q_dtypes)),
        out_shape=[
            pltpu.VMEM((blocks, stacked), jnp.float32),
            pltpu.VMEM((blocks, stacked), jnp.float32),
        ]
        + [jax.ShapeDtypeStruct((per, TEST, features), dtype) for dtype in q_dtypes],
        scratch_shapes=[
            pltpu.VMEM((3, tables, stacked), jnp.float32),
            pltpu.VMEM((tables, features, TEST), jnp.float32),
        ],
        compiler_params=params(32),
        name="query_grads",
    )(owner, slot, *pieces, blk, ab)


def row_grads_kernel(owner, slot, qgt_ref, c_ref, d_ref, e_ref, u_ref, dk_hbm, dv_hbm, dk_s, dv_s, sem):
    blocks, _, features = dk_s.shape
    turned = (((1,), (1,)), ((), ()))

    def flush(b):
        rows = pl.ds(b * BLK, BLK)
        return (
            pltpu.make_async_copy(dk_s.at[b], dk_hbm.at[rows], sem.at[0, b]),
            pltpu.make_async_copy(dv_s.at[b], dv_hbm.at[rows], sem.at[1, b]),
        )

    def block(b, carry):
        at_slot = slot[owner[b]]
        for p in range(features // LANES):
            at = slice(p * LANES, (p + 1) * LANES)
            wide = slice(p * WIDE, (p + 1) * WIDE)
            c = c_ref[pl.ds(b, 1), wide]
            d = d_ref[pl.ds(b, 1), wide]
            q_t = two_heads(qgt_ref[at_slot, at, :].astype(jnp.float32))
            g_t = two_heads(
                qgt_ref[at_slot, features + p * LANES : features + (p + 1) * LANES, :].astype(jnp.float32)
            )
            for_u = (q_t * (c * SCORE_SCALE)).astype(jnp.bfloat16)
            for_e = jnp.concatenate([g_t * c, q_t * (d * SCORE_SCALE)], axis=0).astype(jnp.bfloat16)
            from_e = lax.dot_general(
                e_ref[b, :, wide], for_e, turned, preferred_element_type=jnp.float32
            )
            from_u = lax.dot_general(
                u_ref[b, :, wide], for_u, turned, preferred_element_type=jnp.float32
            )
            dv_s[b, :, at] = from_e[:, :LANES].astype(jnp.bfloat16)
            dk_s[b, :, at] = (from_u + from_e[:, LANES:]).astype(jnp.bfloat16)
        for copy in flush(b):
            copy.start()
        return carry

    lax.fori_loop(0, blocks, block, 0)
    for b in range(blocks):
        for copy in flush(b):
            copy.wait()


def row_grads(owner, slot, qgt, c, d, e_all, u_all):
    blocks, _, stacked = e_all.shape
    features = qgt.shape[1] // 2
    vmem = pl.BlockSpec(memory_space=pltpu.VMEM)
    smem = pl.BlockSpec(memory_space=pltpu.SMEM)
    hbm = pl.BlockSpec(memory_space=pltpu.HBM)
    return pl.pallas_call(
        row_grads_kernel,
        in_specs=[smem] * 2 + [vmem] * 5,
        out_specs=[hbm, hbm],
        out_shape=[jax.ShapeDtypeStruct((blocks * BLK, features), jnp.bfloat16)] * 2,
        scratch_shapes=[
            pltpu.VMEM((blocks, BLK, features), jnp.bfloat16),
            pltpu.VMEM((blocks, BLK, features), jnp.bfloat16),
            pltpu.SemaphoreType.DMA((2, blocks)),
        ],
        compiler_params=params(32),
        name="row_grads",
    )(owner, slot, qgt, c, d, e_all, u_all)


def local(small, query_rows, key_rows, value_rows, cotangent, train_rows, test_rows, block_table):
    chip = lax.axis_index("rows").astype(jnp.int32)
    core = lax.axis_index("pair").astype(jnp.int32)
    device = lax.axis_index(RP).astype(jnp.int32)
    local_rows, features = query_rows.shape
    blocks = key_rows.shape[0] // BLK
    tables = train_rows.shape[0]

    my_blocks = device * blocks + jnp.arange(blocks, dtype=jnp.int32)
    block_ids = jnp.arange(block_table.shape[0], dtype=jnp.int32)
    owner = lax.dynamic_slice_in_dim(block_table, device * blocks, blocks)
    earlier = (block_table[None, :] == owner[:, None]) & (block_ids[None, :] < my_blocks[:, None])
    ordinal = jnp.sum(jnp.where(earlier, 1, 0), axis=1).astype(jnp.int32)
    live = jnp.minimum(table_lookup(owner, train_rows) - ordinal * BLK, BLK).astype(jnp.int32)
    ids = jnp.arange(tables, dtype=jnp.int32)

    both = pack(query_rows, cotangent)
    if small:
        pair = lambda value: lax.ppermute(value, "pair", PAIR)
        step = lambda value, s: lax.ppermute(value, "rows", [(z, z ^ s) for z in range(4)])
        cross = [(2 * z + c, 2 * (z ^ (1 + c)) + c) for z in range(4) for c in range(2)]
        mine = chip ^ (1 + core)
        other = chip ^ (2 - core)
        table_chip, table_core = ids // 2, ids % 2
        not_mine = jnp.where(table_core == core, 0, 1)
        slot_in = 2 * (table_chip ^ chip) + not_mine
        table_of = 2 * (chip ^ (ids // 2)) + (core ^ (ids % 2))
        slot_out = jnp.where(
            table_chip == mine,
            not_mine,
            jnp.where(
                table_chip == other,
                5 - not_mine,
                jnp.where(table_chip == chip, 3 + 4 * not_mine, 2 + 4 * not_mine),
            ),
        ).astype(jnp.int32)
        pieces = []
        for value in [both] + [step(both, s) for s in (1, 2, 3)]:
            pieces += [value, pair(value)]
    else:
        slot_in = slot_out = table_of = ids
        everyone = lax.all_gather(both[0], RP, axis=1, tiled=True)
        pieces = [everyone.reshape(2, tables, TEST, features).swapaxes(0, 1)]

    qgt, e_all, u_all, ab, blk, tab = block_scores(
        owner, live, test_rows, slot_in, table_of, pieces, key_rows, value_rows
    )
    if small:
        tab = tab[None]
        far_tab = step(tab, 3)
        chip_tab = lax.all_gather(tab, "pair", axis=0, tiled=True)
        mine_tab = lax.ppermute(chip_tab, RP, cross)
        stats = [chip_tab, far_tab, pair(far_tab), mine_tab, pair(mine_tab)]
        dtypes = [jnp.float32, jnp.bfloat16]
    else:
        peak = lax.pmax(tab[0], RP)
        sums = lax.psum(tab[1:] * jnp.exp2(tab[0] - peak)[None], RP)
        stats = [jnp.concatenate([peak[None], sums], axis=0)[None]]
        dtypes = [jnp.float32]
    c, d, *q_terms = query_grads(owner, slot_out, stats, blk, ab, dtypes)
    if small:
        keep, send = q_terms
        total = keep + pair(send).astype(jnp.float32)
        to_mine = total[:2].astype(jnp.bfloat16)
        to_far = total[2].astype(jnp.bfloat16)
        got_far = step(to_far, 3)
        got_mine = lax.ppermute(to_mine, RP, cross)
        key_grad, value_grad = row_grads(owner, slot_in, qgt, c, d, e_all, u_all)
        got_mine, key_grad = lax.optimization_barrier((got_mine, key_grad))
        got_other = pair(got_mine[1])
        wide = lambda value: value.astype(jnp.float32)
        query_grad = total[3] + wide(got_far) + wide(got_mine[0]) + wide(got_other)
    else:
        query_grad = lax.psum_scatter(
            q_terms[0].reshape(tables * TEST, features), RP, scatter_dimension=0, tiled=True
        )
        key_grad, value_grad = row_grads(owner, slot_in, qgt, c, d, e_all, u_all)
    return query_grad.astype(jnp.bfloat16), key_grad, value_grad


def solution(mesh):
    sizes = mesh.shape
    tables_of_rows = P(("groups", "rows", "pair"), "mp")
    in_specs = (tables_of_rows,) * 4 + (P("groups"),) * 3
    out_specs = (tables_of_rows,) * 3

    def run(query_rows, *rest):
        local_rows = query_rows.shape[0] // (sizes["groups"] * sizes["rows"] * sizes["pair"])
        small = sizes["rows"] == 4 and sizes["pair"] == 2 and local_rows == TEST
        return jax.shard_map(
            lambda *args: local(small, *args),
            mesh=mesh,
            in_specs=in_specs,
            out_specs=out_specs,
            check_vma=False,
        )(query_rows, *rest)

    return run
```

time: 72.5 us -> 71.9 us (level)
  waiting for transfers between devices: 10 us -> 17.6 us
  local copies, waits for them, and re-layouts: 17.8 us -> 13 us
  starting transfers between devices: 18.7 us -> 14.6 us
  Pallas kernels: 19.7 us -> 21 us
    ppermute x10 -> x13, waiting for transfers between devices: 6.04 us -> 15.1 us  [the longest x5 13.9 us: local(): lax.ppermute(value, 'rows', [(z, z ^ s) for z in range(4)])]
    unnamed x37 -> x20, local copies, waits for them, and re-layouts: 16.2 us -> 12.2 us
    ppermute x10 -> x13, starting transfers between devices: 16.9 us -> 13.2 us  [the longest x5 10.5 us: local(): lax.ppermute(value, 'rows', [(z, z ^ s) for z in range(4)])]
    pallas_call x4 -> x3, Pallas kernels: 18.6 us -> 20 us  [the longest x1 13.3 us: block_scores(): pl.pallas_call(lambda *refs: scores_kernel(len(pieces), *refs), in_specs=...]
    ppermute x1, waiting for transfers between devices: 1.27 us -> 0.01 us  [local(): mine_tab = lax.ppermute(chip_tab, RP, cross)]
    ppermute x1, starting transfers between devices: 1.03 us -> 0.04 us  [local(): mine_tab = lax.ppermute(chip_tab, RP, cross)]
    concatenate x1 -> x0, local copies, waits for them, and re-layouts: 0.84 us -> none  [local(): both = jnp.concatenate([query_rows, cotangent], axis=1)]
  transfers between devices with their start and end apart: 12 -> 15, of which waited for: 6 -> 9; matrix products, arithmetic and copies ran while one was open for 3% -> 3% of each run, Pallas kernels for 11% -> 7%
where the time goes in v2:
time: 71.9 us; the launch traced here: 71.5 us
  Pallas kernels  21 us (29%)
  waiting for transfers between devices  17.6 us (24%)
  starting transfers between devices  14.6 us (20%)
  local copies, waits for them, and re-layouts  13 us (18%)
  other arithmetic  2.43 us (3%)
  blocking collectives  2.08 us (3%)
  between operations  0.75 us (1%)
    ppermute x5, waiting for transfers between devices, local(): lax.ppermute(value, 'rows', [(z, z ^ s) for z in range(4)])  13.9 us
    pallas_call x1, Pallas kernels, block_scores(): pl.pallas_call(lambda *refs: scores_kernel(len(pieces), *refs), in_specs=...  13.3 us
    unnamed x20, local copies, waits for them, and re-layouts  12.2 us
    ppermute x5, starting transfers between devices, local(): lax.ppermute(value, 'rows', [(z, z ^ s) for z in range(4)])  10.5 us
    pallas_call x1, Pallas kernels, row_grads(): pl.pallas_call(row_grads_kernel, in_specs=[smem] * 2 + [vmem] * 5, out_sp...  5.11 us
    ppermute x8, starting transfers between devices, local(): pair = lambda value: lax.ppermute(value, 'pair', PAIR)  2.7 us
    ppermute x1, waiting for transfers between devices, local(): got_mine = lax.ppermute(to_mine, RP, cross)  2.48 us
    all_gather x1, blocking collectives, local(): chip_tab = lax.all_gather(tab, 'pair', axis=0, tiled=True)  2.08 us
  transfers between devices with their start and end apart: 15, of which 9 were waited for; matrix products, arithmetic and copies ran while one was open for 3% of the time, Pallas kernels for 7%

profile of v2, /device:TPU:0, one launch (start us, length us, event | category | flops | bytes accessed | tf_op | source)
XLA Modules:
  0.0 71.5 jit_solution(17844306519719776777)
XLA Ops:
  0.6 1.5 %pack.1.refs_5_ = bf16[1,2,128,256]{3,2,1,0:T(8,128)(2,1)} custom-call(bf16[128,256]{1,0:T(8,128)(2,1)} %query_ref.1, bf16[128,256]{1,0:T(8,128)(2,1)} %grad_ref.1), custom_call_target="tpu_custom_call" | custom-call | tf_op jit(solution)/shard_map/pack/pallas_call | solution.py:52
  2.2 5.1 %collective-permute-start.5 = (bf16[1,2,128,256]{3,2,1,0:T(8,128)(2,1)}, bf16[1,2,128,256]{3,2,1,0:T(8,128)(2,1)S(1)}, u32[]{:S(2)}, u32[]{:S(2)}) collective-permute-start(bf16[1,2,128,256]{3,2,1,0:T(8,128)(2,1)} %pack.1.refs_5_), channel_id=1, source_target_pairs={{0,12},{4,8},{8,4},{12,0},{1,13},{5,9},{9,5},{13,1},{2,14},{6,10},... | collective-permute-start | bytes 393224 | tf_op jit(solution)/shard_map/ppermute | solution.py:320
  7.3 0.0 collective-permute-start.3
  7.3 0.6 collective-permute-start.1
  7.9 0.0 collective-permute-start
  7.9 0.7 %dynamic_slice.3.refs_0_.owner = s32[8]{0:T(128)S(1)} dynamic-slice(s32[64]{0:T(128)} %param.13, s32[]{:T(128)S(6)} %select_n.48), dynamic_slice_sizes={8} | dynamic-slice | bytes 68 | tf_op jit(solution)/shard_map/dynamic_slice | solution.py:311
  8.7 0.8 %select_reduce_fusion.1 = s32[8]{0:T(128)S(1)} fusion(s32[8]{0:T(128)} %param.11, s32[8]{0:T(128)S(1)} %dynamic_slice.3.refs_0_.owner), kind=kLoop, calls=%fused_computation.10 | loop fusion | flops 184 | bytes 96 | tf_op jit(solution)/shard_map/reduce_sum | solution.py:25
  9.5 0.8 %select_reduce_fusion = s32[8]{0:T(128)S(1)} fusion(s32[8]{0:T(128)S(1)} %iota_add_fusion, s32[64]{0:T(128)} %param.13, s32[8]{0:T(128)S(1)} %dynamic_slice.3.refs_0_.owner), kind=kLoop, calls=%fused_computation.8 | loop fusion | flops 2552 | bytes 352 | tf_op jit(solution)/shard_map/reduce_sum | solution.py:313
  10.4 1.6 %collective-permute-done.5.refs_11_ = bf16[1,2,128,256]{3,2,1,0:T(8,128)(2,1)S(1)} collective-permute-done((bf16[1,2,128,256]{3,2,1,0:T(8,128)(2,1)}, bf16[1,2,128,256]{3,2,1,0:T(8,128)(2,1)S(1)}, u32[]{:S(2)}, u32[]{:S(2)}) %collective-permute-start.5) | collective-permute-done | bytes 131104 | tf_op jit(solution)/shard_map/ppermute | solution.py:320
  11.9 0.0 collective-permute-start.6
  11.9 6.6 %collective-permute-done.3.refs_9_ = bf16[1,2,128,256]{3,2,1,0:T(8,128)(2,1)S(1)} collective-permute-done((bf16[1,2,128,256]{3,2,1,0:T(8,128)(2,1)}, bf16[1,2,128,256]{3,2,1,0:T(8,128)(2,1)S(1)}, u32[]{:S(2)}, u32[]{:S(2)}) %collective-permute-start.3) | collective-permute-done | bytes 131104 | tf_op jit(solution)/shard_map/ppermute | solution.py:320
  18.6 0.0 collective-permute-start.4
  18.6 0.0 collective-permute-done.1.refs_7_
  18.6 0.5 collective-permute-start.2
  19.1 0.0 copy-start.5
  19.1 0.6 copy-done.5
  19.8 0.0 collective-permute-done.6.refs_12_
  19.8 0.1 collective-permute-done.4.refs_10_
  19.9 0.2 collective-permute-done.2.refs_8_
  20.1 0.9 %copy-done.4 = bf16[1,2,128,256]{3,2,1,0:T(8,128)(2,1)S(1)} copy-done((bf16[1,2,128,256]{3,2,1,0:T(8,128)(2,1)S(1)}, bf16[1,2,128,256]{3,2,1,0:T(8,128)(2,1)}, u32[]{:S(2)}) %copy-start.4) | copy-done | bytes 131096
  21.0 0.9 %copy-done.6 = bf16[1,2,128,256]{3,2,1,0:T(8,128)(2,1)S(1)} copy-done((bf16[1,2,128,256]{3,2,1,0:T(8,128)(2,1)S(1)}, bf16[1,2,128,256]{3,2,1,0:T(8,128)(2,1)}, u32[]{:S(2)}) %copy-start.6) | copy-done | bytes 131096
  21.9 0.7 copy-done.9
  22.6 13.3 %block_scores.1 = (bf16[8,512,128]{2,1,0:T(8,128)(2,1)S(1)}, bf16[8,512,512]{2,1,0:T(8,128)(2,1)S(1)}, bf16[8,512,512]{2,1,0:T(8,128)(2,1)S(1)}, f32[8,2,256,128...) custom-call(s32[8]{0:T(128)S(1)} %dynamic_slice.3.refs_0_.owner, ...), custom_call_target="tpu_custom_call" | custom-call | tf_op jit(solution)/shard_map/block_scores/pallas_call | solution.py:148
  35.9 1.9 %copy-done = bf16[8,512,512]{2,1,0:T(8,128)(2,1)} copy-done((bf16[8,512,512]{2,1,0:T(8,128)(2,1)}, bf16[8,512,512]{2,1,0:T(8,128)(2,1)S(1)}, u32[]{:S(2)}) %copy-start) | copy-done | bytes 4194328
  37.8 2.0 %copy-done.2 = bf16[8,512,512]{2,1,0:T(8,128)(2,1)} copy-done((bf16[8,512,512]{2,1,0:T(8,128)(2,1)}, bf16[8,512,512]{2,1,0:T(8,128)(2,1)S(1)}, u32[]{:S(2)}) %copy-start.2) | copy-done | bytes 4194328
  39.8 2.1 %all-gather = f32[6,8,512]{2,1,0:T(8,128)S(1)} all-gather(f32[3,8,512]{2,1,0:T(8,128)} %get-tuple-element.17), channel_id=2, replica_groups=mesh['groups'=2,'rows'=4,'mp'=2,'pair'=2] {'pair'}, dimensions={0}, use_global_device_ids=true | all-gather | bytes 147456 | tf_op jit(solution)/shard_map/all_gather | solution.py:351
  41.9 0.0 collective-permute-start.9
  42.0 2.5 %collective-permute-start.7 = (f32[1,3,8,512]{3,2,1,0:T(8,128)}, f32[1,3,8,512]{3,2,1,0:T(8,128)S(1)}, u32[]{:S(2)}, u32[]{:S(2)}) collective-permute-start(f32[1,3,8,512]{3,2,1,0:T(8,128)} %bitcast.1), channel_id=1, source_target_pairs={{0,12},{4,8},{8,4},{12,0},{1,13},{5,9},{9,5},{13,1},{2,14},{6,10},... | collective-permute-start | bytes 147464 | tf_op jit(solution)/shard_map/ppermute | solution.py:320
  44.5 4.3 %collective-permute-done.7.refs_3_ = f32[1,3,8,512]{3,2,1,0:T(8,128)S(1)} collective-permute-done((f32[1,3,8,512]{3,2,1,0:T(8,128)}, f32[1,3,8,512]{3,2,1,0:T(8,128)S(1)}, u32[]{:S(2)}, u32[]{:S(2)}) %collective-permute-start.7) | collective-permute-done | bytes 49184 | tf_op jit(solution)/shard_map/ppermute | solution.py:320
  48.8 0.0 collective-permute-start.8
  48.8 0.5 collective-permute-start.10
  49.3 0.7 collective-permute-done.8.refs_4_
  50.0 0.2 collective-permute-done.10.refs_6_
  50.2 0.8 %copy-done.8 = f32[3,8,512]{2,1,0:T(8,128)S(1)} copy-done((f32[3,8,512]{2,1,0:T(8,128)S(1)}, f32[3,8,512]{2,1,0:T(8,128)}, u32[]{:S(2)}) %copy-start.8) | copy-done | bytes 49176
  51.0 1.1 %query_grads.1 = (f32[8,512]{1,0:T(8,128)S(1)}, f32[8,512]{1,0:T(8,128)S(1)}, f32[4,128,256]{2,1,0:T(8,128)S(1)}, bf16[4,128,256]{2,1,0:T(8,128)(2,1)S(1)}) custom-call(s32[8]{0:T(128)S(1)} %dynamic_slice.3.refs_0_.owner, s32[8]{0:T(128)S(1)} %compare_select_fusion.3.refs_1_, f32[2,3,8,512]{3,2,1,0:T(8,128)S(1)} %bitcast.20, ...), custom_call_target="tpu_custom_call" | custom-call | tf_op jit(solution)/shard_map/query_grads/pallas_call | solution.py:220
  52.1 0.4 collective-permute-start.11
  52.6 2.2 %copy-done.1 = bf16[8,512,512]{2,1,0:T(8,128)(2,1)S(1)} copy-done((bf16[8,512,512]{2,1,0:T(8,128)(2,1)S(1)}, bf16[8,512,512]{2,1,0:T(8,128)(2,1)}, u32[]{:S(2)}) %copy-start.1) | copy-done | bytes 4194328
  54.7 2.2 %copy-done.3 = bf16[8,512,512]{2,1,0:T(8,128)(2,1)S(1)} copy-done((bf16[8,512,512]{2,1,0:T(8,128)(2,1)S(1)}, bf16[8,512,512]{2,1,0:T(8,128)(2,1)}, u32[]{:S(2)}) %copy-start.3) | copy-done | bytes 4194328
  56.9 5.1 %row_grads.1 = (bf16[4096,256]{1,0:T(8,128)(2,1)}, bf16[4096,256]{1,0:T(8,128)(2,1)}) custom-call(s32[8]{0:T(128)S(1)} %dynamic_slice.3.refs_0_.owner, s32[8]{0:T(128)S(1)} %get-tuple-element.34.refs_3_.slot, bf16[8,512,128]{2,1,0:T(8,128)(2,1)S(1)} %get-tuple-element.22.qgt_ref, f32[8,512]{1,0:T(8,128)S(1)} %get-tuple-element.23.c_ref, ...), custom_call_target="tpu_custom_call" | custom-call | tf_op jit(solution)/shard_map/row_grads/pallas_call | solution.py:286
  62.0 0.0 collective-permute-done.11
  62.1 0.1 fusion.6
  62.1 1.3 %collective-permute-start.13 = (bf16[2,128,256]{2,1,0:T(8,128)(2,1)S(1)}, bf16[2,128,256]{2,1,0:T(8,128)(2,1)S(1)}, u32[]{:S(2)}, u32[]{:S(2)}) collective-permute-start(bf16[2,128,256]{2,1,0:T(8,128)(2,1)S(1)} %slice.24), channel_id=1, source_target_pairs={{0,4},{1,9},{4,0},{5,13},{8,12},{9,1},{12,8},{13,5},{2,6},{3,11},{... | collective-permute-start | bytes 393224 | tf_op jit(solution)/shard_map/ppermute | solution.py:367
  63.5 2.2 %collective-permute-start.12 = (bf16[128,256]{1,0:T(8,128)(2,1)S(1)}, bf16[128,256]{1,0:T(8,128)(2,1)S(1)}, u32[]{:S(2)}, u32[]{:S(2)}) collective-permute-start(bf16[128,256]{1,0:T(8,128)(2,1)S(1)} %slice_bitcast_fusion.1), channel_id=1, source_target_pairs={{0,12},{4,8},{8,4},{12,0},{1,13},{5,9},{9,5},{13,1},{2,14},{6,10},... | collective-permute-start | bytes 196616 | tf_op jit(solution)/shard_map/ppermute | solution.py:320
  65.7 2.5 %collective-permute-done.13 = bf16[2,128,256]{2,1,0:T(8,128)(2,1)S(1)} collective-permute-done((bf16[2,128,256]{2,1,0:T(8,128)(2,1)S(1)}, bf16[2,128,256]{2,1,0:T(8,128)(2,1)S(1)}, u32[]{:S(2)}, u32[]{:S(2)}) %collective-permute-start.13) | collective-permute-done | bytes 131104 | tf_op jit(solution)/shard_map/ppermute | solution.py:367
  68.2 1.3 %collective-permute-start.14 = (bf16[128,256]{1,0:T(8,128)(2,1)S(1)}, bf16[128,256]{1,0:T(8,128)(2,1)S(1)}, u32[]{:S(2)}, u32[]{:S(2)}) collective-permute-start(bf16[128,256]{1,0:T(8,128)(2,1)S(1)} %slice_bitcast_fusion.2), channel_id=1, source_target_pairs={{0,1},{1,0},{2,3},{3,2},{4,5},{5,4},{6,7},{7,6},{8,9},{9,8},{10,11... | collective-permute-start | bytes 196616 | tf_op jit(solution)/shard_map/ppermute | solution.py:319
  69.5 1.4 %collective-permute-done.12 = bf16[128,256]{1,0:T(8,128)(2,1)S(1)} collective-permute-done((bf16[128,256]{1,0:T(8,128)(2,1)S(1)}, bf16[128,256]{1,0:T(8,128)(2,1)S(1)}, u32[]{:S(2)}, u32[]{:S(2)}) %collective-permute-start.12) | collective-permute-done | bytes 65568 | tf_op jit(solution)/shard_map/ppermute | solution.py:320
  70.9 0.0 collective-permute-done.14
  70.9 0.7 fusion.3
  (19 shorter events, 0.1 us)
Async XLA Ops:
  2.2 9.8 %collective-permute-start.5 = (bf16[1,2,128,256]{3,2,1,0:T(8,128)(2,1)}, bf16[1,2,128,256]{3,2,1,0:T(8,128)(2,1)S(1)}, u32[]{:S(2)}, u32[]{:S(2)}) collective-permute-start(bf16[1,2,128,256]{3,2,1,0:T(8,128)(2,1)} %pack.1.refs_5_), channel_id=1, source_target_pairs={{0,12},{4,8},{8,4},{12,0},{1,13},{5,9},{9,5},{13,1},{2,14},{6,10},... | collective-permute-start | bytes 393224 | tf_op jit(solution)/shard_map/ppermute | solution.py:320
  7.3 11.3 %collective-permute-start.3 = (bf16[1,2,128,256]{3,2,1,0:T(8,128)(2,1)}, bf16[1,2,128,256]{3,2,1,0:T(8,128)(2,1)S(1)}, u32[]{:S(2)}, u32[]{:S(2)}) collective-permute-start(bf16[1,2,128,256]{3,2,1,0:T(8,128)(2,1)} %pack.1.refs_5_), channel_id=1, source_target_pairs={{0,8},{4,12},{8,0},{12,4},{1,9},{5,13},{9,1},{13,5},{2,10},{6,14},... | collective-permute-start | bytes 393224 | tf_op jit(solution)/shard_map/ppermute | solution.py:320
  7.3 11.3 %collective-permute-start.1 = (bf16[1,2,128,256]{3,2,1,0:T(8,128)(2,1)}, bf16[1,2,128,256]{3,2,1,0:T(8,128)(2,1)S(1)}, u32[]{:S(2)}, u32[]{:S(2)}) collective-permute-start(bf16[1,2,128,256]{3,2,1,0:T(8,128)(2,1)} %pack.1.refs_5_), channel_id=1, source_target_pairs={{0,4},{4,0},{8,12},{12,8},{1,5},{5,1},{9,13},{13,9},{2,6},{6,2},{1... | collective-permute-start | bytes 393224 | tf_op jit(solution)/shard_map/ppermute | solution.py:320
  7.9 11.2 %collective-permute-start = (bf16[1,2,128,256]{3,2,1,0:T(8,128)(2,1)}, bf16[1,2,128,256]{3,2,1,0:T(8,128)(2,1)S(1)}, u32[]{:S(2)}, u32[]{:S(2)}) collective-permute-start(bf16[1,2,128,256]{3,2,1,0:T(8,128)(2,1)} %pack.1.refs_5_), channel_id=1, source_target_pairs={{0,1},{1,0},{2,3},{3,2},{4,5},{5,4},{6,7},{7,6},{8,9},{9,8},{10,11... | collective-permute-start | bytes 393224 | tf_op jit(solution)/shard_map/ppermute | solution.py:319
  11.9 7.8 %collective-permute-start.6 = (bf16[1,2,128,256]{3,2,1,0:T(8,128)(2,1)S(1)}, bf16[1,2,128,256]{3,2,1,0:T(8,128)(2,1)S(1)}, u32[]{:S(2)}, u32[]{:S(2)}) collective-permute-start(bf16[1,2,128,256]{3,2,1,0:T(8,128)(2,1)S(1)} %collective-permute-done.5.refs_11_), channel_id=1, source_target_pairs={{0,1},{1,0},{2,3},{3,2},{4,5},{5,4},{6,7},{7,6},{8,9},{9,8},{10,11... | collective-permute-start | bytes 393224 | tf_op jit(solution)/shard_map/ppermute | solution.py:319
  18.6 1.3 %collective-permute-start.4 = (bf16[1,2,128,256]{3,2,1,0:T(8,128)(2,1)S(1)}, bf16[1,2,128,256]{3,2,1,0:T(8,128)(2,1)S(1)}, u32[]{:S(2)}, u32[]{:S(2)}) collective-permute-start(bf16[1,2,128,256]{3,2,1,0:T(8,128)(2,1)S(1)} %collective-permute-done.3.refs_9_), channel_id=1, source_target_pairs={{0,1},{1,0},{2,3},{3,2},{4,5},{5,4},{6,7},{7,6},{8,9},{9,8},{10,11... | collective-permute-start | bytes 393224 | tf_op jit(solution)/shard_map/ppermute | solution.py:319
  18.6 1.5 %collective-permute-start.2 = (bf16[1,2,128,256]{3,2,1,0:T(8,128)(2,1)S(1)}, bf16[1,2,128,256]{3,2,1,0:T(8,128)(2,1)S(1)}, u32[]{:S(2)}, u32[]{:S(2)}) collective-permute-start(bf16[1,2,128,256]{3,2,1,0:T(8,128)(2,1)S(1)} %collective-permute-done.1.refs_7_), channel_id=1, source_target_pairs={{0,1},{1,0},{2,3},{3,2},{4,5},{5,4},{6,7},{7,6},{8,9},{9,8},{10,11... | collective-permute-start | bytes 393224 | tf_op jit(solution)/shard_map/ppermute | solution.py:319
  19.1 0.7 copy-start.5
  20.1 0.9 %copy-start.4 = (bf16[1,2,128,256]{3,2,1,0:T(8,128)(2,1)S(1)}, bf16[1,2,128,256]{3,2,1,0:T(8,128)(2,1)}, u32[]{:S(2)}) copy-start(bf16[1,2,128,256]{3,2,1,0:T(8,128)(2,1)} %pack.1.refs_5_) | copy-start | bytes 393220
  21.0 0.9 %copy-start.6 = (bf16[1,2,128,256]{3,2,1,0:T(8,128)(2,1)S(1)}, bf16[1,2,128,256]{3,2,1,0:T(8,128)(2,1)}, u32[]{:S(2)}) copy-start(bf16[1,2,128,256]{3,2,1,0:T(8,128)(2,1)} %copy-done.5) | copy-start | bytes 393220
  21.9 0.7 copy-start.9
  35.9 1.9 %copy-start = (bf16[8,512,512]{2,1,0:T(8,128)(2,1)}, bf16[8,512,512]{2,1,0:T(8,128)(2,1)S(1)}, u32[]{:S(2)}) copy-start(bf16[8,512,512]{2,1,0:T(8,128)(2,1)S(1)} %get-tuple-element.25.e_ref) | copy-start | bytes 12582916
  37.8 2.0 %copy-start.2 = (bf16[8,512,512]{2,1,0:T(8,128)(2,1)}, bf16[8,512,512]{2,1,0:T(8,128)(2,1)S(1)}, u32[]{:S(2)}) copy-start(bf16[8,512,512]{2,1,0:T(8,128)(2,1)S(1)} %get-tuple-element.26.u_ref) | copy-start | bytes 12582916
  39.8 2.1 %copy-start.7 = (f32[3,8,512]{2,1,0:T(8,128)}, f32[3,8,512]{2,1,0:T(8,128)S(1)}, u32[]{:S(2)}) copy-start(f32[3,8,512]{2,1,0:T(8,128)S(1)} %get-tuple-element.18.refs_7_) | copy-start | bytes 147460
  41.9 6.9 %collective-permute-start.9 = (f32[2,3,8,512]{3,2,1,0:T(8,128)S(1)}, f32[2,3,8,512]{3,2,1,0:T(8,128)S(1)}, u32[]{:S(2)}, u32[]{:S(2)}) collective-permute-start(f32[2,3,8,512]{3,2,1,0:T(8,128)S(1)} %bitcast.19), channel_id=1, source_target_pairs={{0,4},{1,9},{4,0},{5,13},{8,12},{9,1},{12,8},{13,5},{2,6},{3,11},{... | collective-permute-start | bytes 294920 | tf_op jit(solution)/shard_map/ppermute | solution.py:352
  42.0 6.8 %collective-permute-start.7 = (f32[1,3,8,512]{3,2,1,0:T(8,128)}, f32[1,3,8,512]{3,2,1,0:T(8,128)S(1)}, u32[]{:S(2)}, u32[]{:S(2)}) collective-permute-start(f32[1,3,8,512]{3,2,1,0:T(8,128)} %bitcast.1), channel_id=1, source_target_pairs={{0,12},{4,8},{8,4},{12,0},{1,13},{5,9},{9,5},{13,1},{2,14},{6,10},... | collective-permute-start | bytes 147464 | tf_op jit(solution)/shard_map/ppermute | solution.py:320
  48.8 1.2 %collective-permute-start.8 = (f32[1,3,8,512]{3,2,1,0:T(8,128)S(1)}, f32[1,3,8,512]{3,2,1,0:T(8,128)S(1)}, u32[]{:S(2)}, u32[]{:S(2)}) collective-permute-start(f32[1,3,8,512]{3,2,1,0:T(8,128)S(1)} %collective-permute-done.7.refs_3_), channel_id=1, source_target_pairs={{0,1},{1,0},{2,3},{3,2},{4,5},{5,4},{6,7},{7,6},{8,9},{9,8},{10,11... | collective-permute-start | bytes 147464 | tf_op jit(solution)/shard_map/ppermute | solution.py:319
  48.8 1.5 %collective-permute-start.10 = (f32[2,3,8,512]{3,2,1,0:T(8,128)S(1)}, f32[2,3,8,512]{3,2,1,0:T(8,128)S(1)}, u32[]{:S(2)}, u32[]{:S(2)}) collective-permute-start(f32[2,3,8,512]{3,2,1,0:T(8,128)S(1)} %collective-permute-done.9.refs_5_), channel_id=1, source_target_pairs={{0,1},{1,0},{2,3},{3,2},{4,5},{5,4},{6,7},{7,6},{8,9},{9,8},{10,11... | collective-permute-start | bytes 294920 | tf_op jit(solution)/shard_map/ppermute | solution.py:319
  50.2 0.8 %copy-start.8 = (f32[3,8,512]{2,1,0:T(8,128)S(1)}, f32[3,8,512]{2,1,0:T(8,128)}, u32[]{:S(2)}) copy-start(f32[3,8,512]{2,1,0:T(8,128)} %copy-done.7) | copy-start | bytes 147460
  52.1 9.9 %collective-permute-start.11 = (bf16[4,128,256]{2,1,0:T(8,128)(2,1)S(1)}, bf16[4,128,256]{2,1,0:T(8,128)(2,1)S(1)}, u32[]{:S(2)}, u32[]{:S(2)}) collective-permute-start(bf16[4,128,256]{2,1,0:T(8,128)(2,1)S(1)} %get-tuple-element.21), channel_id=1, source_target_pairs={{0,1},{1,0},{2,3},{3,2},{4,5},{5,4},{6,7},{7,6},{8,9},{9,8},{10,11... | collective-permute-start | bytes 786440 | tf_op jit(solution)/shard_map/ppermute | solution.py:319
  52.6 2.2 %copy-start.1 = (bf16[8,512,512]{2,1,0:T(8,128)(2,1)S(1)}, bf16[8,512,512]{2,1,0:T(8,128)(2,1)}, u32[]{:S(2)}) copy-start(bf16[8,512,512]{2,1,0:T(8,128)(2,1)} %copy-done) | copy-start | bytes 12582916
  54.7 2.2 %copy-start.3 = (bf16[8,512,512]{2,1,0:T(8,128)(2,1)S(1)}, bf16[8,512,512]{2,1,0:T(8,128)(2,1)}, u32[]{:S(2)}) copy-start(bf16[8,512,512]{2,1,0:T(8,128)(2,1)} %copy-done.2) | copy-start | bytes 12582916
  62.1 6.1 %collective-permute-start.13 = (bf16[2,128,256]{2,1,0:T(8,128)(2,1)S(1)}, bf16[2,128,256]{2,1,0:T(8,128)(2,1)S(1)}, u32[]{:S(2)}, u32[]{:S(2)}) collective-permute-start(bf16[2,128,256]{2,1,0:T(8,128)(2,1)S(1)} %slice.24), channel_id=1, source_target_pairs={{0,4},{1,9},{4,0},{5,13},{8,12},{9,1},{12,8},{13,5},{2,6},{3,11},{... | collective-permute-start | bytes 393224 | tf_op jit(solution)/shard_map/ppermute | solution.py:367
  63.5 7.4 %collective-permute-start.12 = (bf16[128,256]{1,0:T(8,128)(2,1)S(1)}, bf16[128,256]{1,0:T(8,128)(2,1)S(1)}, u32[]{:S(2)}, u32[]{:S(2)}) collective-permute-start(bf16[128,256]{1,0:T(8,128)(2,1)S(1)} %slice_bitcast_fusion.1), channel_id=1, source_target_pairs={{0,12},{4,8},{8,4},{12,0},{1,13},{5,9},{9,5},{13,1},{2,14},{6,10},... | collective-permute-start | bytes 196616 | tf_op jit(solution)/shard_map/ppermute | solution.py:320
  68.2 2.6 %collective-permute-start.14 = (bf16[128,256]{1,0:T(8,128)(2,1)S(1)}, bf16[128,256]{1,0:T(8,128)(2,1)S(1)}, u32[]{:S(2)}, u32[]{:S(2)}) collective-permute-start(bf16[128,256]{1,0:T(8,128)(2,1)S(1)} %slice_bitcast_fusion.2), channel_id=1, source_target_pairs={{0,1},{1,0},{2,3},{3,2},{4,5},{5,4},{6,7},{7,6},{8,9},{9,8},{10,11... | collective-permute-start | bytes 196616 | tf_op jit(solution)/shard_map/ppermute | solution.py:319

commit v3 on v2

v3 whole, which is shorter than its diff:
```python
import math

import jax
import jax.numpy as jnp
from jax import lax
from jax.experimental import pallas as pl
from jax.experimental.pallas import tpu as pltpu
from jax.sharding import PartitionSpec as P

HD = 64
TEST = 128
BLK = 512
LANES = 128
WIDE = 2 * TEST

NEG = -1e30
SCORE_SCALE = 1.0 / math.sqrt(HD)
LOG2_SCALE = SCORE_SCALE * math.log2(math.e)
RP = ("rows", "pair")
PAIR = [(0, 1), (1, 0)]


def table_lookup(positions, entries):
    matches = positions[:, None] == jnp.arange(entries.shape[0], dtype=jnp.int32)[None, :]
    return jnp.sum(jnp.where(matches, entries[None, :], 0), axis=1)


def params(mib):
    return pltpu.CompilerParams(vmem_limit_bytes=mib * 1024 * 1024)


def two_heads(rows):
    feature = lax.broadcasted_iota(jnp.int32, rows.shape, 0)
    zero = jnp.zeros_like(rows)
    return jnp.concatenate(
        [jnp.where(feature < HD, rows, zero), jnp.where(feature < HD, zero, rows)], axis=1
    )


def every_copy(copies):
    for copy in copies:
        copy.start()
    return copies


def scores_kernel(count, held, meta, *refs):
    query_pieces, grad_pieces = refs[:count], refs[count : 2 * count]
    key_hbm, value_hbm = refs[2 * count : 2 * count + 2]
    qgt_hbm, e_hbm, u_hbm, blk_hbm, tab_ref = refs[2 * count + 2 : 2 * count + 7]
    qgt_s, e_s, u_s, blk_s, key_s, value_s, held_s, in_sem, out_sem, held_sem, small_sem = refs[
        2 * count + 7 :
    ]
    blocks, _, features = key_s.shape
    tables = qgt_s.shape[0]
    early = every_copy(
        [
            pltpu.make_async_copy(pieces[n], held_s.at[n, m], held_sem.at[n, m])
            for n in range(held)
            for m, pieces in enumerate((query_pieces, grad_pieces))
        ]
    )
    loads = []
    for b in range(blocks):
        rows = pl.ds(b * BLK, BLK)
        loads.append(
            every_copy(
                [
                    pltpu.make_async_copy(key_hbm.at[rows], key_s.at[b], in_sem.at[0, b]),
                    pltpu.make_async_copy(value_hbm.at[rows], value_s.at[b], in_sem.at[1, b]),
                ]
            )
        )
    tab_ref[0] = jnp.full(tab_ref.shape[1:], NEG, jnp.float32)
    tab_ref[1] = jnp.zeros(tab_ref.shape[1:], jnp.float32)
    tab_ref[2] = jnp.zeros(tab_ref.shape[1:], jnp.float32)
    query = lax.broadcasted_iota(jnp.int32, (features, TEST), 1)

    def turn(at_slot, queries, grads):
        grads = grads.T
        qgt_s[at_slot, :features, :] = queries.T
        qgt_s[at_slot, features:, :] = jnp.where(
            query < meta[TESTN, meta[TABLE_OF, at_slot]], grads, jnp.zeros_like(grads)
        )

    per = tables // count
    for n in range(held, count):
        for m in range(per):
            rows = slice(m * TEST, (m + 1) * TEST)
            turn(n * per + m, query_pieces[n][rows, :], grad_pieces[n][rows, :])
    for copy in early:
        copy.wait()
    for n in range(held):
        turn(n, held_s[n, 0], held_s[n, 1])
    stores = every_copy([pltpu.make_async_copy(qgt_s, qgt_hbm, small_sem.at[0])])

    for b in range(blocks):
        for copy in loads[b]:
            copy.wait()
        table = meta[OWNER, b]
        at_slot = meta[SLOT_IN, table]
        key_live = lax.broadcasted_iota(jnp.int32, (BLK, WIDE), 0) < meta[LIVE, b]
        for p in range(features // LANES):
            at = slice(p * LANES, (p + 1) * LANES)
            wide = slice(p * WIDE, (p + 1) * WIDE)
            q_t = qgt_s[at_slot, at, :]
            g_t = qgt_s[at_slot, features + p * LANES : features + (p + 1) * LANES, :]
            scores = jnp.dot(key_s[b, :, at], two_heads(q_t), preferred_element_type=jnp.float32)
            dprobs = jnp.dot(value_s[b, :, at], two_heads(g_t), preferred_element_type=jnp.float32)
            scores = jnp.where(key_live, scores, NEG)
            peak = jnp.max(scores, axis=0, keepdims=True) * LOG2_SCALE
            weights = jnp.exp2(scores * LOG2_SCALE - peak)
            mass = jnp.sum(weights, axis=0, keepdims=True)
            part = jnp.sum(weights * dprobs, axis=0, keepdims=True)
            e_s[b, :, wide] = weights.astype(jnp.bfloat16)
            u_s[b, :, wide] = (weights * (dprobs - part / mass)).astype(jnp.bfloat16)
            blk_s[0, b : b + 1, wide] = peak
            blk_s[1, b : b + 1, wide] = mass
            blk_s[2, b : b + 1, wide] = part
            old = tab_ref[0, pl.ds(table, 1), wide]
            new = jnp.maximum(old, peak)
            old_weight = jnp.exp2(old - new)
            new_weight = jnp.exp2(peak - new)
            tab_ref[0, pl.ds(table, 1), wide] = new
            tab_ref[1, pl.ds(table, 1), wide] = (
                tab_ref[1, pl.ds(table, 1), wide] * old_weight + mass * new_weight
            )
            tab_ref[2, pl.ds(table, 1), wide] = (
                tab_ref[2, pl.ds(table, 1), wide] * old_weight + part * new_weight
            )
        stores += every_copy(
            [
                pltpu.make_async_copy(e_s.at[b], e_hbm.at[b], out_sem.at[0, b]),
                pltpu.make_async_copy(u_s.at[b], u_hbm.at[b], out_sem.at[1, b]),
            ]
        )
    stores += every_copy([pltpu.make_async_copy(blk_s, blk_hbm, small_sem.at[1])])
    for copy in stores:
        copy.wait()


OWNER, LIVE, TESTN, SLOT_IN, TABLE_OF, SLOT_OUT = range(6)


def vmem_spec():
    return pl.BlockSpec(memory_space=pltpu.VMEM)


def smem_spec():
    return pl.BlockSpec(memory_space=pltpu.SMEM)


def hbm_spec():
    return pl.BlockSpec(memory_space=pltpu.HBM)


def in_hbm(value):
    return pltpu.with_memory_space_constraint(value, pltpu.HBM)


def block_scores(meta, tables, held, query_pieces, grad_pieces, key_rows, value_rows):
    features = key_rows.shape[1]
    blocks = key_rows.shape[0] // BLK
    stacked = features // HD * TEST
    count = len(query_pieces)
    pieces = []
    for group in (query_pieces, grad_pieces):
        pieces += [in_hbm(piece) if n < held else piece for n, piece in enumerate(group)]
    specs = [hbm_spec() if n % count < held else vmem_spec() for n in range(2 * count)]
    weights = (blocks, BLK, stacked)
    turned = (tables, 2 * features, TEST)
    return pl.pallas_call(
        lambda *refs: scores_kernel(count, held, *refs),
        in_specs=[smem_spec()] + specs + [hbm_spec()] * 2,
        out_specs=[hbm_spec()] * 4 + [vmem_spec()],
        out_shape=[
            pltpu.HBM(turned, jnp.bfloat16),
            pltpu.HBM(weights, jnp.bfloat16),
            pltpu.HBM(weights, jnp.bfloat16),
            pltpu.HBM((3, blocks, stacked), jnp.float32),
            jax.ShapeDtypeStruct((3, tables, stacked), jnp.float32),
        ],
        scratch_shapes=[
            pltpu.VMEM(turned, jnp.bfloat16),
            pltpu.VMEM(weights, jnp.bfloat16),
            pltpu.VMEM(weights, jnp.bfloat16),
            pltpu.VMEM((3, blocks, stacked), jnp.float32),
            pltpu.VMEM((blocks, BLK, features), jnp.bfloat16),
            pltpu.VMEM((blocks, BLK, features), jnp.bfloat16),
            pltpu.VMEM((max(held, 1), 2, TEST, features), jnp.bfloat16),
            pltpu.SemaphoreType.DMA((2, blocks)),
            pltpu.SemaphoreType.DMA((2, blocks)),
            pltpu.SemaphoreType.DMA((max(held, 1), 2)),
            pltpu.SemaphoreType.DMA((2,)),
        ],
        compiler_params=params(28),
        name="block_scores",
    )(meta, *pieces, in_hbm(key_rows), in_hbm(value_rows))


def query_sums_kernel(key_hbm, e_hbm, u_hbm, blk_hbm, ab_ref, blk_ref, key_s, e_s, u_s, sem, blk_sem):
    blocks, _, features = key_s.shape
    first = every_copy([pltpu.make_async_copy(blk_hbm, blk_ref, blk_sem.at[0])])
    loads = []
    for b in range(blocks):
        loads.append(
            every_copy(
                [
                    pltpu.make_async_copy(key_hbm.at[pl.ds(b * BLK, BLK)], key_s.at[b], sem.at[0, b]),
                    pltpu.make_async_copy(u_hbm.at[b], u_s.at[b], sem.at[1, b]),
                    pltpu.make_async_copy(e_hbm.at[b], e_s.at[b], sem.at[2, b]),
                ]
            )
        )
    for b in range(blocks):
        for copy in loads[b]:
            copy.wait()
        for p in range(features // LANES):
            wide = slice(p * WIDE, (p + 1) * WIDE)
            keys = key_s[b, :, p * LANES : (p + 1) * LANES]
            for n, ref in enumerate((u_s, e_s)):
                product = lax.dot_general(
                    keys, ref[b, :, wide], (((0,), (0,)), ((), ())), preferred_element_type=jnp.float32
                )
                ab_ref[b, n, p * LANES : p * LANES + HD, :] = product[:HD, :TEST]
                ab_ref[b, n, p * LANES + HD : (p + 1) * LANES, :] = product[HD:, TEST:]
    for copy in first:
        copy.wait()


def query_sums(key_rows, e_all, u_all, blk):
    features = key_rows.shape[1]
    blocks, _, stacked = e_all.shape
    return pl.pallas_call(
        query_sums_kernel,
        in_specs=[hbm_spec()] * 4,
        out_specs=[vmem_spec()] * 2,
        out_shape=[
            pltpu.VMEM((blocks, 2, features, TEST), jnp.float32),
            pltpu.VMEM(blk.shape, jnp.float32),
        ],
        scratch_shapes=[
            pltpu.VMEM((blocks, BLK, features), jnp.bfloat16),
            pltpu.VMEM((blocks, BLK, stacked), jnp.bfloat16),
            pltpu.VMEM((blocks, BLK, stacked), jnp.bfloat16),
            pltpu.SemaphoreType.DMA((3, blocks)),
            pltpu.SemaphoreType.DMA((1,)),
        ],
        compiler_params=params(20),
        name="query_sums",
    )(in_hbm(key_rows), in_hbm(e_all), in_hbm(u_all), in_hbm(blk))


def merged(pieces):
    peak = pieces[0][0]
    for piece in pieces[1:]:
        peak = jnp.maximum(peak, piece[0])
    mass = part = 0.0
    for piece in pieces:
        weight = jnp.exp2(piece[0] - peak)
        mass = mass + piece[1] * weight
        part = part + piece[2] * weight
    return peak, mass, part


def query_grad_kernel(count, meta, *refs):
    pieces = refs[:count]
    blk_ref, ab_ref = refs[count : count + 2]
    c_ref, d_ref, *q_refs = refs[count + 2 : -2]
    tab_s, acc_s = refs[-2:]
    blocks = blk_ref.shape[1]
    tables, features, _ = acc_s.shape
    tab_s[0], tab_s[1], tab_s[2] = merged(pieces)
    acc_s[...] = jnp.zeros_like(acc_s)
    for b in range(blocks):
        table = meta[OWNER, b]
        at = meta[SLOT_OUT, table]
        mass = tab_s[1, pl.ds(table, 1), :]
        c = jnp.exp2(blk_ref[0, b : b + 1, :] - tab_s[0, pl.ds(table, 1), :]) / mass
        shift = blk_ref[2, b : b + 1, :] / blk_ref[1, b : b + 1, :]
        d = c * (shift - tab_s[2, pl.ds(table, 1), :] / mass)
        c_ref[b : b + 1, :] = c
        d_ref[b : b + 1, :] = d
        for h in range(features // HD):
            rows = slice(h * HD, (h + 1) * HD)
            lanes = slice(h * TEST, (h + 1) * TEST)
            acc_s[at, rows, :] += c[:, lanes] * ab_ref[b, 0, rows, :] + d[:, lanes] * ab_ref[b, 1, rows, :]
    per = tables // len(q_refs)
    for n in range(tables):
        ref = q_refs[n // per]
        ref[n % per] = (acc_s[n] * SCORE_SCALE).T.astype(ref.dtype)


def query_grads(meta, tables, pieces, blk, ab, q_dtypes):
    blocks, _, features, _ = ab.shape
    stacked = blk.shape[2]
    per = tables // len(q_dtypes)
    return pl.pallas_call(
        lambda *refs: query_grad_kernel(len(pieces), *refs),
        in_specs=[smem_spec()] + [vmem_spec()] * (len(pieces) + 2),
        out_specs=[vmem_spec()] * (2 + len(q_dtypes)),
        out_shape=[
            jax.ShapeDtypeStruct((blocks, stacked), jnp.float32),
            jax.ShapeDtypeStruct((blocks, stacked), jnp.float32),
        ]
        + [jax.ShapeDtypeStruct((per, TEST, features), dtype) for dtype in q_dtypes],
        scratch_shapes=[
            pltpu.VMEM((3, tables, stacked), jnp.float32),
            pltpu.VMEM((tables, features, TEST), jnp.float32),
        ],
        compiler_params=params(10),
        name="query_grads",
    )(meta, *pieces, blk, ab)


def row_grads_kernel(meta, c_ref, d_ref, qgt_hbm, e_hbm, u_hbm, dk_hbm, dv_hbm, *scratch):
    qgt_s, e_s, u_s, dk_s, dv_s, in_sem, out_sem, qgt_sem = scratch
    blocks, _, features = dk_s.shape
    turned = (((1,), (1,)), ((), ()))
    first = every_copy([pltpu.make_async_copy(qgt_hbm, qgt_s, qgt_sem.at[0])])
    loads = []
    for b in range(blocks):
        loads.append(
            every_copy(
                [
                    pltpu.make_async_copy(e_hbm.at[b], e_s.at[b], in_sem.at[0, b]),
                    pltpu.make_async_copy(u_hbm.at[b], u_s.at[b], in_sem.at[1, b]),
                ]
            )
        )
    for copy in first:
        copy.wait()
    stores = []
    for b in range(blocks):
        at_slot = meta[SLOT_IN, meta[OWNER, b]]
        for copy in loads[b]:
            copy.wait()
        for p in range(features // LANES):
            at = slice(p * LANES, (p + 1) * LANES)
            wide = slice(p * WIDE, (p + 1) * WIDE)
            c = c_ref[b : b + 1, wide]
            d = d_ref[b : b + 1, wide]
            q_t = two_heads(qgt_s[at_slot, at, :].astype(jnp.float32))
            g_t = two_heads(
                qgt_s[at_slot, features + p * LANES : features + (p + 1) * LANES, :].astype(jnp.float32)
            )
            for_u = (q_t * (c * SCORE_SCALE)).astype(jnp.bfloat16)
            for_e = jnp.concatenate([g_t * c, q_t * (d * SCORE_SCALE)], axis=0).astype(jnp.bfloat16)
            from_e = lax.dot_general(
                e_s[b, :, wide], for_e, turned, preferred_element_type=jnp.float32
            )
            from_u = lax.dot_general(
                u_s[b, :, wide], for_u, turned, preferred_element_type=jnp.float32
            )
            dv_s[b, :, at] = from_e[:, :LANES].astype(jnp.bfloat16)
            dk_s[b, :, at] = (from_u + from_e[:, LANES:]).astype(jnp.bfloat16)
        rows = pl.ds(b * BLK, BLK)
        stores += every_copy(
            [
                pltpu.make_async_copy(dk_s.at[b], dk_hbm.at[rows], out_sem.at[0, b]),
                pltpu.make_async_copy(dv_s.at[b], dv_hbm.at[rows], out_sem.at[1, b]),
            ]
        )
    for copy in stores:
        copy.wait()


def row_grads(meta, c, d, qgt, e_all, u_all):
    blocks, _, stacked = e_all.shape
    features = qgt.shape[1] // 2
    return pl.pallas_call(
        row_grads_kernel,
        in_specs=[smem_spec()] + [vmem_spec()] * 2 + [hbm_spec()] * 3,
        out_specs=[hbm_spec()] * 2,
        out_shape=[jax.ShapeDtypeStruct((blocks * BLK, features), jnp.bfloat16)] * 2,
        scratch_shapes=[
            pltpu.VMEM(qgt.shape, jnp.bfloat16),
            pltpu.VMEM((blocks, BLK, stacked), jnp.bfloat16),
            pltpu.VMEM((blocks, BLK, stacked), jnp.bfloat16),
            pltpu.VMEM((blocks, BLK, features), jnp.bfloat16),
            pltpu.VMEM((blocks, BLK, features), jnp.bfloat16),
            pltpu.SemaphoreType.DMA((2, blocks)),
            pltpu.SemaphoreType.DMA((2, blocks)),
            pltpu.SemaphoreType.DMA((1,)),
        ],
        compiler_params=params(24),
        name="row_grads",
    )(meta, c, d, in_hbm(qgt), in_hbm(e_all), in_hbm(u_all))


def local(small, query_rows, key_rows, value_rows, cotangent, train_rows, test_rows, block_table):
    chip = lax.axis_index("rows").astype(jnp.int32)
    core = lax.axis_index("pair").astype(jnp.int32)
    device = lax.axis_index(RP).astype(jnp.int32)
    local_rows, features = query_rows.shape
    blocks = key_rows.shape[0] // BLK
    tables = train_rows.shape[0]

    my_blocks = device * blocks + jnp.arange(blocks, dtype=jnp.int32)
    block_ids = jnp.arange(block_table.shape[0], dtype=jnp.int32)
    owner = lax.dynamic_slice_in_dim(block_table, device * blocks, blocks)
    earlier = (block_table[None, :] == owner[:, None]) & (block_ids[None, :] < my_blocks[:, None])
    ordinal = jnp.sum(jnp.where(earlier, 1, 0), axis=1).astype(jnp.int32)
    live = jnp.minimum(table_lookup(owner, train_rows) - ordinal * BLK, BLK).astype(jnp.int32)
    ids = jnp.arange(tables, dtype=jnp.int32)

    pair = lambda value: lax.ppermute(value, "pair", PAIR)
    step = lambda value, s: lax.ppermute(value, "rows", [(z, z ^ s) for z in range(4)])
    if small:
        away = (ids // 2) ^ chip
        not_mine = (ids % 2) ^ core
        slot_in = 2 * away + not_mine
        table_of = 2 * (chip ^ (ids // 2)) + (core ^ (ids % 2))
        slot_out = 4 * not_mine + (away + 3) % 4
        held = 1

        def spread(value):
            pieces = []
            for near in [value] + [step(value, s) for s in (1, 2, 3)]:
                pieces += [near, pair(near)]
            return pieces

    else:
        slot_in = slot_out = table_of = ids
        held = 0
        spread = lambda value: [lax.all_gather(value, RP, axis=0, tiled=True)]

    pad = lambda values: jnp.pad(values, (0, max(blocks, tables) - values.shape[0]))
    meta = jnp.stack([pad(v) for v in (owner, live, test_rows, slot_in, table_of, slot_out)])
    qgt, e_all, u_all, blk, tab = block_scores(
        meta, tables, held, spread(query_rows), spread(cotangent), key_rows, value_rows
    )
    if small:
        stats = spread(tab)
        dtypes = [jnp.float32, jnp.bfloat16]
    else:
        peak = lax.pmax(tab[0], RP)
        sums = lax.psum(tab[1:] * jnp.exp2(tab[0] - peak)[None], RP)
        stats = [jnp.concatenate([peak[None], sums], axis=0)]
        dtypes = [jnp.float32]
    ab, blk = query_sums(key_rows, e_all, u_all, blk)
    c, d, *q_terms = query_grads(meta, tables, stats, blk, ab, dtypes)
    if small:
        keep, send = q_terms
        total = keep + pair(send).astype(jnp.float32)
        low = total.astype(jnp.bfloat16)
        got = [step(low[s - 1], s) for s in (1, 2, 3)]
        low, c = lax.optimization_barrier((low, c))
        key_grad, value_grad = row_grads(meta, c, d, qgt, e_all, u_all)
        query_grad = total[3]
        for value in got:
            query_grad = query_grad + value.astype(jnp.float32)
    else:
        query_grad = lax.psum_scatter(
            q_terms[0].reshape(tables * TEST, features), RP, scatter_dimension=0, tiled=True
        )
        key_grad, value_grad = row_grads(meta, c, d, qgt, e_all, u_all)
    return query_grad.astype(jnp.bfloat16), key_grad, value_grad


def solution(mesh):
    sizes = mesh.shape
    tables_of_rows = P(("groups", "rows", "pair"), "mp")
    in_specs = (tables_of_rows,) * 4 + (P("groups"),) * 3
    out_specs = (tables_of_rows,) * 3

    def run(query_rows, *rest):
        local_rows = query_rows.shape[0] // (sizes["groups"] * sizes["rows"] * sizes["pair"])
        small = sizes["rows"] == 4 and sizes["pair"] == 2 and local_rows == TEST
        return jax.shard_map(
            lambda *args: local(small, *args),
            mesh=mesh,
            in_specs=in_specs,
            out_specs=out_specs,
            check_vma=False,
        )(query_rows, *rest)

    return run
```

time: 71.9 us -> 63.5 us (0.88)
  local copies, waits for them, and re-layouts: 13 us -> 2.15 us
  waiting for transfers between devices: 17.6 us -> 8.83 us
  starting transfers between devices: 14.6 us -> 23.2 us
  Pallas kernels: 21 us -> 25.9 us
  blocking collectives: 2.08 us -> 0 us
    unnamed x20 -> x0, local copies, waits for them, and re-layouts: 12.2 us -> none
    ppermute x5 -> x12, starting transfers between devices: 10.5 us -> 20.4 us  [local(): lax.ppermute(value, 'rows', [(z, z ^ s) for z in range(4)])]
    ppermute x5 -> x12, waiting for transfers between devices: 13.9 us -> 7.64 us  [local(): lax.ppermute(value, 'rows', [(z, z ^ s) for z in range(4)])]
    pallas_call x4, Pallas kernels: 21 us -> 25.9 us  [the longest x1 11 us: block_scores(): pl.pallas_call(lambda *refs: scores_kernel(count, held, *refs), in_specs=...]
    ppermute x2 -> x0, waiting for transfers between devices: 2.48 us -> none  [the longest x1 2.48 us: local(): got_mine = lax.ppermute(to_mine, RP, cross)]
    all_gather x1 -> x0, blocking collectives: 2.08 us -> none  [local(): chip_tab = lax.all_gather(tab, 'pair', axis=0, tiled=True)]
    another operation x0 -> x2, local copies, waits for them, and re-layouts: none -> 1.4 us  [local(): jnp.stack([pad(v) for v in (owner, live, test_rows, slot_in, table_of, sl...]
    ppermute x2 -> x0, starting transfers between devices: 1.38 us -> none  [the longest x1 1.34 us: local(): got_mine = lax.ppermute(to_mine, RP, cross)]
  transfers between devices with their start and end apart: 15 -> 25, of which waited for: 9 -> 5; matrix products, arithmetic and copies ran while one was open for 3% -> 6% of each run, Pallas kernels for 7% -> 22%
where the time goes in v3:
time: 63.5 us; the launch traced here: 63.3 us
  Pallas kernels  25.9 us (41%)
  starting transfers between devices  23.2 us (37%)
  waiting for transfers between devices  8.83 us (14%)
  other arithmetic  2.45 us (4%)
  local copies, waits for them, and re-layouts  2.15 us (3%)
  between operations  0.8 us (1%)
    ppermute x12, starting transfers between devices, local(): lax.ppermute(value, 'rows', [(z, z ^ s) for z in range(4)])  20.4 us
    pallas_call x1, Pallas kernels, block_scores(): pl.pallas_call(lambda *refs: scores_kernel(count, held, *refs), in_specs=...  11 us
    pallas_call x1, Pallas kernels, row_grads(): pl.pallas_call(row_grads_kernel, in_specs=[smem_spec()] + [vmem_spec()] *...  9.23 us
    ppermute x12, waiting for transfers between devices, local(): lax.ppermute(value, 'rows', [(z, z ^ s) for z in range(4)])  7.64 us
    pallas_call x1, Pallas kernels, query_sums(): pl.pallas_call(query_sums_kernel, in_specs=[hbm_spec()] * 4, out_specs=[v...  4.53 us
    ppermute x13, starting transfers between devices, local(): pair = lambda value: lax.ppermute(value, 'pair', PAIR)  2.79 us
    another operation x2, local copies, waits for them, and re-layouts, local(): jnp.stack([pad(v) for v in (owner, live, test_rows, slot_in, table_of, sl...  1.4 us
  transfers between devices with their start and end apart: 25, of which 5 were waited for; matrix products, arithmetic and copies ran while one was open for 6% of the time, Pallas kernels for 22%

profile of v3, /device:TPU:0, one launch (start us, length us, event | category | flops | bytes accessed | tf_op | source)
XLA Modules:
  0.0 63.3 jit_solution(3239152082873571234)
XLA Ops:
  0.6 0.5 collective-permute-start
  1.1 2.7 %collective-permute-start.1 = (bf16[128,256]{1,0:T(8,128)(2,1)}, bf16[128,256]{1,0:T(8,128)(2,1)S(1)}, u32[]{:S(2)}, u32[]{:S(2)}) collective-permute-start(bf16[128,256]{1,0:T(8,128)(2,1)} %refs_1_.1), channel_id=1, source_target_pairs={{0,4},{4,0},{8,12},{12,8},{1,5},{5,1},{9,13},{13,9},{2,6},{6,2},{1... | collective-permute-start | bytes 196616 | tf_op jit(solution)/shard_map/ppermute | solution.py:407
  3.8 2.6 %collective-permute-start.3 = (bf16[128,256]{1,0:T(8,128)(2,1)}, bf16[128,256]{1,0:T(8,128)(2,1)S(1)}, u32[]{:S(2)}, u32[]{:S(2)}) collective-permute-start(bf16[128,256]{1,0:T(8,128)(2,1)} %refs_1_.1), channel_id=1, source_target_pairs={{0,8},{4,12},{8,0},{12,4},{1,9},{5,13},{9,1},{13,5},{2,10},{6,14},... | collective-permute-start | bytes 196616 | tf_op jit(solution)/shard_map/ppermute | solution.py:407
  6.4 0.0 collective-permute-start.5
  6.4 0.0 collective-permute-start.7
  6.4 0.7 %dynamic_slice.3 = s32[8]{0:T(128)S(1)} dynamic-slice(s32[64]{0:T(128)} %param.13, s32[]{:T(128)S(6)} %select_n.59), dynamic_slice_sizes={8} | dynamic-slice | bytes 68 | tf_op jit(solution)/shard_map/dynamic_slice | solution.py:400
  7.1 0.8 %select_reduce_fusion.1 = s32[8]{0:T(128)S(1)} fusion(s32[8]{0:T(128)} %param.11, s32[8]{0:T(128)S(1)} %dynamic_slice.3), kind=kLoop, calls=%fused_computation.11 | loop fusion | flops 184 | bytes 96 | tf_op jit(solution)/shard_map/reduce_sum | solution.py:25
  8.0 0.8 %select_reduce_fusion = s32[8]{0:T(128)S(1)} fusion(s32[8]{0:T(128)S(1)} %iota_add_fusion, s32[64]{0:T(128)} %param.13, s32[8]{0:T(128)S(1)} %dynamic_slice.3), kind=kLoop, calls=%fused_computation.9 | loop fusion | flops 2552 | bytes 352 | tf_op jit(solution)/shard_map/reduce_sum | solution.py:402
  8.8 0.0 collective-permute-done.refs_2_
  8.8 1.0 %collective-permute-start.8 = (bf16[128,256]{1,0:T(8,128)(2,1)}, bf16[128,256]{1,0:T(8,128)(2,1)S(1)}, u32[]{:S(2)}, u32[]{:S(2)}) collective-permute-start(bf16[128,256]{1,0:T(8,128)(2,1)} %refs_9_.1), channel_id=1, source_target_pairs={{0,4},{4,0},{8,12},{12,8},{1,5},{5,1},{9,13},{13,9},{2,6},{6,2},{1... | collective-permute-start | bytes 196616 | tf_op jit(solution)/shard_map/ppermute | solution.py:407
  9.8 0.0 collective-permute-done.1.refs_3_
  9.8 3.5 %collective-permute-start.10 = (bf16[128,256]{1,0:T(8,128)(2,1)}, bf16[128,256]{1,0:T(8,128)(2,1)S(1)}, u32[]{:S(2)}, u32[]{:S(2)}) collective-permute-start(bf16[128,256]{1,0:T(8,128)(2,1)} %refs_9_.1), channel_id=1, source_target_pairs={{0,8},{4,12},{8,0},{12,4},{1,9},{5,13},{9,1},{13,5},{2,10},{6,14},... | collective-permute-start | bytes 196616 | tf_op jit(solution)/shard_map/ppermute | solution.py:407
  13.3 0.0 collective-permute-done.3.refs_5_
  13.3 1.8 %collective-permute-start.12 = (bf16[128,256]{1,0:T(8,128)(2,1)}, bf16[128,256]{1,0:T(8,128)(2,1)S(1)}, u32[]{:S(2)}, u32[]{:S(2)}) collective-permute-start(bf16[128,256]{1,0:T(8,128)(2,1)} %refs_9_.1), channel_id=1, source_target_pairs={{0,12},{4,8},{8,4},{12,0},{1,13},{5,9},{9,5},{13,1},{2,14},{6,10},... | collective-permute-start | bytes 196616 | tf_op jit(solution)/shard_map/ppermute | solution.py:407
  15.1 0.0 collective-permute-done.5.refs_7_
  15.1 0.0 collective-permute-start.2
  15.1 0.6 collective-permute-start.4
  15.7 0.1 collective-permute-start.6
  15.8 2.0 %collective-permute-done.10.refs_13_ = bf16[128,256]{1,0:T(8,128)(2,1)S(1)} collective-permute-done((bf16[128,256]{1,0:T(8,128)(2,1)}, bf16[128,256]{1,0:T(8,128)(2,1)S(1)}, u32[]{:S(2)}, u32[]{:S(2)}) %collective-permute-start.10) | collective-permute-done | bytes 65568 | tf_op jit(solution)/shard_map/ppermute | solution.py:407
  17.8 0.0 collective-permute-start.9
  17.8 1.9 %collective-permute-done.12.refs_15_ = bf16[128,256]{1,0:T(8,128)(2,1)S(1)} collective-permute-done((bf16[128,256]{1,0:T(8,128)(2,1)}, bf16[128,256]{1,0:T(8,128)(2,1)S(1)}, u32[]{:S(2)}, u32[]{:S(2)}) %collective-permute-start.12) | collective-permute-done | bytes 65568 | tf_op jit(solution)/shard_map/ppermute | solution.py:407
  19.6 0.0 collective-permute-start.11
  19.6 0.5 collective-permute-start.13
  20.1 0.7 %dynamic-slice_bitcast_fusion = s32[1,8]{1,0:T(1,128)S(1)} fusion(s32[64]{0:T(128)} %param.13, s32[]{:T(128)S(6)} %select_n.59), kind=kLoop, calls=%fused_computation.30 | loop fusion | bytes 68 | tf_op jit(solution)/shard_map/stack | solution.py:428
  20.9 0.7 %stack.15.refs_0_.meta = s32[6,8]{1,0:T(8,128)S(1)} concatenate(s32[1,8]{1,0:T(1,128)S(1)} %dynamic-slice_bitcast_fusion, s32[1,8]{1,0:T(1,128)S(1)} %minimum_bitcast_fusion, s32[1,8]{1,0:T(1,128)} %bitcast.21, s32[1,8]{1,0:T(1,128)S(1)} %get-tuple-element.37, s32[1,8]{1,0:T(1,128)S(1)} %get-tuple-element.37, s32[1,8]{1,0:T(1,128)S(1)} %get-tuple-element.36), dimensions={0} | concatenate | bytes 384 | tf_op jit(solution)/shard_map/stack | solution.py:428
  21.5 0.0 collective-permute-done.4.refs_6_
  21.5 0.0 collective-permute-done.9.refs_12_
  21.6 0.0 collective-permute-done.11.refs_14_
  21.6 11.0 %block_scores.1 = (bf16[8,512,128]{2,1,0:T(8,128)(2,1)}, bf16[8,512,512]{2,1,0:T(8,128)(2,1)}, bf16[8,512,512]{2,1,0:T(8,128)(2,1)}, f32[3,8,512]{2,1,0:T(8,128)}, f32[3,8,512]{2,1,0:T(8,128)S(1)}) custom-call(s32[6,8]{1,0:T(8,128)S(1)} %stack.15.refs_0_.meta, bf16[128,256]{1,0:T(8,128)(2,1)} %refs_1_.1, bf16[128,256]{1,0:T(8,128)(2,1)S(1)} %collective-permute-done.refs_2_, ...), custom_call_target="tpu_custom_call" | custom-call | tf_op jit(solution)/shard_map/block_scores/pallas_call | solution.py:171
  32.5 1.2 %collective-permute-start.15 = (f32[3,8,512]{2,1,0:T(8,128)S(1)}, f32[3,8,512]{2,1,0:T(8,128)S(1)}, u32[]{:S(2)}, u32[]{:S(2)}) collective-permute-start(f32[3,8,512]{2,1,0:T(8,128)S(1)} %get-tuple-element.17.refs_1_), channel_id=1, source_target_pairs={{0,4},{4,0},{8,12},{12,8},{1,5},{5,1},{9,13},{13,9},{2,6},{6,2},{1... | collective-permute-start | bytes 147464 | tf_op jit(solution)/shard_map/ppermute | solution.py:407
  33.8 1.5 %collective-permute-start.17 = (f32[3,8,512]{2,1,0:T(8,128)S(1)}, f32[3,8,512]{2,1,0:T(8,128)S(1)}, u32[]{:S(2)}, u32[]{:S(2)}) collective-permute-start(f32[3,8,512]{2,1,0:T(8,128)S(1)} %get-tuple-element.17.refs_1_), channel_id=1, source_target_pairs={{0,8},{4,12},{8,0},{12,4},{1,9},{5,13},{9,1},{13,5},{2,10},{6,14},... | collective-permute-start | bytes 147464 | tf_op jit(solution)/shard_map/ppermute | solution.py:407
  35.3 1.7 %collective-permute-start.19 = (f32[3,8,512]{2,1,0:T(8,128)S(1)}, f32[3,8,512]{2,1,0:T(8,128)S(1)}, u32[]{:S(2)}, u32[]{:S(2)}) collective-permute-start(f32[3,8,512]{2,1,0:T(8,128)S(1)} %get-tuple-element.17.refs_1_), channel_id=1, source_target_pairs={{0,12},{4,8},{8,4},{12,0},{1,13},{5,9},{9,5},{13,1},{2,14},{6,10},... | collective-permute-start | bytes 147464 | tf_op jit(solution)/shard_map/ppermute | solution.py:407
  37.0 0.0 collective-permute-start.14
  37.0 0.0 collective-permute-done.15.refs_3_
  37.0 0.5 collective-permute-start.16
  37.5 2.8 %collective-permute-done.17.refs_5_ = f32[3,8,512]{2,1,0:T(8,128)S(1)} collective-permute-done((f32[3,8,512]{2,1,0:T(8,128)S(1)}, f32[3,8,512]{2,1,0:T(8,128)S(1)}, u32[]{:S(2)}, u32[]{:S(2)}) %collective-permute-start.17) | collective-permute-done | bytes 49184 | tf_op jit(solution)/shard_map/ppermute | solution.py:407
  40.3 0.0 collective-permute-start.18
  40.3 1.0 %collective-permute-done.19.refs_7_ = f32[3,8,512]{2,1,0:T(8,128)S(1)} collective-permute-done((f32[3,8,512]{2,1,0:T(8,128)S(1)}, f32[3,8,512]{2,1,0:T(8,128)S(1)}, u32[]{:S(2)}, u32[]{:S(2)}) %collective-permute-start.19) | collective-permute-done | bytes 49184 | tf_op jit(solution)/shard_map/ppermute | solution.py:407
  41.3 4.5 %query_sums.1 = (f32[8,2,256,128]{3,2,1,0:T(8,128)S(1)}, f32[3,8,512]{2,1,0:T(8,128)S(1)}) custom-call(bf16[4096,256]{1,0:T(8,128)(2,1)} %key_hbm.1, bf16[8,512,512]{2,1,0:T(8,128)(2,1)} %get-tuple-element.18.e_hbm, bf16[8,512,512]{2,1,0:T(8,128)(2,1)} %get-tuple-element.19.u_hbm, f32[3,8,512]{2,1,0:T(8,128)} %get-tuple-element.20.blk_hbm), custom_call_target="tpu_custom_call" | custom-call | tf_op jit(solution)/shard_map/query_sums/pallas_call | solution.py:233
  45.8 0.0 collective-permute-done.16.refs_4_
  45.9 1.2 %query_grads.1 = (f32[8,512]{1,0:T(8,128)S(1)}, f32[8,512]{1,0:T(8,128)S(1)}, f32[4,128,256]{2,1,0:T(8,128)S(1)}, bf16[4,128,256]{2,1,0:T(8,128)(2,1)S(1)}) custom-call(s32[6,8]{1,0:T(8,128)S(1)} %stack.15.refs_0_.meta, f32[3,8,512]{2,1,0:T(8,128)S(1)} %get-tuple-element.17.refs_1_, f32[3,8,512]{2,1,0:T(8,128)S(1)} %collective-permute-done.14.refs_2_, ...), custom_call_target="tpu_custom_call" | custom-call | tf_op jit(solution)/shard_map/query_grads/pallas_call | solution.py:297
  47.0 0.6 collective-permute-start.21
  47.6 1.2 %collective-permute-done.21 = bf16[4,128,256]{2,1,0:T(8,128)(2,1)S(1)} collective-permute-done((bf16[4,128,256]{2,1,0:T(8,128)(2,1)S(1)}, bf16[4,128,256]{2,1,0:T(8,128)(2,1)S(1)}, u32[]{:S(2)}, u32[]{:S(2)}) %collective-permute-start.21) | collective-permute-done | bytes 262176 | tf_op jit(solution)/shard_map/ppermute | solution.py:406
  48.8 0.1 fusion.9
  48.9 2.3 %collective-permute-start.24 = (bf16[128,256]{1,0:T(8,128)(2,1)S(1)}, bf16[128,256]{1,0:T(8,128)(2,1)S(1)}, u32[]{:S(2)}, u32[]{:S(2)}) collective-permute-start(bf16[128,256]{1,0:T(8,128)(2,1)S(1)} %get-tuple-element.34), channel_id=1, source_target_pairs={{0,12},{4,8},{8,4},{12,0},{1,13},{5,9},{9,5},{13,1},{2,14},{6,10},... | collective-permute-start | bytes 196616 | tf_op jit(solution)/shard_map/ppermute | solution.py:407
  51.2 2.2 %collective-permute-start.22 = (bf16[128,256]{1,0:T(8,128)(2,1)S(1)}, bf16[128,256]{1,0:T(8,128)(2,1)S(1)}, u32[]{:S(2)}, u32[]{:S(2)}) collective-permute-start(bf16[128,256]{1,0:T(8,128)(2,1)S(1)} %get-tuple-element.33), channel_id=1, source_target_pairs={{0,4},{4,0},{8,12},{12,8},{1,5},{5,1},{9,13},{13,9},{2,6},{6,2},{1... | collective-permute-start | bytes 196616 | tf_op jit(solution)/shard_map/ppermute | solution.py:407
  53.3 9.2 %row_grads.1 = (bf16[4096,256]{1,0:T(8,128)(2,1)}, bf16[4096,256]{1,0:T(8,128)(2,1)}) custom-call(s32[6,8]{1,0:T(8,128)S(1)} %stack.15.refs_0_.meta, f32[8,512]{1,0:T(8,128)S(1)} %get-tuple-element.26.c_ref, f32[8,512]{1,0:T(8,128)S(1)} %get-tuple-element.27.d_ref, bf16[8,512,128]{2,1,0:T(8,128)(2,1)} %get-tuple-element.28.qgt_hbm, ...), custom_call_target="tpu_custom_call" | custom-call | tf_op jit(solution)/shard_map/row_grads/pallas_call | solution.py:370
  62.6 0.7 %fusion.3 = bf16[128,256]{1,0:T(8,128)(2,1)} fusion(f32[4,128,256]{2,1,0:T(8,128)S(1)} %get-tuple-element.32, bf16[128,256]{1,0:T(8,128)(2,1)S(1)} %collective-permute-done.24, bf16[128,256]{1,0:T(8,128)(2,1)S(1)} %collective-permute-done.23, bf16[128,256]{1,0:T(8,128)(2,1)S(1)} %collective-permute-done.22), kind=kLoop, calls=%fused_computation.5 | loop fusion | flops 229376 | bytes 393216 | tf_op jit(solution)/shard_map/convert_element_type | solution.py:457
  (17 shorter events, 0.1 us)
Async XLA Ops:
  0.6 8.2 %collective-permute-start = (bf16[128,256]{1,0:T(8,128)(2,1)}, bf16[128,256]{1,0:T(8,128)(2,1)S(1)}, u32[]{:S(2)}, u32[]{:S(2)}) collective-permute-start(bf16[128,256]{1,0:T(8,128)(2,1)} %refs_1_.1), channel_id=1, source_target_pairs={{0,1},{1,0},{2,3},{3,2},{4,5},{5,4},{6,7},{7,6},{8,9},{9,8},{10,11... | collective-permute-start | bytes 196616 | tf_op jit(solution)/shard_map/ppermute | solution.py:406
  1.1 8.6 %collective-permute-start.1 = (bf16[128,256]{1,0:T(8,128)(2,1)}, bf16[128,256]{1,0:T(8,128)(2,1)S(1)}, u32[]{:S(2)}, u32[]{:S(2)}) collective-permute-start(bf16[128,256]{1,0:T(8,128)(2,1)} %refs_1_.1), channel_id=1, source_target_pairs={{0,4},{4,0},{8,12},{12,8},{1,5},{5,1},{9,13},{13,9},{2,6},{6,2},{1... | collective-permute-start | bytes 196616 | tf_op jit(solution)/shard_map/ppermute | solution.py:407
  3.8 9.5 %collective-permute-start.3 = (bf16[128,256]{1,0:T(8,128)(2,1)}, bf16[128,256]{1,0:T(8,128)(2,1)S(1)}, u32[]{:S(2)}, u32[]{:S(2)}) collective-permute-start(bf16[128,256]{1,0:T(8,128)(2,1)} %refs_1_.1), channel_id=1, source_target_pairs={{0,8},{4,12},{8,0},{12,4},{1,9},{5,13},{9,1},{13,5},{2,10},{6,14},... | collective-permute-start | bytes 196616 | tf_op jit(solution)/shard_map/ppermute | solution.py:407
  6.4 8.7 %collective-permute-start.5 = (bf16[128,256]{1,0:T(8,128)(2,1)}, bf16[128,256]{1,0:T(8,128)(2,1)S(1)}, u32[]{:S(2)}, u32[]{:S(2)}) collective-permute-start(bf16[128,256]{1,0:T(8,128)(2,1)} %refs_1_.1), channel_id=1, source_target_pairs={{0,12},{4,8},{8,4},{12,0},{1,13},{5,9},{9,5},{13,1},{2,14},{6,10},... | collective-permute-start | bytes 196616 | tf_op jit(solution)/shard_map/ppermute | solution.py:407
  6.4 8.7 %collective-permute-start.7 = (bf16[128,256]{1,0:T(8,128)(2,1)}, bf16[128,256]{1,0:T(8,128)(2,1)S(1)}, u32[]{:S(2)}, u32[]{:S(2)}) collective-permute-start(bf16[128,256]{1,0:T(8,128)(2,1)} %refs_9_.1), channel_id=1, source_target_pairs={{0,1},{1,0},{2,3},{3,2},{4,5},{5,4},{6,7},{7,6},{8,9},{9,8},{10,11... | collective-permute-start | bytes 196616 | tf_op jit(solution)/shard_map/ppermute | solution.py:406
  8.8 6.8 %collective-permute-start.8 = (bf16[128,256]{1,0:T(8,128)(2,1)}, bf16[128,256]{1,0:T(8,128)(2,1)S(1)}, u32[]{:S(2)}, u32[]{:S(2)}) collective-permute-start(bf16[128,256]{1,0:T(8,128)(2,1)} %refs_9_.1), channel_id=1, source_target_pairs={{0,4},{4,0},{8,12},{12,8},{1,5},{5,1},{9,13},{13,9},{2,6},{6,2},{1... | collective-permute-start | bytes 196616 | tf_op jit(solution)/shard_map/ppermute | solution.py:407
  9.8 8.0 %collective-permute-start.10 = (bf16[128,256]{1,0:T(8,128)(2,1)}, bf16[128,256]{1,0:T(8,128)(2,1)S(1)}, u32[]{:S(2)}, u32[]{:S(2)}) collective-permute-start(bf16[128,256]{1,0:T(8,128)(2,1)} %refs_9_.1), channel_id=1, source_target_pairs={{0,8},{4,12},{8,0},{12,4},{1,9},{5,13},{9,1},{13,5},{2,10},{6,14},... | collective-permute-start | bytes 196616 | tf_op jit(solution)/shard_map/ppermute | solution.py:407
  13.3 6.3 %collective-permute-start.12 = (bf16[128,256]{1,0:T(8,128)(2,1)}, bf16[128,256]{1,0:T(8,128)(2,1)S(1)}, u32[]{:S(2)}, u32[]{:S(2)}) collective-permute-start(bf16[128,256]{1,0:T(8,128)(2,1)} %refs_9_.1), channel_id=1, source_target_pairs={{0,12},{4,8},{8,4},{12,0},{1,13},{5,9},{9,5},{13,1},{2,14},{6,10},... | collective-permute-start | bytes 196616 | tf_op jit(solution)/shard_map/ppermute | solution.py:407
  15.1 4.6 %collective-permute-start.2 = (bf16[128,256]{1,0:T(8,128)(2,1)S(1)}, bf16[128,256]{1,0:T(8,128)(2,1)S(1)}, u32[]{:S(2)}, u32[]{:S(2)}) collective-permute-start(bf16[128,256]{1,0:T(8,128)(2,1)S(1)} %collective-permute-done.1.refs_3_), channel_id=1, source_target_pairs={{0,1},{1,0},{2,3},{3,2},{4,5},{5,4},{6,7},{7,6},{8,9},{9,8},{10,11... | collective-permute-start | bytes 196616 | tf_op jit(solution)/shard_map/ppermute | solution.py:406
  15.1 6.4 %collective-permute-start.4 = (bf16[128,256]{1,0:T(8,128)(2,1)S(1)}, bf16[128,256]{1,0:T(8,128)(2,1)S(1)}, u32[]{:S(2)}, u32[]{:S(2)}) collective-permute-start(bf16[128,256]{1,0:T(8,128)(2,1)S(1)} %collective-permute-done.3.refs_5_), channel_id=1, source_target_pairs={{0,1},{1,0},{2,3},{3,2},{4,5},{5,4},{6,7},{7,6},{8,9},{9,8},{10,11... | collective-permute-start | bytes 196616 | tf_op jit(solution)/shard_map/ppermute | solution.py:406
  15.7 5.9 %collective-permute-start.6 = (bf16[128,256]{1,0:T(8,128)(2,1)S(1)}, bf16[128,256]{1,0:T(8,128)(2,1)S(1)}, u32[]{:S(2)}, u32[]{:S(2)}) collective-permute-start(bf16[128,256]{1,0:T(8,128)(2,1)S(1)} %collective-permute-done.5.refs_7_), channel_id=1, source_target_pairs={{0,1},{1,0},{2,3},{3,2},{4,5},{5,4},{6,7},{7,6},{8,9},{9,8},{10,11... | collective-permute-start | bytes 196616 | tf_op jit(solution)/shard_map/ppermute | solution.py:406
  17.8 3.8 %collective-permute-start.9 = (bf16[128,256]{1,0:T(8,128)(2,1)S(1)}, bf16[128,256]{1,0:T(8,128)(2,1)S(1)}, u32[]{:S(2)}, u32[]{:S(2)}) collective-permute-start(bf16[128,256]{1,0:T(8,128)(2,1)S(1)} %collective-permute-done.8.refs_11_), channel_id=1, source_target_pairs={{0,1},{1,0},{2,3},{3,2},{4,5},{5,4},{6,7},{7,6},{8,9},{9,8},{10,11... | collective-permute-start | bytes 196616 | tf_op jit(solution)/shard_map/ppermute | solution.py:406
  19.6 1.9 %collective-permute-start.11 = (bf16[128,256]{1,0:T(8,128)(2,1)S(1)}, bf16[128,256]{1,0:T(8,128)(2,1)S(1)}, u32[]{:S(2)}, u32[]{:S(2)}) collective-permute-start(bf16[128,256]{1,0:T(8,128)(2,1)S(1)} %collective-permute-done.10.refs_13_), channel_id=1, source_target_pairs={{0,1},{1,0},{2,3},{3,2},{4,5},{5,4},{6,7},{7,6},{8,9},{9,8},{10,11... | collective-permute-start | bytes 196616 | tf_op jit(solution)/shard_map/ppermute | solution.py:406
  19.6 2.0 %collective-permute-start.13 = (bf16[128,256]{1,0:T(8,128)(2,1)S(1)}, bf16[128,256]{1,0:T(8,128)(2,1)S(1)}, u32[]{:S(2)}, u32[]{:S(2)}) collective-permute-start(bf16[128,256]{1,0:T(8,128)(2,1)S(1)} %collective-permute-done.12.refs_15_), channel_id=1, source_target_pairs={{0,1},{1,0},{2,3},{3,2},{4,5},{5,4},{6,7},{7,6},{8,9},{9,8},{10,11... | collective-permute-start | bytes 196616 | tf_op jit(solution)/shard_map/ppermute | solution.py:406
  32.5 4.5 %collective-permute-start.15 = (f32[3,8,512]{2,1,0:T(8,128)S(1)}, f32[3,8,512]{2,1,0:T(8,128)S(1)}, u32[]{:S(2)}, u32[]{:S(2)}) collective-permute-start(f32[3,8,512]{2,1,0:T(8,128)S(1)} %get-tuple-element.17.refs_1_), channel_id=1, source_target_pairs={{0,4},{4,0},{8,12},{12,8},{1,5},{5,1},{9,13},{13,9},{2,6},{6,2},{1... | collective-permute-start | bytes 147464 | tf_op jit(solution)/shard_map/ppermute | solution.py:407
  33.8 6.5 %collective-permute-start.17 = (f32[3,8,512]{2,1,0:T(8,128)S(1)}, f32[3,8,512]{2,1,0:T(8,128)S(1)}, u32[]{:S(2)}, u32[]{:S(2)}) collective-permute-start(f32[3,8,512]{2,1,0:T(8,128)S(1)} %get-tuple-element.17.refs_1_), channel_id=1, source_target_pairs={{0,8},{4,12},{8,0},{12,4},{1,9},{5,13},{9,1},{13,5},{2,10},{6,14},... | collective-permute-start | bytes 147464 | tf_op jit(solution)/shard_map/ppermute | solution.py:407
  35.3 6.0 %collective-permute-start.19 = (f32[3,8,512]{2,1,0:T(8,128)S(1)}, f32[3,8,512]{2,1,0:T(8,128)S(1)}, u32[]{:S(2)}, u32[]{:S(2)}) collective-permute-start(f32[3,8,512]{2,1,0:T(8,128)S(1)} %get-tuple-element.17.refs_1_), channel_id=1, source_target_pairs={{0,12},{4,8},{8,4},{12,0},{1,13},{5,9},{9,5},{13,1},{2,14},{6,10},... | collective-permute-start | bytes 147464 | tf_op jit(solution)/shard_map/ppermute | solution.py:407
  37.0 8.8 %collective-permute-start.14 = (f32[3,8,512]{2,1,0:T(8,128)S(1)}, f32[3,8,512]{2,1,0:T(8,128)S(1)}, u32[]{:S(2)}, u32[]{:S(2)}) collective-permute-start(f32[3,8,512]{2,1,0:T(8,128)S(1)} %get-tuple-element.17.refs_1_), channel_id=1, source_target_pairs={{0,1},{1,0},{2,3},{3,2},{4,5},{5,4},{6,7},{7,6},{8,9},{9,8},{10,11... | collective-permute-start | bytes 147464 | tf_op jit(solution)/shard_map/ppermute | solution.py:406
  37.0 8.8 %collective-permute-start.16 = (f32[3,8,512]{2,1,0:T(8,128)S(1)}, f32[3,8,512]{2,1,0:T(8,128)S(1)}, u32[]{:S(2)}, u32[]{:S(2)}) collective-permute-start(f32[3,8,512]{2,1,0:T(8,128)S(1)} %collective-permute-done.15.refs_3_), channel_id=1, source_target_pairs={{0,1},{1,0},{2,3},{3,2},{4,5},{5,4},{6,7},{7,6},{8,9},{9,8},{10,11... | collective-permute-start | bytes 147464 | tf_op jit(solution)/shard_map/ppermute | solution.py:406
  40.3 5.5 %collective-permute-start.18 = (f32[3,8,512]{2,1,0:T(8,128)S(1)}, f32[3,8,512]{2,1,0:T(8,128)S(1)}, u32[]{:S(2)}, u32[]{:S(2)}) collective-permute-start(f32[3,8,512]{2,1,0:T(8,128)S(1)} %collective-permute-done.17.refs_5_), channel_id=1, source_target_pairs={{0,1},{1,0},{2,3},{3,2},{4,5},{5,4},{6,7},{7,6},{8,9},{9,8},{10,11... | collective-permute-start | bytes 147464 | tf_op jit(solution)/shard_map/ppermute | solution.py:406
  41.3 4.6 %collective-permute-start.20 = (f32[3,8,512]{2,1,0:T(8,128)S(1)}, f32[3,8,512]{2,1,0:T(8,128)S(1)}, u32[]{:S(2)}, u32[]{:S(2)}) collective-permute-start(f32[3,8,512]{2,1,0:T(8,128)S(1)} %collective-permute-done.19.refs_7_), channel_id=1, source_target_pairs={{0,1},{1,0},{2,3},{3,2},{4,5},{5,4},{6,7},{7,6},{8,9},{9,8},{10,11... | collective-permute-start | bytes 147464 | tf_op jit(solution)/shard_map/ppermute | solution.py:406
  47.0 1.7 %collective-permute-start.21 = (bf16[4,128,256]{2,1,0:T(8,128)(2,1)S(1)}, bf16[4,128,256]{2,1,0:T(8,128)(2,1)S(1)}, u32[]{:S(2)}, u32[]{:S(2)}) collective-permute-start(bf16[4,128,256]{2,1,0:T(8,128)(2,1)S(1)} %get-tuple-element.24), channel_id=1, source_target_pairs={{0,1},{1,0},{2,3},{3,2},{4,5},{5,4},{6,7},{7,6},{8,9},{9,8},{10,11... | collective-permute-start | bytes 786440 | tf_op jit(solution)/shard_map/ppermute | solution.py:406
  48.9 13.7 %collective-permute-start.24 = (bf16[128,256]{1,0:T(8,128)(2,1)S(1)}, bf16[128,256]{1,0:T(8,128)(2,1)S(1)}, u32[]{:S(2)}, u32[]{:S(2)}) collective-permute-start(bf16[128,256]{1,0:T(8,128)(2,1)S(1)} %get-tuple-element.34), channel_id=1, source_target_pairs={{0,12},{4,8},{8,4},{12,0},{1,13},{5,9},{9,5},{13,1},{2,14},{6,10},... | collective-permute-start | bytes 196616 | tf_op jit(solution)/shard_map/ppermute | solution.py:407
  51.2 11.4 %collective-permute-start.23 = (bf16[128,256]{1,0:T(8,128)(2,1)S(1)}, bf16[128,256]{1,0:T(8,128)(2,1)S(1)}, u32[]{:S(2)}, u32[]{:S(2)}) collective-permute-start(bf16[128,256]{1,0:T(8,128)(2,1)S(1)} %get-tuple-element.35), channel_id=1, source_target_pairs={{0,8},{4,12},{8,0},{12,4},{1,9},{5,13},{9,1},{13,5},{2,10},{6,14},... | collective-permute-start | bytes 196616 | tf_op jit(solution)/shard_map/ppermute | solution.py:407
  51.2 11.4 %collective-permute-start.22 = (bf16[128,256]{1,0:T(8,128)(2,1)S(1)}, bf16[128,256]{1,0:T(8,128)(2,1)S(1)}, u32[]{:S(2)}, u32[]{:S(2)}) collective-permute-start(bf16[128,256]{1,0:T(8,128)(2,1)S(1)} %get-tuple-element.33), channel_id=1, source_target_pairs={{0,4},{4,0},{8,12},{12,8},{1,5},{5,1},{9,13},{13,9},{2,6},{6,2},{1... | collective-permute-start | bytes 196616 | tf_op jit(solution)/shard_map/ppermute | solution.py:407

commit v4 on v3

v4 whole, which is shorter than its diff:
```python
import math

import jax
import jax.numpy as jnp
from jax import lax
from jax.experimental import pallas as pl
from jax.experimental.pallas import tpu as pltpu
from jax.sharding import PartitionSpec as P

HD = 64
TEST = 128
BLK = 512
LANES = 128
WIDE = 2 * TEST

NEG = -1e30
SCORE_SCALE = 1.0 / math.sqrt(HD)
LOG2_SCALE = SCORE_SCALE * math.log2(math.e)
RP = ("rows", "pair")
PAIR = [(0, 1), (1, 0)]


def params(mib):
    return pltpu.CompilerParams(vmem_limit_bytes=mib * 1024 * 1024)


def two_heads(rows):
    feature = lax.broadcasted_iota(jnp.int32, rows.shape, 0)
    zero = jnp.zeros_like(rows)
    return jnp.concatenate(
        [jnp.where(feature < HD, rows, zero), jnp.where(feature < HD, zero, rows)], axis=1
    )


def every_copy(copies):
    for copy in copies:
        copy.start()
    return copies


def scores_kernel(count, held, meta, *refs):
    query_pieces, grad_pieces = refs[:count], refs[count : 2 * count]
    key_hbm, value_hbm = refs[2 * count : 2 * count + 2]
    qgt_s, state, blk_hbm, tab_ref = refs[2 * count + 2 : 2 * count + 6]
    blk_s, value_s, held_s, in_sem, held_sem, small_sem = refs[2 * count + 6 :]
    blocks, _, features = value_s.shape
    stacked = features // HD * TEST
    tables = qgt_s.shape[0]
    early = every_copy(
        [
            pltpu.make_async_copy(pieces[n], held_s.at[n, m], held_sem.at[n, m])
            for n in range(held)
            for m, pieces in enumerate((query_pieces, grad_pieces))
        ]
    )
    loads = []
    for b in range(blocks):
        rows = pl.ds(b * BLK, BLK)
        loads.append(
            every_copy(
                [
                    pltpu.make_async_copy(
                        key_hbm.at[rows], state.at[b, :, pl.ds(2 * stacked, features)], in_sem.at[0, b]
                    ),
                    pltpu.make_async_copy(value_hbm.at[rows], value_s.at[b], in_sem.at[1, b]),
                ]
            )
        )
    tab_ref[0] = jnp.full(tab_ref.shape[1:], NEG, jnp.float32)
    tab_ref[1] = jnp.zeros(tab_ref.shape[1:], jnp.float32)
    tab_ref[2] = jnp.zeros(tab_ref.shape[1:], jnp.float32)
    query = lax.broadcasted_iota(jnp.int32, (features, TEST), 1)

    def turn(at_slot, queries, grads):
        grads = grads.T
        qgt_s[at_slot, :features, :] = queries.T
        qgt_s[at_slot, features:, :] = jnp.where(
            query < meta[TESTN, meta[TABLE_OF, at_slot]], grads, jnp.zeros_like(grads)
        )

    per = tables // count
    for n in range(held, count):
        for m in range(per):
            rows = slice(m * TEST, (m + 1) * TEST)
            turn(n * per + m, query_pieces[n][rows, :], grad_pieces[n][rows, :])
    for copy in early:
        copy.wait()
    for n in range(held):
        turn(n, held_s[n, 0], held_s[n, 1])

    for b in range(blocks):
        for copy in loads[b]:
            copy.wait()
        table = meta[OWNER, b]
        at_slot = meta[SLOT_IN, table]
        key_live = lax.broadcasted_iota(jnp.int32, (BLK, WIDE), 0) < meta[LIVE, b]
        for p in range(features // LANES):
            at = slice(p * LANES, (p + 1) * LANES)
            wide = slice(p * WIDE, (p + 1) * WIDE)
            q_t = qgt_s[at_slot, at, :]
            g_t = qgt_s[at_slot, features + p * LANES : features + (p + 1) * LANES, :]
            keys = state[b, :, 2 * stacked + p * LANES : 2 * stacked + (p + 1) * LANES]
            scores = jnp.dot(keys, two_heads(q_t), preferred_element_type=jnp.float32)
            dprobs = jnp.dot(value_s[b, :, at], two_heads(g_t), preferred_element_type=jnp.float32)
            scores = jnp.where(key_live, scores, NEG)
            peak = jnp.max(scores, axis=0, keepdims=True) * LOG2_SCALE
            weights = jnp.exp2(scores * LOG2_SCALE - peak)
            mass = jnp.sum(weights, axis=0, keepdims=True)
            part = jnp.sum(weights * dprobs, axis=0, keepdims=True)
            state[b, :, wide] = weights.astype(jnp.bfloat16)
            state[b, :, stacked + p * WIDE : stacked + (p + 1) * WIDE] = (
                weights * (dprobs - part / mass)
            ).astype(jnp.bfloat16)
            blk_s[0, b : b + 1, wide] = peak
            blk_s[1, b : b + 1, wide] = mass
            blk_s[2, b : b + 1, wide] = part
            old = tab_ref[0, pl.ds(table, 1), wide]
            new = jnp.maximum(old, peak)
            old_weight = jnp.exp2(old - new)
            new_weight = jnp.exp2(peak - new)
            tab_ref[0, pl.ds(table, 1), wide] = new
            tab_ref[1, pl.ds(table, 1), wide] = (
                tab_ref[1, pl.ds(table, 1), wide] * old_weight + mass * new_weight
            )
            tab_ref[2, pl.ds(table, 1), wide] = (
                tab_ref[2, pl.ds(table, 1), wide] * old_weight + part * new_weight
            )
    for copy in every_copy([pltpu.make_async_copy(blk_s, blk_hbm, small_sem.at[0])]):
        copy.wait()


OWNER, LIVE, TESTN, SLOT_IN, TABLE_OF, SLOT_OUT = range(6)


def vmem_spec():
    return pl.BlockSpec(memory_space=pltpu.VMEM)


def smem_spec():
    return pl.BlockSpec(memory_space=pltpu.SMEM)


def hbm_spec():
    return pl.BlockSpec(memory_space=pltpu.HBM)


def in_hbm(value):
    return pltpu.with_memory_space_constraint(value, pltpu.HBM)


def block_scores(meta, tables, held, query_pieces, grad_pieces, key_rows, value_rows):
    features = key_rows.shape[1]
    blocks = key_rows.shape[0] // BLK
    stacked = features // HD * TEST
    count = len(query_pieces)
    pieces = []
    for group in (query_pieces, grad_pieces):
        pieces += [in_hbm(piece) if n < held else piece for n, piece in enumerate(group)]
    specs = [hbm_spec() if n % count < held else vmem_spec() for n in range(2 * count)]
    state = (blocks, BLK, 2 * stacked + features)
    turned = (tables, 2 * features, TEST)
    return pl.pallas_call(
        lambda *refs: scores_kernel(count, held, *refs),
        in_specs=[smem_spec()] + specs + [hbm_spec()] * 2,
        out_specs=[vmem_spec(), vmem_spec(), hbm_spec(), vmem_spec()],
        out_shape=[
            pltpu.VMEM(turned, jnp.bfloat16),
            pltpu.VMEM(state, jnp.bfloat16),
            pltpu.HBM((3, blocks, stacked), jnp.float32),
            jax.ShapeDtypeStruct((3, tables, stacked), jnp.float32),
        ],
        scratch_shapes=[
            pltpu.VMEM((3, blocks, stacked), jnp.float32),
            pltpu.VMEM((blocks, BLK, features), jnp.bfloat16),
            pltpu.VMEM((max(held, 1), 2, TEST, features), jnp.bfloat16),
            pltpu.SemaphoreType.DMA((2, blocks)),
            pltpu.SemaphoreType.DMA((max(held, 1), 2)),
            pltpu.SemaphoreType.DMA((1,)),
        ],
        compiler_params=params(16),
        name="block_scores",
    )(meta, *pieces, in_hbm(key_rows), in_hbm(value_rows))


def query_sums_kernel(state, blk_hbm, ab_ref, blk_ref, state_out, blk_sem):
    blocks, _, features, _ = ab_ref.shape
    stacked = features // HD * TEST
    copy = pltpu.make_async_copy(blk_hbm, blk_ref, blk_sem.at[0])
    copy.start()
    for b in range(blocks):
        for p in range(features // LANES):
            keys = state[b, :, 2 * stacked + p * LANES : 2 * stacked + (p + 1) * LANES]
            for n, first in enumerate((stacked, 0)):
                values = state[b, :, first + p * WIDE : first + (p + 1) * WIDE]
                product = lax.dot_general(
                    keys, values, (((0,), (0,)), ((), ())), preferred_element_type=jnp.float32
                )
                ab_ref[b, n, p * LANES : p * LANES + HD, :] = product[:HD, :TEST]
                ab_ref[b, n, p * LANES + HD : (p + 1) * LANES, :] = product[HD:, TEST:]
    copy.wait()


def query_sums(features, state, blk):
    blocks = state.shape[0]
    return pl.pallas_call(
        query_sums_kernel,
        in_specs=[vmem_spec(), hbm_spec()],
        out_specs=[vmem_spec()] * 3,
        out_shape=[
            pltpu.VMEM((blocks, 2, features, TEST), jnp.float32),
            pltpu.VMEM(blk.shape, jnp.float32),
            pltpu.VMEM(state.shape, jnp.bfloat16),
        ],
        input_output_aliases={0: 2},
        scratch_shapes=[pltpu.SemaphoreType.DMA((1,))],
        compiler_params=params(8),
        name="query_sums",
    )(state, in_hbm(blk))


def merged(pieces):
    peak = pieces[0][0]
    for piece in pieces[1:]:
        peak = jnp.maximum(peak, piece[0])
    mass = part = 0.0
    for piece in pieces:
        weight = jnp.exp2(piece[0] - peak)
        mass = mass + piece[1] * weight
        part = part + piece[2] * weight
    return peak, mass, part


def query_grad_kernel(count, meta, *refs):
    pieces = refs[:count]
    blk_ref, ab_ref = refs[count : count + 2]
    c_ref, d_ref, *q_refs = refs[count + 2 : -2]
    tab_s, acc_s = refs[-2:]
    blocks = blk_ref.shape[1]
    tables, features, _ = acc_s.shape
    tab_s[0], tab_s[1], tab_s[2] = merged(pieces)
    acc_s[...] = jnp.zeros_like(acc_s)
    for b in range(blocks):
        table = meta[OWNER, b]
        at = meta[SLOT_OUT, table]
        mass = tab_s[1, pl.ds(table, 1), :]
        c = jnp.exp2(blk_ref[0, b : b + 1, :] - tab_s[0, pl.ds(table, 1), :]) / mass
        shift = blk_ref[2, b : b + 1, :] / blk_ref[1, b : b + 1, :]
        d = c * (shift - tab_s[2, pl.ds(table, 1), :] / mass)
        c_ref[b : b + 1, :] = c
        d_ref[b : b + 1, :] = d
        for h in range(features // HD):
            rows = slice(h * HD, (h + 1) * HD)
            lanes = slice(h * TEST, (h + 1) * TEST)
            acc_s[at, rows, :] += c[:, lanes] * ab_ref[b, 0, rows, :] + d[:, lanes] * ab_ref[b, 1, rows, :]
    per = tables // len(q_refs)
    for n in range(tables):
        ref = q_refs[n // per]
        ref[n % per] = (acc_s[n] * SCORE_SCALE).T.astype(ref.dtype)


def query_grads(meta, tables, pieces, blk, ab, q_dtypes):
    blocks, _, features, _ = ab.shape
    stacked = blk.shape[2]
    per = tables // len(q_dtypes)
    return pl.pallas_call(
        lambda *refs: query_grad_kernel(len(pieces), *refs),
        in_specs=[smem_spec()] + [vmem_spec()] * (len(pieces) + 2),
        out_specs=[vmem_spec()] * (2 + len(q_dtypes)),
        out_shape=[
            jax.ShapeDtypeStruct((blocks, stacked), jnp.float32),
            jax.ShapeDtypeStruct((blocks, stacked), jnp.float32),
        ]
        + [jax.ShapeDtypeStruct((per, TEST, features), dtype) for dtype in q_dtypes],
        scratch_shapes=[
            pltpu.VMEM((3, tables, stacked), jnp.float32),
            pltpu.VMEM((tables, features, TEST), jnp.float32),
        ],
        compiler_params=params(10),
        name="query_grads",
    )(meta, *pieces, blk, ab)


def row_grads_kernel(meta, c_ref, d_ref, qgt_s, state, dk_hbm, dv_hbm, dk_s, dv_s, out_sem):
    blocks, _, features = dk_s.shape
    stacked = features // HD * TEST
    turned = (((1,), (1,)), ((), ()))
    stores = []
    for b in range(blocks):
        at_slot = meta[SLOT_IN, meta[OWNER, b]]
        for p in range(features // LANES):
            at = slice(p * LANES, (p + 1) * LANES)
            wide = slice(p * WIDE, (p + 1) * WIDE)
            c = c_ref[b : b + 1, wide]
            d = d_ref[b : b + 1, wide]
            q_t = two_heads(qgt_s[at_slot, at, :].astype(jnp.float32))
            g_t = two_heads(
                qgt_s[at_slot, features + p * LANES : features + (p + 1) * LANES, :].astype(jnp.float32)
            )
            for_u = (q_t * (c * SCORE_SCALE)).astype(jnp.bfloat16)
            for_e = jnp.concatenate([g_t * c, q_t * (d * SCORE_SCALE)], axis=0).astype(jnp.bfloat16)
            from_e = lax.dot_general(
                state[b, :, wide], for_e, turned, preferred_element_type=jnp.float32
            )
            moved = state[b, :, stacked + p * WIDE : stacked + (p + 1) * WIDE]
            from_u = lax.dot_general(moved, for_u, turned, preferred_element_type=jnp.float32)
            dv_s[b, :, at] = from_e[:, :LANES].astype(jnp.bfloat16)
            dk_s[b, :, at] = (from_u + from_e[:, LANES:]).astype(jnp.bfloat16)
        rows = pl.ds(b * BLK, BLK)
        stores += every_copy(
            [
                pltpu.make_async_copy(dk_s.at[b], dk_hbm.at[rows], out_sem.at[0, b]),
                pltpu.make_async_copy(dv_s.at[b], dv_hbm.at[rows], out_sem.at[1, b]),
            ]
        )
    for copy in stores:
        copy.wait()


def row_grads(meta, c, d, qgt, state):
    blocks = state.shape[0]
    features = qgt.shape[1] // 2
    return pl.pallas_call(
        row_grads_kernel,
        in_specs=[smem_spec()] + [vmem_spec()] * 4,
        out_specs=[hbm_spec()] * 2,
        out_shape=[jax.ShapeDtypeStruct((blocks * BLK, features), jnp.bfloat16)] * 2,
        scratch_shapes=[
            pltpu.VMEM((blocks, BLK, features), jnp.bfloat16),
            pltpu.VMEM((blocks, BLK, features), jnp.bfloat16),
            pltpu.SemaphoreType.DMA((2, blocks)),
        ],
        compiler_params=params(10),
        name="row_grads",
    )(meta, c, d, qgt, state)


def index_kernel(small, blocks, block_table, train_rows, test_rows, meta, count):
    chip = lax.axis_index("rows").astype(jnp.int32)
    core = lax.axis_index("pair").astype(jnp.int32)
    first = lax.axis_index(RP).astype(jnp.int32) * blocks
    tables = train_rows.shape[0]
    for t in range(tables):
        count[t] = 0
        meta[TESTN, t] = test_rows[t]
        if small:
            away = (t // 2) ^ chip
            not_mine = (t % 2) ^ core
            meta[SLOT_IN, t] = 2 * away + not_mine
            meta[TABLE_OF, t] = 2 * away + not_mine
            meta[SLOT_OUT, t] = 4 * not_mine + ((away + 3) & 3)
        else:
            for row in (SLOT_IN, TABLE_OF, SLOT_OUT):
                meta[row, t] = t

    def earlier(n, carry):
        table = block_table[n]
        count[table] = count[table] + 1
        return carry

    lax.fori_loop(0, first, earlier, 0)
    for b in range(blocks):
        table = block_table[first + b]
        meta[OWNER, b] = table
        meta[LIVE, b] = jnp.minimum(train_rows[table] - count[table] * BLK, BLK)
        count[table] = count[table] + 1


def index_table(small, blocks, block_table, train_rows, test_rows):
    tables = train_rows.shape[0]
    return pl.pallas_call(
        lambda *refs: index_kernel(small, blocks, *refs),
        in_specs=[smem_spec()] * 3,
        out_specs=smem_spec(),
        out_shape=jax.ShapeDtypeStruct((6, max(blocks, tables)), jnp.int32),
        scratch_shapes=[pltpu.SMEM((tables,), jnp.int32)],
        name="index_table",
    )(block_table, train_rows, test_rows)


def local(small, query_rows, key_rows, value_rows, cotangent, train_rows, test_rows, block_table):
    features = query_rows.shape[1]
    blocks = key_rows.shape[0] // BLK
    tables = train_rows.shape[0]
    pair = lambda value: lax.ppermute(value, "pair", PAIR)
    step = lambda value, s: lax.ppermute(value, "rows", [(z, z ^ s) for z in range(4)])
    if small:
        held = 1

        def spread(value):
            pieces = []
            for near in [value] + [step(value, s) for s in (1, 2, 3)]:
                pieces += [near, pair(near)]
            return pieces

    else:
        held = 0
        spread = lambda value: [lax.all_gather(value, RP, axis=0, tiled=True)]

    queries = spread(query_rows)
    grads = spread(cotangent)
    if small:
        block_table, queries[2] = lax.optimization_barrier((block_table, queries[2]))
    meta = index_table(small, blocks, block_table, train_rows, test_rows)
    qgt, state, blk, tab = block_scores(meta, tables, held, queries, grads, key_rows, value_rows)
    if small:
        stats = spread(tab)
        dtypes = [jnp.float32, jnp.bfloat16]
    else:
        peak = lax.pmax(tab[0], RP)
        sums = lax.psum(tab[1:] * jnp.exp2(tab[0] - peak)[None], RP)
        stats = [jnp.concatenate([peak[None], sums], axis=0)]
        dtypes = [jnp.float32]
    ab, blk, state = query_sums(features, state, blk)
    c, d, *q_terms = query_grads(meta, tables, stats, blk, ab, dtypes)
    if small:
        keep, send = q_terms
        total = keep + pair(send).astype(jnp.float32)
        low = total.astype(jnp.bfloat16)
        got = [step(low[s - 1], s) for s in (1, 2, 3)]
        low, c = lax.optimization_barrier((low, c))
        key_grad, value_grad = row_grads(meta, c, d, qgt, state)
        query_grad = total[3]
        for value in got:
            query_grad = query_grad + value.astype(jnp.float32)
    else:
        query_grad = lax.psum_scatter(
            q_terms[0].reshape(tables * TEST, features), RP, scatter_dimension=0, tiled=True
        )
        key_grad, value_grad = row_grads(meta, c, d, qgt, state)
    return query_grad.astype(jnp.bfloat16), key_grad, value_grad


def solution(mesh):
    sizes = mesh.shape
    tables_of_rows = P(("groups", "rows", "pair"), "mp")
    in_specs = (tables_of_rows,) * 4 + (P("groups"),) * 3
    out_specs = (tables_of_rows,) * 3

    def run(query_rows, *rest):
        local_rows = query_rows.shape[0] // (sizes["groups"] * sizes["rows"] * sizes["pair"])
        small = sizes["rows"] == 4 and sizes["pair"] == 2 and local_rows == TEST
        return jax.shard_map(
            lambda *args: local(small, *args),
            mesh=mesh,
            in_specs=in_specs,
            out_specs=out_specs,
            check_vma=False,
        )(query_rows, *rest)

    return run
```

time: 63.5 us -> 54.9 us (0.86)
  Pallas kernels: 25.9 us -> 18.1 us
  waiting for transfers between devices: 8.83 us -> 12.4 us
  other arithmetic: 2.45 us -> 0.73 us
  local copies, waits for them, and re-layouts: 2.15 us -> 0.7 us
  starting transfers between devices: 23.2 us -> 22 us
    pallas_call x1, Pallas kernels: 9.23 us -> 3.9 us  [row_grads(): pl.pallas_call(row_grads_kernel, in_specs=[smem_spec()] + [vmem_spec()] *...]
    ppermute x12, waiting for transfers between devices: 7.64 us -> 11.1 us  [local(): lax.ppermute(value, 'rows', [(z, z ^ s) for z in range(4)])]
    pallas_call x1 -> x2, Pallas kernels: 4.53 us -> 2.65 us  [the longest x1 1.35 us: index_table(): pl.pallas_call(lambda *refs: index_kernel(small, blocks, *refs), in_specs...]
    reduce_sum x2 -> x0, other arithmetic: 1.68 us -> none  [the longest x1 0.84 us: local(): ordinal = jnp.sum(jnp.where(earlier, 1, 0), axis=1).astype(jnp.int32)]
    another operation x2 -> x0, local copies, waits for them, and re-layouts: 1.4 us -> none  [local(): jnp.stack([pad(v) for v in (owner, live, test_rows, slot_in, table_of, sl...]
    ppermute x12, starting transfers between devices: 20.4 us -> 19 us  [local(): lax.ppermute(value, 'rows', [(z, z ^ s) for z in range(4)])]
    dynamic_slice x1 -> x0, local copies, waits for them, and re-layouts: 0.73 us -> none  [local(): owner = lax.dynamic_slice_in_dim(block_table, device * blocks, blocks)]
    unnamed x0 -> x2, local copies, waits for them, and re-layouts: none -> 0.68 us
  transfers between devices with their start and end apart: 25 -> 25, of which waited for: 5 -> 7; matrix products, arithmetic and copies ran while one was open for 6% -> 0% of each run, Pallas kernels for 22% -> 12%
where the time goes in v4:
time: 54.9 us; the launch traced here: 54.7 us
  starting transfers between devices  22 us (40%)
  Pallas kernels  18.1 us (33%)
  waiting for transfers between devices  12.4 us (23%)
  between operations  0.81 us (1%)
  other arithmetic  0.73 us (1%)
  local copies, waits for them, and re-layouts  0.7 us (1%)
    ppermute x12, starting transfers between devices, local(): lax.ppermute(value, 'rows', [(z, z ^ s) for z in range(4)])  19 us
    ppermute x12, waiting for transfers between devices, local(): lax.ppermute(value, 'rows', [(z, z ^ s) for z in range(4)])  11.1 us
    pallas_call x1, Pallas kernels, block_scores(): pl.pallas_call(lambda *refs: scores_kernel(count, held, *refs), in_specs=...  10.4 us
    pallas_call x1, Pallas kernels, row_grads(): pl.pallas_call(row_grads_kernel, in_specs=[smem_spec()] + [vmem_spec()] *...  3.9 us
    ppermute x13, starting transfers between devices, local(): pair = lambda value: lax.ppermute(value, 'pair', PAIR)  2.99 us
    pallas_call x1, Pallas kernels, index_table(): pl.pallas_call(lambda *refs: index_kernel(small, blocks, *refs), in_specs...  1.35 us
    ppermute x13, waiting for transfers between devices, local(): pair = lambda value: lax.ppermute(value, 'pair', PAIR)  1.34 us
    pallas_call x1, Pallas kernels, query_sums(): pl.pallas_call(query_sums_kernel, in_specs=[vmem_spec(), hbm_spec()], out...  1.29 us
  transfers between devices with their start and end apart: 25, of which 7 were waited for; matrix products, arithmetic and copies ran while one was open for 0% of the time, Pallas kernels for 12%

profile of v4, /device:TPU:0, one launch (start us, length us, event | category | flops | bytes accessed | tf_op | source)
XLA Modules:
  0.0 54.7 jit_solution(13000499823411755381)
XLA Ops:
  0.6 3.1 %collective-permute-start = (bf16[128,256]{1,0:T(8,128)(2,1)}, bf16[128,256]{1,0:T(8,128)(2,1)S(1)}, u32[]{:S(2)}, u32[]{:S(2)}) collective-permute-start(bf16[128,256]{1,0:T(8,128)(2,1)} %refs_1_.3), channel_id=1, source_target_pairs={{0,4},{4,0},{8,12},{12,8},{1,5},{5,1},{9,13},{13,9},{2,6},{6,2},{1... | collective-permute-start | bytes 196616 | tf_op jit(solution)/shard_map/ppermute | solution.py:385
  3.7 2.6 %collective-permute-start.10 = (bf16[128,256]{1,0:T(8,128)(2,1)}, bf16[128,256]{1,0:T(8,128)(2,1)S(1)}, u32[]{:S(2)}, u32[]{:S(2)}) collective-permute-start(bf16[128,256]{1,0:T(8,128)(2,1)} %refs_9_.1), channel_id=1, source_target_pairs={{0,8},{4,12},{8,0},{12,4},{1,9},{5,13},{9,1},{13,5},{2,10},{6,14},... | collective-permute-start | bytes 196616 | tf_op jit(solution)/shard_map/ppermute | solution.py:385
  6.3 0.0 collective-permute-start.12
  6.3 1.9 %collective-permute-start.3 = (bf16[128,256]{1,0:T(8,128)(2,1)}, bf16[128,256]{1,0:T(8,128)(2,1)S(1)}, u32[]{:S(2)}, u32[]{:S(2)}) collective-permute-start(bf16[128,256]{1,0:T(8,128)(2,1)} %refs_1_.3), channel_id=1, source_target_pairs={{0,8},{4,12},{8,0},{12,4},{1,9},{5,13},{9,1},{13,5},{2,10},{6,14},... | collective-permute-start | bytes 196616 | tf_op jit(solution)/shard_map/ppermute | solution.py:385
  8.2 1.9 %collective-permute-start.5 = (bf16[128,256]{1,0:T(8,128)(2,1)}, bf16[128,256]{1,0:T(8,128)(2,1)S(1)}, u32[]{:S(2)}, u32[]{:S(2)}) collective-permute-start(bf16[128,256]{1,0:T(8,128)(2,1)} %refs_1_.3), channel_id=1, source_target_pairs={{0,12},{4,8},{8,4},{12,0},{1,13},{5,9},{9,5},{13,1},{2,14},{6,10},... | collective-permute-start | bytes 196616 | tf_op jit(solution)/shard_map/ppermute | solution.py:385
  10.1 0.6 %collective-permute-start.8 = (bf16[128,256]{1,0:T(8,128)(2,1)}, bf16[128,256]{1,0:T(8,128)(2,1)S(1)}, u32[]{:S(2)}, u32[]{:S(2)}) collective-permute-start(bf16[128,256]{1,0:T(8,128)(2,1)} %refs_9_.1), channel_id=1, source_target_pairs={{0,4},{4,0},{8,12},{12,8},{1,5},{5,1},{9,13},{13,9},{2,6},{6,2},{1... | collective-permute-start | bytes 196616 | tf_op jit(solution)/shard_map/ppermute | solution.py:385
  10.7 2.9 %collective-permute-done.10.refs_13_ = bf16[128,256]{1,0:T(8,128)(2,1)S(1)} collective-permute-done((bf16[128,256]{1,0:T(8,128)(2,1)}, bf16[128,256]{1,0:T(8,128)(2,1)S(1)}, u32[]{:S(2)}, u32[]{:S(2)}) %collective-permute-start.10) | collective-permute-done | bytes 65568 | tf_op jit(solution)/shard_map/ppermute | solution.py:385
  13.6 0.0 collective-permute-done.12.refs_15_
  13.6 0.5 collective-permute-start.7
  14.2 3.4 %collective-permute-done.3.refs_5_ = bf16[128,256]{1,0:T(8,128)(2,1)S(1)} collective-permute-done((bf16[128,256]{1,0:T(8,128)(2,1)}, bf16[128,256]{1,0:T(8,128)(2,1)S(1)}, u32[]{:S(2)}, u32[]{:S(2)}) %collective-permute-start.3) | collective-permute-done | bytes 65568 | tf_op jit(solution)/shard_map/ppermute | solution.py:385
  17.6 0.0 collective-permute-done.5.refs_7_
  17.6 0.5 collective-permute-start.13
  18.1 0.0 collective-permute-done.8.refs_11_
  18.1 0.1 collective-permute-start.2
  18.1 0.4 collective-permute-start.4
  18.6 0.0 collective-permute-done.7.refs_10_
  18.6 0.1 collective-permute-start.6
  18.7 0.1 collective-permute-done.11.refs_14_
  18.8 0.3 collective-permute-start.9
  19.1 1.4 %index_table.1.refs_0_.meta = s32[6,8]{1,0:T(8,128)} custom-call(s32[64]{0:T(128)} %refs_0_, s32[8]{0:T(128)} %refs_1_.2, s32[8]{0:T(128)} %refs_2_.1), custom_call_target="tpu_custom_call" | custom-call | tf_op jit(solution)/shard_map/index_table/pallas_call | solution.py:370
  20.5 0.0 collective-permute-done.2.refs_4_
  20.5 0.0 collective-permute-done.4.refs_6_
  20.5 0.0 collective-permute-done.9.refs_12_
  20.5 0.0 copy-start
  20.5 0.7 %copy-done = s32[6,8]{1,0:T(8,128)S(1)} copy-done((s32[6,8]{1,0:T(8,128)S(1)}, s32[6,8]{1,0:T(8,128)}, u32[]{:S(2)}) %copy-start) | copy-done | bytes 216
  21.2 10.4 %block_scores.1 = (bf16[8,512,128]{2,1,0:T(8,128)(2,1)S(1)}, bf16[8,512,1280]{2,1,0:T(8,128)(2,1)S(1)}, f32[3,8,512]{2,1,0:T(8,128)}, f32[3,8,512]{2,1,0:T(8,128)S(1)}) custom-call(s32[6,8]{1,0:T(8,128)S(1)} %copy-done, bf16[128,256]{1,0:T(8,128)(2,1)} %refs_1_.3, bf16[128,256]{1,0:T(8,128)(2,1)S(1)} %collective-permute-done.1.refs_2_, ...), custom_call_target="tpu_custom_call" | custom-call | tf_op jit(solution)/shard_map/block_scores/pallas_call | solution.py:162
  31.6 1.0 %collective-permute-start.15 = (f32[3,8,512]{2,1,0:T(8,128)S(1)}, f32[3,8,512]{2,1,0:T(8,128)S(1)}, u32[]{:S(2)}, u32[]{:S(2)}) collective-permute-start(f32[3,8,512]{2,1,0:T(8,128)S(1)} %get-tuple-element.21.refs_1_), channel_id=1, source_target_pairs={{0,4},{4,0},{8,12},{12,8},{1,5},{5,1},{9,13},{13,9},{2,6},{6,2},{1... | collective-permute-start | bytes 147464 | tf_op jit(solution)/shard_map/ppermute | solution.py:385
  32.6 2.4 %collective-permute-start.17 = (f32[3,8,512]{2,1,0:T(8,128)S(1)}, f32[3,8,512]{2,1,0:T(8,128)S(1)}, u32[]{:S(2)}, u32[]{:S(2)}) collective-permute-start(f32[3,8,512]{2,1,0:T(8,128)S(1)} %get-tuple-element.21.refs_1_), channel_id=1, source_target_pairs={{0,8},{4,12},{8,0},{12,4},{1,9},{5,13},{9,1},{13,5},{2,10},{6,14},... | collective-permute-start | bytes 147464 | tf_op jit(solution)/shard_map/ppermute | solution.py:385
  35.0 1.0 %collective-permute-start.19 = (f32[3,8,512]{2,1,0:T(8,128)S(1)}, f32[3,8,512]{2,1,0:T(8,128)S(1)}, u32[]{:S(2)}, u32[]{:S(2)}) collective-permute-start(f32[3,8,512]{2,1,0:T(8,128)S(1)} %get-tuple-element.21.refs_1_), channel_id=1, source_target_pairs={{0,12},{4,8},{8,4},{12,0},{1,13},{5,9},{9,5},{13,1},{2,14},{6,10},... | collective-permute-start | bytes 147464 | tf_op jit(solution)/shard_map/ppermute | solution.py:385
  36.0 0.0 collective-permute-start.14
  36.1 0.0 collective-permute-done.15.refs_3_
  36.1 0.5 collective-permute-start.16
  36.6 2.2 %collective-permute-done.17.refs_5_ = f32[3,8,512]{2,1,0:T(8,128)S(1)} collective-permute-done((f32[3,8,512]{2,1,0:T(8,128)S(1)}, f32[3,8,512]{2,1,0:T(8,128)S(1)}, u32[]{:S(2)}, u32[]{:S(2)}) %collective-permute-start.17) | collective-permute-done | bytes 49184 | tf_op jit(solution)/shard_map/ppermute | solution.py:385
  38.8 2.1 %collective-permute-done.19.refs_7_ = f32[3,8,512]{2,1,0:T(8,128)S(1)} collective-permute-done((f32[3,8,512]{2,1,0:T(8,128)S(1)}, f32[3,8,512]{2,1,0:T(8,128)S(1)}, u32[]{:S(2)}, u32[]{:S(2)}) %collective-permute-start.19) | collective-permute-done | bytes 49184 | tf_op jit(solution)/shard_map/ppermute | solution.py:385
  40.9 1.3 %query_sums.1 = (f32[8,2,256,128]{3,2,1,0:T(8,128)S(1)}, f32[3,8,512]{2,1,0:T(8,128)S(1)}, bf16[8,512,1280]{2,1,0:T(8,128)(2,1)S(1)}) custom-call(bf16[8,512,1280]{2,1,0:T(8,128)(2,1)S(1)} %get-tuple-element.22.state, f32[3,8,512]{2,1,0:T(8,128)} %get-tuple-element.23.blk_hbm), custom_call_target="tpu_custom_call", output_to_operand_aliasing={{2}: (0, {})} | custom-call | tf_op jit(solution)/shard_map/query_sums/pallas_call | solution.py:205
  42.2 0.0 collective-permute-done.18.refs_6_
  42.2 0.0 collective-permute-done.20.refs_8_
  42.2 1.2 %query_grads.1 = (f32[8,512]{1,0:T(8,128)S(1)}, f32[8,512]{1,0:T(8,128)S(1)}, f32[4,128,256]{2,1,0:T(8,128)S(1)}, bf16[4,128,256]{2,1,0:T(8,128)(2,1)S(1)}) custom-call(s32[6,8]{1,0:T(8,128)S(1)} %copy-done, f32[3,8,512]{2,1,0:T(8,128)S(1)} %get-tuple-element.21.refs_1_, f32[3,8,512]{2,1,0:T(8,128)S(1)} %collective-permute-done.14.refs_2_, ...), custom_call_target="tpu_custom_call" | custom-call | tf_op jit(solution)/shard_map/query_grads/pallas_call | solution.py:265
  43.4 0.6 %collective-permute-start.21 = (bf16[4,128,256]{2,1,0:T(8,128)(2,1)S(1)}, bf16[4,128,256]{2,1,0:T(8,128)(2,1)S(1)}, u32[]{:S(2)}, u32[]{:S(2)}) collective-permute-start(bf16[4,128,256]{2,1,0:T(8,128)(2,1)S(1)} %get-tuple-element.27), channel_id=1, source_target_pairs={{0,1},{1,0},{2,3},{3,2},{4,5},{5,4},{6,7},{7,6},{8,9},{9,8},{10,11... | collective-permute-start | bytes 786440 | tf_op jit(solution)/shard_map/ppermute | solution.py:384
  44.0 1.2 %collective-permute-done.21 = bf16[4,128,256]{2,1,0:T(8,128)(2,1)S(1)} collective-permute-done((bf16[4,128,256]{2,1,0:T(8,128)(2,1)S(1)}, bf16[4,128,256]{2,1,0:T(8,128)(2,1)S(1)}, u32[]{:S(2)}, u32[]{:S(2)}) %collective-permute-start.21) | collective-permute-done | bytes 262176 | tf_op jit(solution)/shard_map/ppermute | solution.py:384
  45.2 0.1 fusion.4
  45.3 0.1 collective-permute-start.22
  45.3 2.6 %collective-permute-start.23 = (bf16[128,256]{1,0:T(8,128)(2,1)S(1)}, bf16[128,256]{1,0:T(8,128)(2,1)S(1)}, u32[]{:S(2)}, u32[]{:S(2)}) collective-permute-start(bf16[128,256]{1,0:T(8,128)(2,1)S(1)} %get-tuple-element.39), channel_id=1, source_target_pairs={{0,8},{4,12},{8,0},{12,4},{1,9},{5,13},{9,1},{13,5},{2,10},{6,14},... | collective-permute-start | bytes 196616 | tf_op jit(solution)/shard_map/ppermute | solution.py:385
  47.9 1.8 %collective-permute-start.24 = (bf16[128,256]{1,0:T(8,128)(2,1)S(1)}, bf16[128,256]{1,0:T(8,128)(2,1)S(1)}, u32[]{:S(2)}, u32[]{:S(2)}) collective-permute-start(bf16[128,256]{1,0:T(8,128)(2,1)S(1)} %get-tuple-element.38), channel_id=1, source_target_pairs={{0,12},{4,8},{8,4},{12,0},{1,13},{5,9},{9,5},{13,1},{2,14},{6,10},... | collective-permute-start | bytes 196616 | tf_op jit(solution)/shard_map/ppermute | solution.py:385
  49.7 3.9 %row_grads.1 = (bf16[4096,256]{1,0:T(8,128)(2,1)}, bf16[4096,256]{1,0:T(8,128)(2,1)}) custom-call(s32[6,8]{1,0:T(8,128)S(1)} %copy-done, f32[8,512]{1,0:T(8,128)S(1)} %get-tuple-element.29.c_ref, f32[8,512]{1,0:T(8,128)S(1)} %get-tuple-element.30.d_ref, bf16[8,512,128]{2,1,0:T(8,128)(2,1)S(1)} %get-tuple-element.31.qgt_s, ...), custom_call_target="tpu_custom_call" | custom-call | tf_op jit(solution)/shard_map/row_grads/pallas_call | solution.py:322
  53.6 0.0 collective-permute-done.22
  53.7 0.4 collective-permute-done.24
  54.1 0.7 %fusion.3 = bf16[128,256]{1,0:T(8,128)(2,1)} fusion(f32[4,128,256]{2,1,0:T(8,128)S(1)} %get-tuple-element.36, bf16[128,256]{1,0:T(8,128)(2,1)S(1)} %collective-permute-done.24, bf16[128,256]{1,0:T(8,128)(2,1)S(1)} %collective-permute-done.23, bf16[128,256]{1,0:T(8,128)(2,1)S(1)} %collective-permute-done.22), kind=kLoop, calls=%fused_computation.5 | loop fusion | flops 229376 | bytes 393216 | tf_op jit(solution)/shard_map/convert_element_type | solution.py:430
  (12 shorter events, 0.0 us)
Async XLA Ops:
  0.6 9.5 %collective-permute-start = (bf16[128,256]{1,0:T(8,128)(2,1)}, bf16[128,256]{1,0:T(8,128)(2,1)S(1)}, u32[]{:S(2)}, u32[]{:S(2)}) collective-permute-start(bf16[128,256]{1,0:T(8,128)(2,1)} %refs_1_.3), channel_id=1, source_target_pairs={{0,4},{4,0},{8,12},{12,8},{1,5},{5,1},{9,13},{13,9},{2,6},{6,2},{1... | collective-permute-start | bytes 196616 | tf_op jit(solution)/shard_map/ppermute | solution.py:385
  3.7 9.9 %collective-permute-start.10 = (bf16[128,256]{1,0:T(8,128)(2,1)}, bf16[128,256]{1,0:T(8,128)(2,1)S(1)}, u32[]{:S(2)}, u32[]{:S(2)}) collective-permute-start(bf16[128,256]{1,0:T(8,128)(2,1)} %refs_9_.1), channel_id=1, source_target_pairs={{0,8},{4,12},{8,0},{12,4},{1,9},{5,13},{9,1},{13,5},{2,10},{6,14},... | collective-permute-start | bytes 196616 | tf_op jit(solution)/shard_map/ppermute | solution.py:385
  6.3 7.3 %collective-permute-start.12 = (bf16[128,256]{1,0:T(8,128)(2,1)}, bf16[128,256]{1,0:T(8,128)(2,1)S(1)}, u32[]{:S(2)}, u32[]{:S(2)}) collective-permute-start(bf16[128,256]{1,0:T(8,128)(2,1)} %refs_9_.1), channel_id=1, source_target_pairs={{0,12},{4,8},{8,4},{12,0},{1,13},{5,9},{9,5},{13,1},{2,14},{6,10},... | collective-permute-start | bytes 196616 | tf_op jit(solution)/shard_map/ppermute | solution.py:385
  6.3 11.2 %collective-permute-start.3 = (bf16[128,256]{1,0:T(8,128)(2,1)}, bf16[128,256]{1,0:T(8,128)(2,1)S(1)}, u32[]{:S(2)}, u32[]{:S(2)}) collective-permute-start(bf16[128,256]{1,0:T(8,128)(2,1)} %refs_1_.3), channel_id=1, source_target_pairs={{0,8},{4,12},{8,0},{12,4},{1,9},{5,13},{9,1},{13,5},{2,10},{6,14},... | collective-permute-start | bytes 196616 | tf_op jit(solution)/shard_map/ppermute | solution.py:385
  8.2 9.3 %collective-permute-start.5 = (bf16[128,256]{1,0:T(8,128)(2,1)}, bf16[128,256]{1,0:T(8,128)(2,1)S(1)}, u32[]{:S(2)}, u32[]{:S(2)}) collective-permute-start(bf16[128,256]{1,0:T(8,128)(2,1)} %refs_1_.3), channel_id=1, source_target_pairs={{0,12},{4,8},{8,4},{12,0},{1,13},{5,9},{9,5},{13,1},{2,14},{6,10},... | collective-permute-start | bytes 196616 | tf_op jit(solution)/shard_map/ppermute | solution.py:385
  10.1 7.9 %collective-permute-start.8 = (bf16[128,256]{1,0:T(8,128)(2,1)}, bf16[128,256]{1,0:T(8,128)(2,1)S(1)}, u32[]{:S(2)}, u32[]{:S(2)}) collective-permute-start(bf16[128,256]{1,0:T(8,128)(2,1)} %refs_9_.1), channel_id=1, source_target_pairs={{0,4},{4,0},{8,12},{12,8},{1,5},{5,1},{9,13},{13,9},{2,6},{6,2},{1... | collective-permute-start | bytes 196616 | tf_op jit(solution)/shard_map/ppermute | solution.py:385
  13.6 4.5 %collective-permute-start.1 = (bf16[128,256]{1,0:T(8,128)(2,1)}, bf16[128,256]{1,0:T(8,128)(2,1)S(1)}, u32[]{:S(2)}, u32[]{:S(2)}) collective-permute-start(bf16[128,256]{1,0:T(8,128)(2,1)} %refs_1_.3), channel_id=1, source_target_pairs={{0,1},{1,0},{2,3},{3,2},{4,5},{5,4},{6,7},{7,6},{8,9},{9,8},{10,11... | collective-permute-start | bytes 196616 | tf_op jit(solution)/shard_map/ppermute | solution.py:384
  13.6 5.0 %collective-permute-start.7 = (bf16[128,256]{1,0:T(8,128)(2,1)}, bf16[128,256]{1,0:T(8,128)(2,1)S(1)}, u32[]{:S(2)}, u32[]{:S(2)}) collective-permute-start(bf16[128,256]{1,0:T(8,128)(2,1)} %refs_9_.1), channel_id=1, source_target_pairs={{0,1},{1,0},{2,3},{3,2},{4,5},{5,4},{6,7},{7,6},{8,9},{9,8},{10,11... | collective-permute-start | bytes 196616 | tf_op jit(solution)/shard_map/ppermute | solution.py:384
  17.6 1.3 %collective-permute-start.11 = (bf16[128,256]{1,0:T(8,128)(2,1)S(1)}, bf16[128,256]{1,0:T(8,128)(2,1)S(1)}, u32[]{:S(2)}, u32[]{:S(2)}) collective-permute-start(bf16[128,256]{1,0:T(8,128)(2,1)S(1)} %collective-permute-done.10.refs_13_), channel_id=1, source_target_pairs={{0,1},{1,0},{2,3},{3,2},{4,5},{5,4},{6,7},{7,6},{8,9},{9,8},{10,11... | collective-permute-start | bytes 196616 | tf_op jit(solution)/shard_map/ppermute | solution.py:384
  17.6 2.9 %collective-permute-start.13 = (bf16[128,256]{1,0:T(8,128)(2,1)S(1)}, bf16[128,256]{1,0:T(8,128)(2,1)S(1)}, u32[]{:S(2)}, u32[]{:S(2)}) collective-permute-start(bf16[128,256]{1,0:T(8,128)(2,1)S(1)} %collective-permute-done.12.refs_15_), channel_id=1, source_target_pairs={{0,1},{1,0},{2,3},{3,2},{4,5},{5,4},{6,7},{7,6},{8,9},{9,8},{10,11... | collective-permute-start | bytes 196616 | tf_op jit(solution)/shard_map/ppermute | solution.py:384
  18.1 2.4 %collective-permute-start.2 = (bf16[128,256]{1,0:T(8,128)(2,1)S(1)}, bf16[128,256]{1,0:T(8,128)(2,1)S(1)}, u32[]{:S(2)}, u32[]{:S(2)}) collective-permute-start(bf16[128,256]{1,0:T(8,128)(2,1)S(1)} %collective-permute-done.refs_3_), channel_id=1, source_target_pairs={{0,1},{1,0},{2,3},{3,2},{4,5},{5,4},{6,7},{7,6},{8,9},{9,8},{10,11... | collective-permute-start | bytes 196616 | tf_op jit(solution)/shard_map/ppermute | solution.py:384
  18.1 2.3 %collective-permute-start.4 = (bf16[128,256]{1,0:T(8,128)(2,1)S(1)}, bf16[128,256]{1,0:T(8,128)(2,1)S(1)}, u32[]{:S(2)}, u32[]{:S(2)}) collective-permute-start(bf16[128,256]{1,0:T(8,128)(2,1)S(1)} %collective-permute-done.3.refs_5_), channel_id=1, source_target_pairs={{0,1},{1,0},{2,3},{3,2},{4,5},{5,4},{6,7},{7,6},{8,9},{9,8},{10,11... | collective-permute-start | bytes 196616 | tf_op jit(solution)/shard_map/ppermute | solution.py:384
  18.6 1.9 %collective-permute-start.6 = (bf16[128,256]{1,0:T(8,128)(2,1)S(1)}, bf16[128,256]{1,0:T(8,128)(2,1)S(1)}, u32[]{:S(2)}, u32[]{:S(2)}) collective-permute-start(bf16[128,256]{1,0:T(8,128)(2,1)S(1)} %collective-permute-done.5.refs_7_), channel_id=1, source_target_pairs={{0,1},{1,0},{2,3},{3,2},{4,5},{5,4},{6,7},{7,6},{8,9},{9,8},{10,11... | collective-permute-start | bytes 196616 | tf_op jit(solution)/shard_map/ppermute | solution.py:384
  18.8 1.7 %collective-permute-start.9 = (bf16[128,256]{1,0:T(8,128)(2,1)S(1)}, bf16[128,256]{1,0:T(8,128)(2,1)S(1)}, u32[]{:S(2)}, u32[]{:S(2)}) collective-permute-start(bf16[128,256]{1,0:T(8,128)(2,1)S(1)} %collective-permute-done.8.refs_11_), channel_id=1, source_target_pairs={{0,1},{1,0},{2,3},{3,2},{4,5},{5,4},{6,7},{7,6},{8,9},{9,8},{10,11... | collective-permute-start | bytes 196616 | tf_op jit(solution)/shard_map/ppermute | solution.py:384
  20.5 0.7 %copy-start = (s32[6,8]{1,0:T(8,128)S(1)}, s32[6,8]{1,0:T(8,128)}, u32[]{:S(2)}) copy-start(s32[6,8]{1,0:T(8,128)} %index_table.1.refs_0_.meta) | copy-start | bytes 580
  31.6 4.5 %collective-permute-start.15 = (f32[3,8,512]{2,1,0:T(8,128)S(1)}, f32[3,8,512]{2,1,0:T(8,128)S(1)}, u32[]{:S(2)}, u32[]{:S(2)}) collective-permute-start(f32[3,8,512]{2,1,0:T(8,128)S(1)} %get-tuple-element.21.refs_1_), channel_id=1, source_target_pairs={{0,4},{4,0},{8,12},{12,8},{1,5},{5,1},{9,13},{13,9},{2,6},{6,2},{1... | collective-permute-start | bytes 147464 | tf_op jit(solution)/shard_map/ppermute | solution.py:385
  32.6 6.2 %collective-permute-start.17 = (f32[3,8,512]{2,1,0:T(8,128)S(1)}, f32[3,8,512]{2,1,0:T(8,128)S(1)}, u32[]{:S(2)}, u32[]{:S(2)}) collective-permute-start(f32[3,8,512]{2,1,0:T(8,128)S(1)} %get-tuple-element.21.refs_1_), channel_id=1, source_target_pairs={{0,8},{4,12},{8,0},{12,4},{1,9},{5,13},{9,1},{13,5},{2,10},{6,14},... | collective-permute-start | bytes 147464 | tf_op jit(solution)/shard_map/ppermute | solution.py:385
  35.0 5.9 %collective-permute-start.19 = (f32[3,8,512]{2,1,0:T(8,128)S(1)}, f32[3,8,512]{2,1,0:T(8,128)S(1)}, u32[]{:S(2)}, u32[]{:S(2)}) collective-permute-start(f32[3,8,512]{2,1,0:T(8,128)S(1)} %get-tuple-element.21.refs_1_), channel_id=1, source_target_pairs={{0,12},{4,8},{8,4},{12,0},{1,13},{5,9},{9,5},{13,1},{2,14},{6,10},... | collective-permute-start | bytes 147464 | tf_op jit(solution)/shard_map/ppermute | solution.py:385
  36.0 6.2 %collective-permute-start.14 = (f32[3,8,512]{2,1,0:T(8,128)S(1)}, f32[3,8,512]{2,1,0:T(8,128)S(1)}, u32[]{:S(2)}, u32[]{:S(2)}) collective-permute-start(f32[3,8,512]{2,1,0:T(8,128)S(1)} %get-tuple-element.21.refs_1_), channel_id=1, source_target_pairs={{0,1},{1,0},{2,3},{3,2},{4,5},{5,4},{6,7},{7,6},{8,9},{9,8},{10,11... | collective-permute-start | bytes 147464 | tf_op jit(solution)/shard_map/ppermute | solution.py:384
  36.1 6.2 %collective-permute-start.16 = (f32[3,8,512]{2,1,0:T(8,128)S(1)}, f32[3,8,512]{2,1,0:T(8,128)S(1)}, u32[]{:S(2)}, u32[]{:S(2)}) collective-permute-start(f32[3,8,512]{2,1,0:T(8,128)S(1)} %collective-permute-done.15.refs_3_), channel_id=1, source_target_pairs={{0,1},{1,0},{2,3},{3,2},{4,5},{5,4},{6,7},{7,6},{8,9},{9,8},{10,11... | collective-permute-start | bytes 147464 | tf_op jit(solution)/shard_map/ppermute | solution.py:384
  38.8 3.5 %collective-permute-start.18 = (f32[3,8,512]{2,1,0:T(8,128)S(1)}, f32[3,8,512]{2,1,0:T(8,128)S(1)}, u32[]{:S(2)}, u32[]{:S(2)}) collective-permute-start(f32[3,8,512]{2,1,0:T(8,128)S(1)} %collective-permute-done.17.refs_5_), channel_id=1, source_target_pairs={{0,1},{1,0},{2,3},{3,2},{4,5},{5,4},{6,7},{7,6},{8,9},{9,8},{10,11... | collective-permute-start | bytes 147464 | tf_op jit(solution)/shard_map/ppermute | solution.py:384
  40.9 1.3 %collective-permute-start.20 = (f32[3,8,512]{2,1,0:T(8,128)S(1)}, f32[3,8,512]{2,1,0:T(8,128)S(1)}, u32[]{:S(2)}, u32[]{:S(2)}) collective-permute-start(f32[3,8,512]{2,1,0:T(8,128)S(1)} %collective-permute-done.19.refs_7_), channel_id=1, source_target_pairs={{0,1},{1,0},{2,3},{3,2},{4,5},{5,4},{6,7},{7,6},{8,9},{9,8},{10,11... | collective-permute-start | bytes 147464 | tf_op jit(solution)/shard_map/ppermute | solution.py:384
  43.4 1.7 %collective-permute-start.21 = (bf16[4,128,256]{2,1,0:T(8,128)(2,1)S(1)}, bf16[4,128,256]{2,1,0:T(8,128)(2,1)S(1)}, u32[]{:S(2)}, u32[]{:S(2)}) collective-permute-start(bf16[4,128,256]{2,1,0:T(8,128)(2,1)S(1)} %get-tuple-element.27), channel_id=1, source_target_pairs={{0,1},{1,0},{2,3},{3,2},{4,5},{5,4},{6,7},{7,6},{8,9},{9,8},{10,11... | collective-permute-start | bytes 786440 | tf_op jit(solution)/shard_map/ppermute | solution.py:384
  45.3 8.4 %collective-permute-start.22 = (bf16[128,256]{1,0:T(8,128)(2,1)S(1)}, bf16[128,256]{1,0:T(8,128)(2,1)S(1)}, u32[]{:S(2)}, u32[]{:S(2)}) collective-permute-start(bf16[128,256]{1,0:T(8,128)(2,1)S(1)} %get-tuple-element.37), channel_id=1, source_target_pairs={{0,4},{4,0},{8,12},{12,8},{1,5},{5,1},{9,13},{13,9},{2,6},{6,2},{1... | collective-permute-start | bytes 196616 | tf_op jit(solution)/shard_map/ppermute | solution.py:385
  45.3 8.3 %collective-permute-start.23 = (bf16[128,256]{1,0:T(8,128)(2,1)S(1)}, bf16[128,256]{1,0:T(8,128)(2,1)S(1)}, u32[]{:S(2)}, u32[]{:S(2)}) collective-permute-start(bf16[128,256]{1,0:T(8,128)(2,1)S(1)} %get-tuple-element.39), channel_id=1, source_target_pairs={{0,8},{4,12},{8,0},{12,4},{1,9},{5,13},{9,1},{13,5},{2,10},{6,14},... | collective-permute-start | bytes 196616 | tf_op jit(solution)/shard_map/ppermute | solution.py:385
  47.9 6.2 %collective-permute-start.24 = (bf16[128,256]{1,0:T(8,128)(2,1)S(1)}, bf16[128,256]{1,0:T(8,128)(2,1)S(1)}, u32[]{:S(2)}, u32[]{:S(2)}) collective-permute-start(bf16[128,256]{1,0:T(8,128)(2,1)S(1)} %get-tuple-element.38), channel_id=1, source_target_pairs={{0,12},{4,8},{8,4},{12,0},{1,13},{5,9},{9,5},{13,1},{2,14},{6,10},... | collective-permute-start | bytes 196616 | tf_op jit(solution)/shard_map/ppermute | solution.py:385

commit v5 on v4

v5 whole, which is shorter than its diff:
```python
import math

import jax
import jax.numpy as jnp
from jax import lax
from jax.experimental import pallas as pl
from jax.experimental.pallas import tpu as pltpu
from jax.sharding import PartitionSpec as P

HD = 64
TEST = 128
BLK = 512
LANES = 128
WIDE = 2 * TEST
CHUNK = 64

NEG = -1e30
SCORE_SCALE = 1.0 / math.sqrt(HD)
LOG2_SCALE = SCORE_SCALE * math.log2(math.e)
RP = ("rows", "pair")
PAIR = [(0, 1), (1, 0)]


def params(mib):
    return pltpu.CompilerParams(vmem_limit_bytes=mib * 1024 * 1024)


def two_heads(rows):
    feature = lax.broadcasted_iota(jnp.int32, rows.shape, 0)
    zero = jnp.zeros_like(rows)
    return jnp.concatenate(
        [jnp.where(feature < HD, rows, zero), jnp.where(feature < HD, zero, rows)], axis=1
    )


def every_copy(copies):
    for copy in copies:
        copy.start()
    return copies


OWNER, LIVE, TESTN, SLOT_IN, TABLE_OF, SLOT_OUT = range(6)


def vmem_spec():
    return pl.BlockSpec(memory_space=pltpu.VMEM)


def smem_spec():
    return pl.BlockSpec(memory_space=pltpu.SMEM)


def hbm_spec():
    return pl.BlockSpec(memory_space=pltpu.HBM)


def in_hbm(value):
    return pltpu.with_memory_space_constraint(value, pltpu.HBM)


def load_kernel(small, table_hbm, train_hbm, test_hbm, key_hbm, value_hbm, meta, state, *scratch):
    block_table, train_rows, test_rows, count, sem, small_sem = scratch
    entries = every_copy(
        [
            pltpu.make_async_copy(table_hbm, block_table, small_sem.at[0]),
            pltpu.make_async_copy(train_hbm, train_rows, small_sem.at[1]),
            pltpu.make_async_copy(test_hbm, test_rows, small_sem.at[2]),
        ]
    )
    blocks = state.shape[0]
    features = key_hbm.shape[1]
    stacked = features // HD * TEST
    loads = []
    for b in range(blocks):
        for n, source in enumerate((key_hbm, value_hbm)):
            lanes = pl.ds(2 * stacked + n * features, features)
            loads.append(
                pltpu.make_async_copy(
                    source.at[pl.ds(b * BLK, BLK)], state.at[b, :, lanes], sem.at[n, b]
                )
            )
    every_copy(loads)
    chip = lax.axis_index("rows").astype(jnp.int32)
    core = lax.axis_index("pair").astype(jnp.int32)
    first = lax.axis_index(RP).astype(jnp.int32) * blocks
    for copy in entries:
        copy.wait()
    for t in range(train_rows.shape[0]):
        count[t] = 0
        meta[TESTN, t] = test_rows[t]
        if small:
            away = (t // 2) ^ chip
            not_mine = (t % 2) ^ core
            meta[SLOT_IN, t] = 2 * away + not_mine
            meta[TABLE_OF, t] = 2 * away + not_mine
            meta[SLOT_OUT, t] = 4 * not_mine + ((away + 3) & 3)
        else:
            for row in (SLOT_IN, TABLE_OF, SLOT_OUT):
                meta[row, t] = t

    def earlier(n, carry):
        table = block_table[n]
        count[table] = count[table] + 1
        return carry

    lax.fori_loop(0, first, earlier, 0)
    for b in range(blocks):
        table = block_table[first + b]
        meta[OWNER, b] = table
        meta[LIVE, b] = jnp.minimum(train_rows[table] - count[table] * BLK, BLK)
        count[table] = count[table] + 1
    for copy in loads:
        copy.wait()


def load_rows(small, block_table, train_rows, test_rows, key_rows, value_rows):
    tables = train_rows.shape[0]
    features = key_rows.shape[1]
    blocks = key_rows.shape[0] // BLK
    stacked = features // HD * TEST
    return pl.pallas_call(
        lambda *refs: load_kernel(small, *refs),
        in_specs=[hbm_spec()] * 5,
        out_specs=[smem_spec(), vmem_spec()],
        out_shape=[
            pltpu.SMEM((6, max(blocks, tables)), jnp.int32),
            pltpu.VMEM((blocks, BLK, 2 * stacked + 2 * features), jnp.bfloat16),
        ],
        scratch_shapes=[
            pltpu.SMEM(block_table.shape, jnp.int32),
            pltpu.SMEM((tables,), jnp.int32),
            pltpu.SMEM((tables,), jnp.int32),
            pltpu.SMEM((tables,), jnp.int32),
            pltpu.SemaphoreType.DMA((2, blocks)),
            pltpu.SemaphoreType.DMA((3,)),
        ],
        compiler_params=params(4),
        name="load_rows",
    )(*map(in_hbm, (block_table, train_rows, test_rows, key_rows, value_rows)))


def turn_pieces(pieces, held, held_s, sem, store):
    early = every_copy(
        [pltpu.make_async_copy(pieces[n], held_s.at[n], sem.at[n]) for n in range(held)]
    )
    at_slot = held
    for piece in pieces[held:]:
        for m in range(piece.shape[0] // TEST):
            store(at_slot, piece[m * TEST : (m + 1) * TEST, :].T)
            at_slot += 1
    for copy in early:
        copy.wait()
    for n in range(held):
        store(n, held_s[n].T)


def fold(values, op):
    return op(values.reshape(CHUNK // 8, 8, WIDE), axis=0)


def units_of(blocks, features):
    return [(b, p) for b in range(blocks) for p in range(features // LANES)]


def weights_kernel(count, held, meta, *refs):
    pieces = refs[:count]
    state, qt_ref, peak_hbm, state_out, peak_s, scores_s, held_s, sem, peak_sem = refs[count:]
    tables, features, _ = qt_ref.shape
    stacked = features // HD * TEST
    units = units_of(state.shape[0], features)

    def store(at_slot, turned):
        qt_ref[at_slot] = turned

    turn_pieces(pieces, held, held_s, sem, store)
    peaks = [None] * len(units)
    for t in range(len(units) + 1):
        if t < len(units):
            b, p = units[t]
            live = meta[LIVE, b]
            queries = two_heads(
                qt_ref[meta[SLOT_IN, meta[OWNER, b]], p * LANES : (p + 1) * LANES, :]
            )
            peak = jnp.full((8, WIDE), NEG, jnp.float32)
        for r in range(0, BLK, CHUNK):
            rows = slice(r, r + CHUNK)
            if t > 0:
                last_b, last_p = units[t - 1]
                weights = jnp.exp2(scores_s[(t - 1) % 2, rows, :] * LOG2_SCALE - peaks[t - 1])
                state_out[last_b, rows, last_p * WIDE : (last_p + 1) * WIDE] = weights.astype(
                    jnp.bfloat16
                )
            if t < len(units):
                keys = state[b, rows, 2 * stacked + p * LANES : 2 * stacked + (p + 1) * LANES]
                scores = jnp.dot(keys, queries, preferred_element_type=jnp.float32)
                row = lax.broadcasted_iota(jnp.int32, scores.shape, 0)
                scores = jnp.where(row < live - r, scores, NEG)
                scores_s[t % 2, rows, :] = scores
                peak = jnp.maximum(peak, fold(scores, jnp.max))
        if t < len(units):
            peaks[t] = jnp.max(peak, axis=0, keepdims=True) * LOG2_SCALE
            peak_s[b : b + 1, p * WIDE : (p + 1) * WIDE] = peaks[t]
    for copy in every_copy([pltpu.make_async_copy(peak_s, peak_hbm, peak_sem.at[0])]):
        copy.wait()


def block_weights(meta, held, pieces, state, features, tables):
    blocks = state.shape[0]
    stacked = features // HD * TEST
    count = len(pieces)
    pieces = [in_hbm(piece) if n < held else piece for n, piece in enumerate(pieces)]
    specs = [hbm_spec() if n < held else vmem_spec() for n in range(count)]
    return pl.pallas_call(
        lambda *refs: weights_kernel(count, held, *refs),
        in_specs=[smem_spec()] + specs + [vmem_spec()],
        out_specs=[vmem_spec(), hbm_spec(), vmem_spec()],
        out_shape=[
            pltpu.VMEM((tables, features, TEST), jnp.bfloat16),
            pltpu.HBM((blocks, stacked), jnp.float32),
            pltpu.VMEM(state.shape, jnp.bfloat16),
        ],
        input_output_aliases={count + 1: 2},
        scratch_shapes=[
            pltpu.VMEM((blocks, stacked), jnp.float32),
            pltpu.VMEM((2, BLK, WIDE), jnp.float32),
            pltpu.VMEM((max(held, 1), TEST, features), jnp.bfloat16),
            pltpu.SemaphoreType.DMA((max(held, 1),)),
            pltpu.SemaphoreType.DMA((1,)),
        ],
        compiler_params=params(10),
        name="block_weights",
    )(meta, *pieces, state)


def moved_kernel(count, held, meta, *refs):
    pieces = refs[:count]
    peak_hbm, state, gt_ref, blk_hbm, tab_ref, state_out = refs[count : count + 6]
    blk_s, tab_s, dprobs_s, held_s, sem, blk_sem = refs[count + 6 :]
    tables, features, _ = gt_ref.shape
    stacked = features // HD * TEST
    blocks = state.shape[0]
    units = units_of(blocks, features)
    peak_copy = pltpu.make_async_copy(peak_hbm, blk_s.at[0], blk_sem.at[0])
    peak_copy.start()
    query = lax.broadcasted_iota(jnp.int32, (features, TEST), 1)

    def store(at_slot, turned):
        live = query < meta[TESTN, meta[TABLE_OF, at_slot]]
        gt_ref[at_slot] = jnp.where(live, turned, jnp.zeros_like(turned))

    turn_pieces(pieces, held, held_s, sem, store)
    means = [None] * len(units)
    zero = jnp.zeros((8, WIDE), jnp.float32)
    for t in range(len(units) + 1):
        if t < len(units):
            b, p = units[t]
            grads = two_heads(
                gt_ref[meta[SLOT_IN, meta[OWNER, b]], p * LANES : (p + 1) * LANES, :]
            )
            mass = part = zero
        for r in range(0, BLK, CHUNK):
            rows = slice(r, r + CHUNK)
            if t > 0:
                last_b, last_p = units[t - 1]
                weights = state[last_b, rows, last_p * WIDE : (last_p + 1) * WIDE]
                moved = weights.astype(jnp.float32) * (dprobs_s[(t - 1) % 2, rows, :] - means[t - 1])
                lanes = slice(stacked + last_p * WIDE, stacked + (last_p + 1) * WIDE)
                state_out[last_b, rows, lanes] = moved.astype(jnp.bfloat16)
            if t < len(units):
                first = 2 * stacked + features + p * LANES
                values = state[b, rows, first : first + LANES]
                dprobs = jnp.dot(values, grads, preferred_element_type=jnp.float32)
                weights = state[b, rows, p * WIDE : (p + 1) * WIDE].astype(jnp.float32)
                mass = mass + fold(weights, jnp.sum)
                part = part + fold(weights * dprobs, jnp.sum)
                dprobs_s[t % 2, rows, :] = dprobs
        if t < len(units):
            wide = slice(p * WIDE, (p + 1) * WIDE)
            mass = jnp.sum(mass, axis=0, keepdims=True)
            means[t] = jnp.sum(part, axis=0, keepdims=True) / mass
            blk_s[1, b : b + 1, wide] = mass
            blk_s[2, b : b + 1, wide] = means[t]
    peak_copy.wait()
    tab_s[0] = jnp.full(tab_s.shape[1:], NEG, jnp.float32)
    tab_s[1] = jnp.zeros(tab_s.shape[1:], jnp.float32)
    tab_s[2] = jnp.zeros(tab_s.shape[1:], jnp.float32)
    for b in range(blocks):
        at = pl.ds(meta[OWNER, b], 1)
        peak, mass, mean = blk_s[0, b : b + 1, :], blk_s[1, b : b + 1, :], blk_s[2, b : b + 1, :]
        old = tab_s[0, at, :]
        new = jnp.maximum(old, peak)
        old_weight = jnp.exp2(old - new)
        new_mass = mass * jnp.exp2(peak - new)
        tab_s[0, at, :] = new
        tab_s[1, at, :] = tab_s[1, at, :] * old_weight + new_mass
        tab_s[2, at, :] = tab_s[2, at, :] * old_weight + new_mass * mean
    here = tab_s[1] > 0.0
    mass = jnp.where(here, tab_s[1], 1.0)
    tab_ref[0] = jnp.where(here, tab_s[0] + jnp.log2(mass), NEG)
    tab_ref[1] = tab_s[2] / mass
    for copy in every_copy([pltpu.make_async_copy(blk_s, blk_hbm, blk_sem.at[0])]):
        copy.wait()


def moved_weights(meta, held, pieces, peak, state, features, tables):
    blocks = state.shape[0]
    stacked = features // HD * TEST
    count = len(pieces)
    pieces = [in_hbm(piece) if n < held else piece for n, piece in enumerate(pieces)]
    specs = [hbm_spec() if n < held else vmem_spec() for n in range(count)]
    return pl.pallas_call(
        lambda *refs: moved_kernel(count, held, *refs),
        in_specs=[smem_spec()] + specs + [hbm_spec(), vmem_spec()],
        out_specs=[vmem_spec(), hbm_spec(), vmem_spec(), vmem_spec()],
        out_shape=[
            pltpu.VMEM((tables, features, TEST), jnp.bfloat16),
            pltpu.HBM((3, blocks, stacked), jnp.float32),
            jax.ShapeDtypeStruct((2, tables, stacked), jnp.float32),
            pltpu.VMEM(state.shape, jnp.bfloat16),
        ],
        input_output_aliases={count + 2: 3},
        scratch_shapes=[
            pltpu.VMEM((3, blocks, stacked), jnp.float32),
            pltpu.VMEM((3, tables, stacked), jnp.float32),
            pltpu.VMEM((2, BLK, WIDE), jnp.float32),
            pltpu.VMEM((max(held, 1), TEST, features), jnp.bfloat16),
            pltpu.SemaphoreType.DMA((max(held, 1),)),
            pltpu.SemaphoreType.DMA((1,)),
        ],
        compiler_params=params(10),
        name="moved_weights",
    )(meta, *pieces, in_hbm(peak), state)


def query_sums_kernel(state, blk_hbm, ab_ref, blk_ref, state_out, blk_sem):
    blocks, _, features, _ = ab_ref.shape
    stacked = features // HD * TEST
    copy = pltpu.make_async_copy(blk_hbm, blk_ref, blk_sem.at[0])
    copy.start()
    for b in range(blocks):
        for p in range(features // LANES):
            keys = state[b, :, 2 * stacked + p * LANES : 2 * stacked + (p + 1) * LANES]
            for n, first in enumerate((stacked, 0)):
                values = state[b, :, first + p * WIDE : first + (p + 1) * WIDE]
                product = lax.dot_general(
                    keys, values, (((0,), (0,)), ((), ())), preferred_element_type=jnp.float32
                )
                ab_ref[b, n, p * LANES : p * LANES + HD, :] = product[:HD, :TEST]
                ab_ref[b, n, p * LANES + HD : (p + 1) * LANES, :] = product[HD:, TEST:]
    copy.wait()


def query_sums(features, state, blk):
    blocks = state.shape[0]
    return pl.pallas_call(
        query_sums_kernel,
        in_specs=[vmem_spec(), hbm_spec()],
        out_specs=[vmem_spec()] * 3,
        out_shape=[
            pltpu.VMEM((blocks, 2, features, TEST), jnp.float32),
            pltpu.VMEM(blk.shape, jnp.float32),
            pltpu.VMEM(state.shape, jnp.bfloat16),
        ],
        input_output_aliases={0: 2},
        scratch_shapes=[pltpu.SemaphoreType.DMA((1,))],
        compiler_params=params(8),
        name="query_sums",
    )(state, in_hbm(blk))


def merged(pieces):
    peak = pieces[0][0]
    for piece in pieces[1:]:
        peak = jnp.maximum(peak, piece[0])
    mass = part = 0.0
    for piece in pieces:
        weight = jnp.exp2(piece[0] - peak)
        mass = mass + weight
        part = part + piece[1] * weight
    return peak, mass, part / mass


def query_grad_kernel(count, meta, *refs):
    pieces = refs[:count]
    blk_ref, ab_ref = refs[count : count + 2]
    c_ref, d_ref, *q_refs = refs[count + 2 : -2]
    tab_s, acc_s = refs[-2:]
    blocks = blk_ref.shape[1]
    tables, features, _ = acc_s.shape
    tab_s[0], tab_s[1], tab_s[2] = merged(pieces)
    acc_s[...] = jnp.zeros_like(acc_s)
    for b in range(blocks):
        table = meta[OWNER, b]
        at = meta[SLOT_OUT, table]
        mass = tab_s[1, pl.ds(table, 1), :]
        c = jnp.exp2(blk_ref[0, b : b + 1, :] - tab_s[0, pl.ds(table, 1), :]) / mass
        d = c * (blk_ref[2, b : b + 1, :] - tab_s[2, pl.ds(table, 1), :])
        c_ref[b : b + 1, :] = c
        d_ref[b : b + 1, :] = d
        for h in range(features // HD):
            rows = slice(h * HD, (h + 1) * HD)
            lanes = slice(h * TEST, (h + 1) * TEST)
            acc_s[at, rows, :] += c[:, lanes] * ab_ref[b, 0, rows, :] + d[:, lanes] * ab_ref[b, 1, rows, :]
    per = tables // len(q_refs)
    for n in range(tables):
        ref = q_refs[n // per]
        ref[n % per] = (acc_s[n] * SCORE_SCALE).T.astype(ref.dtype)


def query_grads(meta, tables, pieces, blk, ab, q_dtypes):
    blocks, _, features, _ = ab.shape
    stacked = blk.shape[2]
    per = tables // len(q_dtypes)
    return pl.pallas_call(
        lambda *refs: query_grad_kernel(len(pieces), *refs),
        in_specs=[smem_spec()] + [vmem_spec()] * (len(pieces) + 2),
        out_specs=[vmem_spec()] * (2 + len(q_dtypes)),
        out_shape=[
            jax.ShapeDtypeStruct((blocks, stacked), jnp.float32),
            jax.ShapeDtypeStruct((blocks, stacked), jnp.float32),
        ]
        + [jax.ShapeDtypeStruct((per, TEST, features), dtype) for dtype in q_dtypes],
        scratch_shapes=[
            pltpu.VMEM((3, tables, stacked), jnp.float32),
            pltpu.VMEM((tables, features, TEST), jnp.float32),
        ],
        compiler_params=params(10),
        name="query_grads",
    )(meta, *pieces, blk, ab)


def row_grads_kernel(meta, c_ref, d_ref, qt_ref, gt_ref, state, dk_hbm, dv_hbm, dk_s, dv_s, out_sem):
    blocks, _, features = dk_s.shape
    stacked = features // HD * TEST
    turned = (((1,), (1,)), ((), ()))
    stores = []
    for b in range(blocks):
        at_slot = meta[SLOT_IN, meta[OWNER, b]]
        for p in range(features // LANES):
            at = slice(p * LANES, (p + 1) * LANES)
            wide = slice(p * WIDE, (p + 1) * WIDE)
            c = c_ref[b : b + 1, wide]
            d = d_ref[b : b + 1, wide]
            q_t = two_heads(qt_ref[at_slot, at, :].astype(jnp.float32))
            g_t = two_heads(gt_ref[at_slot, at, :].astype(jnp.float32))
            for_u = (q_t * (c * SCORE_SCALE)).astype(jnp.bfloat16)
            for_e = jnp.concatenate([g_t * c, q_t * (d * SCORE_SCALE)], axis=0).astype(jnp.bfloat16)
            from_e = lax.dot_general(
                state[b, :, wide], for_e, turned, preferred_element_type=jnp.float32
            )
            moved = state[b, :, stacked + p * WIDE : stacked + (p + 1) * WIDE]
            from_u = lax.dot_general(moved, for_u, turned, preferred_element_type=jnp.float32)
            dv_s[b, :, at] = from_e[:, :LANES].astype(jnp.bfloat16)
            dk_s[b, :, at] = (from_u + from_e[:, LANES:]).astype(jnp.bfloat16)
        rows = pl.ds(b * BLK, BLK)
        stores += every_copy(
            [
                pltpu.make_async_copy(dk_s.at[b], dk_hbm.at[rows], out_sem.at[0, b]),
                pltpu.make_async_copy(dv_s.at[b], dv_hbm.at[rows], out_sem.at[1, b]),
            ]
        )
    for copy in stores:
        copy.wait()


def row_grads(meta, c, d, turned, state):
    blocks = state.shape[0]
    features = turned[0].shape[1]
    return pl.pallas_call(
        row_grads_kernel,
        in_specs=[smem_spec()] + [vmem_spec()] * 5,
        out_specs=[hbm_spec()] * 2,
        out_shape=[jax.ShapeDtypeStruct((blocks * BLK, features), jnp.bfloat16)] * 2,
        scratch_shapes=[
            pltpu.VMEM((blocks, BLK, features), jnp.bfloat16),
            pltpu.VMEM((blocks, BLK, features), jnp.bfloat16),
            pltpu.SemaphoreType.DMA((2, blocks)),
        ],
        compiler_params=params(10),
        name="row_grads",
    )(meta, c, d, *turned, state)


def local(small, query_rows, key_rows, value_rows, cotangent, train_rows, test_rows, block_table):
    features = query_rows.shape[1]
    blocks = key_rows.shape[0] // BLK
    tables = train_rows.shape[0]
    pair = lambda value: lax.ppermute(value, "pair", PAIR)
    step = lambda value, s: lax.ppermute(value, "rows", [(z, z ^ s) for z in range(4)])
    after = lambda value, other: lax.optimization_barrier((value, other))
    load = lambda entries: load_rows(small, entries, train_rows, test_rows, key_rows, value_rows)
    if small:
        held = 1
        near = [step(query_rows, s) for s in (1, 2, 3)]
        near_grads = [step(cotangent, s) for s in (1, 2, 3)]
        block_table, near[0] = after(block_table, near[0])
        meta, state = load(block_table)
        near[0], meta = after(near[0], meta)
        queries = [query_rows, pair(query_rows)]
        for value in near:
            queries += [value, pair(value)]
        qt, peak, state = block_weights(meta, held, queries, state, features, tables)
        *near_grads, qt = lax.optimization_barrier((*near_grads, qt))
        grads = [cotangent, pair(cotangent)]
        for value in near_grads:
            grads += [value, pair(value)]
    else:
        held = 0
        meta, state = load(block_table)
        queries = [lax.all_gather(query_rows, RP, axis=0, tiled=True)]
        qt, peak, state = block_weights(meta, held, queries, state, features, tables)
        grads = [lax.all_gather(cotangent, RP, axis=0, tiled=True)]
    gt, blk, tab, state = moved_weights(meta, held, grads, peak, state, features, tables)
    if small:
        near = [step(tab, s) for s in (1, 2, 3)]
        ab, blk, state = query_sums(features, state, blk)
        *near, ab = lax.optimization_barrier((*near, ab))
        stats = [tab, pair(tab)]
        for value in near:
            stats += [value, pair(value)]
        dtypes = [jnp.float32, jnp.bfloat16]
    else:
        ab, blk, state = query_sums(features, state, blk)
        peak = lax.pmax(tab[0], RP)
        weight = jnp.exp2(tab[0] - peak)
        total, part = lax.psum(jnp.stack([weight, weight * tab[1]]), RP)
        stats = [jnp.stack([peak + jnp.log2(total), part / total])]
        dtypes = [jnp.float32]
    c, d, *q_terms = query_grads(meta, tables, stats, blk, ab, dtypes)
    if small:
        keep, send = q_terms
        total = keep + pair(send).astype(jnp.float32)
        low = total.astype(jnp.bfloat16)
        got = [step(low[s - 1], s) for s in (1, 2, 3)]
        low, c = lax.optimization_barrier((low, c))
        key_grad, value_grad = row_grads(meta, c, d, (qt, gt), state)
        query_grad = total[3]
        for value in got:
            query_grad = query_grad + value.astype(jnp.float32)
    else:
        query_grad = lax.psum_scatter(
            q_terms[0].reshape(tables * TEST, features), RP, scatter_dimension=0, tiled=True
        )
        key_grad, value_grad = row_grads(meta, c, d, (qt, gt), state)
    return query_grad.astype(jnp.bfloat16), key_grad, value_grad


def solution(mesh):
    sizes = mesh.shape
    tables_of_rows = P(("groups", "rows", "pair"), "mp")
    in_specs = (tables_of_rows,) * 4 + (P("groups"),) * 3
    out_specs = (tables_of_rows,) * 3

    def run(query_rows, *rest):
        local_rows = query_rows.shape[0] // (sizes["groups"] * sizes["rows"] * sizes["pair"])
        small = sizes["rows"] == 4 and sizes["pair"] == 2 and local_rows == TEST
        return jax.shard_map(
            lambda *args: local(small, *args),
            mesh=mesh,
            in_specs=in_specs,
            out_specs=out_specs,
            check_vma=False,
        )(query_rows, *rest)

    return run
```

time: 54.9 us -> 51 us (0.929)
  Pallas kernels: 18.1 us -> 16.8 us
  waiting for transfers between devices: 12.4 us -> 11.1 us
  local copies, waits for them, and re-layouts: 0.7 us -> 0.02 us
  starting transfers between devices: 22 us -> 21.4 us
    ppermute x12, waiting for transfers between devices: 11.1 us -> 7.61 us  [local(): lax.ppermute(value, 'rows', [(z, z ^ s) for z in range(4)])]
    ppermute x13, waiting for transfers between devices: 1.34 us -> 3.49 us  [local(): pair = lambda value: lax.ppermute(value, 'pair', PAIR)]
    unnamed x2, local copies, waits for them, and re-layouts: 0.68 us -> 0.01 us
    pallas_call x1, Pallas kernels: 1.17 us -> 0.54 us  [query_grads(): pl.pallas_call(lambda *refs: query_grad_kernel(len(pieces), *refs), in_sp...]
    pallas_call x1, Pallas kernels: 3.9 us -> 3.3 us  [row_grads(): pl.pallas_call(row_grads_kernel, in_specs=[smem_spec()] + [vmem_spec()] *...]
    ppermute x13, starting transfers between devices: 2.99 us -> 2.4 us  [local(): pair = lambda value: lax.ppermute(value, 'pair', PAIR)]
    pallas_call x2 -> x3, Pallas kernels: 11.7 us -> 11.7 us  [the longest x1 4.7 us: block_weights(): pl.pallas_call(lambda *refs: weights_kernel(count, held, *refs), in_specs...]
  transfers between devices with their start and end apart: 25 -> 25, of which waited for: 7 -> 12; matrix products, arithmetic and copies ran while one was open for 0% -> 0% of each run, Pallas kernels for 12% -> 23%
where the time goes in v5:
time: 51 us; the launch traced here: 50.8 us
  starting transfers between devices  21.4 us (42%)
  Pallas kernels  16.8 us (33%)
  waiting for transfers between devices  11.1 us (22%)
  between operations  0.79 us (2%)
  other arithmetic  0.73 us (1%)
    ppermute x12, starting transfers between devices, local(): lax.ppermute(value, 'rows', [(z, z ^ s) for z in range(4)])  19 us
    ppermute x12, waiting for transfers between devices, local(): lax.ppermute(value, 'rows', [(z, z ^ s) for z in range(4)])  7.61 us
    pallas_call x1, Pallas kernels, block_weights(): pl.pallas_call(lambda *refs: weights_kernel(count, held, *refs), in_specs...  4.7 us
    pallas_call x1, Pallas kernels, moved_weights(): pl.pallas_call(lambda *refs: moved_kernel(count, held, *refs), in_specs=[...  4.66 us
    ppermute x13, waiting for transfers between devices, local(): pair = lambda value: lax.ppermute(value, 'pair', PAIR)  3.49 us
    pallas_call x1, Pallas kernels, row_grads(): pl.pallas_call(row_grads_kernel, in_specs=[smem_spec()] + [vmem_spec()] *...  3.3 us
    ppermute x13, starting transfers between devices, local(): pair = lambda value: lax.ppermute(value, 'pair', PAIR)  2.4 us
    pallas_call x1, Pallas kernels, load_rows(): pl.pallas_call(lambda *refs: load_kernel(small, *refs), in_specs=[hbm_spe...  2.3 us
  transfers between devices with their start and end apart: 25, of which 12 were waited for; matrix products, arithmetic and copies ran while one was open for 0% of the time, Pallas kernels for 23%

profile of v5, /device:TPU:0, one launch (start us, length us, event | category | flops | bytes accessed | tf_op | source)
XLA Modules:
  0.0 50.8 jit_solution(6964643163252630547)
XLA Ops:
  0.6 0.0 copy-start
  0.6 3.1 %collective-permute-start = (bf16[128,256]{1,0:T(8,128)(2,1)}, bf16[128,256]{1,0:T(8,128)(2,1)S(1)}, u32[]{:S(2)}, u32[]{:S(2)}) collective-permute-start(bf16[128,256]{1,0:T(8,128)(2,1)} %refs_1_.4), channel_id=1, source_target_pairs={{0,4},{4,0},{8,12},{12,8},{1,5},{5,1},{9,13},{13,9},{2,6},{6,2},{1... | collective-permute-start | bytes 196616 | tf_op jit(solution)/shard_map/ppermute | solution.py:489
  3.7 2.5 %collective-permute-start.9 = (bf16[128,256]{1,0:T(8,128)(2,1)}, bf16[128,256]{1,0:T(8,128)(2,1)S(1)}, u32[]{:S(2)}, u32[]{:S(2)}) collective-permute-start(bf16[128,256]{1,0:T(8,128)(2,1)} %refs_1_.4), channel_id=1, source_target_pairs={{0,12},{4,8},{8,4},{12,0},{1,13},{5,9},{9,5},{13,1},{2,14},{6,10},... | collective-permute-start | bytes 196616 | tf_op jit(solution)/shard_map/ppermute | solution.py:489
  6.2 0.1 collective-permute-start.7
  6.3 0.0 collective-permute-start.5
  6.3 0.0 collective-permute-done.refs_3_
  6.3 2.3 %load_rows.1 = (s32[6,8]{1,0:T(8,128)S(4)}, bf16[8,512,1536]{2,1,0:T(8,128)(2,1)S(1)}) custom-call(s32[64]{0:T(128)} %refs_0_, s32[8]{0:T(128)} %refs_1_.3, s32[8]{0:T(128)} %refs_2_.1, bf16[4096,256]{1,0:T(8,128)(2,1)} %refs_3_.1, bf16[4096,256]{1,0:T(8,128)(2,1)} %refs_4_.1), custom_call_target="tpu_custom_call" | custom-call | tf_op jit(solution)/shard_map/load_rows/pallas_call | solution.py:121
  8.6 0.6 %collective-permute-start.6 = (bf16[128,256]{1,0:T(8,128)(2,1)S(1)}, bf16[128,256]{1,0:T(8,128)(2,1)S(1)}, u32[]{:S(2)}, u32[]{:S(2)}) collective-permute-start(bf16[128,256]{1,0:T(8,128)(2,1)S(1)} %collective-permute-done.refs_3_), channel_id=1, source_target_pairs={{0,1},{1,0},{2,3},{3,2},{4,5},{5,4},{6,7},{7,6},{8,9},{9,8},{10,11... | collective-permute-start | bytes 196616 | tf_op jit(solution)/shard_map/ppermute | solution.py:488
  9.2 1.6 %collective-permute-done.9.refs_7_ = bf16[128,256]{1,0:T(8,128)(2,1)S(1)} collective-permute-done((bf16[128,256]{1,0:T(8,128)(2,1)}, bf16[128,256]{1,0:T(8,128)(2,1)S(1)}, u32[]{:S(2)}, u32[]{:S(2)}) %collective-permute-start.9) | collective-permute-done | bytes 65568 | tf_op jit(solution)/shard_map/ppermute | solution.py:489
  10.8 0.0 collective-permute-start.10
  10.8 2.1 %collective-permute-done.7.refs_5_ = bf16[128,256]{1,0:T(8,128)(2,1)S(1)} collective-permute-done((bf16[128,256]{1,0:T(8,128)(2,1)}, bf16[128,256]{1,0:T(8,128)(2,1)S(1)}, u32[]{:S(2)}, u32[]{:S(2)}) %collective-permute-start.7) | collective-permute-done | bytes 65568 | tf_op jit(solution)/shard_map/ppermute | solution.py:489
  12.9 0.0 collective-permute-start.8
  12.9 0.0 collective-permute-start.2
  12.9 2.9 %collective-permute-start.3 = (bf16[128,256]{1,0:T(8,128)(2,1)S(1)}, bf16[128,256]{1,0:T(8,128)(2,1)S(1)}, u32[]{:S(2)}, u32[]{:S(2)}) collective-permute-start(bf16[128,256]{1,0:T(8,128)(2,1)S(1)} %copy-done), channel_id=1, source_target_pairs={{0,8},{4,12},{8,0},{12,4},{1,9},{5,13},{9,1},{13,5},{2,10},{6,14},... | collective-permute-start | bytes 196616 | tf_op jit(solution)/shard_map/ppermute | solution.py:489
  15.9 0.0 collective-permute-done.6.refs_4_
  15.9 1.4 %collective-permute-start.4 = (bf16[128,256]{1,0:T(8,128)(2,1)S(1)}, bf16[128,256]{1,0:T(8,128)(2,1)S(1)}, u32[]{:S(2)}, u32[]{:S(2)}) collective-permute-start(bf16[128,256]{1,0:T(8,128)(2,1)S(1)} %copy-done), channel_id=1, source_target_pairs={{0,12},{4,8},{8,4},{12,0},{1,13},{5,9},{9,5},{13,1},{2,14},{6,10},... | collective-permute-start | bytes 196616 | tf_op jit(solution)/shard_map/ppermute | solution.py:489
  17.3 0.0 collective-permute-done.10.refs_8_
  17.3 0.0 collective-permute-start.1
  17.3 4.7 %block_weights.1 = (bf16[8,256,128]{2,1,0:T(8,128)(2,1)S(1)}, f32[8,512]{1,0:T(8,128)}, bf16[8,512,1536]{2,1,0:T(8,128)(2,1)S(1)}) custom-call(s32[6,8]{1,0:T(8,128)S(4)} %get-tuple-element.37.refs_0_.meta, bf16[128,256]{1,0:T(8,128)(2,1)} %refs_1_.4, bf16[128,256]{1,0:T(8,128)(2,1)S(1)} %collective-permute-done.5.refs_2_, ...), custom_call_target="tpu_custom_call", output_to_operand_aliasing={{2}: (9, {})} | custom-call | tf_op jit(solution)/shard_map/block_weights/pallas_call | solution.py:213
  22.0 0.0 collective-permute-done.2.refs_3_
  22.0 0.6 %collective-permute-start.11 = (bf16[128,256]{1,0:T(8,128)(2,1)S(1)}, bf16[128,256]{1,0:T(8,128)(2,1)S(1)}, u32[]{:S(2)}, u32[]{:S(2)}) collective-permute-start(bf16[128,256]{1,0:T(8,128)(2,1)S(1)} %collective-permute-done.2.refs_3_), channel_id=1, source_target_pairs={{0,1},{1,0},{2,3},{3,2},{4,5},{5,4},{6,7},{7,6},{8,9},{9,8},{10,11... | collective-permute-start | bytes 196616 | tf_op jit(solution)/shard_map/ppermute | solution.py:488
  22.6 0.1 collective-permute-start.12
  22.7 0.4 collective-permute-start.13
  23.1 0.4 collective-permute-done.11.refs_4_
  23.5 0.4 collective-permute-done.12.refs_6_
  23.9 0.2 collective-permute-done.13.refs_8_
  24.0 4.7 %moved_weights.1 = (bf16[8,256,128]{2,1,0:T(8,128)(2,1)S(1)}, f32[3,8,512]{2,1,0:T(8,128)}, f32[2,8,512]{2,1,0:T(8,128)S(1)}, bf16[8,512,1536]{2,1,0:T(8,128)(2,1)S(1)}) custom-call(s32[6,8]{1,0:T(8,128)S(4)} %get-tuple-element.37.refs_0_.meta, bf16[128,256]{1,0:T(8,128)(2,1)} %refs_1_.5, ...), custom_call_target="tpu_custom_call", output_to_operand_aliasing={{3}: (10, {})} | custom-call | tf_op jit(solution)/shard_map/moved_weights/pallas_call | solution.py:311
  28.7 1.0 %collective-permute-start.15 = (f32[2,8,512]{2,1,0:T(8,128)S(1)}, f32[2,8,512]{2,1,0:T(8,128)S(1)}, u32[]{:S(2)}, u32[]{:S(2)}) collective-permute-start(f32[2,8,512]{2,1,0:T(8,128)S(1)} %get-tuple-element.46.refs_1_), channel_id=1, source_target_pairs={{0,4},{4,0},{8,12},{12,8},{1,5},{5,1},{9,13},{13,9},{2,6},{6,2},{1... | collective-permute-start | bytes 98312 | tf_op jit(solution)/shard_map/ppermute | solution.py:489
  29.7 2.0 %collective-permute-start.16 = (f32[2,8,512]{2,1,0:T(8,128)S(1)}, f32[2,8,512]{2,1,0:T(8,128)S(1)}, u32[]{:S(2)}, u32[]{:S(2)}) collective-permute-start(f32[2,8,512]{2,1,0:T(8,128)S(1)} %get-tuple-element.46.refs_1_), channel_id=1, source_target_pairs={{0,8},{4,12},{8,0},{12,4},{1,9},{5,13},{9,1},{13,5},{2,10},{6,14},... | collective-permute-start | bytes 98312 | tf_op jit(solution)/shard_map/ppermute | solution.py:489
  31.7 1.4 %collective-permute-start.17 = (f32[2,8,512]{2,1,0:T(8,128)S(1)}, f32[2,8,512]{2,1,0:T(8,128)S(1)}, u32[]{:S(2)}, u32[]{:S(2)}) collective-permute-start(f32[2,8,512]{2,1,0:T(8,128)S(1)} %get-tuple-element.46.refs_1_), channel_id=1, source_target_pairs={{0,12},{4,8},{8,4},{12,0},{1,13},{5,9},{9,5},{13,1},{2,14},{6,10},... | collective-permute-start | bytes 98312 | tf_op jit(solution)/shard_map/ppermute | solution.py:489
  33.1 1.3 %query_sums.1 = (f32[8,2,256,128]{3,2,1,0:T(8,128)S(1)}, f32[3,8,512]{2,1,0:T(8,128)S(1)}, bf16[8,512,1536]{2,1,0:T(8,128)(2,1)S(1)}) custom-call(bf16[8,512,1536]{2,1,0:T(8,128)(2,1)S(1)} %get-tuple-element.47.state, f32[3,8,512]{2,1,0:T(8,128)} %get-tuple-element.48.blk_hbm), custom_call_target="tpu_custom_call", output_to_operand_aliasing={{2}: (0, {})} | custom-call | tf_op jit(solution)/shard_map/query_sums/pallas_call | solution.py:355
  34.5 0.9 %collective-permute-done.16.refs_5_ = f32[2,8,512]{2,1,0:T(8,128)S(1)} collective-permute-done((f32[2,8,512]{2,1,0:T(8,128)S(1)}, f32[2,8,512]{2,1,0:T(8,128)S(1)}, u32[]{:S(2)}, u32[]{:S(2)}) %collective-permute-start.16) | collective-permute-done | bytes 32800 | tf_op jit(solution)/shard_map/ppermute | solution.py:489
  35.3 2.1 %collective-permute-done.17.refs_7_ = f32[2,8,512]{2,1,0:T(8,128)S(1)} collective-permute-done((f32[2,8,512]{2,1,0:T(8,128)S(1)}, f32[2,8,512]{2,1,0:T(8,128)S(1)}, u32[]{:S(2)}, u32[]{:S(2)}) %collective-permute-start.17) | collective-permute-done | bytes 32800 | tf_op jit(solution)/shard_map/ppermute | solution.py:489
  37.4 0.5 collective-permute-start.19
  37.9 0.0 collective-permute-start.20
  38.0 0.7 %collective-permute-done.18.refs_4_ = f32[2,8,512]{2,1,0:T(8,128)S(1)} collective-permute-done((f32[2,8,512]{2,1,0:T(8,128)S(1)}, f32[2,8,512]{2,1,0:T(8,128)S(1)}, u32[]{:S(2)}, u32[]{:S(2)}) %collective-permute-start.18) | collective-permute-done | bytes 32800 | tf_op jit(solution)/shard_map/ppermute | solution.py:488
  38.6 0.2 collective-permute-done.19.refs_6_
  38.8 0.3 collective-permute-done.20.refs_8_
  39.2 0.5 %query_grads.1 = (f32[8,512]{1,0:T(8,128)S(1)}, f32[8,512]{1,0:T(8,128)S(1)}, f32[4,128,256]{2,1,0:T(8,128)S(1)}, bf16[4,128,256]{2,1,0:T(8,128)(2,1)S(1)}) custom-call(s32[6,8]{1,0:T(8,128)S(4)} %get-tuple-element.37.refs_0_.meta, f32[2,8,512]{2,1,0:T(8,128)S(1)} %get-tuple-element.46.refs_1_, f32[2,8,512]{2,1,0:T(8,128)S(1)} %collective-permute-done.14.refs_2_, ...), custom_call_target="tpu_custom_call" | custom-call | tf_op jit(solution)/shard_map/query_grads/pallas_call | solution.py:414
  39.7 0.2 collective-permute-start.21
  39.9 1.4 %collective-permute-done.21 = bf16[4,128,256]{2,1,0:T(8,128)(2,1)S(1)} collective-permute-done((bf16[4,128,256]{2,1,0:T(8,128)(2,1)S(1)}, bf16[4,128,256]{2,1,0:T(8,128)(2,1)S(1)}, u32[]{:S(2)}, u32[]{:S(2)}) %collective-permute-start.21) | collective-permute-done | bytes 262176 | tf_op jit(solution)/shard_map/ppermute | solution.py:488
  41.3 0.1 fusion.4
  41.4 0.1 collective-permute-start.22
  41.5 2.0 %collective-permute-start.23 = (bf16[128,256]{1,0:T(8,128)(2,1)S(1)}, bf16[128,256]{1,0:T(8,128)(2,1)S(1)}, u32[]{:S(2)}, u32[]{:S(2)}) collective-permute-start(bf16[128,256]{1,0:T(8,128)(2,1)S(1)} %get-tuple-element.69), channel_id=1, source_target_pairs={{0,8},{4,12},{8,0},{12,4},{1,9},{5,13},{9,1},{13,5},{2,10},{6,14},... | collective-permute-start | bytes 196616 | tf_op jit(solution)/shard_map/ppermute | solution.py:489
  43.5 2.4 %collective-permute-start.24 = (bf16[128,256]{1,0:T(8,128)(2,1)S(1)}, bf16[128,256]{1,0:T(8,128)(2,1)S(1)}, u32[]{:S(2)}, u32[]{:S(2)}) collective-permute-start(bf16[128,256]{1,0:T(8,128)(2,1)S(1)} %get-tuple-element.68), channel_id=1, source_target_pairs={{0,12},{4,8},{8,4},{12,0},{1,13},{5,9},{9,5},{13,1},{2,14},{6,10},... | collective-permute-start | bytes 196616 | tf_op jit(solution)/shard_map/ppermute | solution.py:489
  45.9 3.3 %row_grads.1 = (bf16[4096,256]{1,0:T(8,128)(2,1)}, bf16[4096,256]{1,0:T(8,128)(2,1)}) custom-call(s32[6,8]{1,0:T(8,128)S(4)} %get-tuple-element.37.refs_0_.meta, f32[8,512]{1,0:T(8,128)S(1)} %get-tuple-element.58.c_ref, f32[8,512]{1,0:T(8,128)S(1)} %get-tuple-element.59.d_ref, bf16[8,256,128]{2,1,0:T(8,128)(2,1)S(1)} %get-tuple-element.60.qt_ref, ...), custom_call_target="tpu_custom_call" | custom-call | tf_op jit(solution)/shard_map/row_grads/pallas_call | solution.py:469
  49.2 0.9 %collective-permute-done.23 = bf16[128,256]{1,0:T(8,128)(2,1)S(1)} collective-permute-done((bf16[128,256]{1,0:T(8,128)(2,1)S(1)}, bf16[128,256]{1,0:T(8,128)(2,1)S(1)}, u32[]{:S(2)}, u32[]{:S(2)}) %collective-permute-start.23) | collective-permute-done | bytes 65568 | tf_op jit(solution)/shard_map/ppermute | solution.py:489
  50.1 0.7 %fusion.3 = bf16[128,256]{1,0:T(8,128)(2,1)} fusion(f32[4,128,256]{2,1,0:T(8,128)S(1)} %get-tuple-element.66, bf16[128,256]{1,0:T(8,128)(2,1)S(1)} %collective-permute-done.24, bf16[128,256]{1,0:T(8,128)(2,1)S(1)} %collective-permute-done.23, bf16[128,256]{1,0:T(8,128)(2,1)S(1)} %collective-permute-done.22), kind=kLoop, calls=%fused_computation.5 | loop fusion | flops 229376 | bytes 393216 | tf_op jit(solution)/shard_map/convert_element_type | solution.py:545
  (13 shorter events, 0.0 us)
Async XLA Ops:
  0.6 12.3 %copy-start = (bf16[128,256]{1,0:T(8,128)(2,1)S(1)}, bf16[128,256]{1,0:T(8,128)(2,1)}, u32[]{:S(2)}) copy-start(bf16[128,256]{1,0:T(8,128)(2,1)} %refs_1_.5) | copy-start | bytes 196612
  0.6 5.7 %collective-permute-start = (bf16[128,256]{1,0:T(8,128)(2,1)}, bf16[128,256]{1,0:T(8,128)(2,1)S(1)}, u32[]{:S(2)}, u32[]{:S(2)}) collective-permute-start(bf16[128,256]{1,0:T(8,128)(2,1)} %refs_1_.4), channel_id=1, source_target_pairs={{0,4},{4,0},{8,12},{12,8},{1,5},{5,1},{9,13},{13,9},{2,6},{6,2},{1... | collective-permute-start | bytes 196616 | tf_op jit(solution)/shard_map/ppermute | solution.py:489
  3.7 7.1 %collective-permute-start.9 = (bf16[128,256]{1,0:T(8,128)(2,1)}, bf16[128,256]{1,0:T(8,128)(2,1)S(1)}, u32[]{:S(2)}, u32[]{:S(2)}) collective-permute-start(bf16[128,256]{1,0:T(8,128)(2,1)} %refs_1_.4), channel_id=1, source_target_pairs={{0,12},{4,8},{8,4},{12,0},{1,13},{5,9},{9,5},{13,1},{2,14},{6,10},... | collective-permute-start | bytes 196616 | tf_op jit(solution)/shard_map/ppermute | solution.py:489
  6.2 6.7 %collective-permute-start.7 = (bf16[128,256]{1,0:T(8,128)(2,1)}, bf16[128,256]{1,0:T(8,128)(2,1)S(1)}, u32[]{:S(2)}, u32[]{:S(2)}) collective-permute-start(bf16[128,256]{1,0:T(8,128)(2,1)} %refs_1_.4), channel_id=1, source_target_pairs={{0,8},{4,12},{8,0},{12,4},{1,9},{5,13},{9,1},{13,5},{2,10},{6,14},... | collective-permute-start | bytes 196616 | tf_op jit(solution)/shard_map/ppermute | solution.py:489
  6.3 6.6 %collective-permute-start.5 = (bf16[128,256]{1,0:T(8,128)(2,1)}, bf16[128,256]{1,0:T(8,128)(2,1)S(1)}, u32[]{:S(2)}, u32[]{:S(2)}) collective-permute-start(bf16[128,256]{1,0:T(8,128)(2,1)} %refs_1_.4), channel_id=1, source_target_pairs={{0,1},{1,0},{2,3},{3,2},{4,5},{5,4},{6,7},{7,6},{8,9},{9,8},{10,11... | collective-permute-start | bytes 196616 | tf_op jit(solution)/shard_map/ppermute | solution.py:488
  8.6 7.2 %collective-permute-start.6 = (bf16[128,256]{1,0:T(8,128)(2,1)S(1)}, bf16[128,256]{1,0:T(8,128)(2,1)S(1)}, u32[]{:S(2)}, u32[]{:S(2)}) collective-permute-start(bf16[128,256]{1,0:T(8,128)(2,1)S(1)} %collective-permute-done.refs_3_), channel_id=1, source_target_pairs={{0,1},{1,0},{2,3},{3,2},{4,5},{5,4},{6,7},{7,6},{8,9},{9,8},{10,11... | collective-permute-start | bytes 196616 | tf_op jit(solution)/shard_map/ppermute | solution.py:488
  10.8 6.5 %collective-permute-start.10 = (bf16[128,256]{1,0:T(8,128)(2,1)S(1)}, bf16[128,256]{1,0:T(8,128)(2,1)S(1)}, u32[]{:S(2)}, u32[]{:S(2)}) collective-permute-start(bf16[128,256]{1,0:T(8,128)(2,1)S(1)} %collective-permute-done.9.refs_7_), channel_id=1, source_target_pairs={{0,1},{1,0},{2,3},{3,2},{4,5},{5,4},{6,7},{7,6},{8,9},{9,8},{10,11... | collective-permute-start | bytes 196616 | tf_op jit(solution)/shard_map/ppermute | solution.py:488
  12.9 4.4 %collective-permute-start.8 = (bf16[128,256]{1,0:T(8,128)(2,1)S(1)}, bf16[128,256]{1,0:T(8,128)(2,1)S(1)}, u32[]{:S(2)}, u32[]{:S(2)}) collective-permute-start(bf16[128,256]{1,0:T(8,128)(2,1)S(1)} %collective-permute-done.7.refs_5_), channel_id=1, source_target_pairs={{0,1},{1,0},{2,3},{3,2},{4,5},{5,4},{6,7},{7,6},{8,9},{9,8},{10,11... | collective-permute-start | bytes 196616 | tf_op jit(solution)/shard_map/ppermute | solution.py:488
  12.9 9.1 %collective-permute-start.2 = (bf16[128,256]{1,0:T(8,128)(2,1)S(1)}, bf16[128,256]{1,0:T(8,128)(2,1)S(1)}, u32[]{:S(2)}, u32[]{:S(2)}) collective-permute-start(bf16[128,256]{1,0:T(8,128)(2,1)S(1)} %copy-done), channel_id=1, source_target_pairs={{0,4},{4,0},{8,12},{12,8},{1,5},{5,1},{9,13},{13,9},{2,6},{6,2},{1... | collective-permute-start | bytes 196616 | tf_op jit(solution)/shard_map/ppermute | solution.py:489
  12.9 9.1 %collective-permute-start.3 = (bf16[128,256]{1,0:T(8,128)(2,1)S(1)}, bf16[128,256]{1,0:T(8,128)(2,1)S(1)}, u32[]{:S(2)}, u32[]{:S(2)}) collective-permute-start(bf16[128,256]{1,0:T(8,128)(2,1)S(1)} %copy-done), channel_id=1, source_target_pairs={{0,8},{4,12},{8,0},{12,4},{1,9},{5,13},{9,1},{13,5},{2,10},{6,14},... | collective-permute-start | bytes 196616 | tf_op jit(solution)/shard_map/ppermute | solution.py:489
  15.9 6.2 %collective-permute-start.4 = (bf16[128,256]{1,0:T(8,128)(2,1)S(1)}, bf16[128,256]{1,0:T(8,128)(2,1)S(1)}, u32[]{:S(2)}, u32[]{:S(2)}) collective-permute-start(bf16[128,256]{1,0:T(8,128)(2,1)S(1)} %copy-done), channel_id=1, source_target_pairs={{0,12},{4,8},{8,4},{12,0},{1,13},{5,9},{9,5},{13,1},{2,14},{6,10},... | collective-permute-start | bytes 196616 | tf_op jit(solution)/shard_map/ppermute | solution.py:489
  17.3 5.8 %collective-permute-start.1 = (bf16[128,256]{1,0:T(8,128)(2,1)S(1)}, bf16[128,256]{1,0:T(8,128)(2,1)S(1)}, u32[]{:S(2)}, u32[]{:S(2)}) collective-permute-start(bf16[128,256]{1,0:T(8,128)(2,1)S(1)} %copy-done), channel_id=1, source_target_pairs={{0,1},{1,0},{2,3},{3,2},{4,5},{5,4},{6,7},{7,6},{8,9},{9,8},{10,11... | collective-permute-start | bytes 196616 | tf_op jit(solution)/shard_map/ppermute | solution.py:488
  22.0 1.5 %collective-permute-start.11 = (bf16[128,256]{1,0:T(8,128)(2,1)S(1)}, bf16[128,256]{1,0:T(8,128)(2,1)S(1)}, u32[]{:S(2)}, u32[]{:S(2)}) collective-permute-start(bf16[128,256]{1,0:T(8,128)(2,1)S(1)} %collective-permute-done.2.refs_3_), channel_id=1, source_target_pairs={{0,1},{1,0},{2,3},{3,2},{4,5},{5,4},{6,7},{7,6},{8,9},{9,8},{10,11... | collective-permute-start | bytes 196616 | tf_op jit(solution)/shard_map/ppermute | solution.py:488
  22.6 1.3 %collective-permute-start.12 = (bf16[128,256]{1,0:T(8,128)(2,1)S(1)}, bf16[128,256]{1,0:T(8,128)(2,1)S(1)}, u32[]{:S(2)}, u32[]{:S(2)}) collective-permute-start(bf16[128,256]{1,0:T(8,128)(2,1)S(1)} %collective-permute-done.3.refs_5_), channel_id=1, source_target_pairs={{0,1},{1,0},{2,3},{3,2},{4,5},{5,4},{6,7},{7,6},{8,9},{9,8},{10,11... | collective-permute-start | bytes 196616 | tf_op jit(solution)/shard_map/ppermute | solution.py:488
  22.7 1.3 %collective-permute-start.13 = (bf16[128,256]{1,0:T(8,128)(2,1)S(1)}, bf16[128,256]{1,0:T(8,128)(2,1)S(1)}, u32[]{:S(2)}, u32[]{:S(2)}) collective-permute-start(bf16[128,256]{1,0:T(8,128)(2,1)S(1)} %collective-permute-done.4.refs_7_), channel_id=1, source_target_pairs={{0,1},{1,0},{2,3},{3,2},{4,5},{5,4},{6,7},{7,6},{8,9},{9,8},{10,11... | collective-permute-start | bytes 196616 | tf_op jit(solution)/shard_map/ppermute | solution.py:488
  28.7 5.8 %collective-permute-start.15 = (f32[2,8,512]{2,1,0:T(8,128)S(1)}, f32[2,8,512]{2,1,0:T(8,128)S(1)}, u32[]{:S(2)}, u32[]{:S(2)}) collective-permute-start(f32[2,8,512]{2,1,0:T(8,128)S(1)} %get-tuple-element.46.refs_1_), channel_id=1, source_target_pairs={{0,4},{4,0},{8,12},{12,8},{1,5},{5,1},{9,13},{13,9},{2,6},{6,2},{1... | collective-permute-start | bytes 98312 | tf_op jit(solution)/shard_map/ppermute | solution.py:489
  29.7 5.6 %collective-permute-start.16 = (f32[2,8,512]{2,1,0:T(8,128)S(1)}, f32[2,8,512]{2,1,0:T(8,128)S(1)}, u32[]{:S(2)}, u32[]{:S(2)}) collective-permute-start(f32[2,8,512]{2,1,0:T(8,128)S(1)} %get-tuple-element.46.refs_1_), channel_id=1, source_target_pairs={{0,8},{4,12},{8,0},{12,4},{1,9},{5,13},{9,1},{13,5},{2,10},{6,14},... | collective-permute-start | bytes 98312 | tf_op jit(solution)/shard_map/ppermute | solution.py:489
  31.7 5.7 %collective-permute-start.17 = (f32[2,8,512]{2,1,0:T(8,128)S(1)}, f32[2,8,512]{2,1,0:T(8,128)S(1)}, u32[]{:S(2)}, u32[]{:S(2)}) collective-permute-start(f32[2,8,512]{2,1,0:T(8,128)S(1)} %get-tuple-element.46.refs_1_), channel_id=1, source_target_pairs={{0,12},{4,8},{8,4},{12,0},{1,13},{5,9},{9,5},{13,1},{2,14},{6,10},... | collective-permute-start | bytes 98312 | tf_op jit(solution)/shard_map/ppermute | solution.py:489
  33.1 4.8 %collective-permute-start.14 = (f32[2,8,512]{2,1,0:T(8,128)S(1)}, f32[2,8,512]{2,1,0:T(8,128)S(1)}, u32[]{:S(2)}, u32[]{:S(2)}) collective-permute-start(f32[2,8,512]{2,1,0:T(8,128)S(1)} %get-tuple-element.46.refs_1_), channel_id=1, source_target_pairs={{0,1},{1,0},{2,3},{3,2},{4,5},{5,4},{6,7},{7,6},{8,9},{9,8},{10,11... | collective-permute-start | bytes 98312 | tf_op jit(solution)/shard_map/ppermute | solution.py:488
  37.4 1.2 %collective-permute-start.18 = (f32[2,8,512]{2,1,0:T(8,128)S(1)}, f32[2,8,512]{2,1,0:T(8,128)S(1)}, u32[]{:S(2)}, u32[]{:S(2)}) collective-permute-start(f32[2,8,512]{2,1,0:T(8,128)S(1)} %collective-permute-done.15.refs_3_), channel_id=1, source_target_pairs={{0,1},{1,0},{2,3},{3,2},{4,5},{5,4},{6,7},{7,6},{8,9},{9,8},{10,11... | collective-permute-start | bytes 98312 | tf_op jit(solution)/shard_map/ppermute | solution.py:488
  37.4 1.4 %collective-permute-start.19 = (f32[2,8,512]{2,1,0:T(8,128)S(1)}, f32[2,8,512]{2,1,0:T(8,128)S(1)}, u32[]{:S(2)}, u32[]{:S(2)}) collective-permute-start(f32[2,8,512]{2,1,0:T(8,128)S(1)} %collective-permute-done.16.refs_5_), channel_id=1, source_target_pairs={{0,1},{1,0},{2,3},{3,2},{4,5},{5,4},{6,7},{7,6},{8,9},{9,8},{10,11... | collective-permute-start | bytes 98312 | tf_op jit(solution)/shard_map/ppermute | solution.py:488
  37.9 1.2 %collective-permute-start.20 = (f32[2,8,512]{2,1,0:T(8,128)S(1)}, f32[2,8,512]{2,1,0:T(8,128)S(1)}, u32[]{:S(2)}, u32[]{:S(2)}) collective-permute-start(f32[2,8,512]{2,1,0:T(8,128)S(1)} %collective-permute-done.17.refs_7_), channel_id=1, source_target_pairs={{0,1},{1,0},{2,3},{3,2},{4,5},{5,4},{6,7},{7,6},{8,9},{9,8},{10,11... | collective-permute-start | bytes 98312 | tf_op jit(solution)/shard_map/ppermute | solution.py:488
  39.7 1.6 %collective-permute-start.21 = (bf16[4,128,256]{2,1,0:T(8,128)(2,1)S(1)}, bf16[4,128,256]{2,1,0:T(8,128)(2,1)S(1)}, u32[]{:S(2)}, u32[]{:S(2)}) collective-permute-start(bf16[4,128,256]{2,1,0:T(8,128)(2,1)S(1)} %get-tuple-element.56), channel_id=1, source_target_pairs={{0,1},{1,0},{2,3},{3,2},{4,5},{5,4},{6,7},{7,6},{8,9},{9,8},{10,11... | collective-permute-start | bytes 786440 | tf_op jit(solution)/shard_map/ppermute | solution.py:488
  41.4 7.8 %collective-permute-start.22 = (bf16[128,256]{1,0:T(8,128)(2,1)S(1)}, bf16[128,256]{1,0:T(8,128)(2,1)S(1)}, u32[]{:S(2)}, u32[]{:S(2)}) collective-permute-start(bf16[128,256]{1,0:T(8,128)(2,1)S(1)} %get-tuple-element.67), channel_id=1, source_target_pairs={{0,4},{4,0},{8,12},{12,8},{1,5},{5,1},{9,13},{13,9},{2,6},{6,2},{1... | collective-permute-start | bytes 196616 | tf_op jit(solution)/shard_map/ppermute | solution.py:489
  41.5 8.6 %collective-permute-start.23 = (bf16[128,256]{1,0:T(8,128)(2,1)S(1)}, bf16[128,256]{1,0:T(8,128)(2,1)S(1)}, u32[]{:S(2)}, u32[]{:S(2)}) collective-permute-start(bf16[128,256]{1,0:T(8,128)(2,1)S(1)} %get-tuple-element.69), channel_id=1, source_target_pairs={{0,8},{4,12},{8,0},{12,4},{1,9},{5,13},{9,1},{13,5},{2,10},{6,14},... | collective-permute-start | bytes 196616 | tf_op jit(solution)/shard_map/ppermute | solution.py:489
  43.5 6.7 %collective-permute-start.24 = (bf16[128,256]{1,0:T(8,128)(2,1)S(1)}, bf16[128,256]{1,0:T(8,128)(2,1)S(1)}, u32[]{:S(2)}, u32[]{:S(2)}) collective-permute-start(bf16[128,256]{1,0:T(8,128)(2,1)S(1)} %get-tuple-element.68), channel_id=1, source_target_pairs={{0,12},{4,8},{8,4},{12,0},{1,13},{5,9},{9,5},{13,1},{2,14},{6,10},... | collective-permute-start | bytes 196616 | tf_op jit(solution)/shard_map/ppermute | solution.py:489

commit v6 on v5

--- a/solution.py
+++ b/solution.py
@@ -158,19 +158,35 @@
     return op(values.reshape(CHUNK // 8, 8, WIDE), axis=0)
 
 
+def rows_of(meta, b, p, features):
+    at_slot = meta[SLOT_IN, meta[OWNER, b]]
+    return pl.ds(pl.multiple_of(at_slot * features + p * LANES, LANES), LANES)
+
+
+def put_heads(side, first, b, p, features, row):
+    at = first + b * features // HD + 2 * p
+    side[at : at + 1, :] = row[:, :TEST]
+    side[at + 1 : at + 2, :] = row[:, TEST:]
+
+
+def get_heads(side, row, heads):
+    return jnp.concatenate([side[row + h : row + h + 1, :] for h in range(heads)], axis=1)
+
+
 def units_of(blocks, features):
     return [(b, p) for b in range(blocks) for p in range(features // LANES)]
 
 
 def weights_kernel(count, held, meta, *refs):
     pieces = refs[:count]
-    state, qt_ref, peak_hbm, state_out, peak_s, scores_s, held_s, sem, peak_sem = refs[count:]
-    tables, features, _ = qt_ref.shape
-    stacked = features // HD * TEST
+    state, side, state_out, scores_s, held_s, sem = refs[count:]
+    _, features = held_s.shape[1:]
+    stacked = features // HD * TEST
+    first_peak = side.shape[0] - state.shape[0] * features // HD
     units = units_of(state.shape[0], features)
 
     def store(at_slot, turned):
-        qt_ref[at_slot] = turned
+        side[at_slot * features : (at_slot + 1) * features, :] = turned.astype(jnp.float32)
 
     turn_pieces(pieces, held, held_s, sem, store)
     peaks = [None] * len(units)
@@ -178,9 +194,7 @@
         if t < len(units):
             b, p = units[t]
             live = meta[LIVE, b]
-            queries = two_heads(
-                qt_ref[meta[SLOT_IN, meta[OWNER, b]], p * LANES : (p + 1) * LANES, :]
-            )
+            queries = two_heads(side[rows_of(meta, b, p, features), :]).astype(jnp.bfloat16)
             peak = jnp.full((8, WIDE), NEG, jnp.float32)
         for r in range(0, BLK, CHUNK):
             rows = slice(r, r + CHUNK)
@@ -199,33 +213,27 @@
                 peak = jnp.maximum(peak, fold(scores, jnp.max))
         if t < len(units):
             peaks[t] = jnp.max(peak, axis=0, keepdims=True) * LOG2_SCALE
-            peak_s[b : b + 1, p * WIDE : (p + 1) * WIDE] = peaks[t]
-    for copy in every_copy([pltpu.make_async_copy(peak_s, peak_hbm, peak_sem.at[0])]):
-        copy.wait()
+            put_heads(side, first_peak, b, p, features, peaks[t])
 
 
 def block_weights(meta, held, pieces, state, features, tables):
     blocks = state.shape[0]
-    stacked = features // HD * TEST
     count = len(pieces)
     pieces = [in_hbm(piece) if n < held else piece for n, piece in enumerate(pieces)]
     specs = [hbm_spec() if n < held else vmem_spec() for n in range(count)]
     return pl.pallas_call(
         lambda *refs: weights_kernel(count, held, *refs),
         in_specs=[smem_spec()] + specs + [vmem_spec()],
-        out_specs=[vmem_spec(), hbm_spec(), vmem_spec()],
+        out_specs=[vmem_spec()] * 2,
         out_shape=[
-            pltpu.VMEM((tables, features, TEST), jnp.bfloat16),
-            pltpu.HBM((blocks, stacked), jnp.float32),
+            pltpu.VMEM((tables * features + blocks * features // HD, TEST), jnp.float32),
             pltpu.VMEM(state.shape, jnp.bfloat16),
         ],
-        input_output_aliases={count + 1: 2},
+        input_output_aliases={count + 1: 1},
         scratch_shapes=[
-            pltpu.VMEM((blocks, stacked), jnp.float32),
             pltpu.VMEM((2, BLK, WIDE), jnp.float32),
             pltpu.VMEM((max(held, 1), TEST, features), jnp.bfloat16),
             pltpu.SemaphoreType.DMA((max(held, 1),)),
-            pltpu.SemaphoreType.DMA((1,)),
         ],
         compiler_params=params(10),
         name="block_weights",
@@ -234,19 +242,21 @@
 
 def moved_kernel(count, held, meta, *refs):
     pieces = refs[:count]
-    peak_hbm, state, gt_ref, blk_hbm, tab_ref, state_out = refs[count : count + 6]
-    blk_s, tab_s, dprobs_s, held_s, sem, blk_sem = refs[count + 6 :]
-    tables, features, _ = gt_ref.shape
+    q_side, state, side, tab_ref, state_out = refs[count : count + 5]
+    tab_s, dprobs_s, held_s, sem = refs[count + 5 :]
+    tables = tab_ref.shape[1]
+    _, features = held_s.shape[1:]
     stacked = features // HD * TEST
     blocks = state.shape[0]
+    heads = features // HD
+    first = tables * features
     units = units_of(blocks, features)
-    peak_copy = pltpu.make_async_copy(peak_hbm, blk_s.at[0], blk_sem.at[0])
-    peak_copy.start()
     query = lax.broadcasted_iota(jnp.int32, (features, TEST), 1)
 
     def store(at_slot, turned):
         live = query < meta[TESTN, meta[TABLE_OF, at_slot]]
-        gt_ref[at_slot] = jnp.where(live, turned, jnp.zeros_like(turned))
+        turned = jnp.where(live, turned, jnp.zeros_like(turned)).astype(jnp.float32)
+        side[at_slot * features : (at_slot + 1) * features, :] = turned
 
     turn_pieces(pieces, held, held_s, sem, store)
     means = [None] * len(units)
@@ -254,9 +264,7 @@
     for t in range(len(units) + 1):
         if t < len(units):
             b, p = units[t]
-            grads = two_heads(
-                gt_ref[meta[SLOT_IN, meta[OWNER, b]], p * LANES : (p + 1) * LANES, :]
-            )
+            grads = two_heads(side[rows_of(meta, b, p, features), :]).astype(jnp.bfloat16)
             mass = part = zero
         for r in range(0, BLK, CHUNK):
             rows = slice(r, r + CHUNK)
@@ -267,26 +275,26 @@
                 lanes = slice(stacked + last_p * WIDE, stacked + (last_p + 1) * WIDE)
                 state_out[last_b, rows, lanes] = moved.astype(jnp.bfloat16)
             if t < len(units):
-                first = 2 * stacked + features + p * LANES
-                values = state[b, rows, first : first + LANES]
+                lane = 2 * stacked + features + p * LANES
+                values = state[b, rows, lane : lane + LANES]
                 dprobs = jnp.dot(values, grads, preferred_element_type=jnp.float32)
                 weights = state[b, rows, p * WIDE : (p + 1) * WIDE].astype(jnp.float32)
                 mass = mass + fold(weights, jnp.sum)
                 part = part + fold(weights * dprobs, jnp.sum)
                 dprobs_s[t % 2, rows, :] = dprobs
         if t < len(units):
-            wide = slice(p * WIDE, (p + 1) * WIDE)
             mass = jnp.sum(mass, axis=0, keepdims=True)
             means[t] = jnp.sum(part, axis=0, keepdims=True) / mass
-            blk_s[1, b : b + 1, wide] = mass
-            blk_s[2, b : b + 1, wide] = means[t]
-    peak_copy.wait()
+            put_heads(side, first, b, p, features, means[t])
+            put_heads(side, first + blocks * heads, b, p, features, mass)
     tab_s[0] = jnp.full(tab_s.shape[1:], NEG, jnp.float32)
     tab_s[1] = jnp.zeros(tab_s.shape[1:], jnp.float32)
     tab_s[2] = jnp.zeros(tab_s.shape[1:], jnp.float32)
     for b in range(blocks):
         at = pl.ds(meta[OWNER, b], 1)
-        peak, mass, mean = blk_s[0, b : b + 1, :], blk_s[1, b : b + 1, :], blk_s[2, b : b + 1, :]
+        row = first + b * heads
+        peak, mean = get_heads(q_side, row, heads), get_heads(side, row, heads)
+        mass = get_heads(side, row + blocks * heads, heads)
         old = tab_s[0, at, :]
         new = jnp.maximum(old, peak)
         old_weight = jnp.exp2(old - new)
@@ -298,11 +306,9 @@
     mass = jnp.where(here, tab_s[1], 1.0)
     tab_ref[0] = jnp.where(here, tab_s[0] + jnp.log2(mass), NEG)
     tab_ref[1] = tab_s[2] / mass
-    for copy in every_copy([pltpu.make_async_copy(blk_s, blk_hbm, blk_sem.at[0])]):
-        copy.wait()
-
-
-def moved_weights(meta, held, pieces, peak, state, features, tables):
+
+
+def moved_weights(meta, held, pieces, q_side, state, features, tables):
     blocks = state.shape[0]
     stacked = features // HD * TEST
     count = len(pieces)
@@ -310,33 +316,28 @@
     specs = [hbm_spec() if n < held else vmem_spec() for n in range(count)]
     return pl.pallas_call(
         lambda *refs: moved_kernel(count, held, *refs),
-        in_specs=[smem_spec()] + specs + [hbm_spec(), vmem_spec()],
-        out_specs=[vmem_spec(), hbm_spec(), vmem_spec(), vmem_spec()],
+        in_specs=[smem_spec()] + specs + [vmem_spec()] * 2,
+        out_specs=[vmem_spec()] * 3,
         out_shape=[
-            pltpu.VMEM((tables, features, TEST), jnp.bfloat16),
-            pltpu.HBM((3, blocks, stacked), jnp.float32),
+            pltpu.VMEM((tables * features + 2 * blocks * features // HD, TEST), jnp.float32),
             jax.ShapeDtypeStruct((2, tables, stacked), jnp.float32),
             pltpu.VMEM(state.shape, jnp.bfloat16),
         ],
-        input_output_aliases={count + 2: 3},
+        input_output_aliases={count + 2: 2},
         scratch_shapes=[
-            pltpu.VMEM((3, blocks, stacked), jnp.float32),
             pltpu.VMEM((3, tables, stacked), jnp.float32),
             pltpu.VMEM((2, BLK, WIDE), jnp.float32),
             pltpu.VMEM((max(held, 1), TEST, features), jnp.bfloat16),
             pltpu.SemaphoreType.DMA((max(held, 1),)),
-            pltpu.SemaphoreType.DMA((1,)),
         ],
         compiler_params=params(10),
         name="moved_weights",
-    )(meta, *pieces, in_hbm(peak), state)
-
-
-def query_sums_kernel(state, blk_hbm, ab_ref, blk_ref, state_out, blk_sem):
+    )(meta, *pieces, q_side, state)
+
+
+def query_sums_kernel(state, ab_ref, state_out):
     blocks, _, features, _ = ab_ref.shape
     stacked = features // HD * TEST
-    copy = pltpu.make_async_copy(blk_hbm, blk_ref, blk_sem.at[0])
-    copy.start()
     for b in range(blocks):
         for p in range(features // LANES):
             keys = state[b, :, 2 * stacked + p * LANES : 2 * stacked + (p + 1) * LANES]
@@ -347,25 +348,22 @@
                 )
                 ab_ref[b, n, p * LANES : p * LANES + HD, :] = product[:HD, :TEST]
                 ab_ref[b, n, p * LANES + HD : (p + 1) * LANES, :] = product[HD:, TEST:]
-    copy.wait()
-
-
-def query_sums(features, state, blk):
+
+
+def query_sums(features, state):
     blocks = state.shape[0]
     return pl.pallas_call(
         query_sums_kernel,
-        in_specs=[vmem_spec(), hbm_spec()],
-        out_specs=[vmem_spec()] * 3,
+        in_specs=[vmem_spec()],
+        out_specs=[vmem_spec()] * 2,
         out_shape=[
             pltpu.VMEM((blocks, 2, features, TEST), jnp.float32),
-            pltpu.VMEM(blk.shape, jnp.float32),
             pltpu.VMEM(state.shape, jnp.bfloat16),
         ],
-        input_output_aliases={0: 2},
-        scratch_shapes=[pltpu.SemaphoreType.DMA((1,))],
+        input_output_aliases={0: 1},
         compiler_params=params(8),
         name="query_sums",
-    )(state, in_hbm(blk))
+    )(state)
 
 
 def merged(pieces):
@@ -382,22 +380,24 @@
 
 def query_grad_kernel(count, meta, *refs):
     pieces = refs[:count]
-    blk_ref, ab_ref = refs[count : count + 2]
-    c_ref, d_ref, *q_refs = refs[count + 2 : -2]
+    q_side, g_side, ab_ref = refs[count : count + 3]
+    c_ref, d_ref, *q_refs = refs[count + 3 : -2]
     tab_s, acc_s = refs[-2:]
-    blocks = blk_ref.shape[1]
+    blocks = ab_ref.shape[0]
     tables, features, _ = acc_s.shape
+    heads = features // HD
     tab_s[0], tab_s[1], tab_s[2] = merged(pieces)
     acc_s[...] = jnp.zeros_like(acc_s)
     for b in range(blocks):
-        table = meta[OWNER, b]
-        at = meta[SLOT_OUT, table]
-        mass = tab_s[1, pl.ds(table, 1), :]
-        c = jnp.exp2(blk_ref[0, b : b + 1, :] - tab_s[0, pl.ds(table, 1), :]) / mass
-        d = c * (blk_ref[2, b : b + 1, :] - tab_s[2, pl.ds(table, 1), :])
+        at = meta[SLOT_OUT, meta[OWNER, b]]
+        table = pl.ds(meta[OWNER, b], 1)
+        row = tables * features + b * heads
+        mass = tab_s[1, table, :]
+        c = jnp.exp2(get_heads(q_side, row, heads) - tab_s[0, table, :]) / mass
+        d = c * (get_heads(g_side, row, heads) - tab_s[2, table, :])
         c_ref[b : b + 1, :] = c
         d_ref[b : b + 1, :] = d
-        for h in range(features // HD):
+        for h in range(heads):
             rows = slice(h * HD, (h + 1) * HD)
             lanes = slice(h * TEST, (h + 1) * TEST)
             acc_s[at, rows, :] += c[:, lanes] * ab_ref[b, 0, rows, :] + d[:, lanes] * ab_ref[b, 1, rows, :]
@@ -407,13 +407,13 @@
         ref[n % per] = (acc_s[n] * SCORE_SCALE).T.astype(ref.dtype)
 
 
-def query_grads(meta, tables, pieces, blk, ab, q_dtypes):
+def query_grads(meta, tables, pieces, sides, ab, q_dtypes):
     blocks, _, features, _ = ab.shape
-    stacked = blk.shape[2]
+    stacked = features // HD * TEST
     per = tables // len(q_dtypes)
     return pl.pallas_call(
         lambda *refs: query_grad_kernel(len(pieces), *refs),
-        in_specs=[smem_spec()] + [vmem_spec()] * (len(pieces) + 2),
+        in_specs=[smem_spec()] + [vmem_spec()] * (len(pieces) + 3),
         out_specs=[vmem_spec()] * (2 + len(q_dtypes)),
         out_shape=[
             jax.ShapeDtypeStruct((blocks, stacked), jnp.float32),
@@ -426,23 +426,22 @@
         ],
         compiler_params=params(10),
         name="query_grads",
-    )(meta, *pieces, blk, ab)
-
-
-def row_grads_kernel(meta, c_ref, d_ref, qt_ref, gt_ref, state, dk_hbm, dv_hbm, dk_s, dv_s, out_sem):
+    )(meta, *pieces, *sides, ab)
+
+
+def row_grads_kernel(meta, c_ref, d_ref, q_side, g_side, state, dk_hbm, dv_hbm, dk_s, dv_s, out_sem):
     blocks, _, features = dk_s.shape
     stacked = features // HD * TEST
     turned = (((1,), (1,)), ((), ()))
     stores = []
     for b in range(blocks):
-        at_slot = meta[SLOT_IN, meta[OWNER, b]]
         for p in range(features // LANES):
             at = slice(p * LANES, (p + 1) * LANES)
             wide = slice(p * WIDE, (p + 1) * WIDE)
             c = c_ref[b : b + 1, wide]
             d = d_ref[b : b + 1, wide]
-            q_t = two_heads(qt_ref[at_slot, at, :].astype(jnp.float32))
-            g_t = two_heads(gt_ref[at_slot, at, :].astype(jnp.float32))
+            q_t = two_heads(q_side[rows_of(meta, b, p, features), :])
+            g_t = two_heads(g_side[rows_of(meta, b, p, features), :])
             for_u = (q_t * (c * SCORE_SCALE)).astype(jnp.bfloat16)
             for_e = jnp.concatenate([g_t * c, q_t * (d * SCORE_SCALE)], axis=0).astype(jnp.bfloat16)
             from_e = lax.dot_general(
@@ -463,9 +462,8 @@
         copy.wait()
 
 
-def row_grads(meta, c, d, turned, state):
+def row_grads(meta, c, d, sides, state, features):
     blocks = state.shape[0]
-    features = turned[0].shape[1]
     return pl.pallas_call(
         row_grads_kernel,
         in_specs=[smem_spec()] + [vmem_spec()] * 5,
@@ -478,7 +476,7 @@
         ],
         compiler_params=params(10),
         name="row_grads",
-    )(meta, c, d, *turned, state)
+    )(meta, c, d, *sides, state)
 
 
 def local(small, query_rows, key_rows, value_rows, cotangent, train_rows, test_rows, block_table):
@@ -495,12 +493,13 @@
         near_grads = [step(cotangent, s) for s in (1, 2, 3)]
         block_table, near[0] = after(block_table, near[0])
         meta, state = load(block_table)
-        near[0], meta = after(near[0], meta)
-        queries = [query_rows, pair(query_rows)]
+        own, _ = after(query_rows, meta)
+        near = [after(value, meta)[0] for value in near]
+        queries = [query_rows, pair(own)]
         for value in near:
             queries += [value, pair(value)]
-        qt, peak, state = block_weights(meta, held, queries, state, features, tables)
-        *near_grads, qt = lax.optimization_barrier((*near_grads, qt))
+        q_side, state = block_weights(meta, held, queries, state, features, tables)
+        *near_grads, q_side = lax.optimization_barrier((*near_grads, q_side))
         grads = [cotangent, pair(cotangent)]
         for value in near_grads:
             grads += [value, pair(value)]
@@ -508,32 +507,32 @@
         held = 0
         meta, state = load(block_table)
         queries = [lax.all_gather(query_rows, RP, axis=0, tiled=True)]
-        qt, peak, state = block_weights(meta, held, queries, state, features, tables)
+        q_side, state = block_weights(meta, held, queries, state, features, tables)
         grads = [lax.all_gather(cotangent, RP, axis=0, tiled=True)]
-    gt, blk, tab, state = moved_weights(meta, held, grads, peak, state, features, tables)
+    g_side, tab, state = moved_weights(meta, held, grads, q_side, state, features, tables)
     if small:
         near = [step(tab, s) for s in (1, 2, 3)]
-        ab, blk, state = query_sums(features, state, blk)
+        ab, state = query_sums(features, state)
         *near, ab = lax.optimization_barrier((*near, ab))
         stats = [tab, pair(tab)]
         for value in near:
             stats += [value, pair(value)]
         dtypes = [jnp.float32, jnp.bfloat16]
     else:
-        ab, blk, state = query_sums(features, state, blk)
+        ab, state = query_sums(features, state)
         peak = lax.pmax(tab[0], RP)
         weight = jnp.exp2(tab[0] - peak)
         total, part = lax.psum(jnp.stack([weight, weight * tab[1]]), RP)
         stats = [jnp.stack([peak + jnp.log2(total), part / total])]
         dtypes = [jnp.float32]
-    c, d, *q_terms = query_grads(meta, tables, stats, blk, ab, dtypes)
+    c, d, *q_terms = query_grads(meta, tables, stats, (q_side, g_side), ab, dtypes)
     if small:
         keep, send = q_terms
         total = keep + pair(send).astype(jnp.float32)
         low = total.astype(jnp.bfloat16)
         got = [step(low[s - 1], s) for s in (1, 2, 3)]
         low, c = lax.optimization_barrier((low, c))
-        key_grad, value_grad = row_grads(meta, c, d, (qt, gt), state)
+        key_grad, value_grad = row_grads(meta, c, d, (q_side, g_side), state, features)
         query_grad = total[3]
         for value in got:
             query_grad = query_grad + value.astype(jnp.float32)
@@ -541,7 +540,7 @@
         query_grad = lax.psum_scatter(
             q_terms[0].reshape(tables * TEST, features), RP, scatter_dimension=0, tiled=True
         )
-        key_grad, value_grad = row_grads(meta, c, d, (qt, gt), state)
+        key_grad, value_grad = row_grads(meta, c, d, (q_side, g_side), state, features)
     return query_grad.astype(jnp.bfloat16), key_grad, value_grad
 
 

time: 51 us -> 53.6 us (1.051)
  Pallas kernels: 16.8 us -> 18.9 us
    pallas_call x1, Pallas kernels: 4.66 us -> 5.78 us  [moved_weights(): pl.pallas_call(lambda *refs: moved_kernel(count, held, *refs), in_specs=[...]
    pallas_call x1, Pallas kernels: 4.7 us -> 5.67 us  [block_weights(): pl.pallas_call(lambda *refs: weights_kernel(count, held, *refs), in_specs...]
  transfers between devices with their start and end apart: 25 -> 25, of which waited for: 12 -> 11; matrix products, arithmetic and copies ran while one was open for 0% -> 0% of each run, Pallas kernels for 23% -> 23%
where the time goes in v6:
time: 53.6 us; the launch traced here: 53.4 us
  starting transfers between devices  21.4 us (40%)
  Pallas kernels  18.9 us (35%)
  waiting for transfers between devices  11.6 us (22%)
  between operations  0.81 us (2%)
  other arithmetic  0.74 us (1%)
    ppermute x12, starting transfers between devices, local(): lax.ppermute(value, 'rows', [(z, z ^ s) for z in range(4)])  19 us
    ppermute x12, waiting for transfers between devices, local(): lax.ppermute(value, 'rows', [(z, z ^ s) for z in range(4)])  8.12 us
    pallas_call x1, Pallas kernels, moved_weights(): pl.pallas_call(lambda *refs: moved_kernel(count, held, *refs), in_specs=[...  5.78 us
    pallas_call x1, Pallas kernels, block_weights(): pl.pallas_call(lambda *refs: weights_kernel(count, held, *refs), in_specs...  5.67 us
    ppermute x13, waiting for transfers between devices, local(): pair = lambda value: lax.ppermute(value, 'pair', PAIR)  3.48 us
    pallas_call x1, Pallas kernels, row_grads(): pl.pallas_call(row_grads_kernel, in_specs=[smem_spec()] + [vmem_spec()] *...  3.29 us
    ppermute x13, starting transfers between devices, local(): pair = lambda value: lax.ppermute(value, 'pair', PAIR)  2.41 us
    pallas_call x1, Pallas kernels, load_rows(): pl.pallas_call(lambda *refs: load_kernel(small, *refs), in_specs=[hbm_spe...  2.3 us
  transfers between devices with their start and end apart: 25, of which 11 were waited for; matrix products, arithmetic and copies ran while one was open for 0% of the time, Pallas kernels for 23%

profile of v6, /device:TPU:0, one launch (start us, length us, event | category | flops | bytes accessed | tf_op | source)
XLA Modules:
  0.0 53.4 jit_solution(4263283557518519606)
XLA Ops:
  0.6 0.0 copy-start
  0.6 0.0 copy-start.1
  0.7 3.1 %collective-permute-start = (bf16[128,256]{1,0:T(8,128)(2,1)}, bf16[128,256]{1,0:T(8,128)(2,1)S(1)}, u32[]{:S(2)}, u32[]{:S(2)}) collective-permute-start(bf16[128,256]{1,0:T(8,128)(2,1)} %refs_1_.4), channel_id=1, source_target_pairs={{0,4},{4,0},{8,12},{12,8},{1,5},{5,1},{9,13},{13,9},{2,6},{6,2},{1... | collective-permute-start | bytes 196616 | tf_op jit(solution)/shard_map/ppermute | solution.py:487
  3.7 2.5 %collective-permute-start.9 = (bf16[128,256]{1,0:T(8,128)(2,1)}, bf16[128,256]{1,0:T(8,128)(2,1)S(1)}, u32[]{:S(2)}, u32[]{:S(2)}) collective-permute-start(bf16[128,256]{1,0:T(8,128)(2,1)} %refs_1_.4), channel_id=1, source_target_pairs={{0,12},{4,8},{8,4},{12,0},{1,13},{5,9},{9,5},{13,1},{2,14},{6,10},... | collective-permute-start | bytes 196616 | tf_op jit(solution)/shard_map/ppermute | solution.py:487
  6.2 0.1 collective-permute-start.7
  6.3 0.0 collective-permute-done.refs_3_
  6.3 2.3 %load_rows.1 = (s32[6,8]{1,0:T(8,128)S(4)}, bf16[8,512,1536]{2,1,0:T(8,128)(2,1)S(1)}) custom-call(s32[64]{0:T(128)} %refs_0_, s32[8]{0:T(128)} %refs_1_.3, s32[8]{0:T(128)} %refs_2_.1, bf16[4096,256]{1,0:T(8,128)(2,1)} %refs_3_.1, bf16[4096,256]{1,0:T(8,128)(2,1)} %refs_4_.1), custom_call_target="tpu_custom_call" | custom-call | tf_op jit(solution)/shard_map/load_rows/pallas_call | solution.py:121
  8.6 0.1 collective-permute-start.6
  8.7 2.1 %collective-permute-done.9.refs_7_ = bf16[128,256]{1,0:T(8,128)(2,1)S(1)} collective-permute-done((bf16[128,256]{1,0:T(8,128)(2,1)}, bf16[128,256]{1,0:T(8,128)(2,1)S(1)}, u32[]{:S(2)}, u32[]{:S(2)}) %collective-permute-start.9) | collective-permute-done | bytes 65568 | tf_op jit(solution)/shard_map/ppermute | solution.py:487
  10.8 0.0 collective-permute-start.10
  10.8 2.1 %collective-permute-done.7.refs_5_ = bf16[128,256]{1,0:T(8,128)(2,1)S(1)} collective-permute-done((bf16[128,256]{1,0:T(8,128)(2,1)}, bf16[128,256]{1,0:T(8,128)(2,1)S(1)}, u32[]{:S(2)}, u32[]{:S(2)}) %collective-permute-start.7) | collective-permute-done | bytes 65568 | tf_op jit(solution)/shard_map/ppermute | solution.py:487
  12.9 0.0 collective-permute-start.8
  12.9 0.5 collective-permute-start.5
  13.4 0.0 collective-permute-start.2
  13.4 0.0 collective-permute-done.6.refs_4_
  13.4 3.0 %collective-permute-start.3 = (bf16[128,256]{1,0:T(8,128)(2,1)S(1)}, bf16[128,256]{1,0:T(8,128)(2,1)S(1)}, u32[]{:S(2)}, u32[]{:S(2)}) collective-permute-start(bf16[128,256]{1,0:T(8,128)(2,1)S(1)} %copy-done.1), channel_id=1, source_target_pairs={{0,8},{4,12},{8,0},{12,4},{1,9},{5,13},{9,1},{13,5},{2,10},{6,14},... | collective-permute-start | bytes 196616 | tf_op jit(solution)/shard_map/ppermute | solution.py:487
  16.4 1.4 %collective-permute-start.4 = (bf16[128,256]{1,0:T(8,128)(2,1)S(1)}, bf16[128,256]{1,0:T(8,128)(2,1)S(1)}, u32[]{:S(2)}, u32[]{:S(2)}) collective-permute-start(bf16[128,256]{1,0:T(8,128)(2,1)S(1)} %copy-done.1), channel_id=1, source_target_pairs={{0,12},{4,8},{8,4},{12,0},{1,13},{5,9},{9,5},{13,1},{2,14},{6,10},... | collective-permute-start | bytes 196616 | tf_op jit(solution)/shard_map/ppermute | solution.py:487
  17.8 0.0 collective-permute-start.1
  17.8 0.0 collective-permute-done.5.refs_2_
  17.8 5.7 %block_weights.1 = (f32[2080,128]{1,0:T(8,128)S(1)}, bf16[8,512,1536]{2,1,0:T(8,128)(2,1)S(1)}) custom-call(s32[6,8]{1,0:T(8,128)S(4)} %get-tuple-element.34.refs_0_.meta, bf16[128,256]{1,0:T(8,128)(2,1)} %refs_1_.4, bf16[128,256]{1,0:T(8,128)(2,1)S(1)} %collective-permute-done.5.refs_2_, ...), custom_call_target="tpu_custom_call", output_to_operand_aliasing={{1}: (9, {})} | custom-call | tf_op jit(solution)/shard_map/block_weights/pallas_call | solution.py:224
  23.5 0.0 collective-permute-done.2.refs_3_
  23.5 0.6 %collective-permute-start.11 = (bf16[128,256]{1,0:T(8,128)(2,1)S(1)}, bf16[128,256]{1,0:T(8,128)(2,1)S(1)}, u32[]{:S(2)}, u32[]{:S(2)}) collective-permute-start(bf16[128,256]{1,0:T(8,128)(2,1)S(1)} %collective-permute-done.2.refs_3_), channel_id=1, source_target_pairs={{0,1},{1,0},{2,3},{3,2},{4,5},{5,4},{6,7},{7,6},{8,9},{9,8},{10,11... | collective-permute-start | bytes 196616 | tf_op jit(solution)/shard_map/ppermute | solution.py:486
  24.1 0.1 collective-permute-start.12
  24.2 0.4 collective-permute-start.13
  24.6 0.4 collective-permute-done.11.refs_4_
  25.0 0.4 collective-permute-done.12.refs_6_
  25.3 0.2 collective-permute-done.13.refs_8_
  25.5 5.8 %moved_weights.1 = (f32[2112,128]{1,0:T(8,128)S(1)}, f32[2,8,512]{2,1,0:T(8,128)S(1)}, bf16[8,512,1536]{2,1,0:T(8,128)(2,1)S(1)}) custom-call(s32[6,8]{1,0:T(8,128)S(4)} %get-tuple-element.34.refs_0_.meta, bf16[128,256]{1,0:T(8,128)(2,1)} %refs_1_.5, bf16[128,256]{1,0:T(8,128)(2,1)S(1)} %collective-permute-done.1.refs_2_, ...), custom_call_target="tpu_custom_call", output_to_operand_aliasing={{2}: (10, {})} | custom-call | tf_op jit(solution)/shard_map/moved_weights/pallas_call | solution.py:317
  31.3 0.1 collective-permute-start.15
  31.4 2.9 %collective-permute-start.16 = (f32[2,8,512]{2,1,0:T(8,128)S(1)}, f32[2,8,512]{2,1,0:T(8,128)S(1)}, u32[]{:S(2)}, u32[]{:S(2)}) collective-permute-start(f32[2,8,512]{2,1,0:T(8,128)S(1)} %get-tuple-element.47.refs_1_), channel_id=1, source_target_pairs={{0,8},{4,12},{8,0},{12,4},{1,9},{5,13},{9,1},{13,5},{2,10},{6,14},... | collective-permute-start | bytes 98312 | tf_op jit(solution)/shard_map/ppermute | solution.py:487
  34.3 1.4 %collective-permute-start.17 = (f32[2,8,512]{2,1,0:T(8,128)S(1)}, f32[2,8,512]{2,1,0:T(8,128)S(1)}, u32[]{:S(2)}, u32[]{:S(2)}) collective-permute-start(f32[2,8,512]{2,1,0:T(8,128)S(1)} %get-tuple-element.47.refs_1_), channel_id=1, source_target_pairs={{0,12},{4,8},{8,4},{12,0},{1,13},{5,9},{9,5},{13,1},{2,14},{6,10},... | collective-permute-start | bytes 98312 | tf_op jit(solution)/shard_map/ppermute | solution.py:487
  35.8 1.3 %query_sums.1 = (f32[8,2,256,128]{3,2,1,0:T(8,128)S(1)}, bf16[8,512,1536]{2,1,0:T(8,128)(2,1)S(1)}) custom-call(bf16[8,512,1536]{2,1,0:T(8,128)(2,1)S(1)} %get-tuple-element.48.state), custom_call_target="tpu_custom_call", output_to_operand_aliasing={{1}: (0, {})} | custom-call | tf_op jit(solution)/shard_map/query_sums/pallas_call | solution.py:355
  37.1 3.0 %collective-permute-done.17.refs_7_ = f32[2,8,512]{2,1,0:T(8,128)S(1)} collective-permute-done((f32[2,8,512]{2,1,0:T(8,128)S(1)}, f32[2,8,512]{2,1,0:T(8,128)S(1)}, u32[]{:S(2)}, u32[]{:S(2)}) %collective-permute-start.17) | collective-permute-done | bytes 32800 | tf_op jit(solution)/shard_map/ppermute | solution.py:487
  40.0 0.5 collective-permute-start.19
  40.5 0.0 collective-permute-start.20
  40.5 0.7 %collective-permute-done.18.refs_4_ = f32[2,8,512]{2,1,0:T(8,128)S(1)} collective-permute-done((f32[2,8,512]{2,1,0:T(8,128)S(1)}, f32[2,8,512]{2,1,0:T(8,128)S(1)}, u32[]{:S(2)}, u32[]{:S(2)}) %collective-permute-start.18) | collective-permute-done | bytes 32800 | tf_op jit(solution)/shard_map/ppermute | solution.py:486
  41.2 0.2 collective-permute-done.19.refs_6_
  41.4 0.3 collective-permute-done.20.refs_8_
  41.8 0.6 %query_grads.1 = (f32[8,512]{1,0:T(8,128)S(1)}, f32[8,512]{1,0:T(8,128)S(1)}, f32[4,128,256]{2,1,0:T(8,128)S(1)}, bf16[4,128,256]{2,1,0:T(8,128)(2,1)S(1)}) custom-call(s32[6,8]{1,0:T(8,128)S(4)} %get-tuple-element.34.refs_0_.meta, f32[2,8,512]{2,1,0:T(8,128)S(1)} %get-tuple-element.47.refs_1_, f32[2,8,512]{2,1,0:T(8,128)S(1)} %collective-permute-done.14.refs_2_, ...), custom_call_target="tpu_custom_call" | custom-call | tf_op jit(solution)/shard_map/query_grads/pallas_call | solution.py:414
  42.3 0.2 collective-permute-start.21
  42.6 1.4 %collective-permute-done.21 = bf16[4,128,256]{2,1,0:T(8,128)(2,1)S(1)} collective-permute-done((bf16[4,128,256]{2,1,0:T(8,128)(2,1)S(1)}, bf16[4,128,256]{2,1,0:T(8,128)(2,1)S(1)}, u32[]{:S(2)}, u32[]{:S(2)}) %collective-permute-start.21) | collective-permute-done | bytes 262176 | tf_op jit(solution)/shard_map/ppermute | solution.py:486
  43.9 0.1 fusion.4
  44.0 0.1 collective-permute-start.22
  44.1 2.0 %collective-permute-start.23 = (bf16[128,256]{1,0:T(8,128)(2,1)S(1)}, bf16[128,256]{1,0:T(8,128)(2,1)S(1)}, u32[]{:S(2)}, u32[]{:S(2)}) collective-permute-start(bf16[128,256]{1,0:T(8,128)(2,1)S(1)} %get-tuple-element.67), channel_id=1, source_target_pairs={{0,8},{4,12},{8,0},{12,4},{1,9},{5,13},{9,1},{13,5},{2,10},{6,14},... | collective-permute-start | bytes 196616 | tf_op jit(solution)/shard_map/ppermute | solution.py:487
  46.1 2.4 %collective-permute-start.24 = (bf16[128,256]{1,0:T(8,128)(2,1)S(1)}, bf16[128,256]{1,0:T(8,128)(2,1)S(1)}, u32[]{:S(2)}, u32[]{:S(2)}) collective-permute-start(bf16[128,256]{1,0:T(8,128)(2,1)S(1)} %get-tuple-element.66), channel_id=1, source_target_pairs={{0,12},{4,8},{8,4},{12,0},{1,13},{5,9},{9,5},{13,1},{2,14},{6,10},... | collective-permute-start | bytes 196616 | tf_op jit(solution)/shard_map/ppermute | solution.py:487
  48.5 3.3 %row_grads.1 = (bf16[4096,256]{1,0:T(8,128)(2,1)}, bf16[4096,256]{1,0:T(8,128)(2,1)}) custom-call(s32[6,8]{1,0:T(8,128)S(4)} %get-tuple-element.34.refs_0_.meta, f32[8,512]{1,0:T(8,128)S(1)} %get-tuple-element.58.c_ref, f32[8,512]{1,0:T(8,128)S(1)} %get-tuple-element.59.d_ref, f32[2080,128]{1,0:T(8,128)S(1)} %get-tuple-element.45.refs_9_.q_side, ...), custom_call_target="tpu_custom_call" | custom-call | tf_op jit(solution)/shard_map/row_grads/pallas_call | solution.py:467
  51.8 1.0 %collective-permute-done.23 = bf16[128,256]{1,0:T(8,128)(2,1)S(1)} collective-permute-done((bf16[128,256]{1,0:T(8,128)(2,1)S(1)}, bf16[128,256]{1,0:T(8,128)(2,1)S(1)}, u32[]{:S(2)}, u32[]{:S(2)}) %collective-permute-start.23) | collective-permute-done | bytes 65568 | tf_op jit(solution)/shard_map/ppermute | solution.py:487
  52.8 0.7 %fusion.3 = bf16[128,256]{1,0:T(8,128)(2,1)} fusion(f32[4,128,256]{2,1,0:T(8,128)S(1)} %get-tuple-element.64, bf16[128,256]{1,0:T(8,128)(2,1)S(1)} %collective-permute-done.24, bf16[128,256]{1,0:T(8,128)(2,1)S(1)} %collective-permute-done.23, bf16[128,256]{1,0:T(8,128)(2,1)S(1)} %collective-permute-done.22), kind=kLoop, calls=%fused_computation.5 | loop fusion | flops 229376 | bytes 393216 | tf_op jit(solution)/shard_map/convert_element_type | solution.py:544
  (15 shorter events, 0.1 us)
Async XLA Ops:
  0.6 12.3 %copy-start = (bf16[128,256]{1,0:T(8,128)(2,1)S(1)}, bf16[128,256]{1,0:T(8,128)(2,1)}, u32[]{:S(2)}) copy-start(bf16[128,256]{1,0:T(8,128)(2,1)} %refs_1_.4) | copy-start | bytes 196612
  0.6 12.8 %copy-start.1 = (bf16[128,256]{1,0:T(8,128)(2,1)S(1)}, bf16[128,256]{1,0:T(8,128)(2,1)}, u32[]{:S(2)}) copy-start(bf16[128,256]{1,0:T(8,128)(2,1)} %refs_1_.5) | copy-start | bytes 196612
  0.7 5.7 %collective-permute-start = (bf16[128,256]{1,0:T(8,128)(2,1)}, bf16[128,256]{1,0:T(8,128)(2,1)S(1)}, u32[]{:S(2)}, u32[]{:S(2)}) collective-permute-start(bf16[128,256]{1,0:T(8,128)(2,1)} %refs_1_.4), channel_id=1, source_target_pairs={{0,4},{4,0},{8,12},{12,8},{1,5},{5,1},{9,13},{13,9},{2,6},{6,2},{1... | collective-permute-start | bytes 196616 | tf_op jit(solution)/shard_map/ppermute | solution.py:487
  3.7 7.1 %collective-permute-start.9 = (bf16[128,256]{1,0:T(8,128)(2,1)}, bf16[128,256]{1,0:T(8,128)(2,1)S(1)}, u32[]{:S(2)}, u32[]{:S(2)}) collective-permute-start(bf16[128,256]{1,0:T(8,128)(2,1)} %refs_1_.4), channel_id=1, source_target_pairs={{0,12},{4,8},{8,4},{12,0},{1,13},{5,9},{9,5},{13,1},{2,14},{6,10},... | collective-permute-start | bytes 196616 | tf_op jit(solution)/shard_map/ppermute | solution.py:487
  6.2 6.7 %collective-permute-start.7 = (bf16[128,256]{1,0:T(8,128)(2,1)}, bf16[128,256]{1,0:T(8,128)(2,1)S(1)}, u32[]{:S(2)}, u32[]{:S(2)}) collective-permute-start(bf16[128,256]{1,0:T(8,128)(2,1)} %refs_1_.4), channel_id=1, source_target_pairs={{0,8},{4,12},{8,0},{12,4},{1,9},{5,13},{9,1},{13,5},{2,10},{6,14},... | collective-permute-start | bytes 196616 | tf_op jit(solution)/shard_map/ppermute | solution.py:487
  8.6 4.8 %collective-permute-start.6 = (bf16[128,256]{1,0:T(8,128)(2,1)S(1)}, bf16[128,256]{1,0:T(8,128)(2,1)S(1)}, u32[]{:S(2)}, u32[]{:S(2)}) collective-permute-start(bf16[128,256]{1,0:T(8,128)(2,1)S(1)} %collective-permute-done.refs_3_), channel_id=1, source_target_pairs={{0,1},{1,0},{2,3},{3,2},{4,5},{5,4},{6,7},{7,6},{8,9},{9,8},{10,11... | collective-permute-start | bytes 196616 | tf_op jit(solution)/shard_map/ppermute | solution.py:486
  10.8 5.6 %collective-permute-start.10 = (bf16[128,256]{1,0:T(8,128)(2,1)S(1)}, bf16[128,256]{1,0:T(8,128)(2,1)S(1)}, u32[]{:S(2)}, u32[]{:S(2)}) collective-permute-start(bf16[128,256]{1,0:T(8,128)(2,1)S(1)} %collective-permute-done.9.refs_7_), channel_id=1, source_target_pairs={{0,1},{1,0},{2,3},{3,2},{4,5},{5,4},{6,7},{7,6},{8,9},{9,8},{10,11... | collective-permute-start | bytes 196616 | tf_op jit(solution)/shard_map/ppermute | solution.py:486
  12.9 4.9 %collective-permute-start.8 = (bf16[128,256]{1,0:T(8,128)(2,1)S(1)}, bf16[128,256]{1,0:T(8,128)(2,1)S(1)}, u32[]{:S(2)}, u32[]{:S(2)}) collective-permute-start(bf16[128,256]{1,0:T(8,128)(2,1)S(1)} %collective-permute-done.7.refs_5_), channel_id=1, source_target_pairs={{0,1},{1,0},{2,3},{3,2},{4,5},{5,4},{6,7},{7,6},{8,9},{9,8},{10,11... | collective-permute-start | bytes 196616 | tf_op jit(solution)/shard_map/ppermute | solution.py:486
  12.9 4.9 %collective-permute-start.5 = (bf16[128,256]{1,0:T(8,128)(2,1)S(1)}, bf16[128,256]{1,0:T(8,128)(2,1)S(1)}, u32[]{:S(2)}, u32[]{:S(2)}) collective-permute-start(bf16[128,256]{1,0:T(8,128)(2,1)S(1)} %copy-done), channel_id=1, source_target_pairs={{0,1},{1,0},{2,3},{3,2},{4,5},{5,4},{6,7},{7,6},{8,9},{9,8},{10,11... | collective-permute-start | bytes 196616 | tf_op jit(solution)/shard_map/ppermute | solution.py:486
  13.4 10.1 %collective-permute-start.2 = (bf16[128,256]{1,0:T(8,128)(2,1)S(1)}, bf16[128,256]{1,0:T(8,128)(2,1)S(1)}, u32[]{:S(2)}, u32[]{:S(2)}) collective-permute-start(bf16[128,256]{1,0:T(8,128)(2,1)S(1)} %copy-done.1), channel_id=1, source_target_pairs={{0,4},{4,0},{8,12},{12,8},{1,5},{5,1},{9,13},{13,9},{2,6},{6,2},{1... | collective-permute-start | bytes 196616 | tf_op jit(solution)/shard_map/ppermute | solution.py:487
  13.4 10.1 %collective-permute-start.3 = (bf16[128,256]{1,0:T(8,128)(2,1)S(1)}, bf16[128,256]{1,0:T(8,128)(2,1)S(1)}, u32[]{:S(2)}, u32[]{:S(2)}) collective-permute-start(bf16[128,256]{1,0:T(8,128)(2,1)S(1)} %copy-done.1), channel_id=1, source_target_pairs={{0,8},{4,12},{8,0},{12,4},{1,9},{5,13},{9,1},{13,5},{2,10},{6,14},... | collective-permute-start | bytes 196616 | tf_op jit(solution)/shard_map/ppermute | solution.py:487
  16.4 7.1 %collective-permute-start.4 = (bf16[128,256]{1,0:T(8,128)(2,1)S(1)}, bf16[128,256]{1,0:T(8,128)(2,1)S(1)}, u32[]{:S(2)}, u32[]{:S(2)}) collective-permute-start(bf16[128,256]{1,0:T(8,128)(2,1)S(1)} %copy-done.1), channel_id=1, source_target_pairs={{0,12},{4,8},{8,4},{12,0},{1,13},{5,9},{9,5},{13,1},{2,14},{6,10},... | collective-permute-start | bytes 196616 | tf_op jit(solution)/shard_map/ppermute | solution.py:487
  17.8 6.8 %collective-permute-start.1 = (bf16[128,256]{1,0:T(8,128)(2,1)S(1)}, bf16[128,256]{1,0:T(8,128)(2,1)S(1)}, u32[]{:S(2)}, u32[]{:S(2)}) collective-permute-start(bf16[128,256]{1,0:T(8,128)(2,1)S(1)} %copy-done.1), channel_id=1, source_target_pairs={{0,1},{1,0},{2,3},{3,2},{4,5},{5,4},{6,7},{7,6},{8,9},{9,8},{10,11... | collective-permute-start | bytes 196616 | tf_op jit(solution)/shard_map/ppermute | solution.py:486
  23.5 1.5 %collective-permute-start.11 = (bf16[128,256]{1,0:T(8,128)(2,1)S(1)}, bf16[128,256]{1,0:T(8,128)(2,1)S(1)}, u32[]{:S(2)}, u32[]{:S(2)}) collective-permute-start(bf16[128,256]{1,0:T(8,128)(2,1)S(1)} %collective-permute-done.2.refs_3_), channel_id=1, source_target_pairs={{0,1},{1,0},{2,3},{3,2},{4,5},{5,4},{6,7},{7,6},{8,9},{9,8},{10,11... | collective-permute-start | bytes 196616 | tf_op jit(solution)/shard_map/ppermute | solution.py:486
  24.1 1.3 %collective-permute-start.12 = (bf16[128,256]{1,0:T(8,128)(2,1)S(1)}, bf16[128,256]{1,0:T(8,128)(2,1)S(1)}, u32[]{:S(2)}, u32[]{:S(2)}) collective-permute-start(bf16[128,256]{1,0:T(8,128)(2,1)S(1)} %collective-permute-done.3.refs_5_), channel_id=1, source_target_pairs={{0,1},{1,0},{2,3},{3,2},{4,5},{5,4},{6,7},{7,6},{8,9},{9,8},{10,11... | collective-permute-start | bytes 196616 | tf_op jit(solution)/shard_map/ppermute | solution.py:486
  24.2 1.3 %collective-permute-start.13 = (bf16[128,256]{1,0:T(8,128)(2,1)S(1)}, bf16[128,256]{1,0:T(8,128)(2,1)S(1)}, u32[]{:S(2)}, u32[]{:S(2)}) collective-permute-start(bf16[128,256]{1,0:T(8,128)(2,1)S(1)} %collective-permute-done.4.refs_7_), channel_id=1, source_target_pairs={{0,1},{1,0},{2,3},{3,2},{4,5},{5,4},{6,7},{7,6},{8,9},{9,8},{10,11... | collective-permute-start | bytes 196616 | tf_op jit(solution)/shard_map/ppermute | solution.py:486
  31.3 5.7 %collective-permute-start.15 = (f32[2,8,512]{2,1,0:T(8,128)S(1)}, f32[2,8,512]{2,1,0:T(8,128)S(1)}, u32[]{:S(2)}, u32[]{:S(2)}) collective-permute-start(f32[2,8,512]{2,1,0:T(8,128)S(1)} %get-tuple-element.47.refs_1_), channel_id=1, source_target_pairs={{0,4},{4,0},{8,12},{12,8},{1,5},{5,1},{9,13},{13,9},{2,6},{6,2},{1... | collective-permute-start | bytes 98312 | tf_op jit(solution)/shard_map/ppermute | solution.py:487
  31.4 5.7 %collective-permute-start.16 = (f32[2,8,512]{2,1,0:T(8,128)S(1)}, f32[2,8,512]{2,1,0:T(8,128)S(1)}, u32[]{:S(2)}, u32[]{:S(2)}) collective-permute-start(f32[2,8,512]{2,1,0:T(8,128)S(1)} %get-tuple-element.47.refs_1_), channel_id=1, source_target_pairs={{0,8},{4,12},{8,0},{12,4},{1,9},{5,13},{9,1},{13,5},{2,10},{6,14},... | collective-permute-start | bytes 98312 | tf_op jit(solution)/shard_map/ppermute | solution.py:487
  34.3 5.7 %collective-permute-start.17 = (f32[2,8,512]{2,1,0:T(8,128)S(1)}, f32[2,8,512]{2,1,0:T(8,128)S(1)}, u32[]{:S(2)}, u32[]{:S(2)}) collective-permute-start(f32[2,8,512]{2,1,0:T(8,128)S(1)} %get-tuple-element.47.refs_1_), channel_id=1, source_target_pairs={{0,12},{4,8},{8,4},{12,0},{1,13},{5,9},{9,5},{13,1},{2,14},{6,10},... | collective-permute-start | bytes 98312 | tf_op jit(solution)/shard_map/ppermute | solution.py:487
  35.7 4.8 %collective-permute-start.14 = (f32[2,8,512]{2,1,0:T(8,128)S(1)}, f32[2,8,512]{2,1,0:T(8,128)S(1)}, u32[]{:S(2)}, u32[]{:S(2)}) collective-permute-start(f32[2,8,512]{2,1,0:T(8,128)S(1)} %get-tuple-element.47.refs_1_), channel_id=1, source_target_pairs={{0,1},{1,0},{2,3},{3,2},{4,5},{5,4},{6,7},{7,6},{8,9},{9,8},{10,11... | collective-permute-start | bytes 98312 | tf_op jit(solution)/shard_map/ppermute | solution.py:486
  40.0 1.2 %collective-permute-start.18 = (f32[2,8,512]{2,1,0:T(8,128)S(1)}, f32[2,8,512]{2,1,0:T(8,128)S(1)}, u32[]{:S(2)}, u32[]{:S(2)}) collective-permute-start(f32[2,8,512]{2,1,0:T(8,128)S(1)} %collective-permute-done.15.refs_3_), channel_id=1, source_target_pairs={{0,1},{1,0},{2,3},{3,2},{4,5},{5,4},{6,7},{7,6},{8,9},{9,8},{10,11... | collective-permute-start | bytes 98312 | tf_op jit(solution)/shard_map/ppermute | solution.py:486
  40.0 1.4 %collective-permute-start.19 = (f32[2,8,512]{2,1,0:T(8,128)S(1)}, f32[2,8,512]{2,1,0:T(8,128)S(1)}, u32[]{:S(2)}, u32[]{:S(2)}) collective-permute-start(f32[2,8,512]{2,1,0:T(8,128)S(1)} %collective-permute-done.16.refs_5_), channel_id=1, source_target_pairs={{0,1},{1,0},{2,3},{3,2},{4,5},{5,4},{6,7},{7,6},{8,9},{9,8},{10,11... | collective-permute-start | bytes 98312 | tf_op jit(solution)/shard_map/ppermute | solution.py:486
  40.5 1.2 %collective-permute-start.20 = (f32[2,8,512]{2,1,0:T(8,128)S(1)}, f32[2,8,512]{2,1,0:T(8,128)S(1)}, u32[]{:S(2)}, u32[]{:S(2)}) collective-permute-start(f32[2,8,512]{2,1,0:T(8,128)S(1)} %collective-permute-done.17.refs_7_), channel_id=1, source_target_pairs={{0,1},{1,0},{2,3},{3,2},{4,5},{5,4},{6,7},{7,6},{8,9},{9,8},{10,11... | collective-permute-start | bytes 98312 | tf_op jit(solution)/shard_map/ppermute | solution.py:486
  42.3 1.6 %collective-permute-start.21 = (bf16[4,128,256]{2,1,0:T(8,128)(2,1)S(1)}, bf16[4,128,256]{2,1,0:T(8,128)(2,1)S(1)}, u32[]{:S(2)}, u32[]{:S(2)}) collective-permute-start(bf16[4,128,256]{2,1,0:T(8,128)(2,1)S(1)} %get-tuple-element.56), channel_id=1, source_target_pairs={{0,1},{1,0},{2,3},{3,2},{4,5},{5,4},{6,7},{7,6},{8,9},{9,8},{10,11... | collective-permute-start | bytes 786440 | tf_op jit(solution)/shard_map/ppermute | solution.py:486
  44.0 7.8 %collective-permute-start.22 = (bf16[128,256]{1,0:T(8,128)(2,1)S(1)}, bf16[128,256]{1,0:T(8,128)(2,1)S(1)}, u32[]{:S(2)}, u32[]{:S(2)}) collective-permute-start(bf16[128,256]{1,0:T(8,128)(2,1)S(1)} %get-tuple-element.65), channel_id=1, source_target_pairs={{0,4},{4,0},{8,12},{12,8},{1,5},{5,1},{9,13},{13,9},{2,6},{6,2},{1... | collective-permute-start | bytes 196616 | tf_op jit(solution)/shard_map/ppermute | solution.py:487
  44.1 8.6 %collective-permute-start.23 = (bf16[128,256]{1,0:T(8,128)(2,1)S(1)}, bf16[128,256]{1,0:T(8,128)(2,1)S(1)}, u32[]{:S(2)}, u32[]{:S(2)}) collective-permute-start(bf16[128,256]{1,0:T(8,128)(2,1)S(1)} %get-tuple-element.67), channel_id=1, source_target_pairs={{0,8},{4,12},{8,0},{12,4},{1,9},{5,13},{9,1},{13,5},{2,10},{6,14},... | collective-permute-start | bytes 196616 | tf_op jit(solution)/shard_map/ppermute | solution.py:487
  46.1 6.7 %collective-permute-start.24 = (bf16[128,256]{1,0:T(8,128)(2,1)S(1)}, bf16[128,256]{1,0:T(8,128)(2,1)S(1)}, u32[]{:S(2)}, u32[]{:S(2)}) collective-permute-start(bf16[128,256]{1,0:T(8,128)(2,1)S(1)} %get-tuple-element.66), channel_id=1, source_target_pairs={{0,12},{4,8},{8,4},{12,0},{1,13},{5,9},{9,5},{13,1},{2,14},{6,10},... | collective-permute-start | bytes 196616 | tf_op jit(solution)/shard_map/ppermute | solution.py:487

commit v7 on v6

--- a/solution.py
+++ b/solution.py
@@ -213,7 +213,8 @@
                 peak = jnp.maximum(peak, fold(scores, jnp.max))
         if t < len(units):
             peaks[t] = jnp.max(peak, axis=0, keepdims=True) * LOG2_SCALE
-            put_heads(side, first_peak, b, p, features, peaks[t])
+    for (b, p), peak in zip(units, peaks):
+        put_heads(side, first_peak, b, p, features, peak)
 
 
 def block_weights(meta, held, pieces, state, features, tables):
@@ -243,7 +244,7 @@
 def moved_kernel(count, held, meta, *refs):
     pieces = refs[:count]
     q_side, state, side, tab_ref, state_out = refs[count : count + 5]
-    tab_s, dprobs_s, held_s, sem = refs[count + 5 :]
+    dprobs_s, held_s, sem = refs[count + 5 :]
     tables = tab_ref.shape[1]
     _, features = held_s.shape[1:]
     stacked = features // HD * TEST
@@ -259,7 +260,7 @@
         side[at_slot * features : (at_slot + 1) * features, :] = turned
 
     turn_pieces(pieces, held, held_s, sem, store)
-    means = [None] * len(units)
+    means, masses = [None] * len(units), [None] * len(units)
     zero = jnp.zeros((8, WIDE), jnp.float32)
     for t in range(len(units) + 1):
         if t < len(units):
@@ -284,28 +285,31 @@
                 dprobs_s[t % 2, rows, :] = dprobs
         if t < len(units):
             mass = jnp.sum(mass, axis=0, keepdims=True)
+            masses[t] = mass
             means[t] = jnp.sum(part, axis=0, keepdims=True) / mass
-            put_heads(side, first, b, p, features, means[t])
-            put_heads(side, first + blocks * heads, b, p, features, mass)
-    tab_s[0] = jnp.full(tab_s.shape[1:], NEG, jnp.float32)
-    tab_s[1] = jnp.zeros(tab_s.shape[1:], jnp.float32)
-    tab_s[2] = jnp.zeros(tab_s.shape[1:], jnp.float32)
-    for b in range(blocks):
-        at = pl.ds(meta[OWNER, b], 1)
-        row = first + b * heads
-        peak, mean = get_heads(q_side, row, heads), get_heads(side, row, heads)
-        mass = get_heads(side, row + blocks * heads, heads)
-        old = tab_s[0, at, :]
-        new = jnp.maximum(old, peak)
-        old_weight = jnp.exp2(old - new)
-        new_mass = mass * jnp.exp2(peak - new)
-        tab_s[0, at, :] = new
-        tab_s[1, at, :] = tab_s[1, at, :] * old_weight + new_mass
-        tab_s[2, at, :] = tab_s[2, at, :] * old_weight + new_mass * mean
-    here = tab_s[1] > 0.0
-    mass = jnp.where(here, tab_s[1], 1.0)
-    tab_ref[0] = jnp.where(here, tab_s[0] + jnp.log2(mass), NEG)
-    tab_ref[1] = tab_s[2] / mass
+    for (b, p), mean, mass in zip(units, means, masses):
+        put_heads(side, first, b, p, features, mean)
+        put_heads(side, first + blocks * heads, b, p, features, mass)
+    table = lax.broadcasted_iota(jnp.int32, (tables, stacked), 0)
+    peak = jnp.full((tables, stacked), NEG, jnp.float32)
+    for b in range(blocks):
+        own = table == meta[OWNER, b]
+        block_peak = get_heads(q_side, first + b * heads, heads)
+        peak = jnp.where(own, jnp.maximum(peak, block_peak), peak)
+    total = part = jnp.zeros((tables, stacked), jnp.float32)
+    for b in range(blocks):
+        own = table == meta[OWNER, b]
+        at = b * (features // LANES)
+        mass = jnp.concatenate(masses[at : at + features // LANES], axis=1)
+        mean = jnp.concatenate(means[at : at + features // LANES], axis=1)
+        block_peak = get_heads(q_side, first + b * heads, heads)
+        scaled = jnp.where(own, jnp.exp2(block_peak - peak) * mass, 0.0)
+        total = total + scaled
+        part = part + scaled * mean
+    here = total > 0.0
+    mass = jnp.where(here, total, 1.0)
+    tab_ref[0] = jnp.where(here, peak + jnp.log2(mass), NEG)
+    tab_ref[1] = part / mass
 
 
 def moved_weights(meta, held, pieces, q_side, state, features, tables):
@@ -325,7 +329,6 @@
         ],
         input_output_aliases={count + 2: 2},
         scratch_shapes=[
-            pltpu.VMEM((3, tables, stacked), jnp.float32),
             pltpu.VMEM((2, BLK, WIDE), jnp.float32),
             pltpu.VMEM((max(held, 1), TEST, features), jnp.bfloat16),
             pltpu.SemaphoreType.DMA((max(held, 1),)),
@@ -489,18 +492,19 @@
     load = lambda entries: load_rows(small, entries, train_rows, test_rows, key_rows, value_rows)
     if small:
         held = 1
-        near = [step(query_rows, s) for s in (1, 2, 3)]
-        near_grads = [step(cotangent, s) for s in (1, 2, 3)]
+        near = [step(query_rows, 1), step(query_rows, 2)]
+        near_grads = [step(cotangent, 1), step(cotangent, 2)]
+        near.append(step(near[1], 1))
+        near_grads.append(step(near_grads[1], 1))
         block_table, near[0] = after(block_table, near[0])
         meta, state = load(block_table)
-        own, _ = after(query_rows, meta)
-        near = [after(value, meta)[0] for value in near]
+        own, near[0], near[1], meta = lax.optimization_barrier((query_rows, near[0], near[1], meta))
         queries = [query_rows, pair(own)]
         for value in near:
             queries += [value, pair(value)]
         q_side, state = block_weights(meta, held, queries, state, features, tables)
-        *near_grads, q_side = lax.optimization_barrier((*near_grads, q_side))
-        grads = [cotangent, pair(cotangent)]
+        own, *near_grads, q_side = lax.optimization_barrier((cotangent, *near_grads, q_side))
+        grads = [cotangent, pair(own)]
         for value in near_grads:
             grads += [value, pair(value)]
     else:

time: 53.6 us -> 51.1 us (0.953)
  Pallas kernels: 18.9 us -> 15.7 us
  waiting for transfers between devices: 11.6 us -> 13.3 us
  starting transfers between devices: 21.4 us -> 20.3 us
    pallas_call x1, Pallas kernels: 5.78 us -> 4.06 us  [moved_weights(): pl.pallas_call(lambda *refs: moved_kernel(count, held, *refs), in_specs=[...]
    ppermute x12, waiting for transfers between devices: 8.12 us -> 9.79 us  [local(): lax.ppermute(value, 'rows', [(z, z ^ s) for z in range(4)])]
    pallas_call x1, Pallas kernels: 5.67 us -> 4.23 us  [block_weights(): pl.pallas_call(lambda *refs: weights_kernel(count, held, *refs), in_specs...]
    ppermute x12, starting transfers between devices: 19 us -> 18 us  [local(): lax.ppermute(value, 'rows', [(z, z ^ s) for z in range(4)])]
  transfers between devices with their start and end apart: 25 -> 25, of which waited for: 11 -> 13; matrix products, arithmetic and copies ran while one was open for 0% -> 0% of each run, Pallas kernels for 23% -> 22%
where the time goes in v7:
time: 51.1 us; the launch traced here: 50.9 us
  starting transfers between devices  20.3 us (40%)
  Pallas kernels  15.7 us (31%)
  waiting for transfers between devices  13.3 us (26%)
  between operations  0.79 us (2%)
  other arithmetic  0.74 us (1%)
    ppermute x12, starting transfers between devices, local(): lax.ppermute(value, 'rows', [(z, z ^ s) for z in range(4)])  18 us
    ppermute x12, waiting for transfers between devices, local(): lax.ppermute(value, 'rows', [(z, z ^ s) for z in range(4)])  9.79 us
    pallas_call x1, Pallas kernels, block_weights(): pl.pallas_call(lambda *refs: weights_kernel(count, held, *refs), in_specs...  4.23 us
    pallas_call x1, Pallas kernels, moved_weights(): pl.pallas_call(lambda *refs: moved_kernel(count, held, *refs), in_specs=[...  4.06 us
    ppermute x13, waiting for transfers between devices, local(): pair = lambda value: lax.ppermute(value, 'pair', PAIR)  3.49 us
    pallas_call x1, Pallas kernels, row_grads(): pl.pallas_call(row_grads_kernel, in_specs=[smem_spec()] + [vmem_spec()] *...  3.29 us
    ppermute x13, starting transfers between devices, local(): pair = lambda value: lax.ppermute(value, 'pair', PAIR)  2.34 us
    pallas_call x1, Pallas kernels, load_rows(): pl.pallas_call(lambda *refs: load_kernel(small, *refs), in_specs=[hbm_spe...  2.3 us
  transfers between devices with their start and end apart: 25, of which 13 were waited for; matrix products, arithmetic and copies ran while one was open for 0% of the time, Pallas kernels for 22%

profile of v7, /device:TPU:0, one launch (start us, length us, event | category | flops | bytes accessed | tf_op | source)
XLA Modules:
  0.0 50.9 jit_solution(6471235690664176280)
XLA Ops:
  0.6 0.0 copy-start
  0.6 0.0 copy-start.1
  0.7 3.1 %collective-permute-start = (bf16[128,256]{1,0:T(8,128)(2,1)}, bf16[128,256]{1,0:T(8,128)(2,1)S(1)}, u32[]{:S(2)}, u32[]{:S(2)}) collective-permute-start(bf16[128,256]{1,0:T(8,128)(2,1)} %refs_1_.4), channel_id=1, source_target_pairs={{0,4},{4,0},{8,12},{12,8},{1,5},{5,1},{9,13},{13,9},{2,6},{6,2},{1... | collective-permute-start | bytes 196616 | tf_op jit(solution)/shard_map/ppermute | solution.py:490
  3.7 2.6 %collective-permute-start.1 = (bf16[128,256]{1,0:T(8,128)(2,1)}, bf16[128,256]{1,0:T(8,128)(2,1)S(1)}, u32[]{:S(2)}, u32[]{:S(2)}) collective-permute-start(bf16[128,256]{1,0:T(8,128)(2,1)} %refs_1_.4), channel_id=1, source_target_pairs={{0,8},{4,12},{8,0},{12,4},{1,9},{5,13},{9,1},{13,5},{2,10},{6,14},... | collective-permute-start | bytes 196616 | tf_op jit(solution)/shard_map/ppermute | solution.py:490
  6.3 0.3 collective-permute-start.3
  6.7 0.0 collective-permute-done.refs_3_
  6.7 2.3 %load_rows.1 = (s32[6,8]{1,0:T(8,128)S(4)}, bf16[8,512,1536]{2,1,0:T(8,128)(2,1)S(1)}) custom-call(s32[64]{0:T(128)} %refs_0_, s32[8]{0:T(128)} %refs_1_.3, s32[8]{0:T(128)} %refs_2_.1, bf16[4096,256]{1,0:T(8,128)(2,1)} %refs_3_.1, bf16[4096,256]{1,0:T(8,128)(2,1)} %refs_4_.1), custom_call_target="tpu_custom_call" | custom-call | tf_op jit(solution)/shard_map/load_rows/pallas_call | solution.py:121
  9.0 1.7 %collective-permute-done.1.refs_5_ = bf16[128,256]{1,0:T(8,128)(2,1)S(1)} collective-permute-done((bf16[128,256]{1,0:T(8,128)(2,1)}, bf16[128,256]{1,0:T(8,128)(2,1)S(1)}, u32[]{:S(2)}, u32[]{:S(2)}) %collective-permute-start.1) | collective-permute-done | bytes 65568 | tf_op jit(solution)/shard_map/ppermute | solution.py:490
  10.7 1.0 %collective-permute-start.8 = (bf16[128,256]{1,0:T(8,128)(2,1)S(1)}, bf16[128,256]{1,0:T(8,128)(2,1)S(1)}, u32[]{:S(2)}, u32[]{:S(2)}) collective-permute-start(bf16[128,256]{1,0:T(8,128)(2,1)S(1)} %collective-permute-done.1.refs_5_), channel_id=1, source_target_pairs={{0,4},{4,0},{8,12},{12,8},{1,5},{5,1},{9,13},{13,9},{2,6},{6,2},{1... | collective-permute-start | bytes 196616 | tf_op jit(solution)/shard_map/ppermute | solution.py:490
  11.7 0.5 collective-permute-start.7
  12.2 0.0 collective-permute-start.5
  12.2 2.8 %collective-permute-done.8.refs_7_ = bf16[128,256]{1,0:T(8,128)(2,1)S(1)} collective-permute-done((bf16[128,256]{1,0:T(8,128)(2,1)S(1)}, bf16[128,256]{1,0:T(8,128)(2,1)S(1)}, u32[]{:S(2)}, u32[]{:S(2)}) %collective-permute-start.8) | collective-permute-done | bytes 65568 | tf_op jit(solution)/shard_map/ppermute | solution.py:490
  15.0 1.0 %collective-permute-start.2 = (bf16[128,256]{1,0:T(8,128)(2,1)S(1)}, bf16[128,256]{1,0:T(8,128)(2,1)S(1)}, u32[]{:S(2)}, u32[]{:S(2)}) collective-permute-start(bf16[128,256]{1,0:T(8,128)(2,1)S(1)} %copy-done.1), channel_id=1, source_target_pairs={{0,4},{4,0},{8,12},{12,8},{1,5},{5,1},{9,13},{13,9},{2,6},{6,2},{1... | collective-permute-start | bytes 196616 | tf_op jit(solution)/shard_map/ppermute | solution.py:490
  16.0 1.0 %collective-permute-start.4 = (bf16[128,256]{1,0:T(8,128)(2,1)S(1)}, bf16[128,256]{1,0:T(8,128)(2,1)S(1)}, u32[]{:S(2)}, u32[]{:S(2)}) collective-permute-start(bf16[128,256]{1,0:T(8,128)(2,1)S(1)} %collective-permute-done.3.refs_5_), channel_id=1, source_target_pairs={{0,4},{4,0},{8,12},{12,8},{1,5},{5,1},{9,13},{13,9},{2,6},{6,2},{1... | collective-permute-start | bytes 196616 | tf_op jit(solution)/shard_map/ppermute | solution.py:490
  17.1 0.0 collective-permute-done.5.refs_2_
  17.1 0.0 collective-permute-done.9.refs_8_
  17.1 4.2 %block_weights.1 = (f32[2080,128]{1,0:T(8,128)S(1)}, bf16[8,512,1536]{2,1,0:T(8,128)(2,1)S(1)}) custom-call(s32[6,8]{1,0:T(8,128)S(4)} %get-tuple-element.37.refs_0_.meta, bf16[128,256]{1,0:T(8,128)(2,1)} %refs_1_.4, bf16[128,256]{1,0:T(8,128)(2,1)S(1)} %collective-permute-done.5.refs_2_, ...), custom_call_target="tpu_custom_call", output_to_operand_aliasing={{1}: (9, {})} | custom-call | tf_op jit(solution)/shard_map/block_weights/pallas_call | solution.py:225
  21.3 0.0 collective-permute-done.4.refs_7_
  21.3 0.1 collective-permute-start.11
  21.4 0.5 collective-permute-start.12
  21.9 0.1 collective-permute-start.13
  22.0 0.4 collective-permute-start.10
  22.4 0.2 collective-permute-done.11.refs_4_
  22.7 0.2 collective-permute-done.12.refs_6_
  22.8 0.4 collective-permute-done.13.refs_8_
  23.2 0.2 collective-permute-done.10.refs_2_
  23.3 4.1 %moved_weights.1 = (f32[2112,128]{1,0:T(8,128)S(1)}, f32[2,8,512]{2,1,0:T(8,128)S(1)}, bf16[8,512,1536]{2,1,0:T(8,128)(2,1)S(1)}) custom-call(s32[6,8]{1,0:T(8,128)S(4)} %get-tuple-element.37.refs_0_.meta, bf16[128,256]{1,0:T(8,128)(2,1)} %refs_1_.5, bf16[128,256]{1,0:T(8,128)(2,1)S(1)} %collective-permute-done.10.refs_2_, ...), custom_call_target="tpu_custom_call", output_to_operand_aliasing={{2}: (10, {})} | custom-call | tf_op jit(solution)/shard_map/moved_weights/pallas_call | solution.py:321
  27.4 1.0 %collective-permute-start.15 = (f32[2,8,512]{2,1,0:T(8,128)S(1)}, f32[2,8,512]{2,1,0:T(8,128)S(1)}, u32[]{:S(2)}, u32[]{:S(2)}) collective-permute-start(f32[2,8,512]{2,1,0:T(8,128)S(1)} %get-tuple-element.49.refs_1_), channel_id=1, source_target_pairs={{0,4},{4,0},{8,12},{12,8},{1,5},{5,1},{9,13},{13,9},{2,6},{6,2},{1... | collective-permute-start | bytes 98312 | tf_op jit(solution)/shard_map/ppermute | solution.py:490
  28.5 3.3 %collective-permute-start.16 = (f32[2,8,512]{2,1,0:T(8,128)S(1)}, f32[2,8,512]{2,1,0:T(8,128)S(1)}, u32[]{:S(2)}, u32[]{:S(2)}) collective-permute-start(f32[2,8,512]{2,1,0:T(8,128)S(1)} %get-tuple-element.49.refs_1_), channel_id=1, source_target_pairs={{0,8},{4,12},{8,0},{12,4},{1,9},{5,13},{9,1},{13,5},{2,10},{6,14},... | collective-permute-start | bytes 98312 | tf_op jit(solution)/shard_map/ppermute | solution.py:490
  31.8 0.1 collective-permute-start.17
  31.9 1.3 %query_sums.1 = (f32[8,2,256,128]{3,2,1,0:T(8,128)S(1)}, bf16[8,512,1536]{2,1,0:T(8,128)(2,1)S(1)}) custom-call(bf16[8,512,1536]{2,1,0:T(8,128)(2,1)S(1)} %get-tuple-element.50.state), custom_call_target="tpu_custom_call", output_to_operand_aliasing={{1}: (0, {})} | custom-call | tf_op jit(solution)/shard_map/query_sums/pallas_call | solution.py:358
  33.2 1.1 %collective-permute-done.16.refs_5_ = f32[2,8,512]{2,1,0:T(8,128)S(1)} collective-permute-done((f32[2,8,512]{2,1,0:T(8,128)S(1)}, f32[2,8,512]{2,1,0:T(8,128)S(1)}, u32[]{:S(2)}, u32[]{:S(2)}) %collective-permute-start.16) | collective-permute-done | bytes 32800 | tf_op jit(solution)/shard_map/ppermute | solution.py:490
  34.3 3.2 %collective-permute-done.17.refs_7_ = f32[2,8,512]{2,1,0:T(8,128)S(1)} collective-permute-done((f32[2,8,512]{2,1,0:T(8,128)S(1)}, f32[2,8,512]{2,1,0:T(8,128)S(1)}, u32[]{:S(2)}, u32[]{:S(2)}) %collective-permute-start.17) | collective-permute-done | bytes 32800 | tf_op jit(solution)/shard_map/ppermute | solution.py:490
  37.5 0.5 collective-permute-start.19
  38.0 0.0 collective-permute-start.20
  38.0 0.7 %collective-permute-done.18.refs_4_ = f32[2,8,512]{2,1,0:T(8,128)S(1)} collective-permute-done((f32[2,8,512]{2,1,0:T(8,128)S(1)}, f32[2,8,512]{2,1,0:T(8,128)S(1)}, u32[]{:S(2)}, u32[]{:S(2)}) %collective-permute-start.18) | collective-permute-done | bytes 32800 | tf_op jit(solution)/shard_map/ppermute | solution.py:489
  38.7 0.2 collective-permute-done.19.refs_6_
  38.9 0.3 collective-permute-done.20.refs_8_
  39.2 0.6 %query_grads.1 = (f32[8,512]{1,0:T(8,128)S(1)}, f32[8,512]{1,0:T(8,128)S(1)}, f32[4,128,256]{2,1,0:T(8,128)S(1)}, bf16[4,128,256]{2,1,0:T(8,128)(2,1)S(1)}) custom-call(s32[6,8]{1,0:T(8,128)S(4)} %get-tuple-element.37.refs_0_.meta, f32[2,8,512]{2,1,0:T(8,128)S(1)} %get-tuple-element.49.refs_1_, f32[2,8,512]{2,1,0:T(8,128)S(1)} %collective-permute-done.14.refs_2_, ...), custom_call_target="tpu_custom_call" | custom-call | tf_op jit(solution)/shard_map/query_grads/pallas_call | solution.py:417
  39.8 0.2 collective-permute-start.21
  40.0 1.4 %collective-permute-done.21 = bf16[4,128,256]{2,1,0:T(8,128)(2,1)S(1)} collective-permute-done((bf16[4,128,256]{2,1,0:T(8,128)(2,1)S(1)}, bf16[4,128,256]{2,1,0:T(8,128)(2,1)S(1)}, u32[]{:S(2)}, u32[]{:S(2)}) %collective-permute-start.21) | collective-permute-done | bytes 262176 | tf_op jit(solution)/shard_map/ppermute | solution.py:489
  41.4 0.1 fusion.4
  41.5 0.1 collective-permute-start.22
  41.6 1.0 %collective-permute-start.23 = (bf16[128,256]{1,0:T(8,128)(2,1)S(1)}, bf16[128,256]{1,0:T(8,128)(2,1)S(1)}, u32[]{:S(2)}, u32[]{:S(2)}) collective-permute-start(bf16[128,256]{1,0:T(8,128)(2,1)S(1)} %get-tuple-element.69), channel_id=1, source_target_pairs={{0,8},{4,12},{8,0},{12,4},{1,9},{5,13},{9,1},{13,5},{2,10},{6,14},... | collective-permute-start | bytes 196616 | tf_op jit(solution)/shard_map/ppermute | solution.py:490
  42.5 3.4 %collective-permute-start.24 = (bf16[128,256]{1,0:T(8,128)(2,1)S(1)}, bf16[128,256]{1,0:T(8,128)(2,1)S(1)}, u32[]{:S(2)}, u32[]{:S(2)}) collective-permute-start(bf16[128,256]{1,0:T(8,128)(2,1)S(1)} %get-tuple-element.68), channel_id=1, source_target_pairs={{0,12},{4,8},{8,4},{12,0},{1,13},{5,9},{9,5},{13,1},{2,14},{6,10},... | collective-permute-start | bytes 196616 | tf_op jit(solution)/shard_map/ppermute | solution.py:490
  46.0 3.3 %row_grads.1 = (bf16[4096,256]{1,0:T(8,128)(2,1)}, bf16[4096,256]{1,0:T(8,128)(2,1)}) custom-call(s32[6,8]{1,0:T(8,128)S(4)} %get-tuple-element.37.refs_0_.meta, f32[8,512]{1,0:T(8,128)S(1)} %get-tuple-element.60.c_ref, f32[8,512]{1,0:T(8,128)S(1)} %get-tuple-element.61.d_ref, f32[2080,128]{1,0:T(8,128)S(1)} %get-tuple-element.47.refs_9_.q_side, ...), custom_call_target="tpu_custom_call" | custom-call | tf_op jit(solution)/shard_map/row_grads/pallas_call | solution.py:470
  49.3 1.0 %collective-permute-done.23 = bf16[128,256]{1,0:T(8,128)(2,1)S(1)} collective-permute-done((bf16[128,256]{1,0:T(8,128)(2,1)S(1)}, bf16[128,256]{1,0:T(8,128)(2,1)S(1)}, u32[]{:S(2)}, u32[]{:S(2)}) %collective-permute-start.23) | collective-permute-done | bytes 65568 | tf_op jit(solution)/shard_map/ppermute | solution.py:490
  50.2 0.7 %fusion.3 = bf16[128,256]{1,0:T(8,128)(2,1)} fusion(f32[4,128,256]{2,1,0:T(8,128)S(1)} %get-tuple-element.66, bf16[128,256]{1,0:T(8,128)(2,1)S(1)} %collective-permute-done.24, bf16[128,256]{1,0:T(8,128)(2,1)S(1)} %collective-permute-done.23, bf16[128,256]{1,0:T(8,128)(2,1)S(1)} %collective-permute-done.22), kind=kLoop, calls=%fused_computation.5 | loop fusion | flops 229376 | bytes 393216 | tf_op jit(solution)/shard_map/convert_element_type | solution.py:548
  (15 shorter events, 0.1 us)
Async XLA Ops:
  0.6 11.6 %copy-start = (bf16[128,256]{1,0:T(8,128)(2,1)S(1)}, bf16[128,256]{1,0:T(8,128)(2,1)}, u32[]{:S(2)}) copy-start(bf16[128,256]{1,0:T(8,128)(2,1)} %refs_1_.4) | copy-start | bytes 196612
  0.6 14.3 %copy-start.1 = (bf16[128,256]{1,0:T(8,128)(2,1)S(1)}, bf16[128,256]{1,0:T(8,128)(2,1)}, u32[]{:S(2)}) copy-start(bf16[128,256]{1,0:T(8,128)(2,1)} %refs_1_.5) | copy-start | bytes 196612
  0.7 6.0 %collective-permute-start = (bf16[128,256]{1,0:T(8,128)(2,1)}, bf16[128,256]{1,0:T(8,128)(2,1)S(1)}, u32[]{:S(2)}, u32[]{:S(2)}) collective-permute-start(bf16[128,256]{1,0:T(8,128)(2,1)} %refs_1_.4), channel_id=1, source_target_pairs={{0,4},{4,0},{8,12},{12,8},{1,5},{5,1},{9,13},{13,9},{2,6},{6,2},{1... | collective-permute-start | bytes 196616 | tf_op jit(solution)/shard_map/ppermute | solution.py:490
  3.7 7.0 %collective-permute-start.1 = (bf16[128,256]{1,0:T(8,128)(2,1)}, bf16[128,256]{1,0:T(8,128)(2,1)S(1)}, u32[]{:S(2)}, u32[]{:S(2)}) collective-permute-start(bf16[128,256]{1,0:T(8,128)(2,1)} %refs_1_.4), channel_id=1, source_target_pairs={{0,8},{4,12},{8,0},{12,4},{1,9},{5,13},{9,1},{13,5},{2,10},{6,14},... | collective-permute-start | bytes 196616 | tf_op jit(solution)/shard_map/ppermute | solution.py:490
  6.3 8.6 %collective-permute-start.3 = (bf16[128,256]{1,0:T(8,128)(2,1)}, bf16[128,256]{1,0:T(8,128)(2,1)S(1)}, u32[]{:S(2)}, u32[]{:S(2)}) collective-permute-start(bf16[128,256]{1,0:T(8,128)(2,1)} %refs_1_.5), channel_id=1, source_target_pairs={{0,8},{4,12},{8,0},{12,4},{1,9},{5,13},{9,1},{13,5},{2,10},{6,14},... | collective-permute-start | bytes 196616 | tf_op jit(solution)/shard_map/ppermute | solution.py:490
  10.7 4.3 %collective-permute-start.8 = (bf16[128,256]{1,0:T(8,128)(2,1)S(1)}, bf16[128,256]{1,0:T(8,128)(2,1)S(1)}, u32[]{:S(2)}, u32[]{:S(2)}) collective-permute-start(bf16[128,256]{1,0:T(8,128)(2,1)S(1)} %collective-permute-done.1.refs_5_), channel_id=1, source_target_pairs={{0,4},{4,0},{8,12},{12,8},{1,5},{5,1},{9,13},{13,9},{2,6},{6,2},{1... | collective-permute-start | bytes 196616 | tf_op jit(solution)/shard_map/ppermute | solution.py:490
  11.7 4.3 %collective-permute-start.6 = (bf16[128,256]{1,0:T(8,128)(2,1)S(1)}, bf16[128,256]{1,0:T(8,128)(2,1)S(1)}, u32[]{:S(2)}, u32[]{:S(2)}) collective-permute-start(bf16[128,256]{1,0:T(8,128)(2,1)S(1)} %collective-permute-done.refs_3_), channel_id=1, source_target_pairs={{0,1},{1,0},{2,3},{3,2},{4,5},{5,4},{6,7},{7,6},{8,9},{9,8},{10,11... | collective-permute-start | bytes 196616 | tf_op jit(solution)/shard_map/ppermute | solution.py:489
  11.7 5.4 %collective-permute-start.7 = (bf16[128,256]{1,0:T(8,128)(2,1)S(1)}, bf16[128,256]{1,0:T(8,128)(2,1)S(1)}, u32[]{:S(2)}, u32[]{:S(2)}) collective-permute-start(bf16[128,256]{1,0:T(8,128)(2,1)S(1)} %collective-permute-done.1.refs_5_), channel_id=1, source_target_pairs={{0,1},{1,0},{2,3},{3,2},{4,5},{5,4},{6,7},{7,6},{8,9},{9,8},{10,11... | collective-permute-start | bytes 196616 | tf_op jit(solution)/shard_map/ppermute | solution.py:489
  12.2 4.9 %collective-permute-start.5 = (bf16[128,256]{1,0:T(8,128)(2,1)S(1)}, bf16[128,256]{1,0:T(8,128)(2,1)S(1)}, u32[]{:S(2)}, u32[]{:S(2)}) collective-permute-start(bf16[128,256]{1,0:T(8,128)(2,1)S(1)} %copy-done), channel_id=1, source_target_pairs={{0,1},{1,0},{2,3},{3,2},{4,5},{5,4},{6,7},{7,6},{8,9},{9,8},{10,11... | collective-permute-start | bytes 196616 | tf_op jit(solution)/shard_map/ppermute | solution.py:489
  15.0 2.1 %collective-permute-start.9 = (bf16[128,256]{1,0:T(8,128)(2,1)S(1)}, bf16[128,256]{1,0:T(8,128)(2,1)S(1)}, u32[]{:S(2)}, u32[]{:S(2)}) collective-permute-start(bf16[128,256]{1,0:T(8,128)(2,1)S(1)} %collective-permute-done.8.refs_7_), channel_id=1, source_target_pairs={{0,1},{1,0},{2,3},{3,2},{4,5},{5,4},{6,7},{7,6},{8,9},{9,8},{10,11... | collective-permute-start | bytes 196616 | tf_op jit(solution)/shard_map/ppermute | solution.py:489
  15.0 6.4 %collective-permute-start.2 = (bf16[128,256]{1,0:T(8,128)(2,1)S(1)}, bf16[128,256]{1,0:T(8,128)(2,1)S(1)}, u32[]{:S(2)}, u32[]{:S(2)}) collective-permute-start(bf16[128,256]{1,0:T(8,128)(2,1)S(1)} %copy-done.1), channel_id=1, source_target_pairs={{0,4},{4,0},{8,12},{12,8},{1,5},{5,1},{9,13},{13,9},{2,6},{6,2},{1... | collective-permute-start | bytes 196616 | tf_op jit(solution)/shard_map/ppermute | solution.py:490
  16.0 5.3 %collective-permute-start.4 = (bf16[128,256]{1,0:T(8,128)(2,1)S(1)}, bf16[128,256]{1,0:T(8,128)(2,1)S(1)}, u32[]{:S(2)}, u32[]{:S(2)}) collective-permute-start(bf16[128,256]{1,0:T(8,128)(2,1)S(1)} %collective-permute-done.3.refs_5_), channel_id=1, source_target_pairs={{0,4},{4,0},{8,12},{12,8},{1,5},{5,1},{9,13},{13,9},{2,6},{6,2},{1... | collective-permute-start | bytes 196616 | tf_op jit(solution)/shard_map/ppermute | solution.py:490
  21.3 1.3 %collective-permute-start.11 = (bf16[128,256]{1,0:T(8,128)(2,1)S(1)}, bf16[128,256]{1,0:T(8,128)(2,1)S(1)}, u32[]{:S(2)}, u32[]{:S(2)}) collective-permute-start(bf16[128,256]{1,0:T(8,128)(2,1)S(1)} %collective-permute-done.2.refs_3_), channel_id=1, source_target_pairs={{0,1},{1,0},{2,3},{3,2},{4,5},{5,4},{6,7},{7,6},{8,9},{9,8},{10,11... | collective-permute-start | bytes 196616 | tf_op jit(solution)/shard_map/ppermute | solution.py:489
  21.4 1.4 %collective-permute-start.12 = (bf16[128,256]{1,0:T(8,128)(2,1)S(1)}, bf16[128,256]{1,0:T(8,128)(2,1)S(1)}, u32[]{:S(2)}, u32[]{:S(2)}) collective-permute-start(bf16[128,256]{1,0:T(8,128)(2,1)S(1)} %collective-permute-done.3.refs_5_), channel_id=1, source_target_pairs={{0,1},{1,0},{2,3},{3,2},{4,5},{5,4},{6,7},{7,6},{8,9},{9,8},{10,11... | collective-permute-start | bytes 196616 | tf_op jit(solution)/shard_map/ppermute | solution.py:489
  21.9 1.3 %collective-permute-start.13 = (bf16[128,256]{1,0:T(8,128)(2,1)S(1)}, bf16[128,256]{1,0:T(8,128)(2,1)S(1)}, u32[]{:S(2)}, u32[]{:S(2)}) collective-permute-start(bf16[128,256]{1,0:T(8,128)(2,1)S(1)} %collective-permute-done.4.refs_7_), channel_id=1, source_target_pairs={{0,1},{1,0},{2,3},{3,2},{4,5},{5,4},{6,7},{7,6},{8,9},{9,8},{10,11... | collective-permute-start | bytes 196616 | tf_op jit(solution)/shard_map/ppermute | solution.py:489
  22.0 1.3 %collective-permute-start.10 = (bf16[128,256]{1,0:T(8,128)(2,1)S(1)}, bf16[128,256]{1,0:T(8,128)(2,1)S(1)}, u32[]{:S(2)}, u32[]{:S(2)}) collective-permute-start(bf16[128,256]{1,0:T(8,128)(2,1)S(1)} %copy-done.1), channel_id=1, source_target_pairs={{0,1},{1,0},{2,3},{3,2},{4,5},{5,4},{6,7},{7,6},{8,9},{9,8},{10,11... | collective-permute-start | bytes 196616 | tf_op jit(solution)/shard_map/ppermute | solution.py:489
  27.4 5.7 %collective-permute-start.15 = (f32[2,8,512]{2,1,0:T(8,128)S(1)}, f32[2,8,512]{2,1,0:T(8,128)S(1)}, u32[]{:S(2)}, u32[]{:S(2)}) collective-permute-start(f32[2,8,512]{2,1,0:T(8,128)S(1)} %get-tuple-element.49.refs_1_), channel_id=1, source_target_pairs={{0,4},{4,0},{8,12},{12,8},{1,5},{5,1},{9,13},{13,9},{2,6},{6,2},{1... | collective-permute-start | bytes 98312 | tf_op jit(solution)/shard_map/ppermute | solution.py:490
  28.5 5.8 %collective-permute-start.16 = (f32[2,8,512]{2,1,0:T(8,128)S(1)}, f32[2,8,512]{2,1,0:T(8,128)S(1)}, u32[]{:S(2)}, u32[]{:S(2)}) collective-permute-start(f32[2,8,512]{2,1,0:T(8,128)S(1)} %get-tuple-element.49.refs_1_), channel_id=1, source_target_pairs={{0,8},{4,12},{8,0},{12,4},{1,9},{5,13},{9,1},{13,5},{2,10},{6,14},... | collective-permute-start | bytes 98312 | tf_op jit(solution)/shard_map/ppermute | solution.py:490
  31.8 5.7 %collective-permute-start.17 = (f32[2,8,512]{2,1,0:T(8,128)S(1)}, f32[2,8,512]{2,1,0:T(8,128)S(1)}, u32[]{:S(2)}, u32[]{:S(2)}) collective-permute-start(f32[2,8,512]{2,1,0:T(8,128)S(1)} %get-tuple-element.49.refs_1_), channel_id=1, source_target_pairs={{0,12},{4,8},{8,4},{12,0},{1,13},{5,9},{9,5},{13,1},{2,14},{6,10},... | collective-permute-start | bytes 98312 | tf_op jit(solution)/shard_map/ppermute | solution.py:490
  31.9 6.2 %collective-permute-start.14 = (f32[2,8,512]{2,1,0:T(8,128)S(1)}, f32[2,8,512]{2,1,0:T(8,128)S(1)}, u32[]{:S(2)}, u32[]{:S(2)}) collective-permute-start(f32[2,8,512]{2,1,0:T(8,128)S(1)} %get-tuple-element.49.refs_1_), channel_id=1, source_target_pairs={{0,1},{1,0},{2,3},{3,2},{4,5},{5,4},{6,7},{7,6},{8,9},{9,8},{10,11... | collective-permute-start | bytes 98312 | tf_op jit(solution)/shard_map/ppermute | solution.py:489
  37.5 1.2 %collective-permute-start.18 = (f32[2,8,512]{2,1,0:T(8,128)S(1)}, f32[2,8,512]{2,1,0:T(8,128)S(1)}, u32[]{:S(2)}, u32[]{:S(2)}) collective-permute-start(f32[2,8,512]{2,1,0:T(8,128)S(1)} %collective-permute-done.15.refs_3_), channel_id=1, source_target_pairs={{0,1},{1,0},{2,3},{3,2},{4,5},{5,4},{6,7},{7,6},{8,9},{9,8},{10,11... | collective-permute-start | bytes 98312 | tf_op jit(solution)/shard_map/ppermute | solution.py:489
  37.5 1.4 %collective-permute-start.19 = (f32[2,8,512]{2,1,0:T(8,128)S(1)}, f32[2,8,512]{2,1,0:T(8,128)S(1)}, u32[]{:S(2)}, u32[]{:S(2)}) collective-permute-start(f32[2,8,512]{2,1,0:T(8,128)S(1)} %collective-permute-done.16.refs_5_), channel_id=1, source_target_pairs={{0,1},{1,0},{2,3},{3,2},{4,5},{5,4},{6,7},{7,6},{8,9},{9,8},{10,11... | collective-permute-start | bytes 98312 | tf_op jit(solution)/shard_map/ppermute | solution.py:489
  38.0 1.2 %collective-permute-start.20 = (f32[2,8,512]{2,1,0:T(8,128)S(1)}, f32[2,8,512]{2,1,0:T(8,128)S(1)}, u32[]{:S(2)}, u32[]{:S(2)}) collective-permute-start(f32[2,8,512]{2,1,0:T(8,128)S(1)} %collective-permute-done.17.refs_7_), channel_id=1, source_target_pairs={{0,1},{1,0},{2,3},{3,2},{4,5},{5,4},{6,7},{7,6},{8,9},{9,8},{10,11... | collective-permute-start | bytes 98312 | tf_op jit(solution)/shard_map/ppermute | solution.py:489
  39.8 1.6 %collective-permute-start.21 = (bf16[4,128,256]{2,1,0:T(8,128)(2,1)S(1)}, bf16[4,128,256]{2,1,0:T(8,128)(2,1)S(1)}, u32[]{:S(2)}, u32[]{:S(2)}) collective-permute-start(bf16[4,128,256]{2,1,0:T(8,128)(2,1)S(1)} %get-tuple-element.58), channel_id=1, source_target_pairs={{0,1},{1,0},{2,3},{3,2},{4,5},{5,4},{6,7},{7,6},{8,9},{9,8},{10,11... | collective-permute-start | bytes 786440 | tf_op jit(solution)/shard_map/ppermute | solution.py:489
  41.5 7.8 %collective-permute-start.22 = (bf16[128,256]{1,0:T(8,128)(2,1)S(1)}, bf16[128,256]{1,0:T(8,128)(2,1)S(1)}, u32[]{:S(2)}, u32[]{:S(2)}) collective-permute-start(bf16[128,256]{1,0:T(8,128)(2,1)S(1)} %get-tuple-element.67), channel_id=1, source_target_pairs={{0,4},{4,0},{8,12},{12,8},{1,5},{5,1},{9,13},{13,9},{2,6},{6,2},{1... | collective-permute-start | bytes 196616 | tf_op jit(solution)/shard_map/ppermute | solution.py:490
  41.6 8.6 %collective-permute-start.23 = (bf16[128,256]{1,0:T(8,128)(2,1)S(1)}, bf16[128,256]{1,0:T(8,128)(2,1)S(1)}, u32[]{:S(2)}, u32[]{:S(2)}) collective-permute-start(bf16[128,256]{1,0:T(8,128)(2,1)S(1)} %get-tuple-element.69), channel_id=1, source_target_pairs={{0,8},{4,12},{8,0},{12,4},{1,9},{5,13},{9,1},{13,5},{2,10},{6,14},... | collective-permute-start | bytes 196616 | tf_op jit(solution)/shard_map/ppermute | solution.py:490
  42.5 7.7 %collective-permute-start.24 = (bf16[128,256]{1,0:T(8,128)(2,1)S(1)}, bf16[128,256]{1,0:T(8,128)(2,1)S(1)}, u32[]{:S(2)}, u32[]{:S(2)}) collective-permute-start(bf16[128,256]{1,0:T(8,128)(2,1)S(1)} %get-tuple-element.68), channel_id=1, source_target_pairs={{0,12},{4,8},{8,4},{12,0},{1,13},{5,9},{9,5},{13,1},{2,14},{6,10},... | collective-permute-start | bytes 196616 | tf_op jit(solution)/shard_map/ppermute | solution.py:490

commit v8 on v7

--- a/solution.py
+++ b/solution.py
@@ -58,28 +58,16 @@
     return pltpu.with_memory_space_constraint(value, pltpu.HBM)
 
 
-def load_kernel(small, table_hbm, train_hbm, test_hbm, key_hbm, value_hbm, meta, state, *scratch):
-    block_table, train_rows, test_rows, count, sem, small_sem = scratch
+def index_kernel(small, blocks, table_hbm, train_hbm, test_hbm, query_hbm, meta, query_ref, *scratch):
+    block_table, train_rows, test_rows, count, small_sem = scratch
     entries = every_copy(
         [
             pltpu.make_async_copy(table_hbm, block_table, small_sem.at[0]),
             pltpu.make_async_copy(train_hbm, train_rows, small_sem.at[1]),
             pltpu.make_async_copy(test_hbm, test_rows, small_sem.at[2]),
+            pltpu.make_async_copy(query_hbm, query_ref, small_sem.at[3]),
         ]
     )
-    blocks = state.shape[0]
-    features = key_hbm.shape[1]
-    stacked = features // HD * TEST
-    loads = []
-    for b in range(blocks):
-        for n, source in enumerate((key_hbm, value_hbm)):
-            lanes = pl.ds(2 * stacked + n * features, features)
-            loads.append(
-                pltpu.make_async_copy(
-                    source.at[pl.ds(b * BLK, BLK)], state.at[b, :, lanes], sem.at[n, b]
-                )
-            )
-    every_copy(loads)
     chip = lax.axis_index("rows").astype(jnp.int32)
     core = lax.axis_index("pair").astype(jnp.int32)
     first = lax.axis_index(RP).astype(jnp.int32) * blocks
@@ -109,49 +97,35 @@
         meta[OWNER, b] = table
         meta[LIVE, b] = jnp.minimum(train_rows[table] - count[table] * BLK, BLK)
         count[table] = count[table] + 1
-    for copy in loads:
-        copy.wait()
-
-
-def load_rows(small, block_table, train_rows, test_rows, key_rows, value_rows):
+
+
+def index_table(small, blocks, block_table, train_rows, test_rows, query_rows):
     tables = train_rows.shape[0]
-    features = key_rows.shape[1]
-    blocks = key_rows.shape[0] // BLK
-    stacked = features // HD * TEST
     return pl.pallas_call(
-        lambda *refs: load_kernel(small, *refs),
-        in_specs=[hbm_spec()] * 5,
+        lambda *refs: index_kernel(small, blocks, *refs),
+        in_specs=[hbm_spec()] * 4,
         out_specs=[smem_spec(), vmem_spec()],
         out_shape=[
             pltpu.SMEM((6, max(blocks, tables)), jnp.int32),
-            pltpu.VMEM((blocks, BLK, 2 * stacked + 2 * features), jnp.bfloat16),
+            pltpu.VMEM(query_rows.shape, query_rows.dtype),
         ],
         scratch_shapes=[
             pltpu.SMEM(block_table.shape, jnp.int32),
             pltpu.SMEM((tables,), jnp.int32),
             pltpu.SMEM((tables,), jnp.int32),
             pltpu.SMEM((tables,), jnp.int32),
-            pltpu.SemaphoreType.DMA((2, blocks)),
-            pltpu.SemaphoreType.DMA((3,)),
-        ],
-        compiler_params=params(4),
-        name="load_rows",
-    )(*map(in_hbm, (block_table, train_rows, test_rows, key_rows, value_rows)))
-
-
-def turn_pieces(pieces, held, held_s, sem, store):
-    early = every_copy(
-        [pltpu.make_async_copy(pieces[n], held_s.at[n], sem.at[n]) for n in range(held)]
-    )
-    at_slot = held
-    for piece in pieces[held:]:
+            pltpu.SemaphoreType.DMA((4,)),
+        ],
+        name="index_table",
+    )(*map(in_hbm, (block_table, train_rows, test_rows, query_rows)))
+
+
+def turn_pieces(pieces, store):
+    at_slot = 0
+    for piece in pieces:
         for m in range(piece.shape[0] // TEST):
             store(at_slot, piece[m * TEST : (m + 1) * TEST, :].T)
             at_slot += 1
-    for copy in early:
-        copy.wait()
-    for n in range(held):
-        store(n, held_s[n].T)
 
 
 def fold(values, op):
@@ -177,22 +151,38 @@
     return [(b, p) for b in range(blocks) for p in range(features // LANES)]
 
 
-def weights_kernel(count, held, meta, *refs):
+def weights_kernel(count, meta, *refs):
     pieces = refs[:count]
-    state, side, state_out, scores_s, held_s, sem = refs[count:]
-    _, features = held_s.shape[1:]
-    stacked = features // HD * TEST
-    first_peak = side.shape[0] - state.shape[0] * features // HD
-    units = units_of(state.shape[0], features)
+    key_hbm, value_hbm, side, state, scores_s, sem = refs[count:]
+    blocks = state.shape[0]
+    features = key_hbm.shape[1]
+    stacked = features // HD * TEST
+    first_peak = side.shape[0] - blocks * features // HD
+    units = units_of(blocks, features)
+    loads = []
+    for n, source in enumerate((key_hbm, value_hbm)):
+        lanes = pl.ds(2 * stacked + n * features, features)
+        loads.append(
+            every_copy(
+                [
+                    pltpu.make_async_copy(
+                        source.at[pl.ds(b * BLK, BLK)], state.at[b, :, lanes], sem.at[n, b]
+                    )
+                    for b in range(blocks)
+                ]
+            )
+        )
 
     def store(at_slot, turned):
         side[at_slot * features : (at_slot + 1) * features, :] = turned.astype(jnp.float32)
 
-    turn_pieces(pieces, held, held_s, sem, store)
+    turn_pieces(pieces, store)
     peaks = [None] * len(units)
     for t in range(len(units) + 1):
         if t < len(units):
             b, p = units[t]
+            if p == 0:
+                loads[0][b].wait()
             live = meta[LIVE, b]
             queries = two_heads(side[rows_of(meta, b, p, features), :]).astype(jnp.bfloat16)
             peak = jnp.full((8, WIDE), NEG, jnp.float32)
@@ -201,9 +191,7 @@
             if t > 0:
                 last_b, last_p = units[t - 1]
                 weights = jnp.exp2(scores_s[(t - 1) % 2, rows, :] * LOG2_SCALE - peaks[t - 1])
-                state_out[last_b, rows, last_p * WIDE : (last_p + 1) * WIDE] = weights.astype(
-                    jnp.bfloat16
-                )
+                state[last_b, rows, last_p * WIDE : (last_p + 1) * WIDE] = weights.astype(jnp.bfloat16)
             if t < len(units):
                 keys = state[b, rows, 2 * stacked + p * LANES : 2 * stacked + (p + 1) * LANES]
                 scores = jnp.dot(keys, queries, preferred_element_type=jnp.float32)
@@ -215,38 +203,36 @@
             peaks[t] = jnp.max(peak, axis=0, keepdims=True) * LOG2_SCALE
     for (b, p), peak in zip(units, peaks):
         put_heads(side, first_peak, b, p, features, peak)
-
-
-def block_weights(meta, held, pieces, state, features, tables):
-    blocks = state.shape[0]
-    count = len(pieces)
-    pieces = [in_hbm(piece) if n < held else piece for n, piece in enumerate(pieces)]
-    specs = [hbm_spec() if n < held else vmem_spec() for n in range(count)]
+    for copy in loads[1]:
+        copy.wait()
+
+
+def block_weights(meta, pieces, key_rows, value_rows, tables):
+    features = key_rows.shape[1]
+    blocks = key_rows.shape[0] // BLK
+    stacked = features // HD * TEST
     return pl.pallas_call(
-        lambda *refs: weights_kernel(count, held, *refs),
-        in_specs=[smem_spec()] + specs + [vmem_spec()],
+        lambda *refs: weights_kernel(len(pieces), *refs),
+        in_specs=[smem_spec()] + [vmem_spec()] * len(pieces) + [hbm_spec()] * 2,
         out_specs=[vmem_spec()] * 2,
         out_shape=[
             pltpu.VMEM((tables * features + blocks * features // HD, TEST), jnp.float32),
-            pltpu.VMEM(state.shape, jnp.bfloat16),
-        ],
-        input_output_aliases={count + 1: 1},
+            pltpu.VMEM((blocks, BLK, 2 * stacked + 2 * features), jnp.bfloat16),
+        ],
         scratch_shapes=[
             pltpu.VMEM((2, BLK, WIDE), jnp.float32),
-            pltpu.VMEM((max(held, 1), TEST, features), jnp.bfloat16),
-            pltpu.SemaphoreType.DMA((max(held, 1),)),
+            pltpu.SemaphoreType.DMA((2, blocks)),
         ],
         compiler_params=params(10),
         name="block_weights",
-    )(meta, *pieces, state)
-
-
-def moved_kernel(count, held, meta, *refs):
+    )(meta, *pieces, in_hbm(key_rows), in_hbm(value_rows))
+
+
+def moved_kernel(count, features, meta, *refs):
     pieces = refs[:count]
     q_side, state, side, tab_ref, state_out = refs[count : count + 5]
-    dprobs_s, held_s, sem = refs[count + 5 :]
+    dprobs_s = refs[count + 5]
     tables = tab_ref.shape[1]
-    _, features = held_s.shape[1:]
     stacked = features // HD * TEST
     blocks = state.shape[0]
     heads = features // HD
@@ -259,7 +245,7 @@
         turned = jnp.where(live, turned, jnp.zeros_like(turned)).astype(jnp.float32)
         side[at_slot * features : (at_slot + 1) * features, :] = turned
 
-    turn_pieces(pieces, held, held_s, sem, store)
+    turn_pieces(pieces, store)
     means, masses = [None] * len(units), [None] * len(units)
     zero = jnp.zeros((8, WIDE), jnp.float32)
     for t in range(len(units) + 1):
@@ -312,15 +298,13 @@
     tab_ref[1] = part / mass
 
 
-def moved_weights(meta, held, pieces, q_side, state, features, tables):
+def moved_weights(meta, pieces, q_side, state, features, tables):
     blocks = state.shape[0]
     stacked = features // HD * TEST
     count = len(pieces)
-    pieces = [in_hbm(piece) if n < held else piece for n, piece in enumerate(pieces)]
-    specs = [hbm_spec() if n < held else vmem_spec() for n in range(count)]
     return pl.pallas_call(
-        lambda *refs: moved_kernel(count, held, *refs),
-        in_specs=[smem_spec()] + specs + [vmem_spec()] * 2,
+        lambda *refs: moved_kernel(count, features, *refs),
+        in_specs=[smem_spec()] + [vmem_spec()] * (count + 2),
         out_specs=[vmem_spec()] * 3,
         out_shape=[
             pltpu.VMEM((tables * features + 2 * blocks * features // HD, TEST), jnp.float32),
@@ -328,11 +312,7 @@
             pltpu.VMEM(state.shape, jnp.bfloat16),
         ],
         input_output_aliases={count + 2: 2},
-        scratch_shapes=[
-            pltpu.VMEM((2, BLK, WIDE), jnp.float32),
-            pltpu.VMEM((max(held, 1), TEST, features), jnp.bfloat16),
-            pltpu.SemaphoreType.DMA((max(held, 1),)),
-        ],
+        scratch_shapes=[pltpu.VMEM((2, BLK, WIDE), jnp.float32)],
         compiler_params=params(10),
         name="moved_weights",
     )(meta, *pieces, q_side, state)
@@ -489,31 +469,28 @@
     pair = lambda value: lax.ppermute(value, "pair", PAIR)
     step = lambda value, s: lax.ppermute(value, "rows", [(z, z ^ s) for z in range(4)])
     after = lambda value, other: lax.optimization_barrier((value, other))
-    load = lambda entries: load_rows(small, entries, train_rows, test_rows, key_rows, value_rows)
+    index = lambda entries: index_table(small, blocks, entries, train_rows, test_rows, query_rows)
     if small:
-        held = 1
-        near = [step(query_rows, 1), step(query_rows, 2)]
+        near = [step(query_rows, s) for s in (1, 2, 3)]
         near_grads = [step(cotangent, 1), step(cotangent, 2)]
-        near.append(step(near[1], 1))
         near_grads.append(step(near_grads[1], 1))
         block_table, near[0] = after(block_table, near[0])
-        meta, state = load(block_table)
-        own, near[0], near[1], meta = lax.optimization_barrier((query_rows, near[0], near[1], meta))
-        queries = [query_rows, pair(own)]
+        meta, own = index(block_table)
+        near[0], meta = after(near[0], meta)
+        queries = [own, pair(own)]
         for value in near:
             queries += [value, pair(value)]
-        q_side, state = block_weights(meta, held, queries, state, features, tables)
+        q_side, state = block_weights(meta, queries, key_rows, value_rows, tables)
         own, *near_grads, q_side = lax.optimization_barrier((cotangent, *near_grads, q_side))
-        grads = [cotangent, pair(own)]
+        grads = [own, pair(own)]
         for value in near_grads:
             grads += [value, pair(value)]
     else:
-        held = 0
-        meta, state = load(block_table)
+        meta, _ = index(block_table)
         queries = [lax.all_gather(query_rows, RP, axis=0, tiled=True)]
-        q_side, state = block_weights(meta, held, queries, state, features, tables)
+        q_side, state = block_weights(meta, queries, key_rows, value_rows, tables)
         grads = [lax.all_gather(cotangent, RP, axis=0, tiled=True)]
-    g_side, tab, state = moved_weights(meta, held, grads, q_side, state, features, tables)
+    g_side, tab, state = moved_weights(meta, grads, q_side, state, features, tables)
     if small:
         near = [step(tab, s) for s in (1, 2, 3)]
         ab, state = query_sums(features, state)

time: 51.1 us -> 49.9 us (0.977)
  Pallas kernels: 15.7 us -> 14.1 us
  starting transfers between devices: 20.3 us -> 21.4 us
  waiting for transfers between devices: 13.3 us -> 12.7 us
    pallas_call x3, Pallas kernels: 10.6 us -> 8.96 us  [the longest x1 4.82 us: block_weights(): pl.pallas_call(lambda *refs: weights_kernel(len(pieces), *refs), in_specs...]
    ppermute x12, waiting for transfers between devices: 9.79 us -> 9.22 us  [local(): lax.ppermute(value, 'rows', [(z, z ^ s) for z in range(4)])]
    ppermute x13, starting transfers between devices: 2.34 us -> 2.89 us  [local(): pair = lambda value: lax.ppermute(value, 'pair', PAIR)]
    ppermute x12, starting transfers between devices: 18 us -> 18.5 us  [local(): lax.ppermute(value, 'rows', [(z, z ^ s) for z in range(4)])]
  transfers between devices with their start and end apart: 25 -> 25, of which waited for: 13 -> 12; matrix products, arithmetic and copies ran while one was open for 0% -> 0% of each run, Pallas kernels for 22% -> 21%
where the time goes in v8:
time: 49.9 us; the launch traced here: 49.8 us
  starting transfers between devices  21.4 us (43%)
  Pallas kernels  14.1 us (28%)
  waiting for transfers between devices  12.7 us (25%)
  between operations  0.8 us (2%)
  other arithmetic  0.73 us (1%)
    ppermute x12, starting transfers between devices, local(): lax.ppermute(value, 'rows', [(z, z ^ s) for z in range(4)])  18.5 us
    ppermute x12, waiting for transfers between devices, local(): lax.ppermute(value, 'rows', [(z, z ^ s) for z in range(4)])  9.22 us
    pallas_call x1, Pallas kernels, block_weights(): pl.pallas_call(lambda *refs: weights_kernel(len(pieces), *refs), in_specs...  4.82 us
    ppermute x13, waiting for transfers between devices, local(): pair = lambda value: lax.ppermute(value, 'pair', PAIR)  3.49 us
    pallas_call x1, Pallas kernels, row_grads(): pl.pallas_call(row_grads_kernel, in_specs=[smem_spec()] + [vmem_spec()] *...  3.29 us
    pallas_call x1, Pallas kernels, moved_weights(): pl.pallas_call(lambda *refs: moved_kernel(count, features, *refs), in_spe...  3.26 us
    ppermute x13, starting transfers between devices, local(): pair = lambda value: lax.ppermute(value, 'pair', PAIR)  2.89 us
    pallas_call x1, Pallas kernels, query_sums(): pl.pallas_call(query_sums_kernel, in_specs=[vmem_spec()], out_specs=[vmem...  1.28 us
  transfers between devices with their start and end apart: 25, of which 12 were waited for; matrix products, arithmetic and copies ran while one was open for 0% of the time, Pallas kernels for 21%

profile of v8, /device:TPU:0, one launch (start us, length us, event | category | flops | bytes accessed | tf_op | source)
XLA Modules:
  0.0 49.8 jit_solution(11287156213852594279)
XLA Ops:
  0.6 3.1 %collective-permute-start = (bf16[128,256]{1,0:T(8,128)(2,1)}, bf16[128,256]{1,0:T(8,128)(2,1)S(1)}, u32[]{:S(2)}, u32[]{:S(2)}) collective-permute-start(bf16[128,256]{1,0:T(8,128)(2,1)} %refs_3_.1), channel_id=1, source_target_pairs={{0,4},{4,0},{8,12},{12,8},{1,5},{5,1},{9,13},{13,9},{2,6},{6,2},{1... | collective-permute-start | bytes 196616 | tf_op jit(solution)/shard_map/ppermute | solution.py:470
  3.7 2.6 %collective-permute-start.6 = (bf16[128,256]{1,0:T(8,128)(2,1)}, bf16[128,256]{1,0:T(8,128)(2,1)S(1)}, u32[]{:S(2)}, u32[]{:S(2)}) collective-permute-start(bf16[128,256]{1,0:T(8,128)(2,1)} %refs_3_.1), channel_id=1, source_target_pairs={{0,8},{4,12},{8,0},{12,4},{1,9},{5,13},{9,1},{13,5},{2,10},{6,14},... | collective-permute-start | bytes 196616 | tf_op jit(solution)/shard_map/ppermute | solution.py:470
  6.3 0.0 collective-permute-start.8
  6.3 1.9 %collective-permute-start.2 = (bf16[128,256]{1,0:T(8,128)(2,1)}, bf16[128,256]{1,0:T(8,128)(2,1)S(1)}, u32[]{:S(2)}, u32[]{:S(2)}) collective-permute-start(bf16[128,256]{1,0:T(8,128)(2,1)} %refs_1_.2), channel_id=1, source_target_pairs={{0,8},{4,12},{8,0},{12,4},{1,9},{5,13},{9,1},{13,5},{2,10},{6,14},... | collective-permute-start | bytes 196616 | tf_op jit(solution)/shard_map/ppermute | solution.py:470
  8.2 0.9 %index_table.1 = (s32[6,8]{1,0:T(8,128)S(4)}, bf16[128,256]{1,0:T(8,128)(2,1)S(1)}) custom-call(s32[64]{0:T(128)} %refs_0_, s32[8]{0:T(128)} %refs_1_.1, s32[8]{0:T(128)} %refs_2_.1, bf16[128,256]{1,0:T(8,128)(2,1)} %refs_3_.1), custom_call_target="tpu_custom_call" | custom-call | tf_op jit(solution)/shard_map/index_table/pallas_call | solution.py:104
  9.1 0.1 collective-permute-start.5
  9.2 0.0 copy-start
  9.2 0.5 collective-permute-start.4
  9.7 3.7 %collective-permute-done.6.refs_5_ = bf16[128,256]{1,0:T(8,128)(2,1)S(1)} collective-permute-done((bf16[128,256]{1,0:T(8,128)(2,1)}, bf16[128,256]{1,0:T(8,128)(2,1)S(1)}, u32[]{:S(2)}, u32[]{:S(2)}) %collective-permute-start.6) | collective-permute-done | bytes 65568 | tf_op jit(solution)/shard_map/ppermute | solution.py:470
  13.4 0.5 %collective-permute-start.9 = (bf16[128,256]{1,0:T(8,128)(2,1)S(1)}, bf16[128,256]{1,0:T(8,128)(2,1)S(1)}, u32[]{:S(2)}, u32[]{:S(2)}) collective-permute-start(bf16[128,256]{1,0:T(8,128)(2,1)S(1)} %collective-permute-done.8.refs_7_), channel_id=1, source_target_pairs={{0,1},{1,0},{2,3},{3,2},{4,5},{5,4},{6,7},{7,6},{8,9},{9,8},{10,11... | collective-permute-start | bytes 196616 | tf_op jit(solution)/shard_map/ppermute | solution.py:469
  13.9 1.5 %collective-permute-done.2.refs_5_ = bf16[128,256]{1,0:T(8,128)(2,1)S(1)} collective-permute-done((bf16[128,256]{1,0:T(8,128)(2,1)}, bf16[128,256]{1,0:T(8,128)(2,1)S(1)}, u32[]{:S(2)}, u32[]{:S(2)}) %collective-permute-start.2) | collective-permute-done | bytes 65568 | tf_op jit(solution)/shard_map/ppermute | solution.py:470
  15.4 0.0 collective-permute-start.1
  15.4 0.0 collective-permute-done.5.refs_4_
  15.4 2.0 %collective-permute-start.3 = (bf16[128,256]{1,0:T(8,128)(2,1)S(1)}, bf16[128,256]{1,0:T(8,128)(2,1)S(1)}, u32[]{:S(2)}, u32[]{:S(2)}) collective-permute-start(bf16[128,256]{1,0:T(8,128)(2,1)S(1)} %collective-permute-done.2.refs_5_), channel_id=1, source_target_pairs={{0,4},{4,0},{8,12},{12,8},{1,5},{5,1},{9,13},{13,9},{2,6},{6,2},{1... | collective-permute-start | bytes 196616 | tf_op jit(solution)/shard_map/ppermute | solution.py:470
  17.5 0.0 collective-permute-done.4.refs_2_
  17.5 0.0 collective-permute-done.7.refs_6_
  17.5 0.0 collective-permute-done.9.refs_8_
  17.5 4.8 %block_weights.1 = (f32[2080,128]{1,0:T(8,128)S(1)}, bf16[8,512,1536]{2,1,0:T(8,128)(2,1)S(1)}) custom-call(s32[6,8]{1,0:T(8,128)S(4)} %get-tuple-element.35.refs_0_.meta, bf16[128,256]{1,0:T(8,128)(2,1)S(1)} %get-tuple-element.36.refs_1_, bf16[128,256]{1,0:T(8,128)(2,1)S(1)} %collective-permute-done.4.refs_2_, ...), custom_call_target="tpu_custom_call" | custom-call | tf_op jit(solution)/shard_map/block_weights/pallas_call | solution.py:214
  22.3 0.0 collective-permute-done.1.refs_3_
  22.3 0.1 collective-permute-start.10
  22.4 0.5 collective-permute-start.11
  22.9 0.1 collective-permute-start.12
  23.0 0.4 collective-permute-start.13
  23.4 0.2 collective-permute-done.10.refs_2_
  23.6 0.2 collective-permute-done.11.refs_4_
  23.8 0.4 collective-permute-done.12.refs_6_
  24.2 0.2 collective-permute-done.13.refs_8_
  24.3 3.3 %moved_weights.1 = (f32[2112,128]{1,0:T(8,128)S(1)}, f32[2,8,512]{2,1,0:T(8,128)S(1)}, bf16[8,512,1536]{2,1,0:T(8,128)(2,1)S(1)}) custom-call(s32[6,8]{1,0:T(8,128)S(4)} %get-tuple-element.35.refs_0_.meta, bf16[128,256]{1,0:T(8,128)(2,1)S(1)} %copy-done, bf16[128,256]{1,0:T(8,128)(2,1)S(1)} %collective-permute-done.10.refs_2_, ...), custom_call_target="tpu_custom_call", output_to_operand_aliasing={{2}: (10, {})} | custom-call | tf_op jit(solution)/shard_map/moved_weights/pallas_call | solution.py:305
  27.6 0.1 collective-permute-start.15
  27.7 3.0 %collective-permute-start.16 = (f32[2,8,512]{2,1,0:T(8,128)S(1)}, f32[2,8,512]{2,1,0:T(8,128)S(1)}, u32[]{:S(2)}, u32[]{:S(2)}) collective-permute-start(f32[2,8,512]{2,1,0:T(8,128)S(1)} %get-tuple-element.45.refs_1_), channel_id=1, source_target_pairs={{0,8},{4,12},{8,0},{12,4},{1,9},{5,13},{9,1},{13,5},{2,10},{6,14},... | collective-permute-start | bytes 98312 | tf_op jit(solution)/shard_map/ppermute | solution.py:470
  30.7 1.4 %collective-permute-start.17 = (f32[2,8,512]{2,1,0:T(8,128)S(1)}, f32[2,8,512]{2,1,0:T(8,128)S(1)}, u32[]{:S(2)}, u32[]{:S(2)}) collective-permute-start(f32[2,8,512]{2,1,0:T(8,128)S(1)} %get-tuple-element.45.refs_1_), channel_id=1, source_target_pairs={{0,12},{4,8},{8,4},{12,0},{1,13},{5,9},{9,5},{13,1},{2,14},{6,10},... | collective-permute-start | bytes 98312 | tf_op jit(solution)/shard_map/ppermute | solution.py:470
  32.0 1.3 %query_sums.1 = (f32[8,2,256,128]{3,2,1,0:T(8,128)S(1)}, bf16[8,512,1536]{2,1,0:T(8,128)(2,1)S(1)}) custom-call(bf16[8,512,1536]{2,1,0:T(8,128)(2,1)S(1)} %get-tuple-element.46.state), custom_call_target="tpu_custom_call", output_to_operand_aliasing={{1}: (0, {})} | custom-call | tf_op jit(solution)/shard_map/query_sums/pallas_call | solution.py:338
  33.3 3.0 %collective-permute-done.17.refs_7_ = f32[2,8,512]{2,1,0:T(8,128)S(1)} collective-permute-done((f32[2,8,512]{2,1,0:T(8,128)S(1)}, f32[2,8,512]{2,1,0:T(8,128)S(1)}, u32[]{:S(2)}, u32[]{:S(2)}) %collective-permute-start.17) | collective-permute-done | bytes 32800 | tf_op jit(solution)/shard_map/ppermute | solution.py:470
  36.4 0.5 %collective-permute-start.19 = (f32[2,8,512]{2,1,0:T(8,128)S(1)}, f32[2,8,512]{2,1,0:T(8,128)S(1)}, u32[]{:S(2)}, u32[]{:S(2)}) collective-permute-start(f32[2,8,512]{2,1,0:T(8,128)S(1)} %collective-permute-done.16.refs_5_), channel_id=1, source_target_pairs={{0,1},{1,0},{2,3},{3,2},{4,5},{5,4},{6,7},{7,6},{8,9},{9,8},{10,11... | collective-permute-start | bytes 98312 | tf_op jit(solution)/shard_map/ppermute | solution.py:469
  36.9 0.0 collective-permute-start.20
  36.9 0.7 %collective-permute-done.18.refs_4_ = f32[2,8,512]{2,1,0:T(8,128)S(1)} collective-permute-done((f32[2,8,512]{2,1,0:T(8,128)S(1)}, f32[2,8,512]{2,1,0:T(8,128)S(1)}, u32[]{:S(2)}, u32[]{:S(2)}) %collective-permute-start.18) | collective-permute-done | bytes 32800 | tf_op jit(solution)/shard_map/ppermute | solution.py:469
  37.6 0.2 collective-permute-done.19.refs_6_
  37.8 0.3 collective-permute-done.20.refs_8_
  38.1 0.6 %query_grads.1 = (f32[8,512]{1,0:T(8,128)S(1)}, f32[8,512]{1,0:T(8,128)S(1)}, f32[4,128,256]{2,1,0:T(8,128)S(1)}, bf16[4,128,256]{2,1,0:T(8,128)(2,1)S(1)}) custom-call(s32[6,8]{1,0:T(8,128)S(4)} %get-tuple-element.35.refs_0_.meta, f32[2,8,512]{2,1,0:T(8,128)S(1)} %get-tuple-element.45.refs_1_, f32[2,8,512]{2,1,0:T(8,128)S(1)} %collective-permute-done.14.refs_2_, ...), custom_call_target="tpu_custom_call" | custom-call | tf_op jit(solution)/shard_map/query_grads/pallas_call | solution.py:397
  38.7 0.2 collective-permute-start.21
  38.9 1.4 %collective-permute-done.21 = bf16[4,128,256]{2,1,0:T(8,128)(2,1)S(1)} collective-permute-done((bf16[4,128,256]{2,1,0:T(8,128)(2,1)S(1)}, bf16[4,128,256]{2,1,0:T(8,128)(2,1)S(1)}, u32[]{:S(2)}, u32[]{:S(2)}) %collective-permute-start.21) | collective-permute-done | bytes 262176 | tf_op jit(solution)/shard_map/ppermute | solution.py:469
  40.3 0.1 fusion.4
  40.4 0.1 collective-permute-start.22
  40.5 1.9 %collective-permute-start.23 = (bf16[128,256]{1,0:T(8,128)(2,1)S(1)}, bf16[128,256]{1,0:T(8,128)(2,1)S(1)}, u32[]{:S(2)}, u32[]{:S(2)}) collective-permute-start(bf16[128,256]{1,0:T(8,128)(2,1)S(1)} %get-tuple-element.65), channel_id=1, source_target_pairs={{0,8},{4,12},{8,0},{12,4},{1,9},{5,13},{9,1},{13,5},{2,10},{6,14},... | collective-permute-start | bytes 196616 | tf_op jit(solution)/shard_map/ppermute | solution.py:470
  42.4 2.4 %collective-permute-start.24 = (bf16[128,256]{1,0:T(8,128)(2,1)S(1)}, bf16[128,256]{1,0:T(8,128)(2,1)S(1)}, u32[]{:S(2)}, u32[]{:S(2)}) collective-permute-start(bf16[128,256]{1,0:T(8,128)(2,1)S(1)} %get-tuple-element.64), channel_id=1, source_target_pairs={{0,12},{4,8},{8,4},{12,0},{1,13},{5,9},{9,5},{13,1},{2,14},{6,10},... | collective-permute-start | bytes 196616 | tf_op jit(solution)/shard_map/ppermute | solution.py:470
  44.8 3.3 %row_grads.1 = (bf16[4096,256]{1,0:T(8,128)(2,1)}, bf16[4096,256]{1,0:T(8,128)(2,1)}) custom-call(s32[6,8]{1,0:T(8,128)S(4)} %get-tuple-element.35.refs_0_.meta, f32[8,512]{1,0:T(8,128)S(1)} %get-tuple-element.56.c_ref, f32[8,512]{1,0:T(8,128)S(1)} %get-tuple-element.57.d_ref, f32[2080,128]{1,0:T(8,128)S(1)} %get-tuple-element.43.refs_9_.q_side, ...), custom_call_target="tpu_custom_call" | custom-call | tf_op jit(solution)/shard_map/row_grads/pallas_call | solution.py:450
  48.1 0.9 %collective-permute-done.23 = bf16[128,256]{1,0:T(8,128)(2,1)S(1)} collective-permute-done((bf16[128,256]{1,0:T(8,128)(2,1)S(1)}, bf16[128,256]{1,0:T(8,128)(2,1)S(1)}, u32[]{:S(2)}, u32[]{:S(2)}) %collective-permute-start.23) | collective-permute-done | bytes 65568 | tf_op jit(solution)/shard_map/ppermute | solution.py:470
  49.1 0.7 %fusion.3 = bf16[128,256]{1,0:T(8,128)(2,1)} fusion(f32[4,128,256]{2,1,0:T(8,128)S(1)} %get-tuple-element.62, bf16[128,256]{1,0:T(8,128)(2,1)S(1)} %collective-permute-done.24, bf16[128,256]{1,0:T(8,128)(2,1)S(1)} %collective-permute-done.23, bf16[128,256]{1,0:T(8,128)(2,1)S(1)} %collective-permute-done.22), kind=kLoop, calls=%fused_computation.5 | loop fusion | flops 229376 | bytes 393216 | tf_op jit(solution)/shard_map/convert_element_type | solution.py:525
  (13 shorter events, 0.0 us)
Async XLA Ops:
  0.6 7.6 %collective-permute-start = (bf16[128,256]{1,0:T(8,128)(2,1)}, bf16[128,256]{1,0:T(8,128)(2,1)S(1)}, u32[]{:S(2)}, u32[]{:S(2)}) collective-permute-start(bf16[128,256]{1,0:T(8,128)(2,1)} %refs_3_.1), channel_id=1, source_target_pairs={{0,4},{4,0},{8,12},{12,8},{1,5},{5,1},{9,13},{13,9},{2,6},{6,2},{1... | collective-permute-start | bytes 196616 | tf_op jit(solution)/shard_map/ppermute | solution.py:470
  3.7 9.7 %collective-permute-start.6 = (bf16[128,256]{1,0:T(8,128)(2,1)}, bf16[128,256]{1,0:T(8,128)(2,1)S(1)}, u32[]{:S(2)}, u32[]{:S(2)}) collective-permute-start(bf16[128,256]{1,0:T(8,128)(2,1)} %refs_3_.1), channel_id=1, source_target_pairs={{0,8},{4,12},{8,0},{12,4},{1,9},{5,13},{9,1},{13,5},{2,10},{6,14},... | collective-permute-start | bytes 196616 | tf_op jit(solution)/shard_map/ppermute | solution.py:470
  6.3 7.1 %collective-permute-start.8 = (bf16[128,256]{1,0:T(8,128)(2,1)}, bf16[128,256]{1,0:T(8,128)(2,1)S(1)}, u32[]{:S(2)}, u32[]{:S(2)}) collective-permute-start(bf16[128,256]{1,0:T(8,128)(2,1)} %refs_3_.1), channel_id=1, source_target_pairs={{0,12},{4,8},{8,4},{12,0},{1,13},{5,9},{9,5},{13,1},{2,14},{6,10},... | collective-permute-start | bytes 196616 | tf_op jit(solution)/shard_map/ppermute | solution.py:470
  6.3 9.1 %collective-permute-start.2 = (bf16[128,256]{1,0:T(8,128)(2,1)}, bf16[128,256]{1,0:T(8,128)(2,1)S(1)}, u32[]{:S(2)}, u32[]{:S(2)}) collective-permute-start(bf16[128,256]{1,0:T(8,128)(2,1)} %refs_1_.2), channel_id=1, source_target_pairs={{0,8},{4,12},{8,0},{12,4},{1,9},{5,13},{9,1},{13,5},{2,10},{6,14},... | collective-permute-start | bytes 196616 | tf_op jit(solution)/shard_map/ppermute | solution.py:470
  9.1 6.3 %collective-permute-start.5 = (bf16[128,256]{1,0:T(8,128)(2,1)S(1)}, bf16[128,256]{1,0:T(8,128)(2,1)S(1)}, u32[]{:S(2)}, u32[]{:S(2)}) collective-permute-start(bf16[128,256]{1,0:T(8,128)(2,1)S(1)} %collective-permute-done.refs_3_), channel_id=1, source_target_pairs={{0,1},{1,0},{2,3},{3,2},{4,5},{5,4},{6,7},{7,6},{8,9},{9,8},{10,11... | collective-permute-start | bytes 196616 | tf_op jit(solution)/shard_map/ppermute | solution.py:469
  9.2 13.1 %copy-start = (bf16[128,256]{1,0:T(8,128)(2,1)S(1)}, bf16[128,256]{1,0:T(8,128)(2,1)}, u32[]{:S(2)}) copy-start(bf16[128,256]{1,0:T(8,128)(2,1)} %refs_1_.2) | copy-start | bytes 196612
  9.2 8.3 %collective-permute-start.4 = (bf16[128,256]{1,0:T(8,128)(2,1)S(1)}, bf16[128,256]{1,0:T(8,128)(2,1)S(1)}, u32[]{:S(2)}, u32[]{:S(2)}) collective-permute-start(bf16[128,256]{1,0:T(8,128)(2,1)S(1)} %get-tuple-element.36.refs_1_), channel_id=1, source_target_pairs={{0,1},{1,0},{2,3},{3,2},{4,5},{5,4},{6,7},{7,6},{8,9},{9,8},{10,11... | collective-permute-start | bytes 196616 | tf_op jit(solution)/shard_map/ppermute | solution.py:469
  13.4 4.1 %collective-permute-start.7 = (bf16[128,256]{1,0:T(8,128)(2,1)S(1)}, bf16[128,256]{1,0:T(8,128)(2,1)S(1)}, u32[]{:S(2)}, u32[]{:S(2)}) collective-permute-start(bf16[128,256]{1,0:T(8,128)(2,1)S(1)} %collective-permute-done.6.refs_5_), channel_id=1, source_target_pairs={{0,1},{1,0},{2,3},{3,2},{4,5},{5,4},{6,7},{7,6},{8,9},{9,8},{10,11... | collective-permute-start | bytes 196616 | tf_op jit(solution)/shard_map/ppermute | solution.py:469
  13.4 4.1 %collective-permute-start.9 = (bf16[128,256]{1,0:T(8,128)(2,1)S(1)}, bf16[128,256]{1,0:T(8,128)(2,1)S(1)}, u32[]{:S(2)}, u32[]{:S(2)}) collective-permute-start(bf16[128,256]{1,0:T(8,128)(2,1)S(1)} %collective-permute-done.8.refs_7_), channel_id=1, source_target_pairs={{0,1},{1,0},{2,3},{3,2},{4,5},{5,4},{6,7},{7,6},{8,9},{9,8},{10,11... | collective-permute-start | bytes 196616 | tf_op jit(solution)/shard_map/ppermute | solution.py:469
  15.4 6.9 %collective-permute-start.1 = (bf16[128,256]{1,0:T(8,128)(2,1)}, bf16[128,256]{1,0:T(8,128)(2,1)S(1)}, u32[]{:S(2)}, u32[]{:S(2)}) collective-permute-start(bf16[128,256]{1,0:T(8,128)(2,1)} %refs_1_.2), channel_id=1, source_target_pairs={{0,4},{4,0},{8,12},{12,8},{1,5},{5,1},{9,13},{13,9},{2,6},{6,2},{1... | collective-permute-start | bytes 196616 | tf_op jit(solution)/shard_map/ppermute | solution.py:470
  15.4 6.9 %collective-permute-start.3 = (bf16[128,256]{1,0:T(8,128)(2,1)S(1)}, bf16[128,256]{1,0:T(8,128)(2,1)S(1)}, u32[]{:S(2)}, u32[]{:S(2)}) collective-permute-start(bf16[128,256]{1,0:T(8,128)(2,1)S(1)} %collective-permute-done.2.refs_5_), channel_id=1, source_target_pairs={{0,4},{4,0},{8,12},{12,8},{1,5},{5,1},{9,13},{13,9},{2,6},{6,2},{1... | collective-permute-start | bytes 196616 | tf_op jit(solution)/shard_map/ppermute | solution.py:470
  22.3 1.3 %collective-permute-start.10 = (bf16[128,256]{1,0:T(8,128)(2,1)S(1)}, bf16[128,256]{1,0:T(8,128)(2,1)S(1)}, u32[]{:S(2)}, u32[]{:S(2)}) collective-permute-start(bf16[128,256]{1,0:T(8,128)(2,1)S(1)} %copy-done), channel_id=1, source_target_pairs={{0,1},{1,0},{2,3},{3,2},{4,5},{5,4},{6,7},{7,6},{8,9},{9,8},{10,11... | collective-permute-start | bytes 196616 | tf_op jit(solution)/shard_map/ppermute | solution.py:469
  22.4 1.4 %collective-permute-start.11 = (bf16[128,256]{1,0:T(8,128)(2,1)S(1)}, bf16[128,256]{1,0:T(8,128)(2,1)S(1)}, u32[]{:S(2)}, u32[]{:S(2)}) collective-permute-start(bf16[128,256]{1,0:T(8,128)(2,1)S(1)} %collective-permute-done.1.refs_3_), channel_id=1, source_target_pairs={{0,1},{1,0},{2,3},{3,2},{4,5},{5,4},{6,7},{7,6},{8,9},{9,8},{10,11... | collective-permute-start | bytes 196616 | tf_op jit(solution)/shard_map/ppermute | solution.py:469
  22.9 1.3 %collective-permute-start.12 = (bf16[128,256]{1,0:T(8,128)(2,1)S(1)}, bf16[128,256]{1,0:T(8,128)(2,1)S(1)}, u32[]{:S(2)}, u32[]{:S(2)}) collective-permute-start(bf16[128,256]{1,0:T(8,128)(2,1)S(1)} %collective-permute-done.2.refs_5_), channel_id=1, source_target_pairs={{0,1},{1,0},{2,3},{3,2},{4,5},{5,4},{6,7},{7,6},{8,9},{9,8},{10,11... | collective-permute-start | bytes 196616 | tf_op jit(solution)/shard_map/ppermute | solution.py:469
  23.0 1.3 %collective-permute-start.13 = (bf16[128,256]{1,0:T(8,128)(2,1)S(1)}, bf16[128,256]{1,0:T(8,128)(2,1)S(1)}, u32[]{:S(2)}, u32[]{:S(2)}) collective-permute-start(bf16[128,256]{1,0:T(8,128)(2,1)S(1)} %collective-permute-done.3.refs_7_), channel_id=1, source_target_pairs={{0,1},{1,0},{2,3},{3,2},{4,5},{5,4},{6,7},{7,6},{8,9},{9,8},{10,11... | collective-permute-start | bytes 196616 | tf_op jit(solution)/shard_map/ppermute | solution.py:469
  27.6 5.7 %collective-permute-start.15 = (f32[2,8,512]{2,1,0:T(8,128)S(1)}, f32[2,8,512]{2,1,0:T(8,128)S(1)}, u32[]{:S(2)}, u32[]{:S(2)}) collective-permute-start(f32[2,8,512]{2,1,0:T(8,128)S(1)} %get-tuple-element.45.refs_1_), channel_id=1, source_target_pairs={{0,4},{4,0},{8,12},{12,8},{1,5},{5,1},{9,13},{13,9},{2,6},{6,2},{1... | collective-permute-start | bytes 98312 | tf_op jit(solution)/shard_map/ppermute | solution.py:470
  27.7 5.7 %collective-permute-start.16 = (f32[2,8,512]{2,1,0:T(8,128)S(1)}, f32[2,8,512]{2,1,0:T(8,128)S(1)}, u32[]{:S(2)}, u32[]{:S(2)}) collective-permute-start(f32[2,8,512]{2,1,0:T(8,128)S(1)} %get-tuple-element.45.refs_1_), channel_id=1, source_target_pairs={{0,8},{4,12},{8,0},{12,4},{1,9},{5,13},{9,1},{13,5},{2,10},{6,14},... | collective-permute-start | bytes 98312 | tf_op jit(solution)/shard_map/ppermute | solution.py:470
  30.7 5.7 %collective-permute-start.17 = (f32[2,8,512]{2,1,0:T(8,128)S(1)}, f32[2,8,512]{2,1,0:T(8,128)S(1)}, u32[]{:S(2)}, u32[]{:S(2)}) collective-permute-start(f32[2,8,512]{2,1,0:T(8,128)S(1)} %get-tuple-element.45.refs_1_), channel_id=1, source_target_pairs={{0,12},{4,8},{8,4},{12,0},{1,13},{5,9},{9,5},{13,1},{2,14},{6,10},... | collective-permute-start | bytes 98312 | tf_op jit(solution)/shard_map/ppermute | solution.py:470
  32.0 4.9 %collective-permute-start.14 = (f32[2,8,512]{2,1,0:T(8,128)S(1)}, f32[2,8,512]{2,1,0:T(8,128)S(1)}, u32[]{:S(2)}, u32[]{:S(2)}) collective-permute-start(f32[2,8,512]{2,1,0:T(8,128)S(1)} %get-tuple-element.45.refs_1_), channel_id=1, source_target_pairs={{0,1},{1,0},{2,3},{3,2},{4,5},{5,4},{6,7},{7,6},{8,9},{9,8},{10,11... | collective-permute-start | bytes 98312 | tf_op jit(solution)/shard_map/ppermute | solution.py:469
  36.4 1.2 %collective-permute-start.18 = (f32[2,8,512]{2,1,0:T(8,128)S(1)}, f32[2,8,512]{2,1,0:T(8,128)S(1)}, u32[]{:S(2)}, u32[]{:S(2)}) collective-permute-start(f32[2,8,512]{2,1,0:T(8,128)S(1)} %collective-permute-done.15.refs_3_), channel_id=1, source_target_pairs={{0,1},{1,0},{2,3},{3,2},{4,5},{5,4},{6,7},{7,6},{8,9},{9,8},{10,11... | collective-permute-start | bytes 98312 | tf_op jit(solution)/shard_map/ppermute | solution.py:469
  36.4 1.4 %collective-permute-start.19 = (f32[2,8,512]{2,1,0:T(8,128)S(1)}, f32[2,8,512]{2,1,0:T(8,128)S(1)}, u32[]{:S(2)}, u32[]{:S(2)}) collective-permute-start(f32[2,8,512]{2,1,0:T(8,128)S(1)} %collective-permute-done.16.refs_5_), channel_id=1, source_target_pairs={{0,1},{1,0},{2,3},{3,2},{4,5},{5,4},{6,7},{7,6},{8,9},{9,8},{10,11... | collective-permute-start | bytes 98312 | tf_op jit(solution)/shard_map/ppermute | solution.py:469
  36.9 1.2 %collective-permute-start.20 = (f32[2,8,512]{2,1,0:T(8,128)S(1)}, f32[2,8,512]{2,1,0:T(8,128)S(1)}, u32[]{:S(2)}, u32[]{:S(2)}) collective-permute-start(f32[2,8,512]{2,1,0:T(8,128)S(1)} %collective-permute-done.17.refs_7_), channel_id=1, source_target_pairs={{0,1},{1,0},{2,3},{3,2},{4,5},{5,4},{6,7},{7,6},{8,9},{9,8},{10,11... | collective-permute-start | bytes 98312 | tf_op jit(solution)/shard_map/ppermute | solution.py:469
  38.7 1.6 %collective-permute-start.21 = (bf16[4,128,256]{2,1,0:T(8,128)(2,1)S(1)}, bf16[4,128,256]{2,1,0:T(8,128)(2,1)S(1)}, u32[]{:S(2)}, u32[]{:S(2)}) collective-permute-start(bf16[4,128,256]{2,1,0:T(8,128)(2,1)S(1)} %get-tuple-element.54), channel_id=1, source_target_pairs={{0,1},{1,0},{2,3},{3,2},{4,5},{5,4},{6,7},{7,6},{8,9},{9,8},{10,11... | collective-permute-start | bytes 786440 | tf_op jit(solution)/shard_map/ppermute | solution.py:469
  40.4 7.8 %collective-permute-start.22 = (bf16[128,256]{1,0:T(8,128)(2,1)S(1)}, bf16[128,256]{1,0:T(8,128)(2,1)S(1)}, u32[]{:S(2)}, u32[]{:S(2)}) collective-permute-start(bf16[128,256]{1,0:T(8,128)(2,1)S(1)} %get-tuple-element.63), channel_id=1, source_target_pairs={{0,4},{4,0},{8,12},{12,8},{1,5},{5,1},{9,13},{13,9},{2,6},{6,2},{1... | collective-permute-start | bytes 196616 | tf_op jit(solution)/shard_map/ppermute | solution.py:470
  40.5 8.6 %collective-permute-start.23 = (bf16[128,256]{1,0:T(8,128)(2,1)S(1)}, bf16[128,256]{1,0:T(8,128)(2,1)S(1)}, u32[]{:S(2)}, u32[]{:S(2)}) collective-permute-start(bf16[128,256]{1,0:T(8,128)(2,1)S(1)} %get-tuple-element.65), channel_id=1, source_target_pairs={{0,8},{4,12},{8,0},{12,4},{1,9},{5,13},{9,1},{13,5},{2,10},{6,14},... | collective-permute-start | bytes 196616 | tf_op jit(solution)/shard_map/ppermute | solution.py:470
  42.4 6.7 %collective-permute-start.24 = (bf16[128,256]{1,0:T(8,128)(2,1)S(1)}, bf16[128,256]{1,0:T(8,128)(2,1)S(1)}, u32[]{:S(2)}, u32[]{:S(2)}) collective-permute-start(bf16[128,256]{1,0:T(8,128)(2,1)S(1)} %get-tuple-element.64), channel_id=1, source_target_pairs={{0,12},{4,8},{8,4},{12,0},{1,13},{5,9},{9,5},{13,1},{2,14},{6,10},... | collective-permute-start | bytes 196616 | tf_op jit(solution)/shard_map/ppermute | solution.py:470

commit v9 on v8

--- a/solution.py
+++ b/solution.py
@@ -58,16 +58,28 @@
     return pltpu.with_memory_space_constraint(value, pltpu.HBM)
 
 
-def index_kernel(small, blocks, table_hbm, train_hbm, test_hbm, query_hbm, meta, query_ref, *scratch):
-    block_table, train_rows, test_rows, count, small_sem = scratch
+def index_kernel(small, table_hbm, train_hbm, test_hbm, *refs):
+    query_hbm, key_hbm, value_hbm, meta, query_ref, state = refs[:6]
+    block_table, train_rows, test_rows, count, small_sem, sem = refs[6:]
+    blocks = state.shape[0]
+    features = key_hbm.shape[1]
+    stacked = features // HD * TEST
     entries = every_copy(
         [
             pltpu.make_async_copy(table_hbm, block_table, small_sem.at[0]),
             pltpu.make_async_copy(train_hbm, train_rows, small_sem.at[1]),
             pltpu.make_async_copy(test_hbm, test_rows, small_sem.at[2]),
-            pltpu.make_async_copy(query_hbm, query_ref, small_sem.at[3]),
         ]
     )
+    loads = [pltpu.make_async_copy(query_hbm, query_ref, small_sem.at[3])]
+    for n, source in enumerate((key_hbm, value_hbm)):
+        lanes = pl.ds(2 * stacked + n * features, features)
+        for b in range(blocks):
+            rows = pl.ds(b * BLK, BLK)
+            loads.append(
+                pltpu.make_async_copy(source.at[rows], state.at[b, :, lanes], sem.at[n, b])
+            )
+    every_copy(loads)
     chip = lax.axis_index("rows").astype(jnp.int32)
     core = lax.axis_index("pair").astype(jnp.int32)
     first = lax.axis_index(RP).astype(jnp.int32) * blocks
@@ -97,17 +109,24 @@
         meta[OWNER, b] = table
         meta[LIVE, b] = jnp.minimum(train_rows[table] - count[table] * BLK, BLK)
         count[table] = count[table] + 1
-
-
-def index_table(small, blocks, block_table, train_rows, test_rows, query_rows):
+    for copy in loads:
+        copy.wait()
+
+
+def index_table(small, block_table, train_rows, test_rows, query_rows, key_rows, value_rows):
     tables = train_rows.shape[0]
+    features = key_rows.shape[1]
+    blocks = key_rows.shape[0] // BLK
+    stacked = features // HD * TEST
+    arrays = (block_table, train_rows, test_rows, query_rows, key_rows, value_rows)
     return pl.pallas_call(
-        lambda *refs: index_kernel(small, blocks, *refs),
-        in_specs=[hbm_spec()] * 4,
-        out_specs=[smem_spec(), vmem_spec()],
+        lambda *refs: index_kernel(small, *refs),
+        in_specs=[hbm_spec()] * 6,
+        out_specs=[smem_spec(), vmem_spec(), vmem_spec()],
         out_shape=[
             pltpu.SMEM((6, max(blocks, tables)), jnp.int32),
             pltpu.VMEM(query_rows.shape, query_rows.dtype),
+            pltpu.VMEM((blocks, BLK, 2 * stacked + 2 * features), jnp.bfloat16),
         ],
         scratch_shapes=[
             pltpu.SMEM(block_table.shape, jnp.int32),
@@ -115,9 +134,11 @@
             pltpu.SMEM((tables,), jnp.int32),
             pltpu.SMEM((tables,), jnp.int32),
             pltpu.SemaphoreType.DMA((4,)),
-        ],
+            pltpu.SemaphoreType.DMA((2, blocks)),
+        ],
+        compiler_params=params(4),
         name="index_table",
-    )(*map(in_hbm, (block_table, train_rows, test_rows, query_rows)))
+    )(*map(in_hbm, arrays))
 
 
 def turn_pieces(pieces, store):
@@ -151,27 +172,13 @@
     return [(b, p) for b in range(blocks) for p in range(features // LANES)]
 
 
-def weights_kernel(count, meta, *refs):
+def weights_kernel(count, features, meta, *refs):
     pieces = refs[:count]
-    key_hbm, value_hbm, side, state, scores_s, sem = refs[count:]
-    blocks = state.shape[0]
-    features = key_hbm.shape[1]
+    state, side, state_out, scores_s = refs[count:]
+    blocks = state.shape[0]
     stacked = features // HD * TEST
     first_peak = side.shape[0] - blocks * features // HD
     units = units_of(blocks, features)
-    loads = []
-    for n, source in enumerate((key_hbm, value_hbm)):
-        lanes = pl.ds(2 * stacked + n * features, features)
-        loads.append(
-            every_copy(
-                [
-                    pltpu.make_async_copy(
-                        source.at[pl.ds(b * BLK, BLK)], state.at[b, :, lanes], sem.at[n, b]
-                    )
-                    for b in range(blocks)
-                ]
-            )
-        )
 
     def store(at_slot, turned):
         side[at_slot * features : (at_slot + 1) * features, :] = turned.astype(jnp.float32)
@@ -181,8 +188,6 @@
     for t in range(len(units) + 1):
         if t < len(units):
             b, p = units[t]
-            if p == 0:
-                loads[0][b].wait()
             live = meta[LIVE, b]
             queries = two_heads(side[rows_of(meta, b, p, features), :]).astype(jnp.bfloat16)
             peak = jnp.full((8, WIDE), NEG, jnp.float32)
@@ -191,7 +196,9 @@
             if t > 0:
                 last_b, last_p = units[t - 1]
                 weights = jnp.exp2(scores_s[(t - 1) % 2, rows, :] * LOG2_SCALE - peaks[t - 1])
-                state[last_b, rows, last_p * WIDE : (last_p + 1) * WIDE] = weights.astype(jnp.bfloat16)
+                state_out[last_b, rows, last_p * WIDE : (last_p + 1) * WIDE] = weights.astype(
+                    jnp.bfloat16
+                )
             if t < len(units):
                 keys = state[b, rows, 2 * stacked + p * LANES : 2 * stacked + (p + 1) * LANES]
                 scores = jnp.dot(keys, queries, preferred_element_type=jnp.float32)
@@ -203,29 +210,24 @@
             peaks[t] = jnp.max(peak, axis=0, keepdims=True) * LOG2_SCALE
     for (b, p), peak in zip(units, peaks):
         put_heads(side, first_peak, b, p, features, peak)
-    for copy in loads[1]:
-        copy.wait()
-
-
-def block_weights(meta, pieces, key_rows, value_rows, tables):
-    features = key_rows.shape[1]
-    blocks = key_rows.shape[0] // BLK
-    stacked = features // HD * TEST
+
+
+def block_weights(meta, pieces, state, features, tables):
+    blocks = state.shape[0]
+    count = len(pieces)
     return pl.pallas_call(
-        lambda *refs: weights_kernel(len(pieces), *refs),
-        in_specs=[smem_spec()] + [vmem_spec()] * len(pieces) + [hbm_spec()] * 2,
+        lambda *refs: weights_kernel(count, features, *refs),
+        in_specs=[smem_spec()] + [vmem_spec()] * (count + 1),
         out_specs=[vmem_spec()] * 2,
         out_shape=[
             pltpu.VMEM((tables * features + blocks * features // HD, TEST), jnp.float32),
-            pltpu.VMEM((blocks, BLK, 2 * stacked + 2 * features), jnp.bfloat16),
-        ],
-        scratch_shapes=[
-            pltpu.VMEM((2, BLK, WIDE), jnp.float32),
-            pltpu.SemaphoreType.DMA((2, blocks)),
-        ],
+            pltpu.VMEM(state.shape, jnp.bfloat16),
+        ],
+        input_output_aliases={count + 1: 1},
+        scratch_shapes=[pltpu.VMEM((2, BLK, WIDE), jnp.float32)],
         compiler_params=params(10),
         name="block_weights",
-    )(meta, *pieces, in_hbm(key_rows), in_hbm(value_rows))
+    )(meta, *pieces, state)
 
 
 def moved_kernel(count, features, meta, *refs):
@@ -469,26 +471,28 @@
     pair = lambda value: lax.ppermute(value, "pair", PAIR)
     step = lambda value, s: lax.ppermute(value, "rows", [(z, z ^ s) for z in range(4)])
     after = lambda value, other: lax.optimization_barrier((value, other))
-    index = lambda entries: index_table(small, blocks, entries, train_rows, test_rows, query_rows)
+    index = lambda entries: index_table(
+        small, entries, train_rows, test_rows, query_rows, key_rows, value_rows
+    )
     if small:
         near = [step(query_rows, s) for s in (1, 2, 3)]
         near_grads = [step(cotangent, 1), step(cotangent, 2)]
         near_grads.append(step(near_grads[1], 1))
         block_table, near[0] = after(block_table, near[0])
-        meta, own = index(block_table)
+        meta, own, state = index(block_table)
         near[0], meta = after(near[0], meta)
         queries = [own, pair(own)]
         for value in near:
             queries += [value, pair(value)]
-        q_side, state = block_weights(meta, queries, key_rows, value_rows, tables)
-        own, *near_grads, q_side = lax.optimization_barrier((cotangent, *near_grads, q_side))
-        grads = [own, pair(own)]
+        q_side, state = block_weights(meta, queries, state, features, tables)
+        *near_grads[1:], q_side = lax.optimization_barrier((*near_grads[1:], q_side))
+        grads = [cotangent, pair(cotangent)]
         for value in near_grads:
             grads += [value, pair(value)]
     else:
-        meta, _ = index(block_table)
+        meta, _, state = index(block_table)
         queries = [lax.all_gather(query_rows, RP, axis=0, tiled=True)]
-        q_side, state = block_weights(meta, queries, key_rows, value_rows, tables)
+        q_side, state = block_weights(meta, queries, state, features, tables)
         grads = [lax.all_gather(cotangent, RP, axis=0, tiled=True)]
     g_side, tab, state = moved_weights(meta, grads, q_side, state, features, tables)
     if small:

time: 49.9 us -> 47.5 us (0.952)
  waiting for transfers between devices: 12.7 us -> 11.1 us
  starting transfers between devices: 21.4 us -> 20.5 us
    ppermute x12, waiting for transfers between devices: 9.22 us -> 7.03 us  [local(): lax.ppermute(value, 'rows', [(z, z ^ s) for z in range(4)])]
    ppermute x13, waiting for transfers between devices: 3.49 us -> 4.03 us  [local(): pair = lambda value: lax.ppermute(value, 'pair', PAIR)]
  transfers between devices with their start and end apart: 25 -> 25, of which waited for: 12 -> 13; matrix products, arithmetic and copies ran while one was open for 0% -> 0% of each run, Pallas kernels for 21% -> 22%
where the time goes in v9:
time: 47.5 us; the launch traced here: 47.3 us
  starting transfers between devices  20.5 us (43%)
  Pallas kernels  14.2 us (30%)
  waiting for transfers between devices  11.1 us (23%)
  between operations  0.78 us (2%)
  other arithmetic  0.74 us (2%)
    ppermute x12, starting transfers between devices, local(): lax.ppermute(value, 'rows', [(z, z ^ s) for z in range(4)])  18.1 us
    ppermute x12, waiting for transfers between devices, local(): lax.ppermute(value, 'rows', [(z, z ^ s) for z in range(4)])  7.03 us
    ppermute x13, waiting for transfers between devices, local(): pair = lambda value: lax.ppermute(value, 'pair', PAIR)  4.03 us
    pallas_call x1, Pallas kernels, block_weights(): pl.pallas_call(lambda *refs: weights_kernel(count, features, *refs), in_s...  3.48 us
    pallas_call x1, Pallas kernels, row_grads(): pl.pallas_call(row_grads_kernel, in_specs=[smem_spec()] + [vmem_spec()] *...  3.29 us
    pallas_call x1, Pallas kernels, moved_weights(): pl.pallas_call(lambda *refs: moved_kernel(count, features, *refs), in_spe...  3.26 us
    ppermute x13, starting transfers between devices, local(): pair = lambda value: lax.ppermute(value, 'pair', PAIR)  2.46 us
    pallas_call x1, Pallas kernels, index_table(): pl.pallas_call(lambda *refs: index_kernel(small, *refs), in_specs=[hbm_sp...  2.33 us
  transfers between devices with their start and end apart: 25, of which 13 were waited for; matrix products, arithmetic and copies ran while one was open for 0% of the time, Pallas kernels for 22%

profile of v9, /device:TPU:0, one launch (start us, length us, event | category | flops | bytes accessed | tf_op | source)
XLA Modules:
  0.0 47.3 jit_solution(1602220352310956454)
XLA Ops:
  0.6 3.1 %collective-permute-start = (bf16[128,256]{1,0:T(8,128)(2,1)}, bf16[128,256]{1,0:T(8,128)(2,1)S(1)}, u32[]{:S(2)}, u32[]{:S(2)}) collective-permute-start(bf16[128,256]{1,0:T(8,128)(2,1)} %refs_3_.1), channel_id=1, source_target_pairs={{0,4},{4,0},{8,12},{12,8},{1,5},{5,1},{9,13},{13,9},{2,6},{6,2},{1... | collective-permute-start | bytes 196616 | tf_op jit(solution)/shard_map/ppermute | solution.py:472
  3.7 2.5 %collective-permute-start.10 = (bf16[128,256]{1,0:T(8,128)(2,1)}, bf16[128,256]{1,0:T(8,128)(2,1)S(1)}, u32[]{:S(2)}, u32[]{:S(2)}) collective-permute-start(bf16[128,256]{1,0:T(8,128)(2,1)} %refs_3_.1), channel_id=1, source_target_pairs={{0,12},{4,8},{8,4},{12,0},{1,13},{5,9},{9,5},{13,1},{2,14},{6,10},... | collective-permute-start | bytes 196616 | tf_op jit(solution)/shard_map/ppermute | solution.py:472
  6.2 0.1 collective-permute-start.8
  6.3 2.8 %collective-permute-start.4 = (bf16[128,256]{1,0:T(8,128)(2,1)}, bf16[128,256]{1,0:T(8,128)(2,1)S(1)}, u32[]{:S(2)}, u32[]{:S(2)}) collective-permute-start(bf16[128,256]{1,0:T(8,128)(2,1)} %refs_1_.3), channel_id=1, source_target_pairs={{0,8},{4,12},{8,0},{12,4},{1,9},{5,13},{9,1},{13,5},{2,10},{6,14},... | collective-permute-start | bytes 196616 | tf_op jit(solution)/shard_map/ppermute | solution.py:472
  9.1 0.7 %collective-permute-start.2 = (bf16[128,256]{1,0:T(8,128)(2,1)}, bf16[128,256]{1,0:T(8,128)(2,1)S(1)}, u32[]{:S(2)}, u32[]{:S(2)}) collective-permute-start(bf16[128,256]{1,0:T(8,128)(2,1)} %refs_1_.3), channel_id=1, source_target_pairs={{0,4},{4,0},{8,12},{12,8},{1,5},{5,1},{9,13},{13,9},{2,6},{6,2},{1... | collective-permute-start | bytes 196616 | tf_op jit(solution)/shard_map/ppermute | solution.py:472
  9.8 2.3 %index_table.1 = (s32[6,8]{1,0:T(8,128)S(4)}, bf16[128,256]{1,0:T(8,128)(2,1)S(1)}, bf16[8,512,1536]{2,1,0:T(8,128)(2,1)S(1)}) custom-call(s32[64]{0:T(128)} %refs_0_, s32[8]{0:T(128)} %refs_1_.2, s32[8]{0:T(128)} %refs_2_.1, bf16[128,256]{1,0:T(8,128)(2,1)} %refs_3_.1, bf16[4096,256]{1,0:T(8,128)(2,1)} %refs_4_.1, bf16[4096,256]{1,0:T(8,128)(2,1)} %refs_5_.1), custom_call_target="tpu_custom_call" | custom-call | tf_op jit(solution)/shard_map/index_table/pallas_call | solution.py:122
  12.1 0.1 collective-permute-start.7
  12.2 0.0 collective-permute-done.10.refs_7_
  12.2 0.5 %collective-permute-start.6 = (bf16[128,256]{1,0:T(8,128)(2,1)S(1)}, bf16[128,256]{1,0:T(8,128)(2,1)S(1)}, u32[]{:S(2)}, u32[]{:S(2)}) collective-permute-start(bf16[128,256]{1,0:T(8,128)(2,1)S(1)} %get-tuple-element.35.refs_1_), channel_id=1, source_target_pairs={{0,1},{1,0},{2,3},{3,2},{4,5},{5,4},{6,7},{7,6},{8,9},{9,8},{10,11... | collective-permute-start | bytes 196616 | tf_op jit(solution)/shard_map/ppermute | solution.py:471
  12.7 1.8 %collective-permute-done.8.refs_5_ = bf16[128,256]{1,0:T(8,128)(2,1)S(1)} collective-permute-done((bf16[128,256]{1,0:T(8,128)(2,1)}, bf16[128,256]{1,0:T(8,128)(2,1)S(1)}, u32[]{:S(2)}, u32[]{:S(2)}) %collective-permute-start.8) | collective-permute-done | bytes 65568 | tf_op jit(solution)/shard_map/ppermute | solution.py:472
  14.5 1.3 %collective-permute-done.4.refs_5_ = bf16[128,256]{1,0:T(8,128)(2,1)S(1)} collective-permute-done((bf16[128,256]{1,0:T(8,128)(2,1)}, bf16[128,256]{1,0:T(8,128)(2,1)S(1)}, u32[]{:S(2)}, u32[]{:S(2)}) %collective-permute-start.4) | collective-permute-done | bytes 65568 | tf_op jit(solution)/shard_map/ppermute | solution.py:472
  15.8 0.1 collective-permute-done.2.refs_3_
  15.9 0.0 collective-permute-start.5
  15.9 0.5 collective-permute-start.1
  16.4 0.1 collective-permute-start.3
  16.5 0.0 collective-permute-done.11.refs_8_
  16.5 0.5 %collective-permute-done.9.refs_6_ = bf16[128,256]{1,0:T(8,128)(2,1)S(1)} collective-permute-done((bf16[128,256]{1,0:T(8,128)(2,1)S(1)}, bf16[128,256]{1,0:T(8,128)(2,1)S(1)}, u32[]{:S(2)}, u32[]{:S(2)}) %collective-permute-start.9) | collective-permute-done | bytes 65568 | tf_op jit(solution)/shard_map/ppermute | solution.py:471
  17.0 3.5 %block_weights.1 = (f32[2080,128]{1,0:T(8,128)S(1)}, bf16[8,512,1536]{2,1,0:T(8,128)(2,1)S(1)}) custom-call(s32[6,8]{1,0:T(8,128)S(4)} %get-tuple-element.34.refs_0_.meta, bf16[128,256]{1,0:T(8,128)(2,1)S(1)} %get-tuple-element.35.refs_1_, bf16[128,256]{1,0:T(8,128)(2,1)S(1)} %collective-permute-done.6.refs_2_, ...), custom_call_target="tpu_custom_call", output_to_operand_aliasing={{1}: (9, {})} | custom-call | tf_op jit(solution)/shard_map/block_weights/pallas_call | solution.py:218
  20.6 0.2 collective-permute-start.12
  20.8 0.4 collective-permute-start.13
  21.1 0.7 %collective-permute-done.12.refs_6_ = bf16[128,256]{1,0:T(8,128)(2,1)S(1)} collective-permute-done((bf16[128,256]{1,0:T(8,128)(2,1)S(1)}, bf16[128,256]{1,0:T(8,128)(2,1)S(1)}, u32[]{:S(2)}, u32[]{:S(2)}) %collective-permute-start.12) | collective-permute-done | bytes 65568 | tf_op jit(solution)/shard_map/ppermute | solution.py:471
  21.9 0.2 collective-permute-done.13.refs_8_
  22.0 3.3 %moved_weights.1 = (f32[2112,128]{1,0:T(8,128)S(1)}, f32[2,8,512]{2,1,0:T(8,128)S(1)}, bf16[8,512,1536]{2,1,0:T(8,128)(2,1)S(1)}) custom-call(s32[6,8]{1,0:T(8,128)S(4)} %get-tuple-element.34.refs_0_.meta, bf16[128,256]{1,0:T(8,128)(2,1)S(1)} %copy-done, bf16[128,256]{1,0:T(8,128)(2,1)S(1)} %collective-permute-done.1.refs_2_, ...), custom_call_target="tpu_custom_call", output_to_operand_aliasing={{2}: (10, {})} | custom-call | tf_op jit(solution)/shard_map/moved_weights/pallas_call | solution.py:307
  25.3 1.5 %collective-permute-start.15 = (f32[2,8,512]{2,1,0:T(8,128)S(1)}, f32[2,8,512]{2,1,0:T(8,128)S(1)}, u32[]{:S(2)}, u32[]{:S(2)}) collective-permute-start(f32[2,8,512]{2,1,0:T(8,128)S(1)} %get-tuple-element.43.refs_1_), channel_id=1, source_target_pairs={{0,4},{4,0},{8,12},{12,8},{1,5},{5,1},{9,13},{13,9},{2,6},{6,2},{1... | collective-permute-start | bytes 98312 | tf_op jit(solution)/shard_map/ppermute | solution.py:472
  26.8 1.5 %collective-permute-start.16 = (f32[2,8,512]{2,1,0:T(8,128)S(1)}, f32[2,8,512]{2,1,0:T(8,128)S(1)}, u32[]{:S(2)}, u32[]{:S(2)}) collective-permute-start(f32[2,8,512]{2,1,0:T(8,128)S(1)} %get-tuple-element.43.refs_1_), channel_id=1, source_target_pairs={{0,8},{4,12},{8,0},{12,4},{1,9},{5,13},{9,1},{13,5},{2,10},{6,14},... | collective-permute-start | bytes 98312 | tf_op jit(solution)/shard_map/ppermute | solution.py:472
  28.2 1.5 %collective-permute-start.17 = (f32[2,8,512]{2,1,0:T(8,128)S(1)}, f32[2,8,512]{2,1,0:T(8,128)S(1)}, u32[]{:S(2)}, u32[]{:S(2)}) collective-permute-start(f32[2,8,512]{2,1,0:T(8,128)S(1)} %get-tuple-element.43.refs_1_), channel_id=1, source_target_pairs={{0,12},{4,8},{8,4},{12,0},{1,13},{5,9},{9,5},{13,1},{2,14},{6,10},... | collective-permute-start | bytes 98312 | tf_op jit(solution)/shard_map/ppermute | solution.py:472
  29.7 0.0 collective-permute-start.14
  29.8 1.3 %query_sums.1 = (f32[8,2,256,128]{3,2,1,0:T(8,128)S(1)}, bf16[8,512,1536]{2,1,0:T(8,128)(2,1)S(1)}) custom-call(bf16[8,512,1536]{2,1,0:T(8,128)(2,1)S(1)} %get-tuple-element.44.state), custom_call_target="tpu_custom_call", output_to_operand_aliasing={{1}: (0, {})} | custom-call | tf_op jit(solution)/shard_map/query_sums/pallas_call | solution.py:340
  31.0 0.0 collective-permute-done.15.refs_3_
  31.0 1.2 %collective-permute-done.16.refs_5_ = f32[2,8,512]{2,1,0:T(8,128)S(1)} collective-permute-done((f32[2,8,512]{2,1,0:T(8,128)S(1)}, f32[2,8,512]{2,1,0:T(8,128)S(1)}, u32[]{:S(2)}, u32[]{:S(2)}) %collective-permute-start.16) | collective-permute-done | bytes 32800 | tf_op jit(solution)/shard_map/ppermute | solution.py:472
  32.2 1.7 %collective-permute-done.17.refs_7_ = f32[2,8,512]{2,1,0:T(8,128)S(1)} collective-permute-done((f32[2,8,512]{2,1,0:T(8,128)S(1)}, f32[2,8,512]{2,1,0:T(8,128)S(1)}, u32[]{:S(2)}, u32[]{:S(2)}) %collective-permute-start.17) | collective-permute-done | bytes 32800 | tf_op jit(solution)/shard_map/ppermute | solution.py:472
  33.9 0.0 collective-permute-start.18
  33.9 0.5 %collective-permute-start.19 = (f32[2,8,512]{2,1,0:T(8,128)S(1)}, f32[2,8,512]{2,1,0:T(8,128)S(1)}, u32[]{:S(2)}, u32[]{:S(2)}) collective-permute-start(f32[2,8,512]{2,1,0:T(8,128)S(1)} %collective-permute-done.16.refs_5_), channel_id=1, source_target_pairs={{0,1},{1,0},{2,3},{3,2},{4,5},{5,4},{6,7},{7,6},{8,9},{9,8},{10,11... | collective-permute-start | bytes 98312 | tf_op jit(solution)/shard_map/ppermute | solution.py:471
  34.4 0.0 collective-permute-start.20
  34.4 0.0 collective-permute-done.14.refs_2_
  34.5 0.7 %collective-permute-done.18.refs_4_ = f32[2,8,512]{2,1,0:T(8,128)S(1)} collective-permute-done((f32[2,8,512]{2,1,0:T(8,128)S(1)}, f32[2,8,512]{2,1,0:T(8,128)S(1)}, u32[]{:S(2)}, u32[]{:S(2)}) %collective-permute-start.18) | collective-permute-done | bytes 32800 | tf_op jit(solution)/shard_map/ppermute | solution.py:471
  35.1 0.2 collective-permute-done.19.refs_6_
  35.3 0.3 collective-permute-done.20.refs_8_
  35.7 0.6 %query_grads.1 = (f32[8,512]{1,0:T(8,128)S(1)}, f32[8,512]{1,0:T(8,128)S(1)}, f32[4,128,256]{2,1,0:T(8,128)S(1)}, bf16[4,128,256]{2,1,0:T(8,128)(2,1)S(1)}) custom-call(s32[6,8]{1,0:T(8,128)S(4)} %get-tuple-element.34.refs_0_.meta, f32[2,8,512]{2,1,0:T(8,128)S(1)} %get-tuple-element.43.refs_1_, f32[2,8,512]{2,1,0:T(8,128)S(1)} %collective-permute-done.14.refs_2_, ...), custom_call_target="tpu_custom_call" | custom-call | tf_op jit(solution)/shard_map/query_grads/pallas_call | solution.py:399
  36.2 0.2 collective-permute-start.21
  36.5 1.4 %collective-permute-done.21 = bf16[4,128,256]{2,1,0:T(8,128)(2,1)S(1)} collective-permute-done((bf16[4,128,256]{2,1,0:T(8,128)(2,1)S(1)}, bf16[4,128,256]{2,1,0:T(8,128)(2,1)S(1)}, u32[]{:S(2)}, u32[]{:S(2)}) %collective-permute-start.21) | collective-permute-done | bytes 262176 | tf_op jit(solution)/shard_map/ppermute | solution.py:471
  37.8 0.1 fusion.4
  37.9 0.1 collective-permute-start.22
  38.0 2.1 %collective-permute-start.23 = (bf16[128,256]{1,0:T(8,128)(2,1)S(1)}, bf16[128,256]{1,0:T(8,128)(2,1)S(1)}, u32[]{:S(2)}, u32[]{:S(2)}) collective-permute-start(bf16[128,256]{1,0:T(8,128)(2,1)S(1)} %get-tuple-element.63), channel_id=1, source_target_pairs={{0,8},{4,12},{8,0},{12,4},{1,9},{5,13},{9,1},{13,5},{2,10},{6,14},... | collective-permute-start | bytes 196616 | tf_op jit(solution)/shard_map/ppermute | solution.py:472
  40.1 2.3 %collective-permute-start.24 = (bf16[128,256]{1,0:T(8,128)(2,1)S(1)}, bf16[128,256]{1,0:T(8,128)(2,1)S(1)}, u32[]{:S(2)}, u32[]{:S(2)}) collective-permute-start(bf16[128,256]{1,0:T(8,128)(2,1)S(1)} %get-tuple-element.62), channel_id=1, source_target_pairs={{0,12},{4,8},{8,4},{12,0},{1,13},{5,9},{9,5},{13,1},{2,14},{6,10},... | collective-permute-start | bytes 196616 | tf_op jit(solution)/shard_map/ppermute | solution.py:472
  42.4 3.3 %row_grads.1 = (bf16[4096,256]{1,0:T(8,128)(2,1)}, bf16[4096,256]{1,0:T(8,128)(2,1)}) custom-call(s32[6,8]{1,0:T(8,128)S(4)} %get-tuple-element.34.refs_0_.meta, f32[8,512]{1,0:T(8,128)S(1)} %get-tuple-element.54.c_ref, f32[8,512]{1,0:T(8,128)S(1)} %get-tuple-element.55.d_ref, f32[2080,128]{1,0:T(8,128)S(1)} %get-tuple-element.41.refs_9_.q_side, ...), custom_call_target="tpu_custom_call" | custom-call | tf_op jit(solution)/shard_map/row_grads/pallas_call | solution.py:452
  45.7 0.9 %collective-permute-done.23 = bf16[128,256]{1,0:T(8,128)(2,1)S(1)} collective-permute-done((bf16[128,256]{1,0:T(8,128)(2,1)S(1)}, bf16[128,256]{1,0:T(8,128)(2,1)S(1)}, u32[]{:S(2)}, u32[]{:S(2)}) %collective-permute-start.23) | collective-permute-done | bytes 65568 | tf_op jit(solution)/shard_map/ppermute | solution.py:472
  46.7 0.7 %fusion.3 = bf16[128,256]{1,0:T(8,128)(2,1)} fusion(f32[4,128,256]{2,1,0:T(8,128)S(1)} %get-tuple-element.60, bf16[128,256]{1,0:T(8,128)(2,1)S(1)} %collective-permute-done.24, bf16[128,256]{1,0:T(8,128)(2,1)S(1)} %collective-permute-done.23, bf16[128,256]{1,0:T(8,128)(2,1)S(1)} %collective-permute-done.22), kind=kLoop, calls=%fused_computation.5 | loop fusion | flops 229376 | bytes 393216 | tf_op jit(solution)/shard_map/convert_element_type | solution.py:529
  (13 shorter events, 0.0 us)
Async XLA Ops:
  0.6 15.3 %copy-start = (bf16[128,256]{1,0:T(8,128)(2,1)S(1)}, bf16[128,256]{1,0:T(8,128)(2,1)}, u32[]{:S(2)}) copy-start(bf16[128,256]{1,0:T(8,128)(2,1)} %refs_1_.3) | copy-start | bytes 196612
  0.6 9.2 %collective-permute-start = (bf16[128,256]{1,0:T(8,128)(2,1)}, bf16[128,256]{1,0:T(8,128)(2,1)S(1)}, u32[]{:S(2)}, u32[]{:S(2)}) collective-permute-start(bf16[128,256]{1,0:T(8,128)(2,1)} %refs_3_.1), channel_id=1, source_target_pairs={{0,4},{4,0},{8,12},{12,8},{1,5},{5,1},{9,13},{13,9},{2,6},{6,2},{1... | collective-permute-start | bytes 196616 | tf_op jit(solution)/shard_map/ppermute | solution.py:472
  3.7 8.5 %collective-permute-start.10 = (bf16[128,256]{1,0:T(8,128)(2,1)}, bf16[128,256]{1,0:T(8,128)(2,1)S(1)}, u32[]{:S(2)}, u32[]{:S(2)}) collective-permute-start(bf16[128,256]{1,0:T(8,128)(2,1)} %refs_3_.1), channel_id=1, source_target_pairs={{0,12},{4,8},{8,4},{12,0},{1,13},{5,9},{9,5},{13,1},{2,14},{6,10},... | collective-permute-start | bytes 196616 | tf_op jit(solution)/shard_map/ppermute | solution.py:472
  6.2 8.3 %collective-permute-start.8 = (bf16[128,256]{1,0:T(8,128)(2,1)}, bf16[128,256]{1,0:T(8,128)(2,1)S(1)}, u32[]{:S(2)}, u32[]{:S(2)}) collective-permute-start(bf16[128,256]{1,0:T(8,128)(2,1)} %refs_3_.1), channel_id=1, source_target_pairs={{0,8},{4,12},{8,0},{12,4},{1,9},{5,13},{9,1},{13,5},{2,10},{6,14},... | collective-permute-start | bytes 196616 | tf_op jit(solution)/shard_map/ppermute | solution.py:472
  6.3 9.5 %collective-permute-start.4 = (bf16[128,256]{1,0:T(8,128)(2,1)}, bf16[128,256]{1,0:T(8,128)(2,1)S(1)}, u32[]{:S(2)}, u32[]{:S(2)}) collective-permute-start(bf16[128,256]{1,0:T(8,128)(2,1)} %refs_1_.3), channel_id=1, source_target_pairs={{0,8},{4,12},{8,0},{12,4},{1,9},{5,13},{9,1},{13,5},{2,10},{6,14},... | collective-permute-start | bytes 196616 | tf_op jit(solution)/shard_map/ppermute | solution.py:472
  9.1 6.8 %collective-permute-start.2 = (bf16[128,256]{1,0:T(8,128)(2,1)}, bf16[128,256]{1,0:T(8,128)(2,1)S(1)}, u32[]{:S(2)}, u32[]{:S(2)}) collective-permute-start(bf16[128,256]{1,0:T(8,128)(2,1)} %refs_1_.3), channel_id=1, source_target_pairs={{0,4},{4,0},{8,12},{12,8},{1,5},{5,1},{9,13},{13,9},{2,6},{6,2},{1... | collective-permute-start | bytes 196616 | tf_op jit(solution)/shard_map/ppermute | solution.py:472
  12.1 3.8 %collective-permute-start.7 = (bf16[128,256]{1,0:T(8,128)(2,1)S(1)}, bf16[128,256]{1,0:T(8,128)(2,1)S(1)}, u32[]{:S(2)}, u32[]{:S(2)}) collective-permute-start(bf16[128,256]{1,0:T(8,128)(2,1)S(1)} %collective-permute-done.refs_3_), channel_id=1, source_target_pairs={{0,1},{1,0},{2,3},{3,2},{4,5},{5,4},{6,7},{7,6},{8,9},{9,8},{10,11... | collective-permute-start | bytes 196616 | tf_op jit(solution)/shard_map/ppermute | solution.py:471
  12.2 4.2 %collective-permute-start.6 = (bf16[128,256]{1,0:T(8,128)(2,1)S(1)}, bf16[128,256]{1,0:T(8,128)(2,1)S(1)}, u32[]{:S(2)}, u32[]{:S(2)}) collective-permute-start(bf16[128,256]{1,0:T(8,128)(2,1)S(1)} %get-tuple-element.35.refs_1_), channel_id=1, source_target_pairs={{0,1},{1,0},{2,3},{3,2},{4,5},{5,4},{6,7},{7,6},{8,9},{9,8},{10,11... | collective-permute-start | bytes 196616 | tf_op jit(solution)/shard_map/ppermute | solution.py:471
  14.5 2.0 %collective-permute-start.11 = (bf16[128,256]{1,0:T(8,128)(2,1)S(1)}, bf16[128,256]{1,0:T(8,128)(2,1)S(1)}, u32[]{:S(2)}, u32[]{:S(2)}) collective-permute-start(bf16[128,256]{1,0:T(8,128)(2,1)S(1)} %collective-permute-done.10.refs_7_), channel_id=1, source_target_pairs={{0,1},{1,0},{2,3},{3,2},{4,5},{5,4},{6,7},{7,6},{8,9},{9,8},{10,11... | collective-permute-start | bytes 196616 | tf_op jit(solution)/shard_map/ppermute | solution.py:471
  15.8 1.3 %collective-permute-start.9 = (bf16[128,256]{1,0:T(8,128)(2,1)S(1)}, bf16[128,256]{1,0:T(8,128)(2,1)S(1)}, u32[]{:S(2)}, u32[]{:S(2)}) collective-permute-start(bf16[128,256]{1,0:T(8,128)(2,1)S(1)} %collective-permute-done.8.refs_5_), channel_id=1, source_target_pairs={{0,1},{1,0},{2,3},{3,2},{4,5},{5,4},{6,7},{7,6},{8,9},{9,8},{10,11... | collective-permute-start | bytes 196616 | tf_op jit(solution)/shard_map/ppermute | solution.py:471
  15.9 4.6 %collective-permute-start.5 = (bf16[128,256]{1,0:T(8,128)(2,1)S(1)}, bf16[128,256]{1,0:T(8,128)(2,1)S(1)}, u32[]{:S(2)}, u32[]{:S(2)}) collective-permute-start(bf16[128,256]{1,0:T(8,128)(2,1)S(1)} %collective-permute-done.4.refs_5_), channel_id=1, source_target_pairs={{0,4},{4,0},{8,12},{12,8},{1,5},{5,1},{9,13},{13,9},{2,6},{6,2},{1... | collective-permute-start | bytes 196616 | tf_op jit(solution)/shard_map/ppermute | solution.py:472
  15.9 5.2 %collective-permute-start.1 = (bf16[128,256]{1,0:T(8,128)(2,1)S(1)}, bf16[128,256]{1,0:T(8,128)(2,1)S(1)}, u32[]{:S(2)}, u32[]{:S(2)}) collective-permute-start(bf16[128,256]{1,0:T(8,128)(2,1)S(1)} %copy-done), channel_id=1, source_target_pairs={{0,1},{1,0},{2,3},{3,2},{4,5},{5,4},{6,7},{7,6},{8,9},{9,8},{10,11... | collective-permute-start | bytes 196616 | tf_op jit(solution)/shard_map/ppermute | solution.py:471
  16.4 4.7 %collective-permute-start.3 = (bf16[128,256]{1,0:T(8,128)(2,1)S(1)}, bf16[128,256]{1,0:T(8,128)(2,1)S(1)}, u32[]{:S(2)}, u32[]{:S(2)}) collective-permute-start(bf16[128,256]{1,0:T(8,128)(2,1)S(1)} %collective-permute-done.2.refs_3_), channel_id=1, source_target_pairs={{0,1},{1,0},{2,3},{3,2},{4,5},{5,4},{6,7},{7,6},{8,9},{9,8},{10,11... | collective-permute-start | bytes 196616 | tf_op jit(solution)/shard_map/ppermute | solution.py:471
  20.6 1.3 %collective-permute-start.12 = (bf16[128,256]{1,0:T(8,128)(2,1)S(1)}, bf16[128,256]{1,0:T(8,128)(2,1)S(1)}, u32[]{:S(2)}, u32[]{:S(2)}) collective-permute-start(bf16[128,256]{1,0:T(8,128)(2,1)S(1)} %collective-permute-done.4.refs_5_), channel_id=1, source_target_pairs={{0,1},{1,0},{2,3},{3,2},{4,5},{5,4},{6,7},{7,6},{8,9},{9,8},{10,11... | collective-permute-start | bytes 196616 | tf_op jit(solution)/shard_map/ppermute | solution.py:471
  20.8 1.3 %collective-permute-start.13 = (bf16[128,256]{1,0:T(8,128)(2,1)S(1)}, bf16[128,256]{1,0:T(8,128)(2,1)S(1)}, u32[]{:S(2)}, u32[]{:S(2)}) collective-permute-start(bf16[128,256]{1,0:T(8,128)(2,1)S(1)} %collective-permute-done.5.refs_7_), channel_id=1, source_target_pairs={{0,1},{1,0},{2,3},{3,2},{4,5},{5,4},{6,7},{7,6},{8,9},{9,8},{10,11... | collective-permute-start | bytes 196616 | tf_op jit(solution)/shard_map/ppermute | solution.py:471
  25.3 5.7 %collective-permute-start.15 = (f32[2,8,512]{2,1,0:T(8,128)S(1)}, f32[2,8,512]{2,1,0:T(8,128)S(1)}, u32[]{:S(2)}, u32[]{:S(2)}) collective-permute-start(f32[2,8,512]{2,1,0:T(8,128)S(1)} %get-tuple-element.43.refs_1_), channel_id=1, source_target_pairs={{0,4},{4,0},{8,12},{12,8},{1,5},{5,1},{9,13},{13,9},{2,6},{6,2},{1... | collective-permute-start | bytes 98312 | tf_op jit(solution)/shard_map/ppermute | solution.py:472
  26.8 5.5 %collective-permute-start.16 = (f32[2,8,512]{2,1,0:T(8,128)S(1)}, f32[2,8,512]{2,1,0:T(8,128)S(1)}, u32[]{:S(2)}, u32[]{:S(2)}) collective-permute-start(f32[2,8,512]{2,1,0:T(8,128)S(1)} %get-tuple-element.43.refs_1_), channel_id=1, source_target_pairs={{0,8},{4,12},{8,0},{12,4},{1,9},{5,13},{9,1},{13,5},{2,10},{6,14},... | collective-permute-start | bytes 98312 | tf_op jit(solution)/shard_map/ppermute | solution.py:472
  28.2 5.7 %collective-permute-start.17 = (f32[2,8,512]{2,1,0:T(8,128)S(1)}, f32[2,8,512]{2,1,0:T(8,128)S(1)}, u32[]{:S(2)}, u32[]{:S(2)}) collective-permute-start(f32[2,8,512]{2,1,0:T(8,128)S(1)} %get-tuple-element.43.refs_1_), channel_id=1, source_target_pairs={{0,12},{4,8},{8,4},{12,0},{1,13},{5,9},{9,5},{13,1},{2,14},{6,10},... | collective-permute-start | bytes 98312 | tf_op jit(solution)/shard_map/ppermute | solution.py:472
  29.7 4.7 %collective-permute-start.14 = (f32[2,8,512]{2,1,0:T(8,128)S(1)}, f32[2,8,512]{2,1,0:T(8,128)S(1)}, u32[]{:S(2)}, u32[]{:S(2)}) collective-permute-start(f32[2,8,512]{2,1,0:T(8,128)S(1)} %get-tuple-element.43.refs_1_), channel_id=1, source_target_pairs={{0,1},{1,0},{2,3},{3,2},{4,5},{5,4},{6,7},{7,6},{8,9},{9,8},{10,11... | collective-permute-start | bytes 98312 | tf_op jit(solution)/shard_map/ppermute | solution.py:471
  33.9 1.2 %collective-permute-start.18 = (f32[2,8,512]{2,1,0:T(8,128)S(1)}, f32[2,8,512]{2,1,0:T(8,128)S(1)}, u32[]{:S(2)}, u32[]{:S(2)}) collective-permute-start(f32[2,8,512]{2,1,0:T(8,128)S(1)} %collective-permute-done.15.refs_3_), channel_id=1, source_target_pairs={{0,1},{1,0},{2,3},{3,2},{4,5},{5,4},{6,7},{7,6},{8,9},{9,8},{10,11... | collective-permute-start | bytes 98312 | tf_op jit(solution)/shard_map/ppermute | solution.py:471
  33.9 1.4 %collective-permute-start.19 = (f32[2,8,512]{2,1,0:T(8,128)S(1)}, f32[2,8,512]{2,1,0:T(8,128)S(1)}, u32[]{:S(2)}, u32[]{:S(2)}) collective-permute-start(f32[2,8,512]{2,1,0:T(8,128)S(1)} %collective-permute-done.16.refs_5_), channel_id=1, source_target_pairs={{0,1},{1,0},{2,3},{3,2},{4,5},{5,4},{6,7},{7,6},{8,9},{9,8},{10,11... | collective-permute-start | bytes 98312 | tf_op jit(solution)/shard_map/ppermute | solution.py:471
  34.4 1.2 %collective-permute-start.20 = (f32[2,8,512]{2,1,0:T(8,128)S(1)}, f32[2,8,512]{2,1,0:T(8,128)S(1)}, u32[]{:S(2)}, u32[]{:S(2)}) collective-permute-start(f32[2,8,512]{2,1,0:T(8,128)S(1)} %collective-permute-done.17.refs_7_), channel_id=1, source_target_pairs={{0,1},{1,0},{2,3},{3,2},{4,5},{5,4},{6,7},{7,6},{8,9},{9,8},{10,11... | collective-permute-start | bytes 98312 | tf_op jit(solution)/shard_map/ppermute | solution.py:471
  36.2 1.6 %collective-permute-start.21 = (bf16[4,128,256]{2,1,0:T(8,128)(2,1)S(1)}, bf16[4,128,256]{2,1,0:T(8,128)(2,1)S(1)}, u32[]{:S(2)}, u32[]{:S(2)}) collective-permute-start(bf16[4,128,256]{2,1,0:T(8,128)(2,1)S(1)} %get-tuple-element.52), channel_id=1, source_target_pairs={{0,1},{1,0},{2,3},{3,2},{4,5},{5,4},{6,7},{7,6},{8,9},{9,8},{10,11... | collective-permute-start | bytes 786440 | tf_op jit(solution)/shard_map/ppermute | solution.py:471
  37.9 7.8 %collective-permute-start.22 = (bf16[128,256]{1,0:T(8,128)(2,1)S(1)}, bf16[128,256]{1,0:T(8,128)(2,1)S(1)}, u32[]{:S(2)}, u32[]{:S(2)}) collective-permute-start(bf16[128,256]{1,0:T(8,128)(2,1)S(1)} %get-tuple-element.61), channel_id=1, source_target_pairs={{0,4},{4,0},{8,12},{12,8},{1,5},{5,1},{9,13},{13,9},{2,6},{6,2},{1... | collective-permute-start | bytes 196616 | tf_op jit(solution)/shard_map/ppermute | solution.py:472
  38.0 8.6 %collective-permute-start.23 = (bf16[128,256]{1,0:T(8,128)(2,1)S(1)}, bf16[128,256]{1,0:T(8,128)(2,1)S(1)}, u32[]{:S(2)}, u32[]{:S(2)}) collective-permute-start(bf16[128,256]{1,0:T(8,128)(2,1)S(1)} %get-tuple-element.63), channel_id=1, source_target_pairs={{0,8},{4,12},{8,0},{12,4},{1,9},{5,13},{9,1},{13,5},{2,10},{6,14},... | collective-permute-start | bytes 196616 | tf_op jit(solution)/shard_map/ppermute | solution.py:472
  40.1 6.6 %collective-permute-start.24 = (bf16[128,256]{1,0:T(8,128)(2,1)S(1)}, bf16[128,256]{1,0:T(8,128)(2,1)S(1)}, u32[]{:S(2)}, u32[]{:S(2)}) collective-permute-start(bf16[128,256]{1,0:T(8,128)(2,1)S(1)} %get-tuple-element.62), channel_id=1, source_target_pairs={{0,12},{4,8},{8,4},{12,0},{1,13},{5,9},{9,5},{13,1},{2,14},{6,10},... | collective-permute-start | bytes 196616 | tf_op jit(solution)/shard_map/ppermute | solution.py:472

commit v10 on v9

--- a/solution.py
+++ b/solution.py
@@ -475,10 +475,11 @@
         small, entries, train_rows, test_rows, query_rows, key_rows, value_rows
     )
     if small:
-        near = [step(query_rows, s) for s in (1, 2, 3)]
+        near = [step(query_rows, 1), step(query_rows, 2)]
+        near.append(step(near[1], 1))
         near_grads = [step(cotangent, 1), step(cotangent, 2)]
         near_grads.append(step(near_grads[1], 1))
-        block_table, near[0] = after(block_table, near[0])
+        block_table, _ = after(block_table, near[1])
         meta, own, state = index(block_table)
         near[0], meta = after(near[0], meta)
         queries = [own, pair(own)]

time: 47.5 us -> 48.3 us (1.017)
  starting transfers between devices: 20.5 us -> 21.6 us
    ppermute x12, starting transfers between devices: 18.1 us -> 18.7 us  [local(): lax.ppermute(value, 'rows', [(z, z ^ s) for z in range(4)])]
    ppermute x13, waiting for transfers between devices: 4.03 us -> 3.49 us  [local(): pair = lambda value: lax.ppermute(value, 'pair', PAIR)]
  transfers between devices with their start and end apart: 25 -> 25, of which waited for: 13 -> 11; matrix products, arithmetic and copies ran while one was open for 0% -> 0% of each run, Pallas kernels for 22% -> 22%
where the time goes in v10:
time: 48.3 us; the launch traced here: 48.2 us
  starting transfers between devices  21.6 us (45%)
  Pallas kernels  14.2 us (29%)
  waiting for transfers between devices  10.8 us (22%)
  between operations  0.78 us (2%)
  other arithmetic  0.74 us (2%)
    ppermute x12, starting transfers between devices, local(): lax.ppermute(value, 'rows', [(z, z ^ s) for z in range(4)])  18.7 us
    ppermute x12, waiting for transfers between devices, local(): lax.ppermute(value, 'rows', [(z, z ^ s) for z in range(4)])  7.31 us
    ppermute x13, waiting for transfers between devices, local(): pair = lambda value: lax.ppermute(value, 'pair', PAIR)  3.49 us
    pallas_call x1, Pallas kernels, block_weights(): pl.pallas_call(lambda *refs: weights_kernel(count, features, *refs), in_s...  3.48 us
    pallas_call x1, Pallas kernels, row_grads(): pl.pallas_call(row_grads_kernel, in_specs=[smem_spec()] + [vmem_spec()] *...  3.29 us
    pallas_call x1, Pallas kernels, moved_weights(): pl.pallas_call(lambda *refs: moved_kernel(count, features, *refs), in_spe...  3.26 us
    ppermute x13, starting transfers between devices, local(): pair = lambda value: lax.ppermute(value, 'pair', PAIR)  2.9 us
    pallas_call x1, Pallas kernels, index_table(): pl.pallas_call(lambda *refs: index_kernel(small, *refs), in_specs=[hbm_sp...  2.33 us
  transfers between devices with their start and end apart: 25, of which 11 were waited for; matrix products, arithmetic and copies ran while one was open for 0% of the time, Pallas kernels for 22%

profile of v10, /device:TPU:0, one launch (start us, length us, event | category | flops | bytes accessed | tf_op | source)
XLA Modules:
  0.0 48.2 jit_solution(11408042468399507621)
XLA Ops:
  0.6 4.1 %collective-permute-start.1 = (bf16[128,256]{1,0:T(8,128)(2,1)}, bf16[128,256]{1,0:T(8,128)(2,1)S(1)}, u32[]{:S(2)}, u32[]{:S(2)}) collective-permute-start(bf16[128,256]{1,0:T(8,128)(2,1)} %refs_3_.1), channel_id=1, source_target_pairs={{0,8},{4,12},{8,0},{12,4},{1,9},{5,13},{9,1},{13,5},{2,10},{6,14},... | collective-permute-start | bytes 196616 | tf_op jit(solution)/shard_map/ppermute | solution.py:472
  4.7 1.6 %collective-permute-start = (bf16[128,256]{1,0:T(8,128)(2,1)}, bf16[128,256]{1,0:T(8,128)(2,1)S(1)}, u32[]{:S(2)}, u32[]{:S(2)}) collective-permute-start(bf16[128,256]{1,0:T(8,128)(2,1)} %refs_3_.1), channel_id=1, source_target_pairs={{0,4},{4,0},{8,12},{12,8},{1,5},{5,1},{9,13},{13,9},{2,6},{6,2},{1... | collective-permute-start | bytes 196616 | tf_op jit(solution)/shard_map/ppermute | solution.py:472
  6.3 0.3 collective-permute-start.5
  6.7 1.4 %collective-permute-done.1.refs_5_ = bf16[128,256]{1,0:T(8,128)(2,1)S(1)} collective-permute-done((bf16[128,256]{1,0:T(8,128)(2,1)}, bf16[128,256]{1,0:T(8,128)(2,1)S(1)}, u32[]{:S(2)}, u32[]{:S(2)}) %collective-permute-start.1) | collective-permute-done | bytes 65568 | tf_op jit(solution)/shard_map/ppermute | solution.py:472
  8.0 2.2 %collective-permute-start.10 = (bf16[128,256]{1,0:T(8,128)(2,1)S(1)}, bf16[128,256]{1,0:T(8,128)(2,1)S(1)}, u32[]{:S(2)}, u32[]{:S(2)}) collective-permute-start(bf16[128,256]{1,0:T(8,128)(2,1)S(1)} %collective-permute-done.1.refs_5_), channel_id=1, source_target_pairs={{0,4},{4,0},{8,12},{12,8},{1,5},{5,1},{9,13},{13,9},{2,6},{6,2},{1... | collective-permute-start | bytes 196616 | tf_op jit(solution)/shard_map/ppermute | solution.py:472
  10.2 0.0 collective-permute-start.3
  10.2 2.3 %index_table.1 = (s32[6,8]{1,0:T(8,128)S(4)}, bf16[128,256]{1,0:T(8,128)(2,1)S(1)}, bf16[8,512,1536]{2,1,0:T(8,128)(2,1)S(1)}) custom-call(s32[64]{0:T(128)} %refs_0_, s32[8]{0:T(128)} %refs_1_.2, s32[8]{0:T(128)} %refs_2_.1, bf16[128,256]{1,0:T(8,128)(2,1)} %refs_3_.1, bf16[4096,256]{1,0:T(8,128)(2,1)} %refs_4_.1, bf16[4096,256]{1,0:T(8,128)(2,1)} %refs_5_.1), custom_call_target="tpu_custom_call" | custom-call | tf_op jit(solution)/shard_map/index_table/pallas_call | solution.py:122
  12.5 0.0 collective-permute-done.refs_3_
  12.5 0.1 collective-permute-start.8
  12.6 0.5 %collective-permute-start.7 = (bf16[128,256]{1,0:T(8,128)(2,1)S(1)}, bf16[128,256]{1,0:T(8,128)(2,1)S(1)}, u32[]{:S(2)}, u32[]{:S(2)}) collective-permute-start(bf16[128,256]{1,0:T(8,128)(2,1)S(1)} %get-tuple-element.33.refs_1_), channel_id=1, source_target_pairs={{0,1},{1,0},{2,3},{3,2},{4,5},{5,4},{6,7},{7,6},{8,9},{9,8},{10,11... | collective-permute-start | bytes 196616 | tf_op jit(solution)/shard_map/ppermute | solution.py:471
  13.1 0.0 collective-permute-done.5.refs_5_
  13.1 0.1 collective-permute-start.9
  13.2 0.4 collective-permute-start.11
  13.6 1.0 %collective-permute-done.3.refs_3_ = bf16[128,256]{1,0:T(8,128)(2,1)S(1)} collective-permute-done((bf16[128,256]{1,0:T(8,128)(2,1)}, bf16[128,256]{1,0:T(8,128)(2,1)S(1)}, u32[]{:S(2)}, u32[]{:S(2)}) %collective-permute-start.3) | collective-permute-done | bytes 65568 | tf_op jit(solution)/shard_map/ppermute | solution.py:472
  14.6 1.0 %collective-permute-start.6 = (bf16[128,256]{1,0:T(8,128)(2,1)S(1)}, bf16[128,256]{1,0:T(8,128)(2,1)S(1)}, u32[]{:S(2)}, u32[]{:S(2)}) collective-permute-start(bf16[128,256]{1,0:T(8,128)(2,1)S(1)} %collective-permute-done.5.refs_5_), channel_id=1, source_target_pairs={{0,4},{4,0},{8,12},{12,8},{1,5},{5,1},{9,13},{13,9},{2,6},{6,2},{1... | collective-permute-start | bytes 196616 | tf_op jit(solution)/shard_map/ppermute | solution.py:472
  15.6 0.0 collective-permute-done.8.refs_4_
  15.6 0.0 collective-permute-done.7.refs_2_
  15.7 0.5 %collective-permute-start.4 = (bf16[128,256]{1,0:T(8,128)(2,1)S(1)}, bf16[128,256]{1,0:T(8,128)(2,1)S(1)}, u32[]{:S(2)}, u32[]{:S(2)}) collective-permute-start(bf16[128,256]{1,0:T(8,128)(2,1)S(1)} %collective-permute-done.3.refs_3_), channel_id=1, source_target_pairs={{0,1},{1,0},{2,3},{3,2},{4,5},{5,4},{6,7},{7,6},{8,9},{9,8},{10,11... | collective-permute-start | bytes 196616 | tf_op jit(solution)/shard_map/ppermute | solution.py:471
  16.2 0.0 collective-permute-done.9.refs_6_
  16.2 0.0 collective-permute-done.11.refs_8_
  16.2 3.5 %block_weights.1 = (f32[2080,128]{1,0:T(8,128)S(1)}, bf16[8,512,1536]{2,1,0:T(8,128)(2,1)S(1)}) custom-call(s32[6,8]{1,0:T(8,128)S(4)} %get-tuple-element.32.refs_0_.meta, bf16[128,256]{1,0:T(8,128)(2,1)S(1)} %get-tuple-element.33.refs_1_, bf16[128,256]{1,0:T(8,128)(2,1)S(1)} %collective-permute-done.7.refs_2_, ...), custom_call_target="tpu_custom_call", output_to_operand_aliasing={{1}: (9, {})} | custom-call | tf_op jit(solution)/shard_map/block_weights/pallas_call | solution.py:218
  19.7 0.2 collective-permute-start.12
  19.8 0.4 collective-permute-start.13
  20.2 0.7 %collective-permute-done.12.refs_6_ = bf16[128,256]{1,0:T(8,128)(2,1)S(1)} collective-permute-done((bf16[128,256]{1,0:T(8,128)(2,1)S(1)}, bf16[128,256]{1,0:T(8,128)(2,1)S(1)}, u32[]{:S(2)}, u32[]{:S(2)}) %collective-permute-start.12) | collective-permute-done | bytes 65568 | tf_op jit(solution)/shard_map/ppermute | solution.py:471
  21.0 0.2 collective-permute-done.13.refs_8_
  21.1 3.3 %moved_weights.1 = (f32[2112,128]{1,0:T(8,128)S(1)}, f32[2,8,512]{2,1,0:T(8,128)S(1)}, bf16[8,512,1536]{2,1,0:T(8,128)(2,1)S(1)}) custom-call(s32[6,8]{1,0:T(8,128)S(4)} %get-tuple-element.32.refs_0_.meta, bf16[128,256]{1,0:T(8,128)(2,1)S(1)} %copy-done, bf16[128,256]{1,0:T(8,128)(2,1)S(1)} %collective-permute-done.2.refs_2_, ...), custom_call_target="tpu_custom_call", output_to_operand_aliasing={{2}: (10, {})} | custom-call | tf_op jit(solution)/shard_map/moved_weights/pallas_call | solution.py:307
  24.4 1.1 %collective-permute-start.15 = (f32[2,8,512]{2,1,0:T(8,128)S(1)}, f32[2,8,512]{2,1,0:T(8,128)S(1)}, u32[]{:S(2)}, u32[]{:S(2)}) collective-permute-start(f32[2,8,512]{2,1,0:T(8,128)S(1)} %get-tuple-element.41.refs_1_), channel_id=1, source_target_pairs={{0,4},{4,0},{8,12},{12,8},{1,5},{5,1},{9,13},{13,9},{2,6},{6,2},{1... | collective-permute-start | bytes 98312 | tf_op jit(solution)/shard_map/ppermute | solution.py:472
  25.5 3.5 %collective-permute-start.16 = (f32[2,8,512]{2,1,0:T(8,128)S(1)}, f32[2,8,512]{2,1,0:T(8,128)S(1)}, u32[]{:S(2)}, u32[]{:S(2)}) collective-permute-start(f32[2,8,512]{2,1,0:T(8,128)S(1)} %get-tuple-element.41.refs_1_), channel_id=1, source_target_pairs={{0,8},{4,12},{8,0},{12,4},{1,9},{5,13},{9,1},{13,5},{2,10},{6,14},... | collective-permute-start | bytes 98312 | tf_op jit(solution)/shard_map/ppermute | solution.py:472
  29.0 0.4 collective-permute-start.17
  29.5 1.3 %query_sums.1 = (f32[8,2,256,128]{3,2,1,0:T(8,128)S(1)}, bf16[8,512,1536]{2,1,0:T(8,128)(2,1)S(1)}) custom-call(bf16[8,512,1536]{2,1,0:T(8,128)(2,1)S(1)} %get-tuple-element.42.state), custom_call_target="tpu_custom_call", output_to_operand_aliasing={{1}: (0, {})} | custom-call | tf_op jit(solution)/shard_map/query_sums/pallas_call | solution.py:340
  30.8 0.5 %collective-permute-done.16.refs_5_ = f32[2,8,512]{2,1,0:T(8,128)S(1)} collective-permute-done((f32[2,8,512]{2,1,0:T(8,128)S(1)}, f32[2,8,512]{2,1,0:T(8,128)S(1)}, u32[]{:S(2)}, u32[]{:S(2)}) %collective-permute-start.16) | collective-permute-done | bytes 32800 | tf_op jit(solution)/shard_map/ppermute | solution.py:472
  31.3 3.5 %collective-permute-done.17.refs_7_ = f32[2,8,512]{2,1,0:T(8,128)S(1)} collective-permute-done((f32[2,8,512]{2,1,0:T(8,128)S(1)}, f32[2,8,512]{2,1,0:T(8,128)S(1)}, u32[]{:S(2)}, u32[]{:S(2)}) %collective-permute-start.17) | collective-permute-done | bytes 32800 | tf_op jit(solution)/shard_map/ppermute | solution.py:472
  34.8 0.5 %collective-permute-start.19 = (f32[2,8,512]{2,1,0:T(8,128)S(1)}, f32[2,8,512]{2,1,0:T(8,128)S(1)}, u32[]{:S(2)}, u32[]{:S(2)}) collective-permute-start(f32[2,8,512]{2,1,0:T(8,128)S(1)} %collective-permute-done.16.refs_5_), channel_id=1, source_target_pairs={{0,1},{1,0},{2,3},{3,2},{4,5},{5,4},{6,7},{7,6},{8,9},{9,8},{10,11... | collective-permute-start | bytes 98312 | tf_op jit(solution)/shard_map/ppermute | solution.py:471
  35.3 0.0 collective-permute-start.20
  35.3 0.7 %collective-permute-done.18.refs_4_ = f32[2,8,512]{2,1,0:T(8,128)S(1)} collective-permute-done((f32[2,8,512]{2,1,0:T(8,128)S(1)}, f32[2,8,512]{2,1,0:T(8,128)S(1)}, u32[]{:S(2)}, u32[]{:S(2)}) %collective-permute-start.18) | collective-permute-done | bytes 32800 | tf_op jit(solution)/shard_map/ppermute | solution.py:471
  36.0 0.2 collective-permute-done.19.refs_6_
  36.1 0.3 collective-permute-done.20.refs_8_
  36.5 0.6 %query_grads.1 = (f32[8,512]{1,0:T(8,128)S(1)}, f32[8,512]{1,0:T(8,128)S(1)}, f32[4,128,256]{2,1,0:T(8,128)S(1)}, bf16[4,128,256]{2,1,0:T(8,128)(2,1)S(1)}) custom-call(s32[6,8]{1,0:T(8,128)S(4)} %get-tuple-element.32.refs_0_.meta, f32[2,8,512]{2,1,0:T(8,128)S(1)} %get-tuple-element.41.refs_1_, f32[2,8,512]{2,1,0:T(8,128)S(1)} %collective-permute-done.14.refs_2_, ...), custom_call_target="tpu_custom_call" | custom-call | tf_op jit(solution)/shard_map/query_grads/pallas_call | solution.py:399
  37.1 0.2 collective-permute-start.21
  37.3 1.4 %collective-permute-done.21 = bf16[4,128,256]{2,1,0:T(8,128)(2,1)S(1)} collective-permute-done((bf16[4,128,256]{2,1,0:T(8,128)(2,1)S(1)}, bf16[4,128,256]{2,1,0:T(8,128)(2,1)S(1)}, u32[]{:S(2)}, u32[]{:S(2)}) %collective-permute-start.21) | collective-permute-done | bytes 262176 | tf_op jit(solution)/shard_map/ppermute | solution.py:471
  38.7 0.1 fusion.4
  38.8 0.1 collective-permute-start.22
  38.9 1.3 %collective-permute-start.23 = (bf16[128,256]{1,0:T(8,128)(2,1)S(1)}, bf16[128,256]{1,0:T(8,128)(2,1)S(1)}, u32[]{:S(2)}, u32[]{:S(2)}) collective-permute-start(bf16[128,256]{1,0:T(8,128)(2,1)S(1)} %get-tuple-element.61), channel_id=1, source_target_pairs={{0,8},{4,12},{8,0},{12,4},{1,9},{5,13},{9,1},{13,5},{2,10},{6,14},... | collective-permute-start | bytes 196616 | tf_op jit(solution)/shard_map/ppermute | solution.py:472
  40.1 3.1 %collective-permute-start.24 = (bf16[128,256]{1,0:T(8,128)(2,1)S(1)}, bf16[128,256]{1,0:T(8,128)(2,1)S(1)}, u32[]{:S(2)}, u32[]{:S(2)}) collective-permute-start(bf16[128,256]{1,0:T(8,128)(2,1)S(1)} %get-tuple-element.60), channel_id=1, source_target_pairs={{0,12},{4,8},{8,4},{12,0},{1,13},{5,9},{9,5},{13,1},{2,14},{6,10},... | collective-permute-start | bytes 196616 | tf_op jit(solution)/shard_map/ppermute | solution.py:472
  43.2 3.3 %row_grads.1 = (bf16[4096,256]{1,0:T(8,128)(2,1)}, bf16[4096,256]{1,0:T(8,128)(2,1)}) custom-call(s32[6,8]{1,0:T(8,128)S(4)} %get-tuple-element.32.refs_0_.meta, f32[8,512]{1,0:T(8,128)S(1)} %get-tuple-element.52.c_ref, f32[8,512]{1,0:T(8,128)S(1)} %get-tuple-element.53.d_ref, f32[2080,128]{1,0:T(8,128)S(1)} %get-tuple-element.39.refs_9_.q_side, ...), custom_call_target="tpu_custom_call" | custom-call | tf_op jit(solution)/shard_map/row_grads/pallas_call | solution.py:452
  46.5 0.0 collective-permute-done.22
  46.5 0.9 %collective-permute-done.23 = bf16[128,256]{1,0:T(8,128)(2,1)S(1)} collective-permute-done((bf16[128,256]{1,0:T(8,128)(2,1)S(1)}, bf16[128,256]{1,0:T(8,128)(2,1)S(1)}, u32[]{:S(2)}, u32[]{:S(2)}) %collective-permute-start.23) | collective-permute-done | bytes 65568 | tf_op jit(solution)/shard_map/ppermute | solution.py:472
  47.5 0.7 %fusion.3 = bf16[128,256]{1,0:T(8,128)(2,1)} fusion(f32[4,128,256]{2,1,0:T(8,128)S(1)} %get-tuple-element.58, bf16[128,256]{1,0:T(8,128)(2,1)S(1)} %collective-permute-done.24, bf16[128,256]{1,0:T(8,128)(2,1)S(1)} %collective-permute-done.23, bf16[128,256]{1,0:T(8,128)(2,1)S(1)} %collective-permute-done.22), kind=kLoop, calls=%fused_computation.5 | loop fusion | flops 229376 | bytes 393216 | tf_op jit(solution)/shard_map/convert_element_type | solution.py:530
  (13 shorter events, 0.0 us)
Async XLA Ops:
  0.6 15.0 %copy-start = (bf16[128,256]{1,0:T(8,128)(2,1)S(1)}, bf16[128,256]{1,0:T(8,128)(2,1)}, u32[]{:S(2)}) copy-start(bf16[128,256]{1,0:T(8,128)(2,1)} %refs_1_.3) | copy-start | bytes 196612
  0.6 7.4 %collective-permute-start.1 = (bf16[128,256]{1,0:T(8,128)(2,1)}, bf16[128,256]{1,0:T(8,128)(2,1)S(1)}, u32[]{:S(2)}, u32[]{:S(2)}) collective-permute-start(bf16[128,256]{1,0:T(8,128)(2,1)} %refs_3_.1), channel_id=1, source_target_pairs={{0,8},{4,12},{8,0},{12,4},{1,9},{5,13},{9,1},{13,5},{2,10},{6,14},... | collective-permute-start | bytes 196616 | tf_op jit(solution)/shard_map/ppermute | solution.py:472
  4.7 7.8 %collective-permute-start = (bf16[128,256]{1,0:T(8,128)(2,1)}, bf16[128,256]{1,0:T(8,128)(2,1)S(1)}, u32[]{:S(2)}, u32[]{:S(2)}) collective-permute-start(bf16[128,256]{1,0:T(8,128)(2,1)} %refs_3_.1), channel_id=1, source_target_pairs={{0,4},{4,0},{8,12},{12,8},{1,5},{5,1},{9,13},{13,9},{2,6},{6,2},{1... | collective-permute-start | bytes 196616 | tf_op jit(solution)/shard_map/ppermute | solution.py:472
  6.3 6.8 %collective-permute-start.5 = (bf16[128,256]{1,0:T(8,128)(2,1)}, bf16[128,256]{1,0:T(8,128)(2,1)S(1)}, u32[]{:S(2)}, u32[]{:S(2)}) collective-permute-start(bf16[128,256]{1,0:T(8,128)(2,1)} %refs_1_.3), channel_id=1, source_target_pairs={{0,8},{4,12},{8,0},{12,4},{1,9},{5,13},{9,1},{13,5},{2,10},{6,14},... | collective-permute-start | bytes 196616 | tf_op jit(solution)/shard_map/ppermute | solution.py:472
  8.0 5.2 %collective-permute-start.10 = (bf16[128,256]{1,0:T(8,128)(2,1)S(1)}, bf16[128,256]{1,0:T(8,128)(2,1)S(1)}, u32[]{:S(2)}, u32[]{:S(2)}) collective-permute-start(bf16[128,256]{1,0:T(8,128)(2,1)S(1)} %collective-permute-done.1.refs_5_), channel_id=1, source_target_pairs={{0,4},{4,0},{8,12},{12,8},{1,5},{5,1},{9,13},{13,9},{2,6},{6,2},{1... | collective-permute-start | bytes 196616 | tf_op jit(solution)/shard_map/ppermute | solution.py:472
  10.2 4.5 %collective-permute-start.3 = (bf16[128,256]{1,0:T(8,128)(2,1)}, bf16[128,256]{1,0:T(8,128)(2,1)S(1)}, u32[]{:S(2)}, u32[]{:S(2)}) collective-permute-start(bf16[128,256]{1,0:T(8,128)(2,1)} %refs_1_.3), channel_id=1, source_target_pairs={{0,4},{4,0},{8,12},{12,8},{1,5},{5,1},{9,13},{13,9},{2,6},{6,2},{1... | collective-permute-start | bytes 196616 | tf_op jit(solution)/shard_map/ppermute | solution.py:472
  12.5 3.1 %collective-permute-start.8 = (bf16[128,256]{1,0:T(8,128)(2,1)S(1)}, bf16[128,256]{1,0:T(8,128)(2,1)S(1)}, u32[]{:S(2)}, u32[]{:S(2)}) collective-permute-start(bf16[128,256]{1,0:T(8,128)(2,1)S(1)} %collective-permute-done.refs_3_), channel_id=1, source_target_pairs={{0,1},{1,0},{2,3},{3,2},{4,5},{5,4},{6,7},{7,6},{8,9},{9,8},{10,11... | collective-permute-start | bytes 196616 | tf_op jit(solution)/shard_map/ppermute | solution.py:471
  12.6 3.0 %collective-permute-start.7 = (bf16[128,256]{1,0:T(8,128)(2,1)S(1)}, bf16[128,256]{1,0:T(8,128)(2,1)S(1)}, u32[]{:S(2)}, u32[]{:S(2)}) collective-permute-start(bf16[128,256]{1,0:T(8,128)(2,1)S(1)} %get-tuple-element.33.refs_1_), channel_id=1, source_target_pairs={{0,1},{1,0},{2,3},{3,2},{4,5},{5,4},{6,7},{7,6},{8,9},{9,8},{10,11... | collective-permute-start | bytes 196616 | tf_op jit(solution)/shard_map/ppermute | solution.py:471
  13.1 3.0 %collective-permute-start.9 = (bf16[128,256]{1,0:T(8,128)(2,1)S(1)}, bf16[128,256]{1,0:T(8,128)(2,1)S(1)}, u32[]{:S(2)}, u32[]{:S(2)}) collective-permute-start(bf16[128,256]{1,0:T(8,128)(2,1)S(1)} %collective-permute-done.1.refs_5_), channel_id=1, source_target_pairs={{0,1},{1,0},{2,3},{3,2},{4,5},{5,4},{6,7},{7,6},{8,9},{9,8},{10,11... | collective-permute-start | bytes 196616 | tf_op jit(solution)/shard_map/ppermute | solution.py:471
  13.2 3.0 %collective-permute-start.11 = (bf16[128,256]{1,0:T(8,128)(2,1)S(1)}, bf16[128,256]{1,0:T(8,128)(2,1)S(1)}, u32[]{:S(2)}, u32[]{:S(2)}) collective-permute-start(bf16[128,256]{1,0:T(8,128)(2,1)S(1)} %collective-permute-done.10.refs_7_), channel_id=1, source_target_pairs={{0,1},{1,0},{2,3},{3,2},{4,5},{5,4},{6,7},{7,6},{8,9},{9,8},{10,11... | collective-permute-start | bytes 196616 | tf_op jit(solution)/shard_map/ppermute | solution.py:471
  14.6 5.0 %collective-permute-start.6 = (bf16[128,256]{1,0:T(8,128)(2,1)S(1)}, bf16[128,256]{1,0:T(8,128)(2,1)S(1)}, u32[]{:S(2)}, u32[]{:S(2)}) collective-permute-start(bf16[128,256]{1,0:T(8,128)(2,1)S(1)} %collective-permute-done.5.refs_5_), channel_id=1, source_target_pairs={{0,4},{4,0},{8,12},{12,8},{1,5},{5,1},{9,13},{13,9},{2,6},{6,2},{1... | collective-permute-start | bytes 196616 | tf_op jit(solution)/shard_map/ppermute | solution.py:472
  15.6 4.6 %collective-permute-start.2 = (bf16[128,256]{1,0:T(8,128)(2,1)S(1)}, bf16[128,256]{1,0:T(8,128)(2,1)S(1)}, u32[]{:S(2)}, u32[]{:S(2)}) collective-permute-start(bf16[128,256]{1,0:T(8,128)(2,1)S(1)} %copy-done), channel_id=1, source_target_pairs={{0,1},{1,0},{2,3},{3,2},{4,5},{5,4},{6,7},{7,6},{8,9},{9,8},{10,11... | collective-permute-start | bytes 196616 | tf_op jit(solution)/shard_map/ppermute | solution.py:471
  15.7 4.6 %collective-permute-start.4 = (bf16[128,256]{1,0:T(8,128)(2,1)S(1)}, bf16[128,256]{1,0:T(8,128)(2,1)S(1)}, u32[]{:S(2)}, u32[]{:S(2)}) collective-permute-start(bf16[128,256]{1,0:T(8,128)(2,1)S(1)} %collective-permute-done.3.refs_3_), channel_id=1, source_target_pairs={{0,1},{1,0},{2,3},{3,2},{4,5},{5,4},{6,7},{7,6},{8,9},{9,8},{10,11... | collective-permute-start | bytes 196616 | tf_op jit(solution)/shard_map/ppermute | solution.py:471
  19.7 1.3 %collective-permute-start.12 = (bf16[128,256]{1,0:T(8,128)(2,1)S(1)}, bf16[128,256]{1,0:T(8,128)(2,1)S(1)}, u32[]{:S(2)}, u32[]{:S(2)}) collective-permute-start(bf16[128,256]{1,0:T(8,128)(2,1)S(1)} %collective-permute-done.5.refs_5_), channel_id=1, source_target_pairs={{0,1},{1,0},{2,3},{3,2},{4,5},{5,4},{6,7},{7,6},{8,9},{9,8},{10,11... | collective-permute-start | bytes 196616 | tf_op jit(solution)/shard_map/ppermute | solution.py:471
  19.8 1.3 %collective-permute-start.13 = (bf16[128,256]{1,0:T(8,128)(2,1)S(1)}, bf16[128,256]{1,0:T(8,128)(2,1)S(1)}, u32[]{:S(2)}, u32[]{:S(2)}) collective-permute-start(bf16[128,256]{1,0:T(8,128)(2,1)S(1)} %collective-permute-done.6.refs_7_), channel_id=1, source_target_pairs={{0,1},{1,0},{2,3},{3,2},{4,5},{5,4},{6,7},{7,6},{8,9},{9,8},{10,11... | collective-permute-start | bytes 196616 | tf_op jit(solution)/shard_map/ppermute | solution.py:471
  24.4 6.4 %collective-permute-start.15 = (f32[2,8,512]{2,1,0:T(8,128)S(1)}, f32[2,8,512]{2,1,0:T(8,128)S(1)}, u32[]{:S(2)}, u32[]{:S(2)}) collective-permute-start(f32[2,8,512]{2,1,0:T(8,128)S(1)} %get-tuple-element.41.refs_1_), channel_id=1, source_target_pairs={{0,4},{4,0},{8,12},{12,8},{1,5},{5,1},{9,13},{13,9},{2,6},{6,2},{1... | collective-permute-start | bytes 98312 | tf_op jit(solution)/shard_map/ppermute | solution.py:472
  25.5 5.8 %collective-permute-start.16 = (f32[2,8,512]{2,1,0:T(8,128)S(1)}, f32[2,8,512]{2,1,0:T(8,128)S(1)}, u32[]{:S(2)}, u32[]{:S(2)}) collective-permute-start(f32[2,8,512]{2,1,0:T(8,128)S(1)} %get-tuple-element.41.refs_1_), channel_id=1, source_target_pairs={{0,8},{4,12},{8,0},{12,4},{1,9},{5,13},{9,1},{13,5},{2,10},{6,14},... | collective-permute-start | bytes 98312 | tf_op jit(solution)/shard_map/ppermute | solution.py:472
  29.0 5.7 %collective-permute-start.17 = (f32[2,8,512]{2,1,0:T(8,128)S(1)}, f32[2,8,512]{2,1,0:T(8,128)S(1)}, u32[]{:S(2)}, u32[]{:S(2)}) collective-permute-start(f32[2,8,512]{2,1,0:T(8,128)S(1)} %get-tuple-element.41.refs_1_), channel_id=1, source_target_pairs={{0,12},{4,8},{8,4},{12,0},{1,13},{5,9},{9,5},{13,1},{2,14},{6,10},... | collective-permute-start | bytes 98312 | tf_op jit(solution)/shard_map/ppermute | solution.py:472
  29.5 5.8 %collective-permute-start.14 = (f32[2,8,512]{2,1,0:T(8,128)S(1)}, f32[2,8,512]{2,1,0:T(8,128)S(1)}, u32[]{:S(2)}, u32[]{:S(2)}) collective-permute-start(f32[2,8,512]{2,1,0:T(8,128)S(1)} %get-tuple-element.41.refs_1_), channel_id=1, source_target_pairs={{0,1},{1,0},{2,3},{3,2},{4,5},{5,4},{6,7},{7,6},{8,9},{9,8},{10,11... | collective-permute-start | bytes 98312 | tf_op jit(solution)/shard_map/ppermute | solution.py:471
  34.8 1.2 %collective-permute-start.18 = (f32[2,8,512]{2,1,0:T(8,128)S(1)}, f32[2,8,512]{2,1,0:T(8,128)S(1)}, u32[]{:S(2)}, u32[]{:S(2)}) collective-permute-start(f32[2,8,512]{2,1,0:T(8,128)S(1)} %collective-permute-done.15.refs_3_), channel_id=1, source_target_pairs={{0,1},{1,0},{2,3},{3,2},{4,5},{5,4},{6,7},{7,6},{8,9},{9,8},{10,11... | collective-permute-start | bytes 98312 | tf_op jit(solution)/shard_map/ppermute | solution.py:471
  34.8 1.4 %collective-permute-start.19 = (f32[2,8,512]{2,1,0:T(8,128)S(1)}, f32[2,8,512]{2,1,0:T(8,128)S(1)}, u32[]{:S(2)}, u32[]{:S(2)}) collective-permute-start(f32[2,8,512]{2,1,0:T(8,128)S(1)} %collective-permute-done.16.refs_5_), channel_id=1, source_target_pairs={{0,1},{1,0},{2,3},{3,2},{4,5},{5,4},{6,7},{7,6},{8,9},{9,8},{10,11... | collective-permute-start | bytes 98312 | tf_op jit(solution)/shard_map/ppermute | solution.py:471
  35.3 1.2 %collective-permute-start.20 = (f32[2,8,512]{2,1,0:T(8,128)S(1)}, f32[2,8,512]{2,1,0:T(8,128)S(1)}, u32[]{:S(2)}, u32[]{:S(2)}) collective-permute-start(f32[2,8,512]{2,1,0:T(8,128)S(1)} %collective-permute-done.17.refs_7_), channel_id=1, source_target_pairs={{0,1},{1,0},{2,3},{3,2},{4,5},{5,4},{6,7},{7,6},{8,9},{9,8},{10,11... | collective-permute-start | bytes 98312 | tf_op jit(solution)/shard_map/ppermute | solution.py:471
  37.1 1.6 %collective-permute-start.21 = (bf16[4,128,256]{2,1,0:T(8,128)(2,1)S(1)}, bf16[4,128,256]{2,1,0:T(8,128)(2,1)S(1)}, u32[]{:S(2)}, u32[]{:S(2)}) collective-permute-start(bf16[4,128,256]{2,1,0:T(8,128)(2,1)S(1)} %get-tuple-element.50), channel_id=1, source_target_pairs={{0,1},{1,0},{2,3},{3,2},{4,5},{5,4},{6,7},{7,6},{8,9},{9,8},{10,11... | collective-permute-start | bytes 786440 | tf_op jit(solution)/shard_map/ppermute | solution.py:471
  38.8 7.8 %collective-permute-start.22 = (bf16[128,256]{1,0:T(8,128)(2,1)S(1)}, bf16[128,256]{1,0:T(8,128)(2,1)S(1)}, u32[]{:S(2)}, u32[]{:S(2)}) collective-permute-start(bf16[128,256]{1,0:T(8,128)(2,1)S(1)} %get-tuple-element.59), channel_id=1, source_target_pairs={{0,4},{4,0},{8,12},{12,8},{1,5},{5,1},{9,13},{13,9},{2,6},{6,2},{1... | collective-permute-start | bytes 196616 | tf_op jit(solution)/shard_map/ppermute | solution.py:472
  38.9 8.6 %collective-permute-start.23 = (bf16[128,256]{1,0:T(8,128)(2,1)S(1)}, bf16[128,256]{1,0:T(8,128)(2,1)S(1)}, u32[]{:S(2)}, u32[]{:S(2)}) collective-permute-start(bf16[128,256]{1,0:T(8,128)(2,1)S(1)} %get-tuple-element.61), channel_id=1, source_target_pairs={{0,8},{4,12},{8,0},{12,4},{1,9},{5,13},{9,1},{13,5},{2,10},{6,14},... | collective-permute-start | bytes 196616 | tf_op jit(solution)/shard_map/ppermute | solution.py:472
  40.1 7.4 %collective-permute-start.24 = (bf16[128,256]{1,0:T(8,128)(2,1)S(1)}, bf16[128,256]{1,0:T(8,128)(2,1)S(1)}, u32[]{:S(2)}, u32[]{:S(2)}) collective-permute-start(bf16[128,256]{1,0:T(8,128)(2,1)S(1)} %get-tuple-element.60), channel_id=1, source_target_pairs={{0,12},{4,8},{8,4},{12,0},{1,13},{5,9},{9,5},{13,1},{2,14},{6,10},... | collective-permute-start | bytes 196616 | tf_op jit(solution)/shard_map/ppermute | solution.py:472

commit v11 on v9

--- a/solution.py
+++ b/solution.py
@@ -485,7 +485,7 @@
         for value in near:
             queries += [value, pair(value)]
         q_side, state = block_weights(meta, queries, state, features, tables)
-        *near_grads[1:], q_side = lax.optimization_barrier((*near_grads[1:], q_side))
+        near_grads[2], q_side = after(near_grads[2], q_side)
         grads = [cotangent, pair(cotangent)]
         for value in near_grads:
             grads += [value, pair(value)]
@@ -496,7 +496,7 @@
         grads = [lax.all_gather(cotangent, RP, axis=0, tiled=True)]
     g_side, tab, state = moved_weights(meta, grads, q_side, state, features, tables)
     if small:
-        near = [step(tab, s) for s in (1, 2, 3)]
+        near = [step(tab, s) for s in (3, 2, 1)]
         ab, state = query_sums(features, state)
         *near, ab = lax.optimization_barrier((*near, ab))
         stats = [tab, pair(tab)]
@@ -515,7 +515,7 @@
         keep, send = q_terms
         total = keep + pair(send).astype(jnp.float32)
         low = total.astype(jnp.bfloat16)
-        got = [step(low[s - 1], s) for s in (1, 2, 3)]
+        got = [step(low[s - 1], s) for s in (3, 2, 1)]
         low, c = lax.optimization_barrier((low, c))
         key_grad, value_grad = row_grads(meta, c, d, (q_side, g_side), state, features)
         query_grad = total[3]

time: 47.5 us -> 46.1 us (0.971)
  waiting for transfers between devices: 11.1 us -> 8.5 us
  starting transfers between devices: 20.5 us -> 21.7 us
    ppermute x12, waiting for transfers between devices: 7.03 us -> 4.69 us  [local(): lax.ppermute(value, 'rows', [(z, z ^ s) for z in range(4)])]
    ppermute x12, starting transfers between devices: 18.1 us -> 19.3 us  [local(): lax.ppermute(value, 'rows', [(z, z ^ s) for z in range(4)])]
  transfers between devices with their start and end apart: 25 -> 25, of which waited for: 13 -> 10; matrix products, arithmetic and copies ran while one was open for 0% -> 0% of each run, Pallas kernels for 22% -> 23%
where the time goes in v11:
time: 46.1 us; the launch traced here: 45.9 us
  starting transfers between devices  21.7 us (47%)
  Pallas kernels  14.2 us (31%)
  waiting for transfers between devices  8.5 us (18%)
  between operations  0.76 us (2%)
  other arithmetic  0.74 us (2%)
    ppermute x12, starting transfers between devices, local(): lax.ppermute(value, 'rows', [(z, z ^ s) for z in range(4)])  19.3 us
    ppermute x12, waiting for transfers between devices, local(): lax.ppermute(value, 'rows', [(z, z ^ s) for z in range(4)])  4.69 us
    ppermute x13, waiting for transfers between devices, local(): pair = lambda value: lax.ppermute(value, 'pair', PAIR)  3.81 us
    pallas_call x1, Pallas kernels, block_weights(): pl.pallas_call(lambda *refs: weights_kernel(count, features, *refs), in_s...  3.48 us
    pallas_call x1, Pallas kernels, row_grads(): pl.pallas_call(row_grads_kernel, in_specs=[smem_spec()] + [vmem_spec()] *...  3.29 us
    pallas_call x1, Pallas kernels, moved_weights(): pl.pallas_call(lambda *refs: moved_kernel(count, features, *refs), in_spe...  3.25 us
    ppermute x13, starting transfers between devices, local(): pair = lambda value: lax.ppermute(value, 'pair', PAIR)  2.35 us
    pallas_call x1, Pallas kernels, index_table(): pl.pallas_call(lambda *refs: index_kernel(small, *refs), in_specs=[hbm_sp...  2.33 us
  transfers between devices with their start and end apart: 25, of which 10 were waited for; matrix products, arithmetic and copies ran while one was open for 0% of the time, Pallas kernels for 23%

profile of v11, /device:TPU:0, one launch (start us, length us, event | category | flops | bytes accessed | tf_op | source)
XLA Modules:
  0.0 45.9 jit_solution(16148804958579585269)
XLA Ops:
  0.6 3.1 %collective-permute-start = (bf16[128,256]{1,0:T(8,128)(2,1)}, bf16[128,256]{1,0:T(8,128)(2,1)S(1)}, u32[]{:S(2)}, u32[]{:S(2)}) collective-permute-start(bf16[128,256]{1,0:T(8,128)(2,1)} %refs_3_.1), channel_id=1, source_target_pairs={{0,4},{4,0},{8,12},{12,8},{1,5},{5,1},{9,13},{13,9},{2,6},{6,2},{1... | collective-permute-start | bytes 196616 | tf_op jit(solution)/shard_map/ppermute | solution.py:472
  3.7 2.6 %collective-permute-start.9 = (bf16[128,256]{1,0:T(8,128)(2,1)}, bf16[128,256]{1,0:T(8,128)(2,1)S(1)}, u32[]{:S(2)}, u32[]{:S(2)}) collective-permute-start(bf16[128,256]{1,0:T(8,128)(2,1)} %refs_3_.1), channel_id=1, source_target_pairs={{0,8},{4,12},{8,0},{12,4},{1,9},{5,13},{9,1},{13,5},{2,10},{6,14},... | collective-permute-start | bytes 196616 | tf_op jit(solution)/shard_map/ppermute | solution.py:472
  6.3 0.0 collective-permute-start.11
  6.3 1.9 %collective-permute-start.4 = (bf16[128,256]{1,0:T(8,128)(2,1)}, bf16[128,256]{1,0:T(8,128)(2,1)S(1)}, u32[]{:S(2)}, u32[]{:S(2)}) collective-permute-start(bf16[128,256]{1,0:T(8,128)(2,1)} %refs_1_.3), channel_id=1, source_target_pairs={{0,8},{4,12},{8,0},{12,4},{1,9},{5,13},{9,1},{13,5},{2,10},{6,14},... | collective-permute-start | bytes 196616 | tf_op jit(solution)/shard_map/ppermute | solution.py:472
  8.2 2.5 %collective-permute-start.2 = (bf16[128,256]{1,0:T(8,128)(2,1)}, bf16[128,256]{1,0:T(8,128)(2,1)S(1)}, u32[]{:S(2)}, u32[]{:S(2)}) collective-permute-start(bf16[128,256]{1,0:T(8,128)(2,1)} %refs_1_.3), channel_id=1, source_target_pairs={{0,4},{4,0},{8,12},{12,8},{1,5},{5,1},{9,13},{13,9},{2,6},{6,2},{1... | collective-permute-start | bytes 196616 | tf_op jit(solution)/shard_map/ppermute | solution.py:472
  10.7 2.3 %index_table.1 = (s32[6,8]{1,0:T(8,128)S(4)}, bf16[128,256]{1,0:T(8,128)(2,1)S(1)}, bf16[8,512,1536]{2,1,0:T(8,128)(2,1)S(1)}) custom-call(s32[64]{0:T(128)} %refs_0_, s32[8]{0:T(128)} %refs_1_.2, s32[8]{0:T(128)} %refs_2_.1, bf16[128,256]{1,0:T(8,128)(2,1)} %refs_3_.1, bf16[4096,256]{1,0:T(8,128)(2,1)} %refs_4_.1, bf16[4096,256]{1,0:T(8,128)(2,1)} %refs_5_.1), custom_call_target="tpu_custom_call" | custom-call | tf_op jit(solution)/shard_map/index_table/pallas_call | solution.py:122
  13.0 0.1 collective-permute-start.8
  13.1 0.5 %collective-permute-start.7 = (bf16[128,256]{1,0:T(8,128)(2,1)S(1)}, bf16[128,256]{1,0:T(8,128)(2,1)S(1)}, u32[]{:S(2)}, u32[]{:S(2)}) collective-permute-start(bf16[128,256]{1,0:T(8,128)(2,1)S(1)} %get-tuple-element.34.refs_1_), channel_id=1, source_target_pairs={{0,1},{1,0},{2,3},{3,2},{4,5},{5,4},{6,7},{7,6},{8,9},{9,8},{10,11... | collective-permute-start | bytes 196616 | tf_op jit(solution)/shard_map/ppermute | solution.py:471
  13.6 0.0 collective-permute-done.11.refs_7_
  13.6 0.1 collective-permute-start.10
  13.7 1.7 %collective-permute-done.4.refs_5_ = bf16[128,256]{1,0:T(8,128)(2,1)S(1)} collective-permute-done((bf16[128,256]{1,0:T(8,128)(2,1)}, bf16[128,256]{1,0:T(8,128)(2,1)S(1)}, u32[]{:S(2)}, u32[]{:S(2)}) %collective-permute-start.4) | collective-permute-done | bytes 65568 | tf_op jit(solution)/shard_map/ppermute | solution.py:472
  15.4 0.0 collective-permute-start.12
  15.4 0.0 collective-permute-done.2.refs_3_
  15.4 0.4 collective-permute-start.6
  15.8 0.0 collective-permute-done.8.refs_4_
  15.8 0.2 collective-permute-start.1
  16.0 0.0 collective-permute-done.7.refs_2_
  16.0 0.3 collective-permute-start.5
  16.3 0.0 collective-permute-done.10.refs_6_
  16.3 0.2 collective-permute-start.3
  16.6 0.1 collective-permute-done.12.refs_8_
  16.7 3.5 %block_weights.1 = (f32[2080,128]{1,0:T(8,128)S(1)}, bf16[8,512,1536]{2,1,0:T(8,128)(2,1)S(1)}) custom-call(s32[6,8]{1,0:T(8,128)S(4)} %get-tuple-element.33.refs_0_.meta, bf16[128,256]{1,0:T(8,128)(2,1)S(1)} %get-tuple-element.34.refs_1_, bf16[128,256]{1,0:T(8,128)(2,1)S(1)} %collective-permute-done.7.refs_2_, ...), custom_call_target="tpu_custom_call", output_to_operand_aliasing={{1}: (9, {})} | custom-call | tf_op jit(solution)/shard_map/block_weights/pallas_call | solution.py:218
  20.2 0.2 collective-permute-start.13
  20.4 0.0 collective-permute-done.1.refs_2_
  20.4 0.0 collective-permute-done.5.refs_6_
  20.4 0.0 collective-permute-done.3.refs_4_
  20.4 1.1 %collective-permute-done.13.refs_8_ = bf16[128,256]{1,0:T(8,128)(2,1)S(1)} collective-permute-done((bf16[128,256]{1,0:T(8,128)(2,1)S(1)}, bf16[128,256]{1,0:T(8,128)(2,1)S(1)}, u32[]{:S(2)}, u32[]{:S(2)}) %collective-permute-start.13) | collective-permute-done | bytes 65568 | tf_op jit(solution)/shard_map/ppermute | solution.py:471
  21.5 3.3 %moved_weights.1 = (f32[2112,128]{1,0:T(8,128)S(1)}, f32[2,8,512]{2,1,0:T(8,128)S(1)}, bf16[8,512,1536]{2,1,0:T(8,128)(2,1)S(1)}) custom-call(s32[6,8]{1,0:T(8,128)S(4)} %get-tuple-element.33.refs_0_.meta, bf16[128,256]{1,0:T(8,128)(2,1)S(1)} %copy-done, bf16[128,256]{1,0:T(8,128)(2,1)S(1)} %collective-permute-done.1.refs_2_, ...), custom_call_target="tpu_custom_call", output_to_operand_aliasing={{2}: (10, {})} | custom-call | tf_op jit(solution)/shard_map/moved_weights/pallas_call | solution.py:307
  24.8 2.5 %collective-permute-start.15 = (f32[2,8,512]{2,1,0:T(8,128)S(1)}, f32[2,8,512]{2,1,0:T(8,128)S(1)}, u32[]{:S(2)}, u32[]{:S(2)}) collective-permute-start(f32[2,8,512]{2,1,0:T(8,128)S(1)} %get-tuple-element.41.refs_1_), channel_id=1, source_target_pairs={{0,12},{4,8},{8,4},{12,0},{1,13},{5,9},{9,5},{13,1},{2,14},{6,10},... | collective-permute-start | bytes 98312 | tf_op jit(solution)/shard_map/ppermute | solution.py:472
  27.3 0.5 %collective-permute-start.16 = (f32[2,8,512]{2,1,0:T(8,128)S(1)}, f32[2,8,512]{2,1,0:T(8,128)S(1)}, u32[]{:S(2)}, u32[]{:S(2)}) collective-permute-start(f32[2,8,512]{2,1,0:T(8,128)S(1)} %get-tuple-element.41.refs_1_), channel_id=1, source_target_pairs={{0,8},{4,12},{8,0},{12,4},{1,9},{5,13},{9,1},{13,5},{2,10},{6,14},... | collective-permute-start | bytes 98312 | tf_op jit(solution)/shard_map/ppermute | solution.py:472
  27.8 1.4 %collective-permute-start.17 = (f32[2,8,512]{2,1,0:T(8,128)S(1)}, f32[2,8,512]{2,1,0:T(8,128)S(1)}, u32[]{:S(2)}, u32[]{:S(2)}) collective-permute-start(f32[2,8,512]{2,1,0:T(8,128)S(1)} %get-tuple-element.41.refs_1_), channel_id=1, source_target_pairs={{0,4},{4,0},{8,12},{12,8},{1,5},{5,1},{9,13},{13,9},{2,6},{6,2},{1... | collective-permute-start | bytes 98312 | tf_op jit(solution)/shard_map/ppermute | solution.py:472
  29.2 1.3 %query_sums.1 = (f32[8,2,256,128]{3,2,1,0:T(8,128)S(1)}, bf16[8,512,1536]{2,1,0:T(8,128)(2,1)S(1)}) custom-call(bf16[8,512,1536]{2,1,0:T(8,128)(2,1)S(1)} %get-tuple-element.42.state), custom_call_target="tpu_custom_call", output_to_operand_aliasing={{1}: (0, {})} | custom-call | tf_op jit(solution)/shard_map/query_sums/pallas_call | solution.py:340
  30.5 0.1 collective-permute-done.15.refs_3_
  30.6 1.7 %collective-permute-done.16.refs_5_ = f32[2,8,512]{2,1,0:T(8,128)S(1)} collective-permute-done((f32[2,8,512]{2,1,0:T(8,128)S(1)}, f32[2,8,512]{2,1,0:T(8,128)S(1)}, u32[]{:S(2)}, u32[]{:S(2)}) %collective-permute-start.16) | collective-permute-done | bytes 32800 | tf_op jit(solution)/shard_map/ppermute | solution.py:472
  32.4 0.5 %collective-permute-start.19 = (f32[2,8,512]{2,1,0:T(8,128)S(1)}, f32[2,8,512]{2,1,0:T(8,128)S(1)}, u32[]{:S(2)}, u32[]{:S(2)}) collective-permute-start(f32[2,8,512]{2,1,0:T(8,128)S(1)} %collective-permute-done.16.refs_5_), channel_id=1, source_target_pairs={{0,1},{1,0},{2,3},{3,2},{4,5},{5,4},{6,7},{7,6},{8,9},{9,8},{10,11... | collective-permute-start | bytes 98312 | tf_op jit(solution)/shard_map/ppermute | solution.py:471
  32.9 0.0 collective-permute-start.20
  32.9 0.7 %collective-permute-done.18.refs_4_ = f32[2,8,512]{2,1,0:T(8,128)S(1)} collective-permute-done((f32[2,8,512]{2,1,0:T(8,128)S(1)}, f32[2,8,512]{2,1,0:T(8,128)S(1)}, u32[]{:S(2)}, u32[]{:S(2)}) %collective-permute-start.18) | collective-permute-done | bytes 32800 | tf_op jit(solution)/shard_map/ppermute | solution.py:471
  33.6 0.2 collective-permute-done.19.refs_6_
  33.8 0.3 collective-permute-done.20.refs_8_
  34.1 0.6 %query_grads.1 = (f32[8,512]{1,0:T(8,128)S(1)}, f32[8,512]{1,0:T(8,128)S(1)}, f32[4,128,256]{2,1,0:T(8,128)S(1)}, bf16[4,128,256]{2,1,0:T(8,128)(2,1)S(1)}) custom-call(s32[6,8]{1,0:T(8,128)S(4)} %get-tuple-element.33.refs_0_.meta, f32[2,8,512]{2,1,0:T(8,128)S(1)} %get-tuple-element.41.refs_1_, f32[2,8,512]{2,1,0:T(8,128)S(1)} %collective-permute-done.14.refs_2_, ...), custom_call_target="tpu_custom_call" | custom-call | tf_op jit(solution)/shard_map/query_grads/pallas_call | solution.py:399
  34.7 0.2 collective-permute-start.21
  34.9 1.4 %collective-permute-done.21 = bf16[4,128,256]{2,1,0:T(8,128)(2,1)S(1)} collective-permute-done((bf16[4,128,256]{2,1,0:T(8,128)(2,1)S(1)}, bf16[4,128,256]{2,1,0:T(8,128)(2,1)S(1)}, u32[]{:S(2)}, u32[]{:S(2)}) %collective-permute-start.21) | collective-permute-done | bytes 262176 | tf_op jit(solution)/shard_map/ppermute | solution.py:471
  36.3 0.1 fusion.4
  36.4 2.3 %collective-permute-start.22 = (bf16[128,256]{1,0:T(8,128)(2,1)S(1)}, bf16[128,256]{1,0:T(8,128)(2,1)S(1)}, u32[]{:S(2)}, u32[]{:S(2)}) collective-permute-start(bf16[128,256]{1,0:T(8,128)(2,1)S(1)} %get-tuple-element.59), channel_id=1, source_target_pairs={{0,12},{4,8},{8,4},{12,0},{1,13},{5,9},{9,5},{13,1},{2,14},{6,10},... | collective-permute-start | bytes 196616 | tf_op jit(solution)/shard_map/ppermute | solution.py:472
  38.7 2.1 %collective-permute-start.24 = (bf16[128,256]{1,0:T(8,128)(2,1)S(1)}, bf16[128,256]{1,0:T(8,128)(2,1)S(1)}, u32[]{:S(2)}, u32[]{:S(2)}) collective-permute-start(bf16[128,256]{1,0:T(8,128)(2,1)S(1)} %get-tuple-element.60), channel_id=1, source_target_pairs={{0,4},{4,0},{8,12},{12,8},{1,5},{5,1},{9,13},{13,9},{2,6},{6,2},{1... | collective-permute-start | bytes 196616 | tf_op jit(solution)/shard_map/ppermute | solution.py:472
  40.9 3.3 %row_grads.1 = (bf16[4096,256]{1,0:T(8,128)(2,1)}, bf16[4096,256]{1,0:T(8,128)(2,1)}) custom-call(s32[6,8]{1,0:T(8,128)S(4)} %get-tuple-element.33.refs_0_.meta, f32[8,512]{1,0:T(8,128)S(1)} %get-tuple-element.52.c_ref, f32[8,512]{1,0:T(8,128)S(1)} %get-tuple-element.53.d_ref, f32[2080,128]{1,0:T(8,128)S(1)} %get-tuple-element.39.refs_9_.q_side, ...), custom_call_target="tpu_custom_call" | custom-call | tf_op jit(solution)/shard_map/row_grads/pallas_call | solution.py:452
  44.2 1.1 %collective-permute-done.23 = bf16[128,256]{1,0:T(8,128)(2,1)S(1)} collective-permute-done((bf16[128,256]{1,0:T(8,128)(2,1)S(1)}, bf16[128,256]{1,0:T(8,128)(2,1)S(1)}, u32[]{:S(2)}, u32[]{:S(2)}) %collective-permute-start.23) | collective-permute-done | bytes 65568 | tf_op jit(solution)/shard_map/ppermute | solution.py:472
  45.2 0.7 %fusion.3 = bf16[128,256]{1,0:T(8,128)(2,1)} fusion(f32[4,128,256]{2,1,0:T(8,128)S(1)} %get-tuple-element.58, bf16[128,256]{1,0:T(8,128)(2,1)S(1)} %collective-permute-done.24, bf16[128,256]{1,0:T(8,128)(2,1)S(1)} %collective-permute-done.23, bf16[128,256]{1,0:T(8,128)(2,1)S(1)} %collective-permute-done.22), kind=kLoop, calls=%fused_computation.5 | loop fusion | flops 229376 | bytes 393216 | tf_op jit(solution)/shard_map/convert_element_type | solution.py:529
  (13 shorter events, 0.0 us)
Async XLA Ops:
  0.6 15.2 %copy-start = (bf16[128,256]{1,0:T(8,128)(2,1)S(1)}, bf16[128,256]{1,0:T(8,128)(2,1)}, u32[]{:S(2)}) copy-start(bf16[128,256]{1,0:T(8,128)(2,1)} %refs_1_.3) | copy-start | bytes 196612
  0.6 10.1 %collective-permute-start = (bf16[128,256]{1,0:T(8,128)(2,1)}, bf16[128,256]{1,0:T(8,128)(2,1)S(1)}, u32[]{:S(2)}, u32[]{:S(2)}) collective-permute-start(bf16[128,256]{1,0:T(8,128)(2,1)} %refs_3_.1), channel_id=1, source_target_pairs={{0,4},{4,0},{8,12},{12,8},{1,5},{5,1},{9,13},{13,9},{2,6},{6,2},{1... | collective-permute-start | bytes 196616 | tf_op jit(solution)/shard_map/ppermute | solution.py:472
  3.7 9.4 %collective-permute-start.9 = (bf16[128,256]{1,0:T(8,128)(2,1)}, bf16[128,256]{1,0:T(8,128)(2,1)S(1)}, u32[]{:S(2)}, u32[]{:S(2)}) collective-permute-start(bf16[128,256]{1,0:T(8,128)(2,1)} %refs_3_.1), channel_id=1, source_target_pairs={{0,8},{4,12},{8,0},{12,4},{1,9},{5,13},{9,1},{13,5},{2,10},{6,14},... | collective-permute-start | bytes 196616 | tf_op jit(solution)/shard_map/ppermute | solution.py:472
  6.3 7.3 %collective-permute-start.11 = (bf16[128,256]{1,0:T(8,128)(2,1)}, bf16[128,256]{1,0:T(8,128)(2,1)S(1)}, u32[]{:S(2)}, u32[]{:S(2)}) collective-permute-start(bf16[128,256]{1,0:T(8,128)(2,1)} %refs_3_.1), channel_id=1, source_target_pairs={{0,12},{4,8},{8,4},{12,0},{1,13},{5,9},{9,5},{13,1},{2,14},{6,10},... | collective-permute-start | bytes 196616 | tf_op jit(solution)/shard_map/ppermute | solution.py:472
  6.3 9.1 %collective-permute-start.4 = (bf16[128,256]{1,0:T(8,128)(2,1)}, bf16[128,256]{1,0:T(8,128)(2,1)S(1)}, u32[]{:S(2)}, u32[]{:S(2)}) collective-permute-start(bf16[128,256]{1,0:T(8,128)(2,1)} %refs_1_.3), channel_id=1, source_target_pairs={{0,8},{4,12},{8,0},{12,4},{1,9},{5,13},{9,1},{13,5},{2,10},{6,14},... | collective-permute-start | bytes 196616 | tf_op jit(solution)/shard_map/ppermute | solution.py:472
  8.2 7.2 %collective-permute-start.2 = (bf16[128,256]{1,0:T(8,128)(2,1)}, bf16[128,256]{1,0:T(8,128)(2,1)S(1)}, u32[]{:S(2)}, u32[]{:S(2)}) collective-permute-start(bf16[128,256]{1,0:T(8,128)(2,1)} %refs_1_.3), channel_id=1, source_target_pairs={{0,4},{4,0},{8,12},{12,8},{1,5},{5,1},{9,13},{13,9},{2,6},{6,2},{1... | collective-permute-start | bytes 196616 | tf_op jit(solution)/shard_map/ppermute | solution.py:472
  13.0 2.8 %collective-permute-start.8 = (bf16[128,256]{1,0:T(8,128)(2,1)S(1)}, bf16[128,256]{1,0:T(8,128)(2,1)S(1)}, u32[]{:S(2)}, u32[]{:S(2)}) collective-permute-start(bf16[128,256]{1,0:T(8,128)(2,1)S(1)} %collective-permute-done.refs_3_), channel_id=1, source_target_pairs={{0,1},{1,0},{2,3},{3,2},{4,5},{5,4},{6,7},{7,6},{8,9},{9,8},{10,11... | collective-permute-start | bytes 196616 | tf_op jit(solution)/shard_map/ppermute | solution.py:471
  13.1 2.9 %collective-permute-start.7 = (bf16[128,256]{1,0:T(8,128)(2,1)S(1)}, bf16[128,256]{1,0:T(8,128)(2,1)S(1)}, u32[]{:S(2)}, u32[]{:S(2)}) collective-permute-start(bf16[128,256]{1,0:T(8,128)(2,1)S(1)} %get-tuple-element.34.refs_1_), channel_id=1, source_target_pairs={{0,1},{1,0},{2,3},{3,2},{4,5},{5,4},{6,7},{7,6},{8,9},{9,8},{10,11... | collective-permute-start | bytes 196616 | tf_op jit(solution)/shard_map/ppermute | solution.py:471
  13.6 2.7 %collective-permute-start.10 = (bf16[128,256]{1,0:T(8,128)(2,1)S(1)}, bf16[128,256]{1,0:T(8,128)(2,1)S(1)}, u32[]{:S(2)}, u32[]{:S(2)}) collective-permute-start(bf16[128,256]{1,0:T(8,128)(2,1)S(1)} %collective-permute-done.9.refs_5_), channel_id=1, source_target_pairs={{0,1},{1,0},{2,3},{3,2},{4,5},{5,4},{6,7},{7,6},{8,9},{9,8},{10,11... | collective-permute-start | bytes 196616 | tf_op jit(solution)/shard_map/ppermute | solution.py:471
  15.4 1.3 %collective-permute-start.12 = (bf16[128,256]{1,0:T(8,128)(2,1)S(1)}, bf16[128,256]{1,0:T(8,128)(2,1)S(1)}, u32[]{:S(2)}, u32[]{:S(2)}) collective-permute-start(bf16[128,256]{1,0:T(8,128)(2,1)S(1)} %collective-permute-done.11.refs_7_), channel_id=1, source_target_pairs={{0,1},{1,0},{2,3},{3,2},{4,5},{5,4},{6,7},{7,6},{8,9},{9,8},{10,11... | collective-permute-start | bytes 196616 | tf_op jit(solution)/shard_map/ppermute | solution.py:471
  15.4 4.7 %collective-permute-start.6 = (bf16[128,256]{1,0:T(8,128)(2,1)S(1)}, bf16[128,256]{1,0:T(8,128)(2,1)S(1)}, u32[]{:S(2)}, u32[]{:S(2)}) collective-permute-start(bf16[128,256]{1,0:T(8,128)(2,1)S(1)} %collective-permute-done.4.refs_5_), channel_id=1, source_target_pairs={{0,4},{4,0},{8,12},{12,8},{1,5},{5,1},{9,13},{13,9},{2,6},{6,2},{1... | collective-permute-start | bytes 196616 | tf_op jit(solution)/shard_map/ppermute | solution.py:472
  15.8 4.6 %collective-permute-start.1 = (bf16[128,256]{1,0:T(8,128)(2,1)S(1)}, bf16[128,256]{1,0:T(8,128)(2,1)S(1)}, u32[]{:S(2)}, u32[]{:S(2)}) collective-permute-start(bf16[128,256]{1,0:T(8,128)(2,1)S(1)} %copy-done), channel_id=1, source_target_pairs={{0,1},{1,0},{2,3},{3,2},{4,5},{5,4},{6,7},{7,6},{8,9},{9,8},{10,11... | collective-permute-start | bytes 196616 | tf_op jit(solution)/shard_map/ppermute | solution.py:471
  16.0 4.4 %collective-permute-start.5 = (bf16[128,256]{1,0:T(8,128)(2,1)S(1)}, bf16[128,256]{1,0:T(8,128)(2,1)S(1)}, u32[]{:S(2)}, u32[]{:S(2)}) collective-permute-start(bf16[128,256]{1,0:T(8,128)(2,1)S(1)} %collective-permute-done.4.refs_5_), channel_id=1, source_target_pairs={{0,1},{1,0},{2,3},{3,2},{4,5},{5,4},{6,7},{7,6},{8,9},{9,8},{10,11... | collective-permute-start | bytes 196616 | tf_op jit(solution)/shard_map/ppermute | solution.py:471
  16.3 4.1 %collective-permute-start.3 = (bf16[128,256]{1,0:T(8,128)(2,1)S(1)}, bf16[128,256]{1,0:T(8,128)(2,1)S(1)}, u32[]{:S(2)}, u32[]{:S(2)}) collective-permute-start(bf16[128,256]{1,0:T(8,128)(2,1)S(1)} %collective-permute-done.2.refs_3_), channel_id=1, source_target_pairs={{0,1},{1,0},{2,3},{3,2},{4,5},{5,4},{6,7},{7,6},{8,9},{9,8},{10,11... | collective-permute-start | bytes 196616 | tf_op jit(solution)/shard_map/ppermute | solution.py:471
  20.2 1.3 %collective-permute-start.13 = (bf16[128,256]{1,0:T(8,128)(2,1)S(1)}, bf16[128,256]{1,0:T(8,128)(2,1)S(1)}, u32[]{:S(2)}, u32[]{:S(2)}) collective-permute-start(bf16[128,256]{1,0:T(8,128)(2,1)S(1)} %collective-permute-done.6.refs_7_), channel_id=1, source_target_pairs={{0,1},{1,0},{2,3},{3,2},{4,5},{5,4},{6,7},{7,6},{8,9},{9,8},{10,11... | collective-permute-start | bytes 196616 | tf_op jit(solution)/shard_map/ppermute | solution.py:471
  24.8 5.9 %collective-permute-start.15 = (f32[2,8,512]{2,1,0:T(8,128)S(1)}, f32[2,8,512]{2,1,0:T(8,128)S(1)}, u32[]{:S(2)}, u32[]{:S(2)}) collective-permute-start(f32[2,8,512]{2,1,0:T(8,128)S(1)} %get-tuple-element.41.refs_1_), channel_id=1, source_target_pairs={{0,12},{4,8},{8,4},{12,0},{1,13},{5,9},{9,5},{13,1},{2,14},{6,10},... | collective-permute-start | bytes 98312 | tf_op jit(solution)/shard_map/ppermute | solution.py:472
  27.3 5.1 %collective-permute-start.16 = (f32[2,8,512]{2,1,0:T(8,128)S(1)}, f32[2,8,512]{2,1,0:T(8,128)S(1)}, u32[]{:S(2)}, u32[]{:S(2)}) collective-permute-start(f32[2,8,512]{2,1,0:T(8,128)S(1)} %get-tuple-element.41.refs_1_), channel_id=1, source_target_pairs={{0,8},{4,12},{8,0},{12,4},{1,9},{5,13},{9,1},{13,5},{2,10},{6,14},... | collective-permute-start | bytes 98312 | tf_op jit(solution)/shard_map/ppermute | solution.py:472
  27.8 4.6 %collective-permute-start.17 = (f32[2,8,512]{2,1,0:T(8,128)S(1)}, f32[2,8,512]{2,1,0:T(8,128)S(1)}, u32[]{:S(2)}, u32[]{:S(2)}) collective-permute-start(f32[2,8,512]{2,1,0:T(8,128)S(1)} %get-tuple-element.41.refs_1_), channel_id=1, source_target_pairs={{0,4},{4,0},{8,12},{12,8},{1,5},{5,1},{9,13},{13,9},{2,6},{6,2},{1... | collective-permute-start | bytes 98312 | tf_op jit(solution)/shard_map/ppermute | solution.py:472
  29.2 3.7 %collective-permute-start.14 = (f32[2,8,512]{2,1,0:T(8,128)S(1)}, f32[2,8,512]{2,1,0:T(8,128)S(1)}, u32[]{:S(2)}, u32[]{:S(2)}) collective-permute-start(f32[2,8,512]{2,1,0:T(8,128)S(1)} %get-tuple-element.41.refs_1_), channel_id=1, source_target_pairs={{0,1},{1,0},{2,3},{3,2},{4,5},{5,4},{6,7},{7,6},{8,9},{9,8},{10,11... | collective-permute-start | bytes 98312 | tf_op jit(solution)/shard_map/ppermute | solution.py:471
  32.4 1.2 %collective-permute-start.18 = (f32[2,8,512]{2,1,0:T(8,128)S(1)}, f32[2,8,512]{2,1,0:T(8,128)S(1)}, u32[]{:S(2)}, u32[]{:S(2)}) collective-permute-start(f32[2,8,512]{2,1,0:T(8,128)S(1)} %collective-permute-done.15.refs_3_), channel_id=1, source_target_pairs={{0,1},{1,0},{2,3},{3,2},{4,5},{5,4},{6,7},{7,6},{8,9},{9,8},{10,11... | collective-permute-start | bytes 98312 | tf_op jit(solution)/shard_map/ppermute | solution.py:471
  32.4 1.4 %collective-permute-start.19 = (f32[2,8,512]{2,1,0:T(8,128)S(1)}, f32[2,8,512]{2,1,0:T(8,128)S(1)}, u32[]{:S(2)}, u32[]{:S(2)}) collective-permute-start(f32[2,8,512]{2,1,0:T(8,128)S(1)} %collective-permute-done.16.refs_5_), channel_id=1, source_target_pairs={{0,1},{1,0},{2,3},{3,2},{4,5},{5,4},{6,7},{7,6},{8,9},{9,8},{10,11... | collective-permute-start | bytes 98312 | tf_op jit(solution)/shard_map/ppermute | solution.py:471
  32.9 1.2 %collective-permute-start.20 = (f32[2,8,512]{2,1,0:T(8,128)S(1)}, f32[2,8,512]{2,1,0:T(8,128)S(1)}, u32[]{:S(2)}, u32[]{:S(2)}) collective-permute-start(f32[2,8,512]{2,1,0:T(8,128)S(1)} %collective-permute-done.17.refs_7_), channel_id=1, source_target_pairs={{0,1},{1,0},{2,3},{3,2},{4,5},{5,4},{6,7},{7,6},{8,9},{9,8},{10,11... | collective-permute-start | bytes 98312 | tf_op jit(solution)/shard_map/ppermute | solution.py:471
  34.7 1.6 %collective-permute-start.21 = (bf16[4,128,256]{2,1,0:T(8,128)(2,1)S(1)}, bf16[4,128,256]{2,1,0:T(8,128)(2,1)S(1)}, u32[]{:S(2)}, u32[]{:S(2)}) collective-permute-start(bf16[4,128,256]{2,1,0:T(8,128)(2,1)S(1)} %get-tuple-element.50), channel_id=1, source_target_pairs={{0,1},{1,0},{2,3},{3,2},{4,5},{5,4},{6,7},{7,6},{8,9},{9,8},{10,11... | collective-permute-start | bytes 786440 | tf_op jit(solution)/shard_map/ppermute | solution.py:471
  36.4 7.8 %collective-permute-start.22 = (bf16[128,256]{1,0:T(8,128)(2,1)S(1)}, bf16[128,256]{1,0:T(8,128)(2,1)S(1)}, u32[]{:S(2)}, u32[]{:S(2)}) collective-permute-start(bf16[128,256]{1,0:T(8,128)(2,1)S(1)} %get-tuple-element.59), channel_id=1, source_target_pairs={{0,12},{4,8},{8,4},{12,0},{1,13},{5,9},{9,5},{13,1},{2,14},{6,10},... | collective-permute-start | bytes 196616 | tf_op jit(solution)/shard_map/ppermute | solution.py:472
  38.7 6.5 %collective-permute-start.23 = (bf16[128,256]{1,0:T(8,128)(2,1)S(1)}, bf16[128,256]{1,0:T(8,128)(2,1)S(1)}, u32[]{:S(2)}, u32[]{:S(2)}) collective-permute-start(bf16[128,256]{1,0:T(8,128)(2,1)S(1)} %get-tuple-element.61), channel_id=1, source_target_pairs={{0,8},{4,12},{8,0},{12,4},{1,9},{5,13},{9,1},{13,5},{2,10},{6,14},... | collective-permute-start | bytes 196616 | tf_op jit(solution)/shard_map/ppermute | solution.py:472
  38.7 6.5 %collective-permute-start.24 = (bf16[128,256]{1,0:T(8,128)(2,1)S(1)}, bf16[128,256]{1,0:T(8,128)(2,1)S(1)}, u32[]{:S(2)}, u32[]{:S(2)}) collective-permute-start(bf16[128,256]{1,0:T(8,128)(2,1)S(1)} %get-tuple-element.60), channel_id=1, source_target_pairs={{0,4},{4,0},{8,12},{12,8},{1,5},{5,1},{9,13},{13,9},{2,6},{6,2},{1... | collective-permute-start | bytes 196616 | tf_op jit(solution)/shard_map/ppermute | solution.py:472

commit v12 on v11

--- a/solution.py
+++ b/solution.py
@@ -39,7 +39,7 @@
     return copies
 
 
-OWNER, LIVE, TESTN, SLOT_IN, TABLE_OF, SLOT_OUT = range(6)
+OWNER, LIVE, TESTN, SLOT_IN, TABLE_OF, SLOT_OUT, OUT_TABLE = range(7)
 
 
 def vmem_spec():
@@ -94,8 +94,9 @@
             meta[SLOT_IN, t] = 2 * away + not_mine
             meta[TABLE_OF, t] = 2 * away + not_mine
             meta[SLOT_OUT, t] = 4 * not_mine + ((away + 3) & 3)
+            meta[OUT_TABLE, 4 * not_mine + ((away + 3) & 3)] = t
         else:
-            for row in (SLOT_IN, TABLE_OF, SLOT_OUT):
+            for row in (SLOT_IN, TABLE_OF, SLOT_OUT, OUT_TABLE):
                 meta[row, t] = t
 
     def earlier(n, carry):
@@ -124,7 +125,7 @@
         in_specs=[hbm_spec()] * 6,
         out_specs=[smem_spec(), vmem_spec(), vmem_spec()],
         out_shape=[
-            pltpu.SMEM((6, max(blocks, tables)), jnp.int32),
+            pltpu.SMEM((7, max(blocks, tables)), jnp.int32),
             pltpu.VMEM(query_rows.shape, query_rows.dtype),
             pltpu.VMEM((blocks, BLK, 2 * stacked + 2 * features), jnp.bfloat16),
         ],
@@ -320,37 +321,6 @@
     )(meta, *pieces, q_side, state)
 
 
-def query_sums_kernel(state, ab_ref, state_out):
-    blocks, _, features, _ = ab_ref.shape
-    stacked = features // HD * TEST
-    for b in range(blocks):
-        for p in range(features // LANES):
-            keys = state[b, :, 2 * stacked + p * LANES : 2 * stacked + (p + 1) * LANES]
-            for n, first in enumerate((stacked, 0)):
-                values = state[b, :, first + p * WIDE : first + (p + 1) * WIDE]
-                product = lax.dot_general(
-                    keys, values, (((0,), (0,)), ((), ())), preferred_element_type=jnp.float32
-                )
-                ab_ref[b, n, p * LANES : p * LANES + HD, :] = product[:HD, :TEST]
-                ab_ref[b, n, p * LANES + HD : (p + 1) * LANES, :] = product[HD:, TEST:]
-
-
-def query_sums(features, state):
-    blocks = state.shape[0]
-    return pl.pallas_call(
-        query_sums_kernel,
-        in_specs=[vmem_spec()],
-        out_specs=[vmem_spec()] * 2,
-        out_shape=[
-            pltpu.VMEM((blocks, 2, features, TEST), jnp.float32),
-            pltpu.VMEM(state.shape, jnp.bfloat16),
-        ],
-        input_output_aliases={0: 1},
-        compiler_params=params(8),
-        name="query_sums",
-    )(state)
-
-
 def merged(pieces):
     peak = pieces[0][0]
     for piece in pieces[1:]:
@@ -363,55 +333,130 @@
     return peak, mass, part / mass
 
 
-def query_grad_kernel(count, meta, *refs):
-    pieces = refs[:count]
-    q_side, g_side, ab_ref = refs[count : count + 3]
-    c_ref, d_ref, *q_refs = refs[count + 3 : -2]
-    tab_s, acc_s = refs[-2:]
+def query_sums_kernel(state, ab_ref, state_out):
+    blocks, _, features, _ = ab_ref.shape
+    stacked = features // HD * TEST
+    for b in range(blocks):
+        for p in range(features // LANES):
+            keys = state[b, :, 2 * stacked + p * LANES : 2 * stacked + (p + 1) * LANES]
+            for n, first in enumerate((stacked, 0)):
+                values = state[b, :, first + p * WIDE : first + (p + 1) * WIDE]
+                product = lax.dot_general(
+                    keys, values, (((0,), (0,)), ((), ())), preferred_element_type=jnp.float32
+                )
+                ab_ref[b, n, p * LANES : p * LANES + HD, :] = product[:HD, :TEST]
+                ab_ref[b, n, p * LANES + HD : (p + 1) * LANES, :] = product[HD:, TEST:]
+
+
+def query_sums(features, state):
+    blocks = state.shape[0]
+    return pl.pallas_call(
+        query_sums_kernel,
+        in_specs=[vmem_spec()],
+        out_specs=[vmem_spec()] * 2,
+        out_shape=[
+            pltpu.VMEM((blocks, 2, features, TEST), jnp.float32),
+            pltpu.VMEM(state.shape, jnp.bfloat16),
+        ],
+        input_output_aliases={0: 1},
+        compiler_params=params(8),
+        name="query_sums",
+    )(state)
+
+
+def chip_sums_kernel(count, meta, *refs):
+    tabs = refs[:count]
+    q_side, g_side, ab_ref, *sums, acc_s, tab_s = refs[count:]
+    tables, _, features, _ = acc_s.shape
     blocks = ab_ref.shape[0]
-    tables, features, _ = acc_s.shape
     heads = features // HD
-    tab_s[0], tab_s[1], tab_s[2] = merged(pieces)
+    tab_s[0], tab_s[1], tab_s[2] = merged(tabs)
     acc_s[...] = jnp.zeros_like(acc_s)
     for b in range(blocks):
         at = meta[SLOT_OUT, meta[OWNER, b]]
         table = pl.ds(meta[OWNER, b], 1)
         row = tables * features + b * heads
-        mass = tab_s[1, table, :]
-        c = jnp.exp2(get_heads(q_side, row, heads) - tab_s[0, table, :]) / mass
+        c = jnp.exp2(get_heads(q_side, row, heads) - tab_s[0, table, :]) / tab_s[1, table, :]
         d = c * (get_heads(g_side, row, heads) - tab_s[2, table, :])
-        c_ref[b : b + 1, :] = c
-        d_ref[b : b + 1, :] = d
         for h in range(heads):
             rows = slice(h * HD, (h + 1) * HD)
             lanes = slice(h * TEST, (h + 1) * TEST)
-            acc_s[at, rows, :] += c[:, lanes] * ab_ref[b, 0, rows, :] + d[:, lanes] * ab_ref[b, 1, rows, :]
-    per = tables // len(q_refs)
-    for n in range(tables):
-        ref = q_refs[n // per]
-        ref[n % per] = (acc_s[n] * SCORE_SCALE).T.astype(ref.dtype)
-
-
-def query_grads(meta, tables, pieces, sides, ab, q_dtypes):
-    blocks, _, features, _ = ab.shape
-    stacked = features // HD * TEST
-    per = tables // len(q_dtypes)
-    return pl.pallas_call(
-        lambda *refs: query_grad_kernel(len(pieces), *refs),
-        in_specs=[smem_spec()] + [vmem_spec()] * (len(pieces) + 3),
+            moved, plain = ab_ref[b, 0, rows, :], ab_ref[b, 1, rows, :]
+            acc_s[at, 0, rows, :] += c[:, lanes] * moved + d[:, lanes] * plain
+            acc_s[at, 1, rows, :] += c[:, lanes] * plain
+    per = tables // len(sums)
+    for n, ref in enumerate(sums):
+        ref[...] = acc_s[n * per : (n + 1) * per].astype(ref.dtype)
+
+
+def chip_sums(meta, tabs, q_side, g_side, ab, features, dtypes):
+    tables, stacked = tabs[0].shape[1:]
+    count = len(tabs)
+    per = tables // len(dtypes)
+    return pl.pallas_call(
+        lambda *refs: chip_sums_kernel(count, *refs),
+        in_specs=[smem_spec()] + [vmem_spec()] * (count + 3),
+        out_specs=[vmem_spec()] * len(dtypes),
+        out_shape=[jax.ShapeDtypeStruct((per, 2, features, TEST), dtype) for dtype in dtypes],
+        scratch_shapes=[
+            pltpu.VMEM((tables, 2, features, TEST), jnp.float32),
+            pltpu.VMEM((3, tables, stacked), jnp.float32),
+        ],
+        compiler_params=params(10),
+        name="chip_sums",
+    )(meta, *tabs, q_side, g_side, ab)
+
+
+def query_grad_kernel(near, count, held, meta, *refs):
+    chip, pieces = refs[:near], refs[near : near + count]
+    count += near
+    sums = refs[count : count + held]
+    q_side, g_side, c_ref, d_ref, *outs, chip_s, tab_s = refs[count + held :]
+    blocks, stacked = c_ref.shape
+    heads = stacked // TEST
+    first = q_side.shape[0] - blocks * heads
+    chip_s[0], chip_s[1], chip_s[2] = merged(chip)
+    tab_s[0], tab_s[1], tab_s[2] = merged(pieces)
+    for n, ref in enumerate(outs):
+        table = pl.ds(meta[OUT_TABLE, n], 1)
+        c = jnp.exp2(chip_s[0, table, :] - tab_s[0, table, :])
+        c = c * chip_s[1, table, :] / tab_s[1, table, :]
+        d = c * (chip_s[2, table, :] - tab_s[2, table, :])
+        parts = []
+        for h in range(heads):
+            rows = slice(h * HD, (h + 1) * HD)
+            lanes = slice(h * TEST, (h + 1) * TEST)
+            moved = sum(value[n, 0, rows, :].astype(jnp.float32) for value in sums)
+            plain = sum(value[n, 1, rows, :].astype(jnp.float32) for value in sums)
+            parts.append(c[:, lanes] * moved + d[:, lanes] * plain)
+        ref[...] = (jnp.concatenate(parts, axis=0) * SCORE_SCALE).T.astype(ref.dtype)
+    for b in range(blocks):
+        table = pl.ds(meta[OWNER, b], 1)
+        row = first + b * heads
+        c = jnp.exp2(get_heads(q_side, row, heads) - tab_s[0, table, :]) / tab_s[1, table, :]
+        c_ref[b : b + 1, :] = c
+        d_ref[b : b + 1, :] = c * (get_heads(g_side, row, heads) - tab_s[2, table, :])
+
+
+def query_grads(meta, chip, pieces, sums, q_side, g_side, blocks, q_dtypes):
+    tables, stacked = pieces[0].shape[1:]
+    features = sums[0].shape[2]
+    return pl.pallas_call(
+        lambda *refs: query_grad_kernel(len(chip), len(pieces), len(sums), *refs),
+        in_specs=[smem_spec()] + [vmem_spec()] * (len(chip) + len(pieces) + len(sums) + 2),
         out_specs=[vmem_spec()] * (2 + len(q_dtypes)),
         out_shape=[
             jax.ShapeDtypeStruct((blocks, stacked), jnp.float32),
             jax.ShapeDtypeStruct((blocks, stacked), jnp.float32),
         ]
-        + [jax.ShapeDtypeStruct((per, TEST, features), dtype) for dtype in q_dtypes],
+        + [jax.ShapeDtypeStruct((TEST, features), dtype) for dtype in q_dtypes],
         scratch_shapes=[
             pltpu.VMEM((3, tables, stacked), jnp.float32),
-            pltpu.VMEM((tables, features, TEST), jnp.float32),
+            pltpu.VMEM((3, tables, stacked), jnp.float32),
         ],
         compiler_params=params(10),
         name="query_grads",
-    )(meta, *pieces, *sides, ab)
+    )(meta, *chip, *pieces, *sums, q_side, g_side)
 
 
 def row_grads_kernel(meta, c_ref, d_ref, q_side, g_side, state, dk_hbm, dv_hbm, dk_s, dv_s, out_sem):
@@ -497,33 +542,37 @@
     g_side, tab, state = moved_weights(meta, grads, q_side, state, features, tables)
     if small:
         near = [step(tab, s) for s in (3, 2, 1)]
+        own = [tab, pair(tab)]
         ab, state = query_sums(features, state)
         *near, ab = lax.optimization_barrier((*near, ab))
-        stats = [tab, pair(tab)]
+        keep, send = chip_sums(
+            meta, own, q_side, g_side, ab, features, [jnp.float32, jnp.bfloat16]
+        )
+        received = pair(send)
+        stats = own
         for value in near:
-            stats += [value, pair(value)]
-        dtypes = [jnp.float32, jnp.bfloat16]
+            stats = stats + [value, pair(value)]
+        dtypes = [jnp.bfloat16] * 3 + [jnp.float32]
+        c, d, *low, query_grad = query_grads(
+            meta, own, stats, [keep, received], q_side, g_side, blocks, dtypes
+        )
+        got = [step(low[s - 1], s) for s in (3, 2, 1)]
+        *low, c = lax.optimization_barrier((*low, c))
+        key_grad, value_grad = row_grads(meta, c, d, (q_side, g_side), state, features)
+        for value in got:
+            query_grad = query_grad + value.astype(jnp.float32)
     else:
         ab, state = query_sums(features, state)
+        (sums,) = chip_sums(meta, [tab], q_side, g_side, ab, features, [jnp.float32])
         peak = lax.pmax(tab[0], RP)
         weight = jnp.exp2(tab[0] - peak)
         total, part = lax.psum(jnp.stack([weight, weight * tab[1]]), RP)
-        stats = [jnp.stack([peak + jnp.log2(total), part / total])]
-        dtypes = [jnp.float32]
-    c, d, *q_terms = query_grads(meta, tables, stats, (q_side, g_side), ab, dtypes)
-    if small:
-        keep, send = q_terms
-        total = keep + pair(send).astype(jnp.float32)
-        low = total.astype(jnp.bfloat16)
-        got = [step(low[s - 1], s) for s in (3, 2, 1)]
-        low, c = lax.optimization_barrier((low, c))
-        key_grad, value_grad = row_grads(meta, c, d, (q_side, g_side), state, features)
-        query_grad = total[3]
-        for value in got:
-            query_grad = query_grad + value.astype(jnp.float32)
-    else:
+        rest = jnp.stack([peak + jnp.log2(total), part / total])
+        c, d, *terms = query_grads(
+            meta, [tab], [rest], [sums], q_side, g_side, blocks, [jnp.float32] * tables
+        )
         query_grad = lax.psum_scatter(
-            q_terms[0].reshape(tables * TEST, features), RP, scatter_dimension=0, tiled=True
+            jnp.concatenate(terms, axis=0), RP, scatter_dimension=0, tiled=True
         )
         key_grad, value_grad = row_grads(meta, c, d, (q_side, g_side), state, features)
     return query_grad.astype(jnp.bfloat16), key_grad, value_grad

time: 46.1 us -> 45.1 us (0.978)
  waiting for transfers between devices: 8.5 us -> 7.01 us
    ppermute x13, waiting for transfers between devices: 3.81 us -> 2.26 us  [local(): pair = lambda value: lax.ppermute(value, 'pair', PAIR)]
  transfers between devices with their start and end apart: 25 -> 25, of which waited for: 10 -> 7; matrix products, arithmetic and copies ran while one was open for 0% -> 0% of each run, Pallas kernels for 23% -> 23%
where the time goes in v12:
time: 45.1 us; the launch traced here: 44.9 us
  starting transfers between devices  22 us (49%)
  Pallas kernels  14.5 us (32%)
  waiting for transfers between devices  7.01 us (16%)
  between operations  0.75 us (2%)
  other arithmetic  0.66 us (1%)
    ppermute x12, starting transfers between devices, local(): lax.ppermute(value, 'rows', [(z, z ^ s) for z in range(4)])  19.3 us
    ppermute x12, waiting for transfers between devices, local(): lax.ppermute(value, 'rows', [(z, z ^ s) for z in range(4)])  4.74 us
    pallas_call x1, Pallas kernels, block_weights(): pl.pallas_call(lambda *refs: weights_kernel(count, features, *refs), in_s...  3.48 us
    pallas_call x1, Pallas kernels, row_grads(): pl.pallas_call(row_grads_kernel, in_specs=[smem_spec()] + [vmem_spec()] *...  3.29 us
    pallas_call x1, Pallas kernels, moved_weights(): pl.pallas_call(lambda *refs: moved_kernel(count, features, *refs), in_spe...  3.25 us
    ppermute x13, starting transfers between devices, local(): pair = lambda value: lax.ppermute(value, 'pair', PAIR)  2.68 us
    pallas_call x1, Pallas kernels, index_table(): pl.pallas_call(lambda *refs: index_kernel(small, *refs), in_specs=[hbm_sp...  2.33 us
    ppermute x13, waiting for transfers between devices, local(): pair = lambda value: lax.ppermute(value, 'pair', PAIR)  2.26 us
  transfers between devices with their start and end apart: 25, of which 7 were waited for; matrix products, arithmetic and copies ran while one was open for 0% of the time, Pallas kernels for 23%

profile of v12, /device:TPU:0, one launch (start us, length us, event | category | flops | bytes accessed | tf_op | source)
XLA Modules:
  0.0 44.9 jit_solution(16506582243711497145)
XLA Ops:
  0.6 3.1 %collective-permute-start = (bf16[128,256]{1,0:T(8,128)(2,1)}, bf16[128,256]{1,0:T(8,128)(2,1)S(1)}, u32[]{:S(2)}, u32[]{:S(2)}) collective-permute-start(bf16[128,256]{1,0:T(8,128)(2,1)} %refs_3_.1), channel_id=1, source_target_pairs={{0,4},{4,0},{8,12},{12,8},{1,5},{5,1},{9,13},{13,9},{2,6},{6,2},{1... | collective-permute-start | bytes 196616 | tf_op jit(solution)/shard_map/ppermute | solution.py:517
  3.7 2.6 %collective-permute-start.9 = (bf16[128,256]{1,0:T(8,128)(2,1)}, bf16[128,256]{1,0:T(8,128)(2,1)S(1)}, u32[]{:S(2)}, u32[]{:S(2)}) collective-permute-start(bf16[128,256]{1,0:T(8,128)(2,1)} %refs_3_.1), channel_id=1, source_target_pairs={{0,8},{4,12},{8,0},{12,4},{1,9},{5,13},{9,1},{13,5},{2,10},{6,14},... | collective-permute-start | bytes 196616 | tf_op jit(solution)/shard_map/ppermute | solution.py:517
  6.3 1.9 %collective-permute-start.4 = (bf16[128,256]{1,0:T(8,128)(2,1)}, bf16[128,256]{1,0:T(8,128)(2,1)S(1)}, u32[]{:S(2)}, u32[]{:S(2)}) collective-permute-start(bf16[128,256]{1,0:T(8,128)(2,1)} %refs_1_.3), channel_id=1, source_target_pairs={{0,8},{4,12},{8,0},{12,4},{1,9},{5,13},{9,1},{13,5},{2,10},{6,14},... | collective-permute-start | bytes 196616 | tf_op jit(solution)/shard_map/ppermute | solution.py:517
  8.2 2.5 %collective-permute-start.2 = (bf16[128,256]{1,0:T(8,128)(2,1)}, bf16[128,256]{1,0:T(8,128)(2,1)S(1)}, u32[]{:S(2)}, u32[]{:S(2)}) collective-permute-start(bf16[128,256]{1,0:T(8,128)(2,1)} %refs_1_.3), channel_id=1, source_target_pairs={{0,4},{4,0},{8,12},{12,8},{1,5},{5,1},{9,13},{13,9},{2,6},{6,2},{1... | collective-permute-start | bytes 196616 | tf_op jit(solution)/shard_map/ppermute | solution.py:517
  10.7 0.0 collective-permute-done.refs_3_
  10.7 2.3 %index_table.1 = (s32[7,8]{1,0:T(8,128)S(4)}, bf16[128,256]{1,0:T(8,128)(2,1)S(1)}, bf16[8,512,1536]{2,1,0:T(8,128)(2,1)S(1)}) custom-call(s32[64]{0:T(128)} %refs_0_, s32[8]{0:T(128)} %refs_1_.2, s32[8]{0:T(128)} %refs_2_.1, bf16[128,256]{1,0:T(8,128)(2,1)} %refs_3_.1, bf16[4096,256]{1,0:T(8,128)(2,1)} %refs_4_.1, bf16[4096,256]{1,0:T(8,128)(2,1)} %refs_5_.1), custom_call_target="tpu_custom_call" | custom-call | tf_op jit(solution)/shard_map/index_table/pallas_call | solution.py:123
  13.0 0.1 collective-permute-start.8
  13.1 0.0 collective-permute-done.9.refs_5_
  13.1 0.5 %collective-permute-start.7 = (bf16[128,256]{1,0:T(8,128)(2,1)S(1)}, bf16[128,256]{1,0:T(8,128)(2,1)S(1)}, u32[]{:S(2)}, u32[]{:S(2)}) collective-permute-start(bf16[128,256]{1,0:T(8,128)(2,1)S(1)} %get-tuple-element.38.refs_1_), channel_id=1, source_target_pairs={{0,1},{1,0},{2,3},{3,2},{4,5},{5,4},{6,7},{7,6},{8,9},{9,8},{10,11... | collective-permute-start | bytes 196616 | tf_op jit(solution)/shard_map/ppermute | solution.py:516
  13.6 0.0 collective-permute-done.11.refs_7_
  13.6 0.1 collective-permute-start.10
  13.7 1.7 %collective-permute-done.4.refs_5_ = bf16[128,256]{1,0:T(8,128)(2,1)S(1)} collective-permute-done((bf16[128,256]{1,0:T(8,128)(2,1)}, bf16[128,256]{1,0:T(8,128)(2,1)S(1)}, u32[]{:S(2)}, u32[]{:S(2)}) %collective-permute-start.4) | collective-permute-done | bytes 65568 | tf_op jit(solution)/shard_map/ppermute | solution.py:517
  15.4 0.4 collective-permute-start.6
  15.8 0.0 collective-permute-done.8.refs_4_
  15.8 0.2 collective-permute-start.1
  16.0 0.3 collective-permute-start.5
  16.3 0.0 collective-permute-done.10.refs_6_
  16.3 0.2 collective-permute-start.3
  16.6 0.1 collective-permute-done.12.refs_8_
  16.7 3.5 %block_weights.1 = (f32[2080,128]{1,0:T(8,128)S(1)}, bf16[8,512,1536]{2,1,0:T(8,128)(2,1)S(1)}) custom-call(s32[7,8]{1,0:T(8,128)S(4)} %get-tuple-element.37.refs_0_.meta, bf16[128,256]{1,0:T(8,128)(2,1)S(1)} %get-tuple-element.38.refs_1_, bf16[128,256]{1,0:T(8,128)(2,1)S(1)} %collective-permute-done.7.refs_2_, ...), custom_call_target="tpu_custom_call", output_to_operand_aliasing={{1}: (9, {})} | custom-call | tf_op jit(solution)/shard_map/block_weights/pallas_call | solution.py:219
  20.2 0.0 collective-permute-done.6.refs_7_
  20.2 0.2 collective-permute-start.13
  20.4 1.1 %collective-permute-done.13.refs_8_ = bf16[128,256]{1,0:T(8,128)(2,1)S(1)} collective-permute-done((bf16[128,256]{1,0:T(8,128)(2,1)S(1)}, bf16[128,256]{1,0:T(8,128)(2,1)S(1)}, u32[]{:S(2)}, u32[]{:S(2)}) %collective-permute-start.13) | collective-permute-done | bytes 65568 | tf_op jit(solution)/shard_map/ppermute | solution.py:516
  21.5 3.3 %moved_weights.1 = (f32[2112,128]{1,0:T(8,128)S(1)}, f32[2,8,512]{2,1,0:T(8,128)S(1)}, bf16[8,512,1536]{2,1,0:T(8,128)(2,1)S(1)}) custom-call(s32[7,8]{1,0:T(8,128)S(4)} %get-tuple-element.37.refs_0_.meta, bf16[128,256]{1,0:T(8,128)(2,1)S(1)} %copy-done, bf16[128,256]{1,0:T(8,128)(2,1)S(1)} %collective-permute-done.1.refs_2_, ...), custom_call_target="tpu_custom_call", output_to_operand_aliasing={{2}: (10, {})} | custom-call | tf_op jit(solution)/shard_map/moved_weights/pallas_call | solution.py:308
  24.8 2.5 %collective-permute-start.15 = (f32[2,8,512]{2,1,0:T(8,128)S(1)}, f32[2,8,512]{2,1,0:T(8,128)S(1)}, u32[]{:S(2)}, u32[]{:S(2)}) collective-permute-start(f32[2,8,512]{2,1,0:T(8,128)S(1)} %get-tuple-element.45.refs_1_.refs_3_), channel_id=1, source_target_pairs={{0,12},{4,8},{8,4},{12,0},{1,13},{5,9},{9,5},{13,1},{2,14},{6,10},... | collective-permute-start | bytes 98312 | tf_op jit(solution)/shard_map/ppermute | solution.py:517
  27.3 0.5 %collective-permute-start.16 = (f32[2,8,512]{2,1,0:T(8,128)S(1)}, f32[2,8,512]{2,1,0:T(8,128)S(1)}, u32[]{:S(2)}, u32[]{:S(2)}) collective-permute-start(f32[2,8,512]{2,1,0:T(8,128)S(1)} %get-tuple-element.45.refs_1_.refs_3_), channel_id=1, source_target_pairs={{0,8},{4,12},{8,0},{12,4},{1,9},{5,13},{9,1},{13,5},{2,10},{6,14},... | collective-permute-start | bytes 98312 | tf_op jit(solution)/shard_map/ppermute | solution.py:517
  27.8 1.4 %collective-permute-start.17 = (f32[2,8,512]{2,1,0:T(8,128)S(1)}, f32[2,8,512]{2,1,0:T(8,128)S(1)}, u32[]{:S(2)}, u32[]{:S(2)}) collective-permute-start(f32[2,8,512]{2,1,0:T(8,128)S(1)} %get-tuple-element.45.refs_1_.refs_3_), channel_id=1, source_target_pairs={{0,4},{4,0},{8,12},{12,8},{1,5},{5,1},{9,13},{13,9},{2,6},{6,2},{1... | collective-permute-start | bytes 98312 | tf_op jit(solution)/shard_map/ppermute | solution.py:517
  29.2 0.0 collective-permute-start.14
  29.2 1.3 %query_sums.1 = (f32[8,2,256,128]{3,2,1,0:T(8,128)S(1)}, bf16[8,512,1536]{2,1,0:T(8,128)(2,1)S(1)}) custom-call(bf16[8,512,1536]{2,1,0:T(8,128)(2,1)S(1)} %get-tuple-element.46.state), custom_call_target="tpu_custom_call", output_to_operand_aliasing={{1}: (0, {})} | custom-call | tf_op jit(solution)/shard_map/query_sums/pallas_call | solution.py:353
  30.5 0.1 collective-permute-done.15.refs_5_
  30.6 1.8 %collective-permute-done.16.refs_7_ = f32[2,8,512]{2,1,0:T(8,128)S(1)} collective-permute-done((f32[2,8,512]{2,1,0:T(8,128)S(1)}, f32[2,8,512]{2,1,0:T(8,128)S(1)}, u32[]{:S(2)}, u32[]{:S(2)}) %collective-permute-start.16) | collective-permute-done | bytes 32800 | tf_op jit(solution)/shard_map/ppermute | solution.py:517
  32.4 0.0 collective-permute-done.17.refs_9_
  32.4 0.0 collective-permute-done.14.refs_2_.refs_4_
  32.4 0.5 %chip_sums.1 = (f32[4,2,256,128]{3,2,1,0:T(8,128)S(1)}, bf16[4,2,256,128]{3,2,1,0:T(8,128)(2,1)S(1)}) custom-call(s32[7,8]{1,0:T(8,128)S(4)} %get-tuple-element.37.refs_0_.meta, f32[2,8,512]{2,1,0:T(8,128)S(1)} %get-tuple-element.45.refs_1_.refs_3_, f32[2,8,512]{2,1,0:T(8,128)S(1)} %collective-permute-done.14.refs_2_.refs_4_, ...), custom_call_target="tpu_custom_call" | custom-call | tf_op jit(solution)/shard_map/chip_sums/pallas_call | solution.py:396
  33.0 0.1 collective-permute-start.21
  33.1 0.5 %collective-permute-start.18 = (f32[2,8,512]{2,1,0:T(8,128)S(1)}, f32[2,8,512]{2,1,0:T(8,128)S(1)}, u32[]{:S(2)}, u32[]{:S(2)}) collective-permute-start(f32[2,8,512]{2,1,0:T(8,128)S(1)} %collective-permute-done.15.refs_5_), channel_id=1, source_target_pairs={{0,1},{1,0},{2,3},{3,2},{4,5},{5,4},{6,7},{7,6},{8,9},{9,8},{10,11... | collective-permute-start | bytes 98312 | tf_op jit(solution)/shard_map/ppermute | solution.py:516
  33.6 0.1 collective-permute-start.19
  33.6 0.4 collective-permute-start.20
  34.1 0.9 %collective-permute-done.18.refs_6_ = f32[2,8,512]{2,1,0:T(8,128)S(1)} collective-permute-done((f32[2,8,512]{2,1,0:T(8,128)S(1)}, f32[2,8,512]{2,1,0:T(8,128)S(1)}, u32[]{:S(2)}, u32[]{:S(2)}) %collective-permute-start.18) | collective-permute-done | bytes 32800 | tf_op jit(solution)/shard_map/ppermute | solution.py:516
  35.0 0.0 collective-permute-done.19.refs_8_
  35.1 0.0 collective-permute-done.20.refs_10_
  35.1 0.0 collective-permute-done.21.refs_12_
  35.1 0.3 query_grads.1
  35.4 2.2 %collective-permute-start.22 = (bf16[128,256]{1,0:T(8,128)(2,1)S(1)}, bf16[128,256]{1,0:T(8,128)(2,1)S(1)}, u32[]{:S(2)}, u32[]{:S(2)}) collective-permute-start(bf16[128,256]{1,0:T(8,128)(2,1)S(1)} %get-tuple-element.56), channel_id=1, source_target_pairs={{0,12},{4,8},{8,4},{12,0},{1,13},{5,9},{9,5},{13,1},{2,14},{6,10},... | collective-permute-start | bytes 196616 | tf_op jit(solution)/shard_map/ppermute | solution.py:517
  37.7 2.2 %collective-permute-start.24 = (bf16[128,256]{1,0:T(8,128)(2,1)S(1)}, bf16[128,256]{1,0:T(8,128)(2,1)S(1)}, u32[]{:S(2)}, u32[]{:S(2)}) collective-permute-start(bf16[128,256]{1,0:T(8,128)(2,1)S(1)} %get-tuple-element.58), channel_id=1, source_target_pairs={{0,4},{4,0},{8,12},{12,8},{1,5},{5,1},{9,13},{13,9},{2,6},{6,2},{1... | collective-permute-start | bytes 196616 | tf_op jit(solution)/shard_map/ppermute | solution.py:517
  39.9 3.3 %row_grads.1 = (bf16[4096,256]{1,0:T(8,128)(2,1)}, bf16[4096,256]{1,0:T(8,128)(2,1)}) custom-call(s32[7,8]{1,0:T(8,128)S(4)} %get-tuple-element.37.refs_0_.meta, f32[8,512]{1,0:T(8,128)S(1)} %get-tuple-element.60.c_ref, f32[8,512]{1,0:T(8,128)S(1)} %get-tuple-element.61.d_ref, f32[2080,128]{1,0:T(8,128)S(1)} %get-tuple-element.43.refs_9_.refs_3_.refs_13_.q_side, ...), custom_call_target="tpu_custom_call" | custom-call | tf_op jit(solution)/shard_map/row_grads/pallas_call | solution.py:497
  43.2 1.1 %collective-permute-done.23 = bf16[128,256]{1,0:T(8,128)(2,1)S(1)} collective-permute-done((bf16[128,256]{1,0:T(8,128)(2,1)S(1)}, bf16[128,256]{1,0:T(8,128)(2,1)S(1)}, u32[]{:S(2)}, u32[]{:S(2)}) %collective-permute-start.23) | collective-permute-done | bytes 65568 | tf_op jit(solution)/shard_map/ppermute | solution.py:517
  44.3 0.7 %add_convert_fusion = bf16[128,256]{1,0:T(8,128)(2,1)} fusion(bf16[128,256]{1,0:T(8,128)(2,1)S(1)} %collective-permute-done.24, bf16[128,256]{1,0:T(8,128)(2,1)S(1)} %collective-permute-done.23, f32[128,256]{1,0:T(8,128)S(1)} %get-tuple-element.55, bf16[128,256]{1,0:T(8,128)(2,1)S(1)} %collective-permute-done.22), kind=kLoop, calls=%fused_computation | loop fusion | flops 229376 | bytes 393216 | tf_op jit(solution)/shard_map/convert_element_type | solution.py:578
  (12 shorter events, 0.0 us)
Async XLA Ops:
  0.6 15.2 %copy-start = (bf16[128,256]{1,0:T(8,128)(2,1)S(1)}, bf16[128,256]{1,0:T(8,128)(2,1)}, u32[]{:S(2)}) copy-start(bf16[128,256]{1,0:T(8,128)(2,1)} %refs_1_.3) | copy-start | bytes 196612
  0.6 10.1 %collective-permute-start = (bf16[128,256]{1,0:T(8,128)(2,1)}, bf16[128,256]{1,0:T(8,128)(2,1)S(1)}, u32[]{:S(2)}, u32[]{:S(2)}) collective-permute-start(bf16[128,256]{1,0:T(8,128)(2,1)} %refs_3_.1), channel_id=1, source_target_pairs={{0,4},{4,0},{8,12},{12,8},{1,5},{5,1},{9,13},{13,9},{2,6},{6,2},{1... | collective-permute-start | bytes 196616 | tf_op jit(solution)/shard_map/ppermute | solution.py:517
  3.7 9.4 %collective-permute-start.9 = (bf16[128,256]{1,0:T(8,128)(2,1)}, bf16[128,256]{1,0:T(8,128)(2,1)S(1)}, u32[]{:S(2)}, u32[]{:S(2)}) collective-permute-start(bf16[128,256]{1,0:T(8,128)(2,1)} %refs_3_.1), channel_id=1, source_target_pairs={{0,8},{4,12},{8,0},{12,4},{1,9},{5,13},{9,1},{13,5},{2,10},{6,14},... | collective-permute-start | bytes 196616 | tf_op jit(solution)/shard_map/ppermute | solution.py:517
  6.3 7.3 %collective-permute-start.11 = (bf16[128,256]{1,0:T(8,128)(2,1)}, bf16[128,256]{1,0:T(8,128)(2,1)S(1)}, u32[]{:S(2)}, u32[]{:S(2)}) collective-permute-start(bf16[128,256]{1,0:T(8,128)(2,1)} %refs_3_.1), channel_id=1, source_target_pairs={{0,12},{4,8},{8,4},{12,0},{1,13},{5,9},{9,5},{13,1},{2,14},{6,10},... | collective-permute-start | bytes 196616 | tf_op jit(solution)/shard_map/ppermute | solution.py:517
  6.3 9.1 %collective-permute-start.4 = (bf16[128,256]{1,0:T(8,128)(2,1)}, bf16[128,256]{1,0:T(8,128)(2,1)S(1)}, u32[]{:S(2)}, u32[]{:S(2)}) collective-permute-start(bf16[128,256]{1,0:T(8,128)(2,1)} %refs_1_.3), channel_id=1, source_target_pairs={{0,8},{4,12},{8,0},{12,4},{1,9},{5,13},{9,1},{13,5},{2,10},{6,14},... | collective-permute-start | bytes 196616 | tf_op jit(solution)/shard_map/ppermute | solution.py:517
  8.2 7.2 %collective-permute-start.2 = (bf16[128,256]{1,0:T(8,128)(2,1)}, bf16[128,256]{1,0:T(8,128)(2,1)S(1)}, u32[]{:S(2)}, u32[]{:S(2)}) collective-permute-start(bf16[128,256]{1,0:T(8,128)(2,1)} %refs_1_.3), channel_id=1, source_target_pairs={{0,4},{4,0},{8,12},{12,8},{1,5},{5,1},{9,13},{13,9},{2,6},{6,2},{1... | collective-permute-start | bytes 196616 | tf_op jit(solution)/shard_map/ppermute | solution.py:517
  13.0 2.8 %collective-permute-start.8 = (bf16[128,256]{1,0:T(8,128)(2,1)S(1)}, bf16[128,256]{1,0:T(8,128)(2,1)S(1)}, u32[]{:S(2)}, u32[]{:S(2)}) collective-permute-start(bf16[128,256]{1,0:T(8,128)(2,1)S(1)} %collective-permute-done.refs_3_), channel_id=1, source_target_pairs={{0,1},{1,0},{2,3},{3,2},{4,5},{5,4},{6,7},{7,6},{8,9},{9,8},{10,11... | collective-permute-start | bytes 196616 | tf_op jit(solution)/shard_map/ppermute | solution.py:516
  13.1 2.9 %collective-permute-start.7 = (bf16[128,256]{1,0:T(8,128)(2,1)S(1)}, bf16[128,256]{1,0:T(8,128)(2,1)S(1)}, u32[]{:S(2)}, u32[]{:S(2)}) collective-permute-start(bf16[128,256]{1,0:T(8,128)(2,1)S(1)} %get-tuple-element.38.refs_1_), channel_id=1, source_target_pairs={{0,1},{1,0},{2,3},{3,2},{4,5},{5,4},{6,7},{7,6},{8,9},{9,8},{10,11... | collective-permute-start | bytes 196616 | tf_op jit(solution)/shard_map/ppermute | solution.py:516
  13.6 2.7 %collective-permute-start.10 = (bf16[128,256]{1,0:T(8,128)(2,1)S(1)}, bf16[128,256]{1,0:T(8,128)(2,1)S(1)}, u32[]{:S(2)}, u32[]{:S(2)}) collective-permute-start(bf16[128,256]{1,0:T(8,128)(2,1)S(1)} %collective-permute-done.9.refs_5_), channel_id=1, source_target_pairs={{0,1},{1,0},{2,3},{3,2},{4,5},{5,4},{6,7},{7,6},{8,9},{9,8},{10,11... | collective-permute-start | bytes 196616 | tf_op jit(solution)/shard_map/ppermute | solution.py:516
  15.4 1.3 %collective-permute-start.12 = (bf16[128,256]{1,0:T(8,128)(2,1)S(1)}, bf16[128,256]{1,0:T(8,128)(2,1)S(1)}, u32[]{:S(2)}, u32[]{:S(2)}) collective-permute-start(bf16[128,256]{1,0:T(8,128)(2,1)S(1)} %collective-permute-done.11.refs_7_), channel_id=1, source_target_pairs={{0,1},{1,0},{2,3},{3,2},{4,5},{5,4},{6,7},{7,6},{8,9},{9,8},{10,11... | collective-permute-start | bytes 196616 | tf_op jit(solution)/shard_map/ppermute | solution.py:516
  15.4 4.7 %collective-permute-start.6 = (bf16[128,256]{1,0:T(8,128)(2,1)S(1)}, bf16[128,256]{1,0:T(8,128)(2,1)S(1)}, u32[]{:S(2)}, u32[]{:S(2)}) collective-permute-start(bf16[128,256]{1,0:T(8,128)(2,1)S(1)} %collective-permute-done.4.refs_5_), channel_id=1, source_target_pairs={{0,4},{4,0},{8,12},{12,8},{1,5},{5,1},{9,13},{13,9},{2,6},{6,2},{1... | collective-permute-start | bytes 196616 | tf_op jit(solution)/shard_map/ppermute | solution.py:517
  15.8 4.6 %collective-permute-start.1 = (bf16[128,256]{1,0:T(8,128)(2,1)S(1)}, bf16[128,256]{1,0:T(8,128)(2,1)S(1)}, u32[]{:S(2)}, u32[]{:S(2)}) collective-permute-start(bf16[128,256]{1,0:T(8,128)(2,1)S(1)} %copy-done), channel_id=1, source_target_pairs={{0,1},{1,0},{2,3},{3,2},{4,5},{5,4},{6,7},{7,6},{8,9},{9,8},{10,11... | collective-permute-start | bytes 196616 | tf_op jit(solution)/shard_map/ppermute | solution.py:516
  16.0 4.4 %collective-permute-start.5 = (bf16[128,256]{1,0:T(8,128)(2,1)S(1)}, bf16[128,256]{1,0:T(8,128)(2,1)S(1)}, u32[]{:S(2)}, u32[]{:S(2)}) collective-permute-start(bf16[128,256]{1,0:T(8,128)(2,1)S(1)} %collective-permute-done.4.refs_5_), channel_id=1, source_target_pairs={{0,1},{1,0},{2,3},{3,2},{4,5},{5,4},{6,7},{7,6},{8,9},{9,8},{10,11... | collective-permute-start | bytes 196616 | tf_op jit(solution)/shard_map/ppermute | solution.py:516
  16.3 4.1 %collective-permute-start.3 = (bf16[128,256]{1,0:T(8,128)(2,1)S(1)}, bf16[128,256]{1,0:T(8,128)(2,1)S(1)}, u32[]{:S(2)}, u32[]{:S(2)}) collective-permute-start(bf16[128,256]{1,0:T(8,128)(2,1)S(1)} %collective-permute-done.2.refs_3_), channel_id=1, source_target_pairs={{0,1},{1,0},{2,3},{3,2},{4,5},{5,4},{6,7},{7,6},{8,9},{9,8},{10,11... | collective-permute-start | bytes 196616 | tf_op jit(solution)/shard_map/ppermute | solution.py:516
  20.2 1.3 %collective-permute-start.13 = (bf16[128,256]{1,0:T(8,128)(2,1)S(1)}, bf16[128,256]{1,0:T(8,128)(2,1)S(1)}, u32[]{:S(2)}, u32[]{:S(2)}) collective-permute-start(bf16[128,256]{1,0:T(8,128)(2,1)S(1)} %collective-permute-done.6.refs_7_), channel_id=1, source_target_pairs={{0,1},{1,0},{2,3},{3,2},{4,5},{5,4},{6,7},{7,6},{8,9},{9,8},{10,11... | collective-permute-start | bytes 196616 | tf_op jit(solution)/shard_map/ppermute | solution.py:516
  24.8 5.9 %collective-permute-start.15 = (f32[2,8,512]{2,1,0:T(8,128)S(1)}, f32[2,8,512]{2,1,0:T(8,128)S(1)}, u32[]{:S(2)}, u32[]{:S(2)}) collective-permute-start(f32[2,8,512]{2,1,0:T(8,128)S(1)} %get-tuple-element.45.refs_1_.refs_3_), channel_id=1, source_target_pairs={{0,12},{4,8},{8,4},{12,0},{1,13},{5,9},{9,5},{13,1},{2,14},{6,10},... | collective-permute-start | bytes 98312 | tf_op jit(solution)/shard_map/ppermute | solution.py:517
  27.3 5.1 %collective-permute-start.16 = (f32[2,8,512]{2,1,0:T(8,128)S(1)}, f32[2,8,512]{2,1,0:T(8,128)S(1)}, u32[]{:S(2)}, u32[]{:S(2)}) collective-permute-start(f32[2,8,512]{2,1,0:T(8,128)S(1)} %get-tuple-element.45.refs_1_.refs_3_), channel_id=1, source_target_pairs={{0,8},{4,12},{8,0},{12,4},{1,9},{5,13},{9,1},{13,5},{2,10},{6,14},... | collective-permute-start | bytes 98312 | tf_op jit(solution)/shard_map/ppermute | solution.py:517
  27.8 4.6 %collective-permute-start.17 = (f32[2,8,512]{2,1,0:T(8,128)S(1)}, f32[2,8,512]{2,1,0:T(8,128)S(1)}, u32[]{:S(2)}, u32[]{:S(2)}) collective-permute-start(f32[2,8,512]{2,1,0:T(8,128)S(1)} %get-tuple-element.45.refs_1_.refs_3_), channel_id=1, source_target_pairs={{0,4},{4,0},{8,12},{12,8},{1,5},{5,1},{9,13},{13,9},{2,6},{6,2},{1... | collective-permute-start | bytes 98312 | tf_op jit(solution)/shard_map/ppermute | solution.py:517
  29.2 3.2 %collective-permute-start.14 = (f32[2,8,512]{2,1,0:T(8,128)S(1)}, f32[2,8,512]{2,1,0:T(8,128)S(1)}, u32[]{:S(2)}, u32[]{:S(2)}) collective-permute-start(f32[2,8,512]{2,1,0:T(8,128)S(1)} %get-tuple-element.45.refs_1_.refs_3_), channel_id=1, source_target_pairs={{0,1},{1,0},{2,3},{3,2},{4,5},{5,4},{6,7},{7,6},{8,9},{9,8},{10,11... | collective-permute-start | bytes 98312 | tf_op jit(solution)/shard_map/ppermute | solution.py:516
  33.0 2.1 %collective-permute-start.21 = (bf16[4,2,256,128]{3,2,1,0:T(8,128)(2,1)S(1)}, bf16[4,2,256,128]{3,2,1,0:T(8,128)(2,1)S(1)}, u32[]{:S(2)}, u32[]{:S(2)}) collective-permute-start(bf16[4,2,256,128]{3,2,1,0:T(8,128)(2,1)S(1)} %get-tuple-element.54), channel_id=1, source_target_pairs={{0,1},{1,0},{2,3},{3,2},{4,5},{5,4},{6,7},{7,6},{8,9},{9,8},{10,11... | collective-permute-start | bytes 1572872 | tf_op jit(solution)/shard_map/ppermute | solution.py:516
  33.1 1.9 %collective-permute-start.18 = (f32[2,8,512]{2,1,0:T(8,128)S(1)}, f32[2,8,512]{2,1,0:T(8,128)S(1)}, u32[]{:S(2)}, u32[]{:S(2)}) collective-permute-start(f32[2,8,512]{2,1,0:T(8,128)S(1)} %collective-permute-done.15.refs_5_), channel_id=1, source_target_pairs={{0,1},{1,0},{2,3},{3,2},{4,5},{5,4},{6,7},{7,6},{8,9},{9,8},{10,11... | collective-permute-start | bytes 98312 | tf_op jit(solution)/shard_map/ppermute | solution.py:516
  33.6 1.5 %collective-permute-start.19 = (f32[2,8,512]{2,1,0:T(8,128)S(1)}, f32[2,8,512]{2,1,0:T(8,128)S(1)}, u32[]{:S(2)}, u32[]{:S(2)}) collective-permute-start(f32[2,8,512]{2,1,0:T(8,128)S(1)} %collective-permute-done.16.refs_7_), channel_id=1, source_target_pairs={{0,1},{1,0},{2,3},{3,2},{4,5},{5,4},{6,7},{7,6},{8,9},{9,8},{10,11... | collective-permute-start | bytes 98312 | tf_op jit(solution)/shard_map/ppermute | solution.py:516
  33.6 1.5 %collective-permute-start.20 = (f32[2,8,512]{2,1,0:T(8,128)S(1)}, f32[2,8,512]{2,1,0:T(8,128)S(1)}, u32[]{:S(2)}, u32[]{:S(2)}) collective-permute-start(f32[2,8,512]{2,1,0:T(8,128)S(1)} %collective-permute-done.17.refs_9_), channel_id=1, source_target_pairs={{0,1},{1,0},{2,3},{3,2},{4,5},{5,4},{6,7},{7,6},{8,9},{9,8},{10,11... | collective-permute-start | bytes 98312 | tf_op jit(solution)/shard_map/ppermute | solution.py:516
  35.4 7.8 %collective-permute-start.22 = (bf16[128,256]{1,0:T(8,128)(2,1)S(1)}, bf16[128,256]{1,0:T(8,128)(2,1)S(1)}, u32[]{:S(2)}, u32[]{:S(2)}) collective-permute-start(bf16[128,256]{1,0:T(8,128)(2,1)S(1)} %get-tuple-element.56), channel_id=1, source_target_pairs={{0,12},{4,8},{8,4},{12,0},{1,13},{5,9},{9,5},{13,1},{2,14},{6,10},... | collective-permute-start | bytes 196616 | tf_op jit(solution)/shard_map/ppermute | solution.py:517
  37.7 6.6 %collective-permute-start.23 = (bf16[128,256]{1,0:T(8,128)(2,1)S(1)}, bf16[128,256]{1,0:T(8,128)(2,1)S(1)}, u32[]{:S(2)}, u32[]{:S(2)}) collective-permute-start(bf16[128,256]{1,0:T(8,128)(2,1)S(1)} %get-tuple-element.57), channel_id=1, source_target_pairs={{0,8},{4,12},{8,0},{12,4},{1,9},{5,13},{9,1},{13,5},{2,10},{6,14},... | collective-permute-start | bytes 196616 | tf_op jit(solution)/shard_map/ppermute | solution.py:517
  37.7 6.6 %collective-permute-start.24 = (bf16[128,256]{1,0:T(8,128)(2,1)S(1)}, bf16[128,256]{1,0:T(8,128)(2,1)S(1)}, u32[]{:S(2)}, u32[]{:S(2)}) collective-permute-start(bf16[128,256]{1,0:T(8,128)(2,1)S(1)} %get-tuple-element.58), channel_id=1, source_target_pairs={{0,4},{4,0},{8,12},{12,8},{1,5},{5,1},{9,13},{13,9},{2,6},{6,2},{1... | collective-permute-start | bytes 196616 | tf_op jit(solution)/shard_map/ppermute | solution.py:517

commit v13 on v12

--- a/solution.py
+++ b/solution.py
@@ -523,7 +523,7 @@
         near = [step(query_rows, s) for s in (1, 2, 3)]
         near_grads = [step(cotangent, 1), step(cotangent, 2)]
         near_grads.append(step(near_grads[1], 1))
-        block_table, near[0] = after(block_table, near[0])
+        block_table, near[1] = after(block_table, near[1])
         meta, own, state = index(block_table)
         near[0], meta = after(near[0], meta)
         queries = [own, pair(own)]

time: 45.1 us -> 44.7 us (level)
  waiting for transfers between devices: 7.01 us -> 6.02 us
  starting transfers between devices: 22 us -> 22.6 us
    ppermute x12, waiting for transfers between devices: 4.74 us -> 4.08 us  [local(): lax.ppermute(value, 'rows', [(z, z ^ s) for z in range(4)])]
  transfers between devices with their start and end apart: 25 -> 25, of which waited for: 7 -> 6; matrix products, arithmetic and copies ran while one was open for 0% -> 0% of each run, Pallas kernels for 23% -> 23%
where the time goes in v13:
time: 44.7 us; the launch traced here: 44.5 us
  starting transfers between devices  22.6 us (51%)
  Pallas kernels  14.5 us (32%)
  waiting for transfers between devices  6.02 us (13%)
  between operations  0.76 us (2%)
  other arithmetic  0.66 us (1%)
    ppermute x12, starting transfers between devices, local(): lax.ppermute(value, 'rows', [(z, z ^ s) for z in range(4)])  19.8 us
    ppermute x12, waiting for transfers between devices, local(): lax.ppermute(value, 'rows', [(z, z ^ s) for z in range(4)])  4.08 us
    pallas_call x1, Pallas kernels, block_weights(): pl.pallas_call(lambda *refs: weights_kernel(count, features, *refs), in_s...  3.48 us
    pallas_call x1, Pallas kernels, row_grads(): pl.pallas_call(row_grads_kernel, in_specs=[smem_spec()] + [vmem_spec()] *...  3.29 us
    pallas_call x1, Pallas kernels, moved_weights(): pl.pallas_call(lambda *refs: moved_kernel(count, features, *refs), in_spe...  3.27 us
    ppermute x13, starting transfers between devices, local(): pair = lambda value: lax.ppermute(value, 'pair', PAIR)  2.81 us
    pallas_call x1, Pallas kernels, index_table(): pl.pallas_call(lambda *refs: index_kernel(small, *refs), in_specs=[hbm_sp...  2.33 us
    ppermute x13, waiting for transfers between devices, local(): pair = lambda value: lax.ppermute(value, 'pair', PAIR)  1.94 us
  transfers between devices with their start and end apart: 25, of which 6 were waited for; matrix products, arithmetic and copies ran while one was open for 0% of the time, Pallas kernels for 23%

profile of v13, /device:TPU:0, one launch (start us, length us, event | category | flops | bytes accessed | tf_op | source)
XLA Modules:
  0.0 44.5 jit_solution(3553792569276611373)
XLA Ops:
  0.6 4.1 %collective-permute-start.1 = (bf16[128,256]{1,0:T(8,128)(2,1)}, bf16[128,256]{1,0:T(8,128)(2,1)S(1)}, u32[]{:S(2)}, u32[]{:S(2)}) collective-permute-start(bf16[128,256]{1,0:T(8,128)(2,1)} %refs_3_.1), channel_id=1, source_target_pairs={{0,8},{4,12},{8,0},{12,4},{1,9},{5,13},{9,1},{13,5},{2,10},{6,14},... | collective-permute-start | bytes 196616 | tf_op jit(solution)/shard_map/ppermute | solution.py:517
  4.7 1.6 %collective-permute-start = (bf16[128,256]{1,0:T(8,128)(2,1)}, bf16[128,256]{1,0:T(8,128)(2,1)S(1)}, u32[]{:S(2)}, u32[]{:S(2)}) collective-permute-start(bf16[128,256]{1,0:T(8,128)(2,1)} %refs_3_.1), channel_id=1, source_target_pairs={{0,4},{4,0},{8,12},{12,8},{1,5},{5,1},{9,13},{13,9},{2,6},{6,2},{1... | collective-permute-start | bytes 196616 | tf_op jit(solution)/shard_map/ppermute | solution.py:517
  6.3 1.9 %collective-permute-start.5 = (bf16[128,256]{1,0:T(8,128)(2,1)}, bf16[128,256]{1,0:T(8,128)(2,1)S(1)}, u32[]{:S(2)}, u32[]{:S(2)}) collective-permute-start(bf16[128,256]{1,0:T(8,128)(2,1)} %refs_1_.3), channel_id=1, source_target_pairs={{0,8},{4,12},{8,0},{12,4},{1,9},{5,13},{9,1},{13,5},{2,10},{6,14},... | collective-permute-start | bytes 196616 | tf_op jit(solution)/shard_map/ppermute | solution.py:517
  8.2 2.5 %collective-permute-start.3 = (bf16[128,256]{1,0:T(8,128)(2,1)}, bf16[128,256]{1,0:T(8,128)(2,1)S(1)}, u32[]{:S(2)}, u32[]{:S(2)}) collective-permute-start(bf16[128,256]{1,0:T(8,128)(2,1)} %refs_1_.3), channel_id=1, source_target_pairs={{0,4},{4,0},{8,12},{12,8},{1,5},{5,1},{9,13},{13,9},{2,6},{6,2},{1... | collective-permute-start | bytes 196616 | tf_op jit(solution)/shard_map/ppermute | solution.py:517
  10.7 0.0 collective-permute-done.1.refs_5_
  10.7 2.3 %index_table.1 = (s32[7,8]{1,0:T(8,128)S(4)}, bf16[128,256]{1,0:T(8,128)(2,1)S(1)}, bf16[8,512,1536]{2,1,0:T(8,128)(2,1)S(1)}) custom-call(s32[64]{0:T(128)} %refs_0_, s32[8]{0:T(128)} %refs_1_.2, s32[8]{0:T(128)} %refs_2_.1, bf16[128,256]{1,0:T(8,128)(2,1)} %refs_3_.1, bf16[4096,256]{1,0:T(8,128)(2,1)} %refs_4_.1, bf16[4096,256]{1,0:T(8,128)(2,1)} %refs_5_.1), custom_call_target="tpu_custom_call" | custom-call | tf_op jit(solution)/shard_map/index_table/pallas_call | solution.py:123
  13.0 0.0 collective-permute-done.refs_3_
  13.1 0.1 collective-permute-start.9
  13.1 0.5 %collective-permute-start.8 = (bf16[128,256]{1,0:T(8,128)(2,1)S(1)}, bf16[128,256]{1,0:T(8,128)(2,1)S(1)}, u32[]{:S(2)}, u32[]{:S(2)}) collective-permute-start(bf16[128,256]{1,0:T(8,128)(2,1)S(1)} %get-tuple-element.37.refs_1_), channel_id=1, source_target_pairs={{0,1},{1,0},{2,3},{3,2},{4,5},{5,4},{6,7},{7,6},{8,9},{9,8},{10,11... | collective-permute-start | bytes 196616 | tf_op jit(solution)/shard_map/ppermute | solution.py:516
  13.6 0.0 collective-permute-done.11.refs_7_
  13.6 0.1 collective-permute-start.10
  13.7 0.7 %collective-permute-done.5.refs_5_ = bf16[128,256]{1,0:T(8,128)(2,1)S(1)} collective-permute-done((bf16[128,256]{1,0:T(8,128)(2,1)}, bf16[128,256]{1,0:T(8,128)(2,1)S(1)}, u32[]{:S(2)}, u32[]{:S(2)}) %collective-permute-start.5) | collective-permute-done | bytes 65568 | tf_op jit(solution)/shard_map/ppermute | solution.py:517
  14.4 0.0 collective-permute-start.12
  14.4 0.0 collective-permute-done.3.refs_3_
  14.4 0.8 %collective-permute-start.7 = (bf16[128,256]{1,0:T(8,128)(2,1)S(1)}, bf16[128,256]{1,0:T(8,128)(2,1)S(1)}, u32[]{:S(2)}, u32[]{:S(2)}) collective-permute-start(bf16[128,256]{1,0:T(8,128)(2,1)S(1)} %collective-permute-done.5.refs_5_), channel_id=1, source_target_pairs={{0,4},{4,0},{8,12},{12,8},{1,5},{5,1},{9,13},{13,9},{2,6},{6,2},{1... | collective-permute-start | bytes 196616 | tf_op jit(solution)/shard_map/ppermute | solution.py:517
  15.2 0.0 collective-permute-done.9.refs_4_
  15.2 0.0 collective-permute-done.8.refs_2_
  15.2 0.5 %collective-permute-start.6 = (bf16[128,256]{1,0:T(8,128)(2,1)S(1)}, bf16[128,256]{1,0:T(8,128)(2,1)S(1)}, u32[]{:S(2)}, u32[]{:S(2)}) collective-permute-start(bf16[128,256]{1,0:T(8,128)(2,1)S(1)} %collective-permute-done.5.refs_5_), channel_id=1, source_target_pairs={{0,1},{1,0},{2,3},{3,2},{4,5},{5,4},{6,7},{7,6},{8,9},{9,8},{10,11... | collective-permute-start | bytes 196616 | tf_op jit(solution)/shard_map/ppermute | solution.py:516
  15.7 0.0 collective-permute-done.10.refs_6_
  15.7 0.1 collective-permute-start.4
  15.8 3.5 %block_weights.1 = (f32[2080,128]{1,0:T(8,128)S(1)}, bf16[8,512,1536]{2,1,0:T(8,128)(2,1)S(1)}) custom-call(s32[7,8]{1,0:T(8,128)S(4)} %get-tuple-element.36.refs_0_.meta, bf16[128,256]{1,0:T(8,128)(2,1)S(1)} %get-tuple-element.37.refs_1_, bf16[128,256]{1,0:T(8,128)(2,1)S(1)} %collective-permute-done.8.refs_2_, ...), custom_call_target="tpu_custom_call", output_to_operand_aliasing={{1}: (9, {})} | custom-call | tf_op jit(solution)/shard_map/block_weights/pallas_call | solution.py:219
  19.3 0.5 %collective-permute-start.13 = (bf16[128,256]{1,0:T(8,128)(2,1)S(1)}, bf16[128,256]{1,0:T(8,128)(2,1)S(1)}, u32[]{:S(2)}, u32[]{:S(2)}) collective-permute-start(bf16[128,256]{1,0:T(8,128)(2,1)S(1)} %collective-permute-done.7.refs_7_), channel_id=1, source_target_pairs={{0,1},{1,0},{2,3},{3,2},{4,5},{5,4},{6,7},{7,6},{8,9},{9,8},{10,11... | collective-permute-start | bytes 196616 | tf_op jit(solution)/shard_map/ppermute | solution.py:516
  19.8 0.0 collective-permute-done.2.refs_2_
  19.8 0.9 %collective-permute-done.13.refs_8_ = bf16[128,256]{1,0:T(8,128)(2,1)S(1)} collective-permute-done((bf16[128,256]{1,0:T(8,128)(2,1)S(1)}, bf16[128,256]{1,0:T(8,128)(2,1)S(1)}, u32[]{:S(2)}, u32[]{:S(2)}) %collective-permute-start.13) | collective-permute-done | bytes 65568 | tf_op jit(solution)/shard_map/ppermute | solution.py:516
  20.7 3.3 %moved_weights.1 = (f32[2112,128]{1,0:T(8,128)S(1)}, f32[2,8,512]{2,1,0:T(8,128)S(1)}, bf16[8,512,1536]{2,1,0:T(8,128)(2,1)S(1)}) custom-call(s32[7,8]{1,0:T(8,128)S(4)} %get-tuple-element.36.refs_0_.meta, bf16[128,256]{1,0:T(8,128)(2,1)S(1)} %copy-done, bf16[128,256]{1,0:T(8,128)(2,1)S(1)} %collective-permute-done.2.refs_2_, ...), custom_call_target="tpu_custom_call", output_to_operand_aliasing={{2}: (10, {})} | custom-call | tf_op jit(solution)/shard_map/moved_weights/pallas_call | solution.py:308
  24.0 3.0 %collective-permute-start.15 = (f32[2,8,512]{2,1,0:T(8,128)S(1)}, f32[2,8,512]{2,1,0:T(8,128)S(1)}, u32[]{:S(2)}, u32[]{:S(2)}) collective-permute-start(f32[2,8,512]{2,1,0:T(8,128)S(1)} %get-tuple-element.45.refs_1_.refs_3_), channel_id=1, source_target_pairs={{0,12},{4,8},{8,4},{12,0},{1,13},{5,9},{9,5},{13,1},{2,14},{6,10},... | collective-permute-start | bytes 98312 | tf_op jit(solution)/shard_map/ppermute | solution.py:517
  27.0 0.2 collective-permute-start.16
  27.2 1.2 %collective-permute-start.17 = (f32[2,8,512]{2,1,0:T(8,128)S(1)}, f32[2,8,512]{2,1,0:T(8,128)S(1)}, u32[]{:S(2)}, u32[]{:S(2)}) collective-permute-start(f32[2,8,512]{2,1,0:T(8,128)S(1)} %get-tuple-element.45.refs_1_.refs_3_), channel_id=1, source_target_pairs={{0,4},{4,0},{8,12},{12,8},{1,5},{5,1},{9,13},{13,9},{2,6},{6,2},{1... | collective-permute-start | bytes 98312 | tf_op jit(solution)/shard_map/ppermute | solution.py:517
  28.4 0.0 collective-permute-start.14
  28.4 1.3 %query_sums.1 = (f32[8,2,256,128]{3,2,1,0:T(8,128)S(1)}, bf16[8,512,1536]{2,1,0:T(8,128)(2,1)S(1)}) custom-call(bf16[8,512,1536]{2,1,0:T(8,128)(2,1)S(1)} %get-tuple-element.46.state), custom_call_target="tpu_custom_call", output_to_operand_aliasing={{1}: (0, {})} | custom-call | tf_op jit(solution)/shard_map/query_sums/pallas_call | solution.py:353
  29.7 0.1 collective-permute-done.15.refs_5_
  29.8 2.2 %collective-permute-done.16.refs_7_ = f32[2,8,512]{2,1,0:T(8,128)S(1)} collective-permute-done((f32[2,8,512]{2,1,0:T(8,128)S(1)}, f32[2,8,512]{2,1,0:T(8,128)S(1)}, u32[]{:S(2)}, u32[]{:S(2)}) %collective-permute-start.16) | collective-permute-done | bytes 32800 | tf_op jit(solution)/shard_map/ppermute | solution.py:517
  32.0 0.0 collective-permute-done.14.refs_2_.refs_4_
  32.0 0.5 %chip_sums.1 = (f32[4,2,256,128]{3,2,1,0:T(8,128)S(1)}, bf16[4,2,256,128]{3,2,1,0:T(8,128)(2,1)S(1)}) custom-call(s32[7,8]{1,0:T(8,128)S(4)} %get-tuple-element.36.refs_0_.meta, f32[2,8,512]{2,1,0:T(8,128)S(1)} %get-tuple-element.45.refs_1_.refs_3_, f32[2,8,512]{2,1,0:T(8,128)S(1)} %collective-permute-done.14.refs_2_.refs_4_, ...), custom_call_target="tpu_custom_call" | custom-call | tf_op jit(solution)/shard_map/chip_sums/pallas_call | solution.py:396
  32.6 0.1 collective-permute-start.21
  32.6 0.5 %collective-permute-start.18 = (f32[2,8,512]{2,1,0:T(8,128)S(1)}, f32[2,8,512]{2,1,0:T(8,128)S(1)}, u32[]{:S(2)}, u32[]{:S(2)}) collective-permute-start(f32[2,8,512]{2,1,0:T(8,128)S(1)} %collective-permute-done.15.refs_5_), channel_id=1, source_target_pairs={{0,1},{1,0},{2,3},{3,2},{4,5},{5,4},{6,7},{7,6},{8,9},{9,8},{10,11... | collective-permute-start | bytes 98312 | tf_op jit(solution)/shard_map/ppermute | solution.py:516
  33.1 0.1 collective-permute-start.19
  33.2 0.4 collective-permute-start.20
  33.6 0.9 %collective-permute-done.18.refs_6_ = f32[2,8,512]{2,1,0:T(8,128)S(1)} collective-permute-done((f32[2,8,512]{2,1,0:T(8,128)S(1)}, f32[2,8,512]{2,1,0:T(8,128)S(1)}, u32[]{:S(2)}, u32[]{:S(2)}) %collective-permute-start.18) | collective-permute-done | bytes 32800 | tf_op jit(solution)/shard_map/ppermute | solution.py:516
  34.6 0.0 collective-permute-done.19.refs_8_
  34.6 0.0 collective-permute-done.20.refs_10_
  34.7 0.3 query_grads.1
  35.0 2.3 %collective-permute-start.22 = (bf16[128,256]{1,0:T(8,128)(2,1)S(1)}, bf16[128,256]{1,0:T(8,128)(2,1)S(1)}, u32[]{:S(2)}, u32[]{:S(2)}) collective-permute-start(bf16[128,256]{1,0:T(8,128)(2,1)S(1)} %get-tuple-element.56), channel_id=1, source_target_pairs={{0,12},{4,8},{8,4},{12,0},{1,13},{5,9},{9,5},{13,1},{2,14},{6,10},... | collective-permute-start | bytes 196616 | tf_op jit(solution)/shard_map/ppermute | solution.py:517
  37.3 0.1 collective-permute-start.23
  37.3 2.1 %collective-permute-start.24 = (bf16[128,256]{1,0:T(8,128)(2,1)S(1)}, bf16[128,256]{1,0:T(8,128)(2,1)S(1)}, u32[]{:S(2)}, u32[]{:S(2)}) collective-permute-start(bf16[128,256]{1,0:T(8,128)(2,1)S(1)} %get-tuple-element.58), channel_id=1, source_target_pairs={{0,4},{4,0},{8,12},{12,8},{1,5},{5,1},{9,13},{13,9},{2,6},{6,2},{1... | collective-permute-start | bytes 196616 | tf_op jit(solution)/shard_map/ppermute | solution.py:517
  39.4 3.3 %row_grads.1 = (bf16[4096,256]{1,0:T(8,128)(2,1)}, bf16[4096,256]{1,0:T(8,128)(2,1)}) custom-call(s32[7,8]{1,0:T(8,128)S(4)} %get-tuple-element.36.refs_0_.meta, f32[8,512]{1,0:T(8,128)S(1)} %get-tuple-element.60.c_ref, f32[8,512]{1,0:T(8,128)S(1)} %get-tuple-element.61.d_ref, f32[2080,128]{1,0:T(8,128)S(1)} %get-tuple-element.43.refs_9_.refs_3_.refs_13_.q_side, ...), custom_call_target="tpu_custom_call" | custom-call | tf_op jit(solution)/shard_map/row_grads/pallas_call | solution.py:497
  42.8 1.1 %collective-permute-done.23 = bf16[128,256]{1,0:T(8,128)(2,1)S(1)} collective-permute-done((bf16[128,256]{1,0:T(8,128)(2,1)S(1)}, bf16[128,256]{1,0:T(8,128)(2,1)S(1)}, u32[]{:S(2)}, u32[]{:S(2)}) %collective-permute-start.23) | collective-permute-done | bytes 65568 | tf_op jit(solution)/shard_map/ppermute | solution.py:517
  43.8 0.7 %add_convert_fusion = bf16[128,256]{1,0:T(8,128)(2,1)} fusion(bf16[128,256]{1,0:T(8,128)(2,1)S(1)} %collective-permute-done.24, bf16[128,256]{1,0:T(8,128)(2,1)S(1)} %collective-permute-done.23, f32[128,256]{1,0:T(8,128)S(1)} %get-tuple-element.55, bf16[128,256]{1,0:T(8,128)(2,1)S(1)} %collective-permute-done.22), kind=kLoop, calls=%fused_computation | loop fusion | flops 229376 | bytes 393216 | tf_op jit(solution)/shard_map/convert_element_type | solution.py:578
  (12 shorter events, 0.0 us)
Async XLA Ops:
  0.6 14.6 %copy-start = (bf16[128,256]{1,0:T(8,128)(2,1)S(1)}, bf16[128,256]{1,0:T(8,128)(2,1)}, u32[]{:S(2)}) copy-start(bf16[128,256]{1,0:T(8,128)(2,1)} %refs_1_.3) | copy-start | bytes 196612
  0.6 10.1 %collective-permute-start.1 = (bf16[128,256]{1,0:T(8,128)(2,1)}, bf16[128,256]{1,0:T(8,128)(2,1)S(1)}, u32[]{:S(2)}, u32[]{:S(2)}) collective-permute-start(bf16[128,256]{1,0:T(8,128)(2,1)} %refs_3_.1), channel_id=1, source_target_pairs={{0,8},{4,12},{8,0},{12,4},{1,9},{5,13},{9,1},{13,5},{2,10},{6,14},... | collective-permute-start | bytes 196616 | tf_op jit(solution)/shard_map/ppermute | solution.py:517
  4.7 8.3 %collective-permute-start = (bf16[128,256]{1,0:T(8,128)(2,1)}, bf16[128,256]{1,0:T(8,128)(2,1)S(1)}, u32[]{:S(2)}, u32[]{:S(2)}) collective-permute-start(bf16[128,256]{1,0:T(8,128)(2,1)} %refs_3_.1), channel_id=1, source_target_pairs={{0,4},{4,0},{8,12},{12,8},{1,5},{5,1},{9,13},{13,9},{2,6},{6,2},{1... | collective-permute-start | bytes 196616 | tf_op jit(solution)/shard_map/ppermute | solution.py:517
  6.3 7.3 %collective-permute-start.11 = (bf16[128,256]{1,0:T(8,128)(2,1)}, bf16[128,256]{1,0:T(8,128)(2,1)S(1)}, u32[]{:S(2)}, u32[]{:S(2)}) collective-permute-start(bf16[128,256]{1,0:T(8,128)(2,1)} %refs_3_.1), channel_id=1, source_target_pairs={{0,12},{4,8},{8,4},{12,0},{1,13},{5,9},{9,5},{13,1},{2,14},{6,10},... | collective-permute-start | bytes 196616 | tf_op jit(solution)/shard_map/ppermute | solution.py:517
  6.3 8.1 %collective-permute-start.5 = (bf16[128,256]{1,0:T(8,128)(2,1)}, bf16[128,256]{1,0:T(8,128)(2,1)S(1)}, u32[]{:S(2)}, u32[]{:S(2)}) collective-permute-start(bf16[128,256]{1,0:T(8,128)(2,1)} %refs_1_.3), channel_id=1, source_target_pairs={{0,8},{4,12},{8,0},{12,4},{1,9},{5,13},{9,1},{13,5},{2,10},{6,14},... | collective-permute-start | bytes 196616 | tf_op jit(solution)/shard_map/ppermute | solution.py:517
  8.2 6.2 %collective-permute-start.3 = (bf16[128,256]{1,0:T(8,128)(2,1)}, bf16[128,256]{1,0:T(8,128)(2,1)S(1)}, u32[]{:S(2)}, u32[]{:S(2)}) collective-permute-start(bf16[128,256]{1,0:T(8,128)(2,1)} %refs_1_.3), channel_id=1, source_target_pairs={{0,4},{4,0},{8,12},{12,8},{1,5},{5,1},{9,13},{13,9},{2,6},{6,2},{1... | collective-permute-start | bytes 196616 | tf_op jit(solution)/shard_map/ppermute | solution.py:517
  13.1 2.1 %collective-permute-start.9 = (bf16[128,256]{1,0:T(8,128)(2,1)S(1)}, bf16[128,256]{1,0:T(8,128)(2,1)S(1)}, u32[]{:S(2)}, u32[]{:S(2)}) collective-permute-start(bf16[128,256]{1,0:T(8,128)(2,1)S(1)} %collective-permute-done.refs_3_), channel_id=1, source_target_pairs={{0,1},{1,0},{2,3},{3,2},{4,5},{5,4},{6,7},{7,6},{8,9},{9,8},{10,11... | collective-permute-start | bytes 196616 | tf_op jit(solution)/shard_map/ppermute | solution.py:516
  13.1 2.1 %collective-permute-start.8 = (bf16[128,256]{1,0:T(8,128)(2,1)S(1)}, bf16[128,256]{1,0:T(8,128)(2,1)S(1)}, u32[]{:S(2)}, u32[]{:S(2)}) collective-permute-start(bf16[128,256]{1,0:T(8,128)(2,1)S(1)} %get-tuple-element.37.refs_1_), channel_id=1, source_target_pairs={{0,1},{1,0},{2,3},{3,2},{4,5},{5,4},{6,7},{7,6},{8,9},{9,8},{10,11... | collective-permute-start | bytes 196616 | tf_op jit(solution)/shard_map/ppermute | solution.py:516
  13.6 2.1 %collective-permute-start.10 = (bf16[128,256]{1,0:T(8,128)(2,1)S(1)}, bf16[128,256]{1,0:T(8,128)(2,1)S(1)}, u32[]{:S(2)}, u32[]{:S(2)}) collective-permute-start(bf16[128,256]{1,0:T(8,128)(2,1)S(1)} %collective-permute-done.1.refs_5_), channel_id=1, source_target_pairs={{0,1},{1,0},{2,3},{3,2},{4,5},{5,4},{6,7},{7,6},{8,9},{9,8},{10,11... | collective-permute-start | bytes 196616 | tf_op jit(solution)/shard_map/ppermute | solution.py:516
  14.4 1.4 %collective-permute-start.12 = (bf16[128,256]{1,0:T(8,128)(2,1)S(1)}, bf16[128,256]{1,0:T(8,128)(2,1)S(1)}, u32[]{:S(2)}, u32[]{:S(2)}) collective-permute-start(bf16[128,256]{1,0:T(8,128)(2,1)S(1)} %collective-permute-done.11.refs_7_), channel_id=1, source_target_pairs={{0,1},{1,0},{2,3},{3,2},{4,5},{5,4},{6,7},{7,6},{8,9},{9,8},{10,11... | collective-permute-start | bytes 196616 | tf_op jit(solution)/shard_map/ppermute | solution.py:516
  14.4 4.9 %collective-permute-start.7 = (bf16[128,256]{1,0:T(8,128)(2,1)S(1)}, bf16[128,256]{1,0:T(8,128)(2,1)S(1)}, u32[]{:S(2)}, u32[]{:S(2)}) collective-permute-start(bf16[128,256]{1,0:T(8,128)(2,1)S(1)} %collective-permute-done.5.refs_5_), channel_id=1, source_target_pairs={{0,4},{4,0},{8,12},{12,8},{1,5},{5,1},{9,13},{13,9},{2,6},{6,2},{1... | collective-permute-start | bytes 196616 | tf_op jit(solution)/shard_map/ppermute | solution.py:517
  15.2 4.6 %collective-permute-start.2 = (bf16[128,256]{1,0:T(8,128)(2,1)S(1)}, bf16[128,256]{1,0:T(8,128)(2,1)S(1)}, u32[]{:S(2)}, u32[]{:S(2)}) collective-permute-start(bf16[128,256]{1,0:T(8,128)(2,1)S(1)} %copy-done), channel_id=1, source_target_pairs={{0,1},{1,0},{2,3},{3,2},{4,5},{5,4},{6,7},{7,6},{8,9},{9,8},{10,11... | collective-permute-start | bytes 196616 | tf_op jit(solution)/shard_map/ppermute | solution.py:516
  15.2 4.6 %collective-permute-start.6 = (bf16[128,256]{1,0:T(8,128)(2,1)S(1)}, bf16[128,256]{1,0:T(8,128)(2,1)S(1)}, u32[]{:S(2)}, u32[]{:S(2)}) collective-permute-start(bf16[128,256]{1,0:T(8,128)(2,1)S(1)} %collective-permute-done.5.refs_5_), channel_id=1, source_target_pairs={{0,1},{1,0},{2,3},{3,2},{4,5},{5,4},{6,7},{7,6},{8,9},{9,8},{10,11... | collective-permute-start | bytes 196616 | tf_op jit(solution)/shard_map/ppermute | solution.py:516
  15.7 4.1 %collective-permute-start.4 = (bf16[128,256]{1,0:T(8,128)(2,1)S(1)}, bf16[128,256]{1,0:T(8,128)(2,1)S(1)}, u32[]{:S(2)}, u32[]{:S(2)}) collective-permute-start(bf16[128,256]{1,0:T(8,128)(2,1)S(1)} %collective-permute-done.3.refs_3_), channel_id=1, source_target_pairs={{0,1},{1,0},{2,3},{3,2},{4,5},{5,4},{6,7},{7,6},{8,9},{9,8},{10,11... | collective-permute-start | bytes 196616 | tf_op jit(solution)/shard_map/ppermute | solution.py:516
  19.3 1.4 %collective-permute-start.13 = (bf16[128,256]{1,0:T(8,128)(2,1)S(1)}, bf16[128,256]{1,0:T(8,128)(2,1)S(1)}, u32[]{:S(2)}, u32[]{:S(2)}) collective-permute-start(bf16[128,256]{1,0:T(8,128)(2,1)S(1)} %collective-permute-done.7.refs_7_), channel_id=1, source_target_pairs={{0,1},{1,0},{2,3},{3,2},{4,5},{5,4},{6,7},{7,6},{8,9},{9,8},{10,11... | collective-permute-start | bytes 196616 | tf_op jit(solution)/shard_map/ppermute | solution.py:516
  24.0 5.8 %collective-permute-start.15 = (f32[2,8,512]{2,1,0:T(8,128)S(1)}, f32[2,8,512]{2,1,0:T(8,128)S(1)}, u32[]{:S(2)}, u32[]{:S(2)}) collective-permute-start(f32[2,8,512]{2,1,0:T(8,128)S(1)} %get-tuple-element.45.refs_1_.refs_3_), channel_id=1, source_target_pairs={{0,12},{4,8},{8,4},{12,0},{1,13},{5,9},{9,5},{13,1},{2,14},{6,10},... | collective-permute-start | bytes 98312 | tf_op jit(solution)/shard_map/ppermute | solution.py:517
  27.0 5.0 %collective-permute-start.16 = (f32[2,8,512]{2,1,0:T(8,128)S(1)}, f32[2,8,512]{2,1,0:T(8,128)S(1)}, u32[]{:S(2)}, u32[]{:S(2)}) collective-permute-start(f32[2,8,512]{2,1,0:T(8,128)S(1)} %get-tuple-element.45.refs_1_.refs_3_), channel_id=1, source_target_pairs={{0,8},{4,12},{8,0},{12,4},{1,9},{5,13},{9,1},{13,5},{2,10},{6,14},... | collective-permute-start | bytes 98312 | tf_op jit(solution)/shard_map/ppermute | solution.py:517
  27.2 4.8 %collective-permute-start.17 = (f32[2,8,512]{2,1,0:T(8,128)S(1)}, f32[2,8,512]{2,1,0:T(8,128)S(1)}, u32[]{:S(2)}, u32[]{:S(2)}) collective-permute-start(f32[2,8,512]{2,1,0:T(8,128)S(1)} %get-tuple-element.45.refs_1_.refs_3_), channel_id=1, source_target_pairs={{0,4},{4,0},{8,12},{12,8},{1,5},{5,1},{9,13},{13,9},{2,6},{6,2},{1... | collective-permute-start | bytes 98312 | tf_op jit(solution)/shard_map/ppermute | solution.py:517
  28.4 3.6 %collective-permute-start.14 = (f32[2,8,512]{2,1,0:T(8,128)S(1)}, f32[2,8,512]{2,1,0:T(8,128)S(1)}, u32[]{:S(2)}, u32[]{:S(2)}) collective-permute-start(f32[2,8,512]{2,1,0:T(8,128)S(1)} %get-tuple-element.45.refs_1_.refs_3_), channel_id=1, source_target_pairs={{0,1},{1,0},{2,3},{3,2},{4,5},{5,4},{6,7},{7,6},{8,9},{9,8},{10,11... | collective-permute-start | bytes 98312 | tf_op jit(solution)/shard_map/ppermute | solution.py:516
  32.6 2.1 %collective-permute-start.21 = (bf16[4,2,256,128]{3,2,1,0:T(8,128)(2,1)S(1)}, bf16[4,2,256,128]{3,2,1,0:T(8,128)(2,1)S(1)}, u32[]{:S(2)}, u32[]{:S(2)}) collective-permute-start(bf16[4,2,256,128]{3,2,1,0:T(8,128)(2,1)S(1)} %get-tuple-element.54), channel_id=1, source_target_pairs={{0,1},{1,0},{2,3},{3,2},{4,5},{5,4},{6,7},{7,6},{8,9},{9,8},{10,11... | collective-permute-start | bytes 1572872 | tf_op jit(solution)/shard_map/ppermute | solution.py:516
  32.6 1.9 %collective-permute-start.18 = (f32[2,8,512]{2,1,0:T(8,128)S(1)}, f32[2,8,512]{2,1,0:T(8,128)S(1)}, u32[]{:S(2)}, u32[]{:S(2)}) collective-permute-start(f32[2,8,512]{2,1,0:T(8,128)S(1)} %collective-permute-done.15.refs_5_), channel_id=1, source_target_pairs={{0,1},{1,0},{2,3},{3,2},{4,5},{5,4},{6,7},{7,6},{8,9},{9,8},{10,11... | collective-permute-start | bytes 98312 | tf_op jit(solution)/shard_map/ppermute | solution.py:516
  33.1 1.5 %collective-permute-start.19 = (f32[2,8,512]{2,1,0:T(8,128)S(1)}, f32[2,8,512]{2,1,0:T(8,128)S(1)}, u32[]{:S(2)}, u32[]{:S(2)}) collective-permute-start(f32[2,8,512]{2,1,0:T(8,128)S(1)} %collective-permute-done.16.refs_7_), channel_id=1, source_target_pairs={{0,1},{1,0},{2,3},{3,2},{4,5},{5,4},{6,7},{7,6},{8,9},{9,8},{10,11... | collective-permute-start | bytes 98312 | tf_op jit(solution)/shard_map/ppermute | solution.py:516
  33.2 1.5 %collective-permute-start.20 = (f32[2,8,512]{2,1,0:T(8,128)S(1)}, f32[2,8,512]{2,1,0:T(8,128)S(1)}, u32[]{:S(2)}, u32[]{:S(2)}) collective-permute-start(f32[2,8,512]{2,1,0:T(8,128)S(1)} %collective-permute-done.17.refs_9_), channel_id=1, source_target_pairs={{0,1},{1,0},{2,3},{3,2},{4,5},{5,4},{6,7},{7,6},{8,9},{9,8},{10,11... | collective-permute-start | bytes 98312 | tf_op jit(solution)/shard_map/ppermute | solution.py:516
  35.0 7.8 %collective-permute-start.22 = (bf16[128,256]{1,0:T(8,128)(2,1)S(1)}, bf16[128,256]{1,0:T(8,128)(2,1)S(1)}, u32[]{:S(2)}, u32[]{:S(2)}) collective-permute-start(bf16[128,256]{1,0:T(8,128)(2,1)S(1)} %get-tuple-element.56), channel_id=1, source_target_pairs={{0,12},{4,8},{8,4},{12,0},{1,13},{5,9},{9,5},{13,1},{2,14},{6,10},... | collective-permute-start | bytes 196616 | tf_op jit(solution)/shard_map/ppermute | solution.py:517
  37.3 6.6 %collective-permute-start.23 = (bf16[128,256]{1,0:T(8,128)(2,1)S(1)}, bf16[128,256]{1,0:T(8,128)(2,1)S(1)}, u32[]{:S(2)}, u32[]{:S(2)}) collective-permute-start(bf16[128,256]{1,0:T(8,128)(2,1)S(1)} %get-tuple-element.57), channel_id=1, source_target_pairs={{0,8},{4,12},{8,0},{12,4},{1,9},{5,13},{9,1},{13,5},{2,10},{6,14},... | collective-permute-start | bytes 196616 | tf_op jit(solution)/shard_map/ppermute | solution.py:517
  37.3 6.5 %collective-permute-start.24 = (bf16[128,256]{1,0:T(8,128)(2,1)S(1)}, bf16[128,256]{1,0:T(8,128)(2,1)S(1)}, u32[]{:S(2)}, u32[]{:S(2)}) collective-permute-start(bf16[128,256]{1,0:T(8,128)(2,1)S(1)} %get-tuple-element.58), channel_id=1, source_target_pairs={{0,4},{4,0},{8,12},{12,8},{1,5},{5,1},{9,13},{13,9},{2,6},{6,2},{1... | collective-permute-start | bytes 196616 | tf_op jit(solution)/shard_map/ppermute | solution.py:517

commit v14 on v13

--- a/solution.py
+++ b/solution.py
@@ -541,7 +541,7 @@
         grads = [lax.all_gather(cotangent, RP, axis=0, tiled=True)]
     g_side, tab, state = moved_weights(meta, grads, q_side, state, features, tables)
     if small:
-        near = [step(tab, s) for s in (3, 2, 1)]
+        near = [step(tab, s) for s in (2, 3, 1)]
         own = [tab, pair(tab)]
         ab, state = query_sums(features, state)
         *near, ab = lax.optimization_barrier((*near, ab))
@@ -556,7 +556,7 @@
         c, d, *low, query_grad = query_grads(
             meta, own, stats, [keep, received], q_side, g_side, blocks, dtypes
         )
-        got = [step(low[s - 1], s) for s in (3, 2, 1)]
+        got = [step(low[s - 1], s) for s in (2, 3, 1)]
         *low, c = lax.optimization_barrier((*low, c))
         key_grad, value_grad = row_grads(meta, c, d, (q_side, g_side), state, features)
         for value in got:

time: 44.7 us -> 45.4 us (1.016)
  waiting for transfers between devices: 6.02 us -> 8.29 us
  starting transfers between devices: 22.6 us -> 21 us
    ppermute x12, waiting for transfers between devices: 4.08 us -> 6.34 us  [local(): lax.ppermute(value, 'rows', [(z, z ^ s) for z in range(4)])]
    ppermute x12, starting transfers between devices: 19.8 us -> 18.2 us  [local(): lax.ppermute(value, 'rows', [(z, z ^ s) for z in range(4)])]
  transfers between devices with their start and end apart: 25 -> 25, of which waited for: 6 -> 7; matrix products, arithmetic and copies ran while one was open for 0% -> 0% of each run, Pallas kernels for 23% -> 23%
where the time goes in v14:
time: 45.4 us; the launch traced here: 45.3 us
  starting transfers between devices  21 us (46%)
  Pallas kernels  14.5 us (32%)
  waiting for transfers between devices  8.29 us (18%)
  between operations  0.76 us (2%)
  other arithmetic  0.66 us (1%)
    ppermute x12, starting transfers between devices, local(): lax.ppermute(value, 'rows', [(z, z ^ s) for z in range(4)])  18.2 us
    ppermute x12, waiting for transfers between devices, local(): lax.ppermute(value, 'rows', [(z, z ^ s) for z in range(4)])  6.34 us
    pallas_call x1, Pallas kernels, block_weights(): pl.pallas_call(lambda *refs: weights_kernel(count, features, *refs), in_s...  3.48 us
    pallas_call x1, Pallas kernels, row_grads(): pl.pallas_call(row_grads_kernel, in_specs=[smem_spec()] + [vmem_spec()] *...  3.29 us
    pallas_call x1, Pallas kernels, moved_weights(): pl.pallas_call(lambda *refs: moved_kernel(count, features, *refs), in_spe...  3.27 us
    ppermute x13, starting transfers between devices, local(): pair = lambda value: lax.ppermute(value, 'pair', PAIR)  2.82 us
    pallas_call x1, Pallas kernels, index_table(): pl.pallas_call(lambda *refs: index_kernel(small, *refs), in_specs=[hbm_sp...  2.33 us
    ppermute x13, waiting for transfers between devices, local(): pair = lambda value: lax.ppermute(value, 'pair', PAIR)  1.94 us
  transfers between devices with their start and end apart: 25, of which 7 were waited for; matrix products, arithmetic and copies ran while one was open for 0% of the time, Pallas kernels for 23%

profile of v14, /device:TPU:0, one launch (start us, length us, event | category | flops | bytes accessed | tf_op | source)
XLA Modules:
  0.0 45.3 jit_solution(6073228499252921114)
XLA Ops:
  0.6 4.1 %collective-permute-start.1 = (bf16[128,256]{1,0:T(8,128)(2,1)}, bf16[128,256]{1,0:T(8,128)(2,1)S(1)}, u32[]{:S(2)}, u32[]{:S(2)}) collective-permute-start(bf16[128,256]{1,0:T(8,128)(2,1)} %refs_3_.1), channel_id=1, source_target_pairs={{0,8},{4,12},{8,0},{12,4},{1,9},{5,13},{9,1},{13,5},{2,10},{6,14},... | collective-permute-start | bytes 196616 | tf_op jit(solution)/shard_map/ppermute | solution.py:517
  4.7 1.6 %collective-permute-start = (bf16[128,256]{1,0:T(8,128)(2,1)}, bf16[128,256]{1,0:T(8,128)(2,1)S(1)}, u32[]{:S(2)}, u32[]{:S(2)}) collective-permute-start(bf16[128,256]{1,0:T(8,128)(2,1)} %refs_3_.1), channel_id=1, source_target_pairs={{0,4},{4,0},{8,12},{12,8},{1,5},{5,1},{9,13},{13,9},{2,6},{6,2},{1... | collective-permute-start | bytes 196616 | tf_op jit(solution)/shard_map/ppermute | solution.py:517
  6.3 0.0 collective-permute-start.11
  6.3 1.9 %collective-permute-start.5 = (bf16[128,256]{1,0:T(8,128)(2,1)}, bf16[128,256]{1,0:T(8,128)(2,1)S(1)}, u32[]{:S(2)}, u32[]{:S(2)}) collective-permute-start(bf16[128,256]{1,0:T(8,128)(2,1)} %refs_1_.3), channel_id=1, source_target_pairs={{0,8},{4,12},{8,0},{12,4},{1,9},{5,13},{9,1},{13,5},{2,10},{6,14},... | collective-permute-start | bytes 196616 | tf_op jit(solution)/shard_map/ppermute | solution.py:517
  8.2 2.5 %collective-permute-start.3 = (bf16[128,256]{1,0:T(8,128)(2,1)}, bf16[128,256]{1,0:T(8,128)(2,1)S(1)}, u32[]{:S(2)}, u32[]{:S(2)}) collective-permute-start(bf16[128,256]{1,0:T(8,128)(2,1)} %refs_1_.3), channel_id=1, source_target_pairs={{0,4},{4,0},{8,12},{12,8},{1,5},{5,1},{9,13},{13,9},{2,6},{6,2},{1... | collective-permute-start | bytes 196616 | tf_op jit(solution)/shard_map/ppermute | solution.py:517
  10.7 2.3 %index_table.1 = (s32[7,8]{1,0:T(8,128)S(4)}, bf16[128,256]{1,0:T(8,128)(2,1)S(1)}, bf16[8,512,1536]{2,1,0:T(8,128)(2,1)S(1)}) custom-call(s32[64]{0:T(128)} %refs_0_, s32[8]{0:T(128)} %refs_1_.2, s32[8]{0:T(128)} %refs_2_.1, bf16[128,256]{1,0:T(8,128)(2,1)} %refs_3_.1, bf16[4096,256]{1,0:T(8,128)(2,1)} %refs_4_.1, bf16[4096,256]{1,0:T(8,128)(2,1)} %refs_5_.1), custom_call_target="tpu_custom_call" | custom-call | tf_op jit(solution)/shard_map/index_table/pallas_call | solution.py:123
  13.0 0.0 collective-permute-done.refs_3_
  13.1 0.1 collective-permute-start.9
  13.1 0.5 %collective-permute-start.8 = (bf16[128,256]{1,0:T(8,128)(2,1)S(1)}, bf16[128,256]{1,0:T(8,128)(2,1)S(1)}, u32[]{:S(2)}, u32[]{:S(2)}) collective-permute-start(bf16[128,256]{1,0:T(8,128)(2,1)S(1)} %get-tuple-element.37.refs_1_), channel_id=1, source_target_pairs={{0,1},{1,0},{2,3},{3,2},{4,5},{5,4},{6,7},{7,6},{8,9},{9,8},{10,11... | collective-permute-start | bytes 196616 | tf_op jit(solution)/shard_map/ppermute | solution.py:516
  13.6 0.1 collective-permute-start.10
  13.7 0.7 %collective-permute-done.5.refs_5_ = bf16[128,256]{1,0:T(8,128)(2,1)S(1)} collective-permute-done((bf16[128,256]{1,0:T(8,128)(2,1)}, bf16[128,256]{1,0:T(8,128)(2,1)S(1)}, u32[]{:S(2)}, u32[]{:S(2)}) %collective-permute-start.5) | collective-permute-done | bytes 65568 | tf_op jit(solution)/shard_map/ppermute | solution.py:517
  14.4 0.8 %collective-permute-start.7 = (bf16[128,256]{1,0:T(8,128)(2,1)S(1)}, bf16[128,256]{1,0:T(8,128)(2,1)S(1)}, u32[]{:S(2)}, u32[]{:S(2)}) collective-permute-start(bf16[128,256]{1,0:T(8,128)(2,1)S(1)} %collective-permute-done.5.refs_5_), channel_id=1, source_target_pairs={{0,4},{4,0},{8,12},{12,8},{1,5},{5,1},{9,13},{13,9},{2,6},{6,2},{1... | collective-permute-start | bytes 196616 | tf_op jit(solution)/shard_map/ppermute | solution.py:517
  15.2 0.0 collective-permute-start.2
  15.2 0.5 %collective-permute-start.6 = (bf16[128,256]{1,0:T(8,128)(2,1)S(1)}, bf16[128,256]{1,0:T(8,128)(2,1)S(1)}, u32[]{:S(2)}, u32[]{:S(2)}) collective-permute-start(bf16[128,256]{1,0:T(8,128)(2,1)S(1)} %collective-permute-done.5.refs_5_), channel_id=1, source_target_pairs={{0,1},{1,0},{2,3},{3,2},{4,5},{5,4},{6,7},{7,6},{8,9},{9,8},{10,11... | collective-permute-start | bytes 196616 | tf_op jit(solution)/shard_map/ppermute | solution.py:516
  15.7 0.1 collective-permute-start.4
  15.8 0.0 collective-permute-done.12.refs_8_
  15.8 3.5 %block_weights.1 = (f32[2080,128]{1,0:T(8,128)S(1)}, bf16[8,512,1536]{2,1,0:T(8,128)(2,1)S(1)}) custom-call(s32[7,8]{1,0:T(8,128)S(4)} %get-tuple-element.36.refs_0_.meta, bf16[128,256]{1,0:T(8,128)(2,1)S(1)} %get-tuple-element.37.refs_1_, bf16[128,256]{1,0:T(8,128)(2,1)S(1)} %collective-permute-done.8.refs_2_, ...), custom_call_target="tpu_custom_call", output_to_operand_aliasing={{1}: (9, {})} | custom-call | tf_op jit(solution)/shard_map/block_weights/pallas_call | solution.py:219
  19.3 0.0 collective-permute-done.7.refs_7_
  19.3 0.5 %collective-permute-start.13 = (bf16[128,256]{1,0:T(8,128)(2,1)S(1)}, bf16[128,256]{1,0:T(8,128)(2,1)S(1)}, u32[]{:S(2)}, u32[]{:S(2)}) collective-permute-start(bf16[128,256]{1,0:T(8,128)(2,1)S(1)} %collective-permute-done.7.refs_7_), channel_id=1, source_target_pairs={{0,1},{1,0},{2,3},{3,2},{4,5},{5,4},{6,7},{7,6},{8,9},{9,8},{10,11... | collective-permute-start | bytes 196616 | tf_op jit(solution)/shard_map/ppermute | solution.py:516
  19.8 0.0 collective-permute-done.2.refs_2_
  19.8 0.0 collective-permute-done.6.refs_6_
  19.8 0.0 collective-permute-done.4.refs_4_
  19.8 0.9 %collective-permute-done.13.refs_8_ = bf16[128,256]{1,0:T(8,128)(2,1)S(1)} collective-permute-done((bf16[128,256]{1,0:T(8,128)(2,1)S(1)}, bf16[128,256]{1,0:T(8,128)(2,1)S(1)}, u32[]{:S(2)}, u32[]{:S(2)}) %collective-permute-start.13) | collective-permute-done | bytes 65568 | tf_op jit(solution)/shard_map/ppermute | solution.py:516
  20.7 3.3 %moved_weights.1 = (f32[2112,128]{1,0:T(8,128)S(1)}, f32[2,8,512]{2,1,0:T(8,128)S(1)}, bf16[8,512,1536]{2,1,0:T(8,128)(2,1)S(1)}) custom-call(s32[7,8]{1,0:T(8,128)S(4)} %get-tuple-element.36.refs_0_.meta, bf16[128,256]{1,0:T(8,128)(2,1)S(1)} %copy-done, bf16[128,256]{1,0:T(8,128)(2,1)S(1)} %collective-permute-done.2.refs_2_, ...), custom_call_target="tpu_custom_call", output_to_operand_aliasing={{2}: (10, {})} | custom-call | tf_op jit(solution)/shard_map/moved_weights/pallas_call | solution.py:308
  24.0 3.2 %collective-permute-start.15 = (f32[2,8,512]{2,1,0:T(8,128)S(1)}, f32[2,8,512]{2,1,0:T(8,128)S(1)}, u32[]{:S(2)}, u32[]{:S(2)}) collective-permute-start(f32[2,8,512]{2,1,0:T(8,128)S(1)} %get-tuple-element.45.refs_1_.refs_3_), channel_id=1, source_target_pairs={{0,8},{4,12},{8,0},{12,4},{1,9},{5,13},{9,1},{13,5},{2,10},{6,14},... | collective-permute-start | bytes 98312 | tf_op jit(solution)/shard_map/ppermute | solution.py:517
  27.2 0.5 %collective-permute-start.16 = (f32[2,8,512]{2,1,0:T(8,128)S(1)}, f32[2,8,512]{2,1,0:T(8,128)S(1)}, u32[]{:S(2)}, u32[]{:S(2)}) collective-permute-start(f32[2,8,512]{2,1,0:T(8,128)S(1)} %get-tuple-element.45.refs_1_.refs_3_), channel_id=1, source_target_pairs={{0,12},{4,8},{8,4},{12,0},{1,13},{5,9},{9,5},{13,1},{2,14},{6,10},... | collective-permute-start | bytes 98312 | tf_op jit(solution)/shard_map/ppermute | solution.py:517
  27.7 0.1 collective-permute-start.17
  27.8 1.3 %query_sums.1 = (f32[8,2,256,128]{3,2,1,0:T(8,128)S(1)}, bf16[8,512,1536]{2,1,0:T(8,128)(2,1)S(1)}) custom-call(bf16[8,512,1536]{2,1,0:T(8,128)(2,1)S(1)} %get-tuple-element.46.state), custom_call_target="tpu_custom_call", output_to_operand_aliasing={{1}: (0, {})} | custom-call | tf_op jit(solution)/shard_map/query_sums/pallas_call | solution.py:353
  29.1 0.9 %collective-permute-done.15.refs_5_ = f32[2,8,512]{2,1,0:T(8,128)S(1)} collective-permute-done((f32[2,8,512]{2,1,0:T(8,128)S(1)}, f32[2,8,512]{2,1,0:T(8,128)S(1)}, u32[]{:S(2)}, u32[]{:S(2)}) %collective-permute-start.15) | collective-permute-done | bytes 32800 | tf_op jit(solution)/shard_map/ppermute | solution.py:517
  30.0 2.9 %collective-permute-done.16.refs_7_ = f32[2,8,512]{2,1,0:T(8,128)S(1)} collective-permute-done((f32[2,8,512]{2,1,0:T(8,128)S(1)}, f32[2,8,512]{2,1,0:T(8,128)S(1)}, u32[]{:S(2)}, u32[]{:S(2)}) %collective-permute-start.16) | collective-permute-done | bytes 32800 | tf_op jit(solution)/shard_map/ppermute | solution.py:517
  32.9 0.0 collective-permute-done.14.refs_2_.refs_4_
  32.9 0.5 %chip_sums.1 = (f32[4,2,256,128]{3,2,1,0:T(8,128)S(1)}, bf16[4,2,256,128]{3,2,1,0:T(8,128)(2,1)S(1)}) custom-call(s32[7,8]{1,0:T(8,128)S(4)} %get-tuple-element.36.refs_0_.meta, f32[2,8,512]{2,1,0:T(8,128)S(1)} %get-tuple-element.45.refs_1_.refs_3_, f32[2,8,512]{2,1,0:T(8,128)S(1)} %collective-permute-done.14.refs_2_.refs_4_, ...), custom_call_target="tpu_custom_call" | custom-call | tf_op jit(solution)/shard_map/chip_sums/pallas_call | solution.py:396
  33.4 0.1 collective-permute-start.21
  33.5 0.5 %collective-permute-start.18 = (f32[2,8,512]{2,1,0:T(8,128)S(1)}, f32[2,8,512]{2,1,0:T(8,128)S(1)}, u32[]{:S(2)}, u32[]{:S(2)}) collective-permute-start(f32[2,8,512]{2,1,0:T(8,128)S(1)} %collective-permute-done.15.refs_5_), channel_id=1, source_target_pairs={{0,1},{1,0},{2,3},{3,2},{4,5},{5,4},{6,7},{7,6},{8,9},{9,8},{10,11... | collective-permute-start | bytes 98312 | tf_op jit(solution)/shard_map/ppermute | solution.py:516
  34.0 0.1 collective-permute-start.19
  34.1 0.4 collective-permute-start.20
  34.5 0.9 %collective-permute-done.18.refs_6_ = f32[2,8,512]{2,1,0:T(8,128)S(1)} collective-permute-done((f32[2,8,512]{2,1,0:T(8,128)S(1)}, f32[2,8,512]{2,1,0:T(8,128)S(1)}, u32[]{:S(2)}, u32[]{:S(2)}) %collective-permute-start.18) | collective-permute-done | bytes 32800 | tf_op jit(solution)/shard_map/ppermute | solution.py:516
  35.4 0.0 collective-permute-done.19.refs_8_
  35.5 0.0 collective-permute-done.20.refs_10_
  35.5 0.0 collective-permute-done.21.refs_12_
  35.5 0.3 query_grads.1
  35.9 1.0 %collective-permute-start.22 = (bf16[128,256]{1,0:T(8,128)(2,1)S(1)}, bf16[128,256]{1,0:T(8,128)(2,1)S(1)}, u32[]{:S(2)}, u32[]{:S(2)}) collective-permute-start(bf16[128,256]{1,0:T(8,128)(2,1)S(1)} %get-tuple-element.56), channel_id=1, source_target_pairs={{0,8},{4,12},{8,0},{12,4},{1,9},{5,13},{9,1},{13,5},{2,10},{6,14},... | collective-permute-start | bytes 196616 | tf_op jit(solution)/shard_map/ppermute | solution.py:517
  36.8 1.2 %collective-permute-start.23 = (bf16[128,256]{1,0:T(8,128)(2,1)S(1)}, bf16[128,256]{1,0:T(8,128)(2,1)S(1)}, u32[]{:S(2)}, u32[]{:S(2)}) collective-permute-start(bf16[128,256]{1,0:T(8,128)(2,1)S(1)} %get-tuple-element.57), channel_id=1, source_target_pairs={{0,12},{4,8},{8,4},{12,0},{1,13},{5,9},{9,5},{13,1},{2,14},{6,10},... | collective-permute-start | bytes 196616 | tf_op jit(solution)/shard_map/ppermute | solution.py:517
  38.0 1.4 %collective-permute-start.24 = (bf16[128,256]{1,0:T(8,128)(2,1)S(1)}, bf16[128,256]{1,0:T(8,128)(2,1)S(1)}, u32[]{:S(2)}, u32[]{:S(2)}) collective-permute-start(bf16[128,256]{1,0:T(8,128)(2,1)S(1)} %get-tuple-element.58), channel_id=1, source_target_pairs={{0,4},{4,0},{8,12},{12,8},{1,5},{5,1},{9,13},{13,9},{2,6},{6,2},{1... | collective-permute-start | bytes 196616 | tf_op jit(solution)/shard_map/ppermute | solution.py:517
  39.4 3.3 %row_grads.1 = (bf16[4096,256]{1,0:T(8,128)(2,1)}, bf16[4096,256]{1,0:T(8,128)(2,1)}) custom-call(s32[7,8]{1,0:T(8,128)S(4)} %get-tuple-element.36.refs_0_.meta, f32[8,512]{1,0:T(8,128)S(1)} %get-tuple-element.60.c_ref, f32[8,512]{1,0:T(8,128)S(1)} %get-tuple-element.61.d_ref, f32[2080,128]{1,0:T(8,128)S(1)} %get-tuple-element.43.refs_9_.refs_3_.refs_13_.q_side, ...), custom_call_target="tpu_custom_call" | custom-call | tf_op jit(solution)/shard_map/row_grads/pallas_call | solution.py:497
  42.7 0.6 %collective-permute-done.22 = bf16[128,256]{1,0:T(8,128)(2,1)S(1)} collective-permute-done((bf16[128,256]{1,0:T(8,128)(2,1)S(1)}, bf16[128,256]{1,0:T(8,128)(2,1)S(1)}, u32[]{:S(2)}, u32[]{:S(2)}) %collective-permute-start.22) | collective-permute-done | bytes 65568 | tf_op jit(solution)/shard_map/ppermute | solution.py:517
  43.3 1.3 %collective-permute-done.24 = bf16[128,256]{1,0:T(8,128)(2,1)S(1)} collective-permute-done((bf16[128,256]{1,0:T(8,128)(2,1)S(1)}, bf16[128,256]{1,0:T(8,128)(2,1)S(1)}, u32[]{:S(2)}, u32[]{:S(2)}) %collective-permute-start.24) | collective-permute-done | bytes 65568 | tf_op jit(solution)/shard_map/ppermute | solution.py:517
  44.6 0.7 %add_convert_fusion = bf16[128,256]{1,0:T(8,128)(2,1)} fusion(bf16[128,256]{1,0:T(8,128)(2,1)S(1)} %collective-permute-done.24, bf16[128,256]{1,0:T(8,128)(2,1)S(1)} %collective-permute-done.23, f32[128,256]{1,0:T(8,128)S(1)} %get-tuple-element.55, bf16[128,256]{1,0:T(8,128)(2,1)S(1)} %collective-permute-done.22), kind=kLoop, calls=%fused_computation | loop fusion | flops 229376 | bytes 393216 | tf_op jit(solution)/shard_map/convert_element_type | solution.py:578
  (12 shorter events, 0.0 us)
Async XLA Ops:
  0.6 14.6 %copy-start = (bf16[128,256]{1,0:T(8,128)(2,1)S(1)}, bf16[128,256]{1,0:T(8,128)(2,1)}, u32[]{:S(2)}) copy-start(bf16[128,256]{1,0:T(8,128)(2,1)} %refs_1_.3) | copy-start | bytes 196612
  0.6 10.1 %collective-permute-start.1 = (bf16[128,256]{1,0:T(8,128)(2,1)}, bf16[128,256]{1,0:T(8,128)(2,1)S(1)}, u32[]{:S(2)}, u32[]{:S(2)}) collective-permute-start(bf16[128,256]{1,0:T(8,128)(2,1)} %refs_3_.1), channel_id=1, source_target_pairs={{0,8},{4,12},{8,0},{12,4},{1,9},{5,13},{9,1},{13,5},{2,10},{6,14},... | collective-permute-start | bytes 196616 | tf_op jit(solution)/shard_map/ppermute | solution.py:517
  4.7 8.3 %collective-permute-start = (bf16[128,256]{1,0:T(8,128)(2,1)}, bf16[128,256]{1,0:T(8,128)(2,1)S(1)}, u32[]{:S(2)}, u32[]{:S(2)}) collective-permute-start(bf16[128,256]{1,0:T(8,128)(2,1)} %refs_3_.1), channel_id=1, source_target_pairs={{0,4},{4,0},{8,12},{12,8},{1,5},{5,1},{9,13},{13,9},{2,6},{6,2},{1... | collective-permute-start | bytes 196616 | tf_op jit(solution)/shard_map/ppermute | solution.py:517
  6.3 7.3 %collective-permute-start.11 = (bf16[128,256]{1,0:T(8,128)(2,1)}, bf16[128,256]{1,0:T(8,128)(2,1)S(1)}, u32[]{:S(2)}, u32[]{:S(2)}) collective-permute-start(bf16[128,256]{1,0:T(8,128)(2,1)} %refs_3_.1), channel_id=1, source_target_pairs={{0,12},{4,8},{8,4},{12,0},{1,13},{5,9},{9,5},{13,1},{2,14},{6,10},... | collective-permute-start | bytes 196616 | tf_op jit(solution)/shard_map/ppermute | solution.py:517
  6.3 8.1 %collective-permute-start.5 = (bf16[128,256]{1,0:T(8,128)(2,1)}, bf16[128,256]{1,0:T(8,128)(2,1)S(1)}, u32[]{:S(2)}, u32[]{:S(2)}) collective-permute-start(bf16[128,256]{1,0:T(8,128)(2,1)} %refs_1_.3), channel_id=1, source_target_pairs={{0,8},{4,12},{8,0},{12,4},{1,9},{5,13},{9,1},{13,5},{2,10},{6,14},... | collective-permute-start | bytes 196616 | tf_op jit(solution)/shard_map/ppermute | solution.py:517
  8.2 6.2 %collective-permute-start.3 = (bf16[128,256]{1,0:T(8,128)(2,1)}, bf16[128,256]{1,0:T(8,128)(2,1)S(1)}, u32[]{:S(2)}, u32[]{:S(2)}) collective-permute-start(bf16[128,256]{1,0:T(8,128)(2,1)} %refs_1_.3), channel_id=1, source_target_pairs={{0,4},{4,0},{8,12},{12,8},{1,5},{5,1},{9,13},{13,9},{2,6},{6,2},{1... | collective-permute-start | bytes 196616 | tf_op jit(solution)/shard_map/ppermute | solution.py:517
  13.1 2.1 %collective-permute-start.9 = (bf16[128,256]{1,0:T(8,128)(2,1)S(1)}, bf16[128,256]{1,0:T(8,128)(2,1)S(1)}, u32[]{:S(2)}, u32[]{:S(2)}) collective-permute-start(bf16[128,256]{1,0:T(8,128)(2,1)S(1)} %collective-permute-done.refs_3_), channel_id=1, source_target_pairs={{0,1},{1,0},{2,3},{3,2},{4,5},{5,4},{6,7},{7,6},{8,9},{9,8},{10,11... | collective-permute-start | bytes 196616 | tf_op jit(solution)/shard_map/ppermute | solution.py:516
  13.1 2.1 %collective-permute-start.8 = (bf16[128,256]{1,0:T(8,128)(2,1)S(1)}, bf16[128,256]{1,0:T(8,128)(2,1)S(1)}, u32[]{:S(2)}, u32[]{:S(2)}) collective-permute-start(bf16[128,256]{1,0:T(8,128)(2,1)S(1)} %get-tuple-element.37.refs_1_), channel_id=1, source_target_pairs={{0,1},{1,0},{2,3},{3,2},{4,5},{5,4},{6,7},{7,6},{8,9},{9,8},{10,11... | collective-permute-start | bytes 196616 | tf_op jit(solution)/shard_map/ppermute | solution.py:516
  13.6 2.1 %collective-permute-start.10 = (bf16[128,256]{1,0:T(8,128)(2,1)S(1)}, bf16[128,256]{1,0:T(8,128)(2,1)S(1)}, u32[]{:S(2)}, u32[]{:S(2)}) collective-permute-start(bf16[128,256]{1,0:T(8,128)(2,1)S(1)} %collective-permute-done.1.refs_5_), channel_id=1, source_target_pairs={{0,1},{1,0},{2,3},{3,2},{4,5},{5,4},{6,7},{7,6},{8,9},{9,8},{10,11... | collective-permute-start | bytes 196616 | tf_op jit(solution)/shard_map/ppermute | solution.py:516
  14.4 1.4 %collective-permute-start.12 = (bf16[128,256]{1,0:T(8,128)(2,1)S(1)}, bf16[128,256]{1,0:T(8,128)(2,1)S(1)}, u32[]{:S(2)}, u32[]{:S(2)}) collective-permute-start(bf16[128,256]{1,0:T(8,128)(2,1)S(1)} %collective-permute-done.11.refs_7_), channel_id=1, source_target_pairs={{0,1},{1,0},{2,3},{3,2},{4,5},{5,4},{6,7},{7,6},{8,9},{9,8},{10,11... | collective-permute-start | bytes 196616 | tf_op jit(solution)/shard_map/ppermute | solution.py:516
  14.4 4.9 %collective-permute-start.7 = (bf16[128,256]{1,0:T(8,128)(2,1)S(1)}, bf16[128,256]{1,0:T(8,128)(2,1)S(1)}, u32[]{:S(2)}, u32[]{:S(2)}) collective-permute-start(bf16[128,256]{1,0:T(8,128)(2,1)S(1)} %collective-permute-done.5.refs_5_), channel_id=1, source_target_pairs={{0,4},{4,0},{8,12},{12,8},{1,5},{5,1},{9,13},{13,9},{2,6},{6,2},{1... | collective-permute-start | bytes 196616 | tf_op jit(solution)/shard_map/ppermute | solution.py:517
  15.2 4.6 %collective-permute-start.2 = (bf16[128,256]{1,0:T(8,128)(2,1)S(1)}, bf16[128,256]{1,0:T(8,128)(2,1)S(1)}, u32[]{:S(2)}, u32[]{:S(2)}) collective-permute-start(bf16[128,256]{1,0:T(8,128)(2,1)S(1)} %copy-done), channel_id=1, source_target_pairs={{0,1},{1,0},{2,3},{3,2},{4,5},{5,4},{6,7},{7,6},{8,9},{9,8},{10,11... | collective-permute-start | bytes 196616 | tf_op jit(solution)/shard_map/ppermute | solution.py:516
  15.2 4.6 %collective-permute-start.6 = (bf16[128,256]{1,0:T(8,128)(2,1)S(1)}, bf16[128,256]{1,0:T(8,128)(2,1)S(1)}, u32[]{:S(2)}, u32[]{:S(2)}) collective-permute-start(bf16[128,256]{1,0:T(8,128)(2,1)S(1)} %collective-permute-done.5.refs_5_), channel_id=1, source_target_pairs={{0,1},{1,0},{2,3},{3,2},{4,5},{5,4},{6,7},{7,6},{8,9},{9,8},{10,11... | collective-permute-start | bytes 196616 | tf_op jit(solution)/shard_map/ppermute | solution.py:516
  15.7 4.1 %collective-permute-start.4 = (bf16[128,256]{1,0:T(8,128)(2,1)S(1)}, bf16[128,256]{1,0:T(8,128)(2,1)S(1)}, u32[]{:S(2)}, u32[]{:S(2)}) collective-permute-start(bf16[128,256]{1,0:T(8,128)(2,1)S(1)} %collective-permute-done.3.refs_3_), channel_id=1, source_target_pairs={{0,1},{1,0},{2,3},{3,2},{4,5},{5,4},{6,7},{7,6},{8,9},{9,8},{10,11... | collective-permute-start | bytes 196616 | tf_op jit(solution)/shard_map/ppermute | solution.py:516
  19.3 1.4 %collective-permute-start.13 = (bf16[128,256]{1,0:T(8,128)(2,1)S(1)}, bf16[128,256]{1,0:T(8,128)(2,1)S(1)}, u32[]{:S(2)}, u32[]{:S(2)}) collective-permute-start(bf16[128,256]{1,0:T(8,128)(2,1)S(1)} %collective-permute-done.7.refs_7_), channel_id=1, source_target_pairs={{0,1},{1,0},{2,3},{3,2},{4,5},{5,4},{6,7},{7,6},{8,9},{9,8},{10,11... | collective-permute-start | bytes 196616 | tf_op jit(solution)/shard_map/ppermute | solution.py:516
  24.0 6.0 %collective-permute-start.15 = (f32[2,8,512]{2,1,0:T(8,128)S(1)}, f32[2,8,512]{2,1,0:T(8,128)S(1)}, u32[]{:S(2)}, u32[]{:S(2)}) collective-permute-start(f32[2,8,512]{2,1,0:T(8,128)S(1)} %get-tuple-element.45.refs_1_.refs_3_), channel_id=1, source_target_pairs={{0,8},{4,12},{8,0},{12,4},{1,9},{5,13},{9,1},{13,5},{2,10},{6,14},... | collective-permute-start | bytes 98312 | tf_op jit(solution)/shard_map/ppermute | solution.py:517
  27.2 5.7 %collective-permute-start.16 = (f32[2,8,512]{2,1,0:T(8,128)S(1)}, f32[2,8,512]{2,1,0:T(8,128)S(1)}, u32[]{:S(2)}, u32[]{:S(2)}) collective-permute-start(f32[2,8,512]{2,1,0:T(8,128)S(1)} %get-tuple-element.45.refs_1_.refs_3_), channel_id=1, source_target_pairs={{0,12},{4,8},{8,4},{12,0},{1,13},{5,9},{9,5},{13,1},{2,14},{6,10},... | collective-permute-start | bytes 98312 | tf_op jit(solution)/shard_map/ppermute | solution.py:517
  27.7 5.2 %collective-permute-start.17 = (f32[2,8,512]{2,1,0:T(8,128)S(1)}, f32[2,8,512]{2,1,0:T(8,128)S(1)}, u32[]{:S(2)}, u32[]{:S(2)}) collective-permute-start(f32[2,8,512]{2,1,0:T(8,128)S(1)} %get-tuple-element.45.refs_1_.refs_3_), channel_id=1, source_target_pairs={{0,4},{4,0},{8,12},{12,8},{1,5},{5,1},{9,13},{13,9},{2,6},{6,2},{1... | collective-permute-start | bytes 98312 | tf_op jit(solution)/shard_map/ppermute | solution.py:517
  27.8 5.1 %collective-permute-start.14 = (f32[2,8,512]{2,1,0:T(8,128)S(1)}, f32[2,8,512]{2,1,0:T(8,128)S(1)}, u32[]{:S(2)}, u32[]{:S(2)}) collective-permute-start(f32[2,8,512]{2,1,0:T(8,128)S(1)} %get-tuple-element.45.refs_1_.refs_3_), channel_id=1, source_target_pairs={{0,1},{1,0},{2,3},{3,2},{4,5},{5,4},{6,7},{7,6},{8,9},{9,8},{10,11... | collective-permute-start | bytes 98312 | tf_op jit(solution)/shard_map/ppermute | solution.py:516
  33.4 2.1 %collective-permute-start.21 = (bf16[4,2,256,128]{3,2,1,0:T(8,128)(2,1)S(1)}, bf16[4,2,256,128]{3,2,1,0:T(8,128)(2,1)S(1)}, u32[]{:S(2)}, u32[]{:S(2)}) collective-permute-start(bf16[4,2,256,128]{3,2,1,0:T(8,128)(2,1)S(1)} %get-tuple-element.54), channel_id=1, source_target_pairs={{0,1},{1,0},{2,3},{3,2},{4,5},{5,4},{6,7},{7,6},{8,9},{9,8},{10,11... | collective-permute-start | bytes 1572872 | tf_op jit(solution)/shard_map/ppermute | solution.py:516
  33.5 1.9 %collective-permute-start.18 = (f32[2,8,512]{2,1,0:T(8,128)S(1)}, f32[2,8,512]{2,1,0:T(8,128)S(1)}, u32[]{:S(2)}, u32[]{:S(2)}) collective-permute-start(f32[2,8,512]{2,1,0:T(8,128)S(1)} %collective-permute-done.15.refs_5_), channel_id=1, source_target_pairs={{0,1},{1,0},{2,3},{3,2},{4,5},{5,4},{6,7},{7,6},{8,9},{9,8},{10,11... | collective-permute-start | bytes 98312 | tf_op jit(solution)/shard_map/ppermute | solution.py:516
  34.0 1.5 %collective-permute-start.19 = (f32[2,8,512]{2,1,0:T(8,128)S(1)}, f32[2,8,512]{2,1,0:T(8,128)S(1)}, u32[]{:S(2)}, u32[]{:S(2)}) collective-permute-start(f32[2,8,512]{2,1,0:T(8,128)S(1)} %collective-permute-done.16.refs_7_), channel_id=1, source_target_pairs={{0,1},{1,0},{2,3},{3,2},{4,5},{5,4},{6,7},{7,6},{8,9},{9,8},{10,11... | collective-permute-start | bytes 98312 | tf_op jit(solution)/shard_map/ppermute | solution.py:516
  34.1 1.5 %collective-permute-start.20 = (f32[2,8,512]{2,1,0:T(8,128)S(1)}, f32[2,8,512]{2,1,0:T(8,128)S(1)}, u32[]{:S(2)}, u32[]{:S(2)}) collective-permute-start(f32[2,8,512]{2,1,0:T(8,128)S(1)} %collective-permute-done.17.refs_9_), channel_id=1, source_target_pairs={{0,1},{1,0},{2,3},{3,2},{4,5},{5,4},{6,7},{7,6},{8,9},{9,8},{10,11... | collective-permute-start | bytes 98312 | tf_op jit(solution)/shard_map/ppermute | solution.py:516
  35.9 7.5 %collective-permute-start.22 = (bf16[128,256]{1,0:T(8,128)(2,1)S(1)}, bf16[128,256]{1,0:T(8,128)(2,1)S(1)}, u32[]{:S(2)}, u32[]{:S(2)}) collective-permute-start(bf16[128,256]{1,0:T(8,128)(2,1)S(1)} %get-tuple-element.56), channel_id=1, source_target_pairs={{0,8},{4,12},{8,0},{12,4},{1,9},{5,13},{9,1},{13,5},{2,10},{6,14},... | collective-permute-start | bytes 196616 | tf_op jit(solution)/shard_map/ppermute | solution.py:517
  36.8 6.5 %collective-permute-start.23 = (bf16[128,256]{1,0:T(8,128)(2,1)S(1)}, bf16[128,256]{1,0:T(8,128)(2,1)S(1)}, u32[]{:S(2)}, u32[]{:S(2)}) collective-permute-start(bf16[128,256]{1,0:T(8,128)(2,1)S(1)} %get-tuple-element.57), channel_id=1, source_target_pairs={{0,12},{4,8},{8,4},{12,0},{1,13},{5,9},{9,5},{13,1},{2,14},{6,10},... | collective-permute-start | bytes 196616 | tf_op jit(solution)/shard_map/ppermute | solution.py:517
  38.0 6.6 %collective-permute-start.24 = (bf16[128,256]{1,0:T(8,128)(2,1)S(1)}, bf16[128,256]{1,0:T(8,128)(2,1)S(1)}, u32[]{:S(2)}, u32[]{:S(2)}) collective-permute-start(bf16[128,256]{1,0:T(8,128)(2,1)S(1)} %get-tuple-element.58), channel_id=1, source_target_pairs={{0,4},{4,0},{8,12},{12,8},{1,5},{5,1},{9,13},{13,9},{2,6},{6,2},{1... | collective-permute-start | bytes 196616 | tf_op jit(solution)/shard_map/ppermute | solution.py:517

commit v15 on v13

--- a/solution.py
+++ b/solution.py
@@ -530,7 +530,7 @@
         for value in near:
             queries += [value, pair(value)]
         q_side, state = block_weights(meta, queries, state, features, tables)
-        near_grads[2], q_side = after(near_grads[2], q_side)
+        *near_grads[1:], q_side = lax.optimization_barrier((*near_grads[1:], q_side))
         grads = [cotangent, pair(cotangent)]
         for value in near_grads:
             grads += [value, pair(value)]

time: 44.7 us -> 45 us (level)
  transfers between devices with their start and end apart: 25 -> 25, of which waited for: 6 -> 7; matrix products, arithmetic and copies ran while one was open for 0% -> 0% of each run, Pallas kernels for 23% -> 23%
where the time goes in v15:
time: 45 us; the launch traced here: 44.8 us
  starting transfers between devices  22.6 us (50%)
  Pallas kernels  14.5 us (32%)
  waiting for transfers between devices  6.35 us (14%)
  between operations  0.76 us (2%)
  other arithmetic  0.66 us (1%)
    ppermute x12, starting transfers between devices, local(): lax.ppermute(value, 'rows', [(z, z ^ s) for z in range(4)])  19.8 us
    ppermute x12, waiting for transfers between devices, local(): lax.ppermute(value, 'rows', [(z, z ^ s) for z in range(4)])  4.41 us
    pallas_call x1, Pallas kernels, block_weights(): pl.pallas_call(lambda *refs: weights_kernel(count, features, *refs), in_s...  3.48 us
    pallas_call x1, Pallas kernels, row_grads(): pl.pallas_call(row_grads_kernel, in_specs=[smem_spec()] + [vmem_spec()] *...  3.29 us
    pallas_call x1, Pallas kernels, moved_weights(): pl.pallas_call(lambda *refs: moved_kernel(count, features, *refs), in_spe...  3.26 us
    ppermute x13, starting transfers between devices, local(): pair = lambda value: lax.ppermute(value, 'pair', PAIR)  2.81 us
    pallas_call x1, Pallas kernels, index_table(): pl.pallas_call(lambda *refs: index_kernel(small, *refs), in_specs=[hbm_sp...  2.33 us
    ppermute x13, waiting for transfers between devices, local(): pair = lambda value: lax.ppermute(value, 'pair', PAIR)  1.94 us
  transfers between devices with their start and end apart: 25, of which 7 were waited for; matrix products, arithmetic and copies ran while one was open for 0% of the time, Pallas kernels for 23%

profile of v15, /device:TPU:0, one launch (start us, length us, event | category | flops | bytes accessed | tf_op | source)
XLA Modules:
  0.0 44.8 jit_solution(16821277090324995641)
XLA Ops:
  0.6 4.1 %collective-permute-start.1 = (bf16[128,256]{1,0:T(8,128)(2,1)}, bf16[128,256]{1,0:T(8,128)(2,1)S(1)}, u32[]{:S(2)}, u32[]{:S(2)}) collective-permute-start(bf16[128,256]{1,0:T(8,128)(2,1)} %refs_3_.1), channel_id=1, source_target_pairs={{0,8},{4,12},{8,0},{12,4},{1,9},{5,13},{9,1},{13,5},{2,10},{6,14},... | collective-permute-start | bytes 196616 | tf_op jit(solution)/shard_map/ppermute | solution.py:517
  4.7 1.6 %collective-permute-start = (bf16[128,256]{1,0:T(8,128)(2,1)}, bf16[128,256]{1,0:T(8,128)(2,1)S(1)}, u32[]{:S(2)}, u32[]{:S(2)}) collective-permute-start(bf16[128,256]{1,0:T(8,128)(2,1)} %refs_3_.1), channel_id=1, source_target_pairs={{0,4},{4,0},{8,12},{12,8},{1,5},{5,1},{9,13},{13,9},{2,6},{6,2},{1... | collective-permute-start | bytes 196616 | tf_op jit(solution)/shard_map/ppermute | solution.py:517
  6.3 0.0 collective-permute-start.10
  6.3 1.9 %collective-permute-start.5 = (bf16[128,256]{1,0:T(8,128)(2,1)}, bf16[128,256]{1,0:T(8,128)(2,1)S(1)}, u32[]{:S(2)}, u32[]{:S(2)}) collective-permute-start(bf16[128,256]{1,0:T(8,128)(2,1)} %refs_1_.3), channel_id=1, source_target_pairs={{0,8},{4,12},{8,0},{12,4},{1,9},{5,13},{9,1},{13,5},{2,10},{6,14},... | collective-permute-start | bytes 196616 | tf_op jit(solution)/shard_map/ppermute | solution.py:517
  8.2 2.5 %collective-permute-start.3 = (bf16[128,256]{1,0:T(8,128)(2,1)}, bf16[128,256]{1,0:T(8,128)(2,1)S(1)}, u32[]{:S(2)}, u32[]{:S(2)}) collective-permute-start(bf16[128,256]{1,0:T(8,128)(2,1)} %refs_1_.3), channel_id=1, source_target_pairs={{0,4},{4,0},{8,12},{12,8},{1,5},{5,1},{9,13},{13,9},{2,6},{6,2},{1... | collective-permute-start | bytes 196616 | tf_op jit(solution)/shard_map/ppermute | solution.py:517
  10.7 0.0 collective-permute-done.1.refs_5_
  10.7 2.3 %index_table.1 = (s32[7,8]{1,0:T(8,128)S(4)}, bf16[128,256]{1,0:T(8,128)(2,1)S(1)}, bf16[8,512,1536]{2,1,0:T(8,128)(2,1)S(1)}) custom-call(s32[64]{0:T(128)} %refs_0_, s32[8]{0:T(128)} %refs_1_.2, s32[8]{0:T(128)} %refs_2_.1, bf16[128,256]{1,0:T(8,128)(2,1)} %refs_3_.1, bf16[4096,256]{1,0:T(8,128)(2,1)} %refs_4_.1, bf16[4096,256]{1,0:T(8,128)(2,1)} %refs_5_.1), custom_call_target="tpu_custom_call" | custom-call | tf_op jit(solution)/shard_map/index_table/pallas_call | solution.py:123
  13.0 0.0 collective-permute-done.refs_3_
  13.1 0.1 collective-permute-start.8
  13.1 0.5 %collective-permute-start.7 = (bf16[128,256]{1,0:T(8,128)(2,1)S(1)}, bf16[128,256]{1,0:T(8,128)(2,1)S(1)}, u32[]{:S(2)}, u32[]{:S(2)}) collective-permute-start(bf16[128,256]{1,0:T(8,128)(2,1)S(1)} %get-tuple-element.38.refs_1_), channel_id=1, source_target_pairs={{0,1},{1,0},{2,3},{3,2},{4,5},{5,4},{6,7},{7,6},{8,9},{9,8},{10,11... | collective-permute-start | bytes 196616 | tf_op jit(solution)/shard_map/ppermute | solution.py:516
  13.6 0.0 collective-permute-done.10.refs_7_
  13.6 0.1 collective-permute-start.9
  13.7 0.7 %collective-permute-done.5.refs_5_ = bf16[128,256]{1,0:T(8,128)(2,1)S(1)} collective-permute-done((bf16[128,256]{1,0:T(8,128)(2,1)}, bf16[128,256]{1,0:T(8,128)(2,1)S(1)}, u32[]{:S(2)}, u32[]{:S(2)}) %collective-permute-start.5) | collective-permute-done | bytes 65568 | tf_op jit(solution)/shard_map/ppermute | solution.py:517
  14.4 0.0 collective-permute-start.11
  14.4 0.0 collective-permute-done.3.refs_3_
  14.4 0.8 %collective-permute-start.6 = (bf16[128,256]{1,0:T(8,128)(2,1)S(1)}, bf16[128,256]{1,0:T(8,128)(2,1)S(1)}, u32[]{:S(2)}, u32[]{:S(2)}) collective-permute-start(bf16[128,256]{1,0:T(8,128)(2,1)S(1)} %collective-permute-done.5.refs_5_), channel_id=1, source_target_pairs={{0,4},{4,0},{8,12},{12,8},{1,5},{5,1},{9,13},{13,9},{2,6},{6,2},{1... | collective-permute-start | bytes 196616 | tf_op jit(solution)/shard_map/ppermute | solution.py:517
  15.2 0.0 collective-permute-done.8.refs_4_
  15.2 0.0 collective-permute-start.2
  15.2 0.0 collective-permute-done.7.refs_2_
  15.2 0.5 %collective-permute-start.4 = (bf16[128,256]{1,0:T(8,128)(2,1)S(1)}, bf16[128,256]{1,0:T(8,128)(2,1)S(1)}, u32[]{:S(2)}, u32[]{:S(2)}) collective-permute-start(bf16[128,256]{1,0:T(8,128)(2,1)S(1)} %collective-permute-done.3.refs_3_), channel_id=1, source_target_pairs={{0,1},{1,0},{2,3},{3,2},{4,5},{5,4},{6,7},{7,6},{8,9},{9,8},{10,11... | collective-permute-start | bytes 196616 | tf_op jit(solution)/shard_map/ppermute | solution.py:516
  15.7 0.0 collective-permute-done.9.refs_6_
  15.7 3.5 %block_weights.1 = (f32[2080,128]{1,0:T(8,128)S(1)}, bf16[8,512,1536]{2,1,0:T(8,128)(2,1)S(1)}) custom-call(s32[7,8]{1,0:T(8,128)S(4)} %get-tuple-element.37.refs_0_.meta, bf16[128,256]{1,0:T(8,128)(2,1)S(1)} %get-tuple-element.38.refs_1_, bf16[128,256]{1,0:T(8,128)(2,1)S(1)} %collective-permute-done.7.refs_2_, ...), custom_call_target="tpu_custom_call", output_to_operand_aliasing={{1}: (9, {})} | custom-call | tf_op jit(solution)/shard_map/block_weights/pallas_call | solution.py:219
  19.2 0.2 collective-permute-start.12
  19.4 0.4 collective-permute-start.13
  19.8 0.7 %collective-permute-done.12.refs_6_ = bf16[128,256]{1,0:T(8,128)(2,1)S(1)} collective-permute-done((bf16[128,256]{1,0:T(8,128)(2,1)S(1)}, bf16[128,256]{1,0:T(8,128)(2,1)S(1)}, u32[]{:S(2)}, u32[]{:S(2)}) %collective-permute-start.12) | collective-permute-done | bytes 65568 | tf_op jit(solution)/shard_map/ppermute | solution.py:516
  20.5 0.2 collective-permute-done.13.refs_8_
  20.7 3.3 %moved_weights.1 = (f32[2112,128]{1,0:T(8,128)S(1)}, f32[2,8,512]{2,1,0:T(8,128)S(1)}, bf16[8,512,1536]{2,1,0:T(8,128)(2,1)S(1)}) custom-call(s32[7,8]{1,0:T(8,128)S(4)} %get-tuple-element.37.refs_0_.meta, bf16[128,256]{1,0:T(8,128)(2,1)S(1)} %copy-done, bf16[128,256]{1,0:T(8,128)(2,1)S(1)} %collective-permute-done.2.refs_2_, ...), custom_call_target="tpu_custom_call", output_to_operand_aliasing={{2}: (10, {})} | custom-call | tf_op jit(solution)/shard_map/moved_weights/pallas_call | solution.py:308
  24.0 3.2 %collective-permute-start.15 = (f32[2,8,512]{2,1,0:T(8,128)S(1)}, f32[2,8,512]{2,1,0:T(8,128)S(1)}, u32[]{:S(2)}, u32[]{:S(2)}) collective-permute-start(f32[2,8,512]{2,1,0:T(8,128)S(1)} %get-tuple-element.47.refs_1_.refs_3_), channel_id=1, source_target_pairs={{0,12},{4,8},{8,4},{12,0},{1,13},{5,9},{9,5},{13,1},{2,14},{6,10},... | collective-permute-start | bytes 98312 | tf_op jit(solution)/shard_map/ppermute | solution.py:517
  27.2 0.1 collective-permute-start.16
  27.2 1.2 %collective-permute-start.17 = (f32[2,8,512]{2,1,0:T(8,128)S(1)}, f32[2,8,512]{2,1,0:T(8,128)S(1)}, u32[]{:S(2)}, u32[]{:S(2)}) collective-permute-start(f32[2,8,512]{2,1,0:T(8,128)S(1)} %get-tuple-element.47.refs_1_.refs_3_), channel_id=1, source_target_pairs={{0,4},{4,0},{8,12},{12,8},{1,5},{5,1},{9,13},{13,9},{2,6},{6,2},{1... | collective-permute-start | bytes 98312 | tf_op jit(solution)/shard_map/ppermute | solution.py:517
  28.4 1.3 %query_sums.1 = (f32[8,2,256,128]{3,2,1,0:T(8,128)S(1)}, bf16[8,512,1536]{2,1,0:T(8,128)(2,1)S(1)}) custom-call(bf16[8,512,1536]{2,1,0:T(8,128)(2,1)S(1)} %get-tuple-element.48.state), custom_call_target="tpu_custom_call", output_to_operand_aliasing={{1}: (0, {})} | custom-call | tf_op jit(solution)/shard_map/query_sums/pallas_call | solution.py:353
  29.7 0.1 collective-permute-done.15.refs_5_
  29.8 2.6 %collective-permute-done.16.refs_7_ = f32[2,8,512]{2,1,0:T(8,128)S(1)} collective-permute-done((f32[2,8,512]{2,1,0:T(8,128)S(1)}, f32[2,8,512]{2,1,0:T(8,128)S(1)}, u32[]{:S(2)}, u32[]{:S(2)}) %collective-permute-start.16) | collective-permute-done | bytes 32800 | tf_op jit(solution)/shard_map/ppermute | solution.py:517
  32.3 0.5 %chip_sums.1 = (f32[4,2,256,128]{3,2,1,0:T(8,128)S(1)}, bf16[4,2,256,128]{3,2,1,0:T(8,128)(2,1)S(1)}) custom-call(s32[7,8]{1,0:T(8,128)S(4)} %get-tuple-element.37.refs_0_.meta, f32[2,8,512]{2,1,0:T(8,128)S(1)} %get-tuple-element.47.refs_1_.refs_3_, f32[2,8,512]{2,1,0:T(8,128)S(1)} %collective-permute-done.14.refs_2_.refs_4_, ...), custom_call_target="tpu_custom_call" | custom-call | tf_op jit(solution)/shard_map/chip_sums/pallas_call | solution.py:396
  32.9 0.1 collective-permute-start.21
  33.0 0.5 %collective-permute-start.18 = (f32[2,8,512]{2,1,0:T(8,128)S(1)}, f32[2,8,512]{2,1,0:T(8,128)S(1)}, u32[]{:S(2)}, u32[]{:S(2)}) collective-permute-start(f32[2,8,512]{2,1,0:T(8,128)S(1)} %collective-permute-done.15.refs_5_), channel_id=1, source_target_pairs={{0,1},{1,0},{2,3},{3,2},{4,5},{5,4},{6,7},{7,6},{8,9},{9,8},{10,11... | collective-permute-start | bytes 98312 | tf_op jit(solution)/shard_map/ppermute | solution.py:516
  33.5 0.1 collective-permute-start.19
  33.5 0.4 collective-permute-start.20
  34.0 0.9 %collective-permute-done.18.refs_6_ = f32[2,8,512]{2,1,0:T(8,128)S(1)} collective-permute-done((f32[2,8,512]{2,1,0:T(8,128)S(1)}, f32[2,8,512]{2,1,0:T(8,128)S(1)}, u32[]{:S(2)}, u32[]{:S(2)}) %collective-permute-start.18) | collective-permute-done | bytes 32800 | tf_op jit(solution)/shard_map/ppermute | solution.py:516
  34.9 0.0 collective-permute-done.19.refs_8_
  34.9 0.0 collective-permute-done.20.refs_10_
  35.0 0.3 query_grads.1
  35.3 1.9 %collective-permute-start.22 = (bf16[128,256]{1,0:T(8,128)(2,1)S(1)}, bf16[128,256]{1,0:T(8,128)(2,1)S(1)}, u32[]{:S(2)}, u32[]{:S(2)}) collective-permute-start(bf16[128,256]{1,0:T(8,128)(2,1)S(1)} %get-tuple-element.58), channel_id=1, source_target_pairs={{0,12},{4,8},{8,4},{12,0},{1,13},{5,9},{9,5},{13,1},{2,14},{6,10},... | collective-permute-start | bytes 196616 | tf_op jit(solution)/shard_map/ppermute | solution.py:517
  37.2 2.5 %collective-permute-start.24 = (bf16[128,256]{1,0:T(8,128)(2,1)S(1)}, bf16[128,256]{1,0:T(8,128)(2,1)S(1)}, u32[]{:S(2)}, u32[]{:S(2)}) collective-permute-start(bf16[128,256]{1,0:T(8,128)(2,1)S(1)} %get-tuple-element.60), channel_id=1, source_target_pairs={{0,4},{4,0},{8,12},{12,8},{1,5},{5,1},{9,13},{13,9},{2,6},{6,2},{1... | collective-permute-start | bytes 196616 | tf_op jit(solution)/shard_map/ppermute | solution.py:517
  39.8 3.3 %row_grads.1 = (bf16[4096,256]{1,0:T(8,128)(2,1)}, bf16[4096,256]{1,0:T(8,128)(2,1)}) custom-call(s32[7,8]{1,0:T(8,128)S(4)} %get-tuple-element.37.refs_0_.meta, f32[8,512]{1,0:T(8,128)S(1)} %get-tuple-element.62.c_ref, f32[8,512]{1,0:T(8,128)S(1)} %get-tuple-element.63.d_ref, f32[2080,128]{1,0:T(8,128)S(1)} %get-tuple-element.45.refs_9_.refs_3_.refs_13_.q_side, ...), custom_call_target="tpu_custom_call" | custom-call | tf_op jit(solution)/shard_map/row_grads/pallas_call | solution.py:497
  43.1 1.1 %collective-permute-done.23 = bf16[128,256]{1,0:T(8,128)(2,1)S(1)} collective-permute-done((bf16[128,256]{1,0:T(8,128)(2,1)S(1)}, bf16[128,256]{1,0:T(8,128)(2,1)S(1)}, u32[]{:S(2)}, u32[]{:S(2)}) %collective-permute-start.23) | collective-permute-done | bytes 65568 | tf_op jit(solution)/shard_map/ppermute | solution.py:517
  44.2 0.0 collective-permute-done.24
  44.2 0.7 %add_convert_fusion = bf16[128,256]{1,0:T(8,128)(2,1)} fusion(bf16[128,256]{1,0:T(8,128)(2,1)S(1)} %collective-permute-done.24, bf16[128,256]{1,0:T(8,128)(2,1)S(1)} %collective-permute-done.23, f32[128,256]{1,0:T(8,128)S(1)} %get-tuple-element.57, bf16[128,256]{1,0:T(8,128)(2,1)S(1)} %collective-permute-done.22), kind=kLoop, calls=%fused_computation | loop fusion | flops 229376 | bytes 393216 | tf_op jit(solution)/shard_map/convert_element_type | solution.py:578
  (12 shorter events, 0.0 us)
Async XLA Ops:
  0.6 14.6 %copy-start = (bf16[128,256]{1,0:T(8,128)(2,1)S(1)}, bf16[128,256]{1,0:T(8,128)(2,1)}, u32[]{:S(2)}) copy-start(bf16[128,256]{1,0:T(8,128)(2,1)} %refs_1_.3) | copy-start | bytes 196612
  0.6 10.1 %collective-permute-start.1 = (bf16[128,256]{1,0:T(8,128)(2,1)}, bf16[128,256]{1,0:T(8,128)(2,1)S(1)}, u32[]{:S(2)}, u32[]{:S(2)}) collective-permute-start(bf16[128,256]{1,0:T(8,128)(2,1)} %refs_3_.1), channel_id=1, source_target_pairs={{0,8},{4,12},{8,0},{12,4},{1,9},{5,13},{9,1},{13,5},{2,10},{6,14},... | collective-permute-start | bytes 196616 | tf_op jit(solution)/shard_map/ppermute | solution.py:517
  4.7 8.3 %collective-permute-start = (bf16[128,256]{1,0:T(8,128)(2,1)}, bf16[128,256]{1,0:T(8,128)(2,1)S(1)}, u32[]{:S(2)}, u32[]{:S(2)}) collective-permute-start(bf16[128,256]{1,0:T(8,128)(2,1)} %refs_3_.1), channel_id=1, source_target_pairs={{0,4},{4,0},{8,12},{12,8},{1,5},{5,1},{9,13},{13,9},{2,6},{6,2},{1... | collective-permute-start | bytes 196616 | tf_op jit(solution)/shard_map/ppermute | solution.py:517
  6.3 7.3 %collective-permute-start.10 = (bf16[128,256]{1,0:T(8,128)(2,1)}, bf16[128,256]{1,0:T(8,128)(2,1)S(1)}, u32[]{:S(2)}, u32[]{:S(2)}) collective-permute-start(bf16[128,256]{1,0:T(8,128)(2,1)} %refs_3_.1), channel_id=1, source_target_pairs={{0,12},{4,8},{8,4},{12,0},{1,13},{5,9},{9,5},{13,1},{2,14},{6,10},... | collective-permute-start | bytes 196616 | tf_op jit(solution)/shard_map/ppermute | solution.py:517
  6.3 8.1 %collective-permute-start.5 = (bf16[128,256]{1,0:T(8,128)(2,1)}, bf16[128,256]{1,0:T(8,128)(2,1)S(1)}, u32[]{:S(2)}, u32[]{:S(2)}) collective-permute-start(bf16[128,256]{1,0:T(8,128)(2,1)} %refs_1_.3), channel_id=1, source_target_pairs={{0,8},{4,12},{8,0},{12,4},{1,9},{5,13},{9,1},{13,5},{2,10},{6,14},... | collective-permute-start | bytes 196616 | tf_op jit(solution)/shard_map/ppermute | solution.py:517
  8.2 6.2 %collective-permute-start.3 = (bf16[128,256]{1,0:T(8,128)(2,1)}, bf16[128,256]{1,0:T(8,128)(2,1)S(1)}, u32[]{:S(2)}, u32[]{:S(2)}) collective-permute-start(bf16[128,256]{1,0:T(8,128)(2,1)} %refs_1_.3), channel_id=1, source_target_pairs={{0,4},{4,0},{8,12},{12,8},{1,5},{5,1},{9,13},{13,9},{2,6},{6,2},{1... | collective-permute-start | bytes 196616 | tf_op jit(solution)/shard_map/ppermute | solution.py:517
  13.1 2.1 %collective-permute-start.8 = (bf16[128,256]{1,0:T(8,128)(2,1)S(1)}, bf16[128,256]{1,0:T(8,128)(2,1)S(1)}, u32[]{:S(2)}, u32[]{:S(2)}) collective-permute-start(bf16[128,256]{1,0:T(8,128)(2,1)S(1)} %collective-permute-done.refs_3_), channel_id=1, source_target_pairs={{0,1},{1,0},{2,3},{3,2},{4,5},{5,4},{6,7},{7,6},{8,9},{9,8},{10,11... | collective-permute-start | bytes 196616 | tf_op jit(solution)/shard_map/ppermute | solution.py:516
  13.1 2.1 %collective-permute-start.7 = (bf16[128,256]{1,0:T(8,128)(2,1)S(1)}, bf16[128,256]{1,0:T(8,128)(2,1)S(1)}, u32[]{:S(2)}, u32[]{:S(2)}) collective-permute-start(bf16[128,256]{1,0:T(8,128)(2,1)S(1)} %get-tuple-element.38.refs_1_), channel_id=1, source_target_pairs={{0,1},{1,0},{2,3},{3,2},{4,5},{5,4},{6,7},{7,6},{8,9},{9,8},{10,11... | collective-permute-start | bytes 196616 | tf_op jit(solution)/shard_map/ppermute | solution.py:516
  13.6 2.1 %collective-permute-start.9 = (bf16[128,256]{1,0:T(8,128)(2,1)S(1)}, bf16[128,256]{1,0:T(8,128)(2,1)S(1)}, u32[]{:S(2)}, u32[]{:S(2)}) collective-permute-start(bf16[128,256]{1,0:T(8,128)(2,1)S(1)} %collective-permute-done.1.refs_5_), channel_id=1, source_target_pairs={{0,1},{1,0},{2,3},{3,2},{4,5},{5,4},{6,7},{7,6},{8,9},{9,8},{10,11... | collective-permute-start | bytes 196616 | tf_op jit(solution)/shard_map/ppermute | solution.py:516
  14.4 1.3 %collective-permute-start.11 = (bf16[128,256]{1,0:T(8,128)(2,1)S(1)}, bf16[128,256]{1,0:T(8,128)(2,1)S(1)}, u32[]{:S(2)}, u32[]{:S(2)}) collective-permute-start(bf16[128,256]{1,0:T(8,128)(2,1)S(1)} %collective-permute-done.10.refs_7_), channel_id=1, source_target_pairs={{0,1},{1,0},{2,3},{3,2},{4,5},{5,4},{6,7},{7,6},{8,9},{9,8},{10,11... | collective-permute-start | bytes 196616 | tf_op jit(solution)/shard_map/ppermute | solution.py:516
  14.4 4.8 %collective-permute-start.6 = (bf16[128,256]{1,0:T(8,128)(2,1)S(1)}, bf16[128,256]{1,0:T(8,128)(2,1)S(1)}, u32[]{:S(2)}, u32[]{:S(2)}) collective-permute-start(bf16[128,256]{1,0:T(8,128)(2,1)S(1)} %collective-permute-done.5.refs_5_), channel_id=1, source_target_pairs={{0,4},{4,0},{8,12},{12,8},{1,5},{5,1},{9,13},{13,9},{2,6},{6,2},{1... | collective-permute-start | bytes 196616 | tf_op jit(solution)/shard_map/ppermute | solution.py:517
  15.2 4.6 %collective-permute-start.2 = (bf16[128,256]{1,0:T(8,128)(2,1)S(1)}, bf16[128,256]{1,0:T(8,128)(2,1)S(1)}, u32[]{:S(2)}, u32[]{:S(2)}) collective-permute-start(bf16[128,256]{1,0:T(8,128)(2,1)S(1)} %copy-done), channel_id=1, source_target_pairs={{0,1},{1,0},{2,3},{3,2},{4,5},{5,4},{6,7},{7,6},{8,9},{9,8},{10,11... | collective-permute-start | bytes 196616 | tf_op jit(solution)/shard_map/ppermute | solution.py:516
  15.2 4.6 %collective-permute-start.4 = (bf16[128,256]{1,0:T(8,128)(2,1)S(1)}, bf16[128,256]{1,0:T(8,128)(2,1)S(1)}, u32[]{:S(2)}, u32[]{:S(2)}) collective-permute-start(bf16[128,256]{1,0:T(8,128)(2,1)S(1)} %collective-permute-done.3.refs_3_), channel_id=1, source_target_pairs={{0,1},{1,0},{2,3},{3,2},{4,5},{5,4},{6,7},{7,6},{8,9},{9,8},{10,11... | collective-permute-start | bytes 196616 | tf_op jit(solution)/shard_map/ppermute | solution.py:516
  19.2 1.3 %collective-permute-start.12 = (bf16[128,256]{1,0:T(8,128)(2,1)S(1)}, bf16[128,256]{1,0:T(8,128)(2,1)S(1)}, u32[]{:S(2)}, u32[]{:S(2)}) collective-permute-start(bf16[128,256]{1,0:T(8,128)(2,1)S(1)} %collective-permute-done.5.refs_5_), channel_id=1, source_target_pairs={{0,1},{1,0},{2,3},{3,2},{4,5},{5,4},{6,7},{7,6},{8,9},{9,8},{10,11... | collective-permute-start | bytes 196616 | tf_op jit(solution)/shard_map/ppermute | solution.py:516
  19.4 1.3 %collective-permute-start.13 = (bf16[128,256]{1,0:T(8,128)(2,1)S(1)}, bf16[128,256]{1,0:T(8,128)(2,1)S(1)}, u32[]{:S(2)}, u32[]{:S(2)}) collective-permute-start(bf16[128,256]{1,0:T(8,128)(2,1)S(1)} %collective-permute-done.6.refs_7_), channel_id=1, source_target_pairs={{0,1},{1,0},{2,3},{3,2},{4,5},{5,4},{6,7},{7,6},{8,9},{9,8},{10,11... | collective-permute-start | bytes 196616 | tf_op jit(solution)/shard_map/ppermute | solution.py:516
  24.0 5.8 %collective-permute-start.15 = (f32[2,8,512]{2,1,0:T(8,128)S(1)}, f32[2,8,512]{2,1,0:T(8,128)S(1)}, u32[]{:S(2)}, u32[]{:S(2)}) collective-permute-start(f32[2,8,512]{2,1,0:T(8,128)S(1)} %get-tuple-element.47.refs_1_.refs_3_), channel_id=1, source_target_pairs={{0,12},{4,8},{8,4},{12,0},{1,13},{5,9},{9,5},{13,1},{2,14},{6,10},... | collective-permute-start | bytes 98312 | tf_op jit(solution)/shard_map/ppermute | solution.py:517
  27.2 5.2 %collective-permute-start.16 = (f32[2,8,512]{2,1,0:T(8,128)S(1)}, f32[2,8,512]{2,1,0:T(8,128)S(1)}, u32[]{:S(2)}, u32[]{:S(2)}) collective-permute-start(f32[2,8,512]{2,1,0:T(8,128)S(1)} %get-tuple-element.47.refs_1_.refs_3_), channel_id=1, source_target_pairs={{0,8},{4,12},{8,0},{12,4},{1,9},{5,13},{9,1},{13,5},{2,10},{6,14},... | collective-permute-start | bytes 98312 | tf_op jit(solution)/shard_map/ppermute | solution.py:517
  27.2 5.1 %collective-permute-start.17 = (f32[2,8,512]{2,1,0:T(8,128)S(1)}, f32[2,8,512]{2,1,0:T(8,128)S(1)}, u32[]{:S(2)}, u32[]{:S(2)}) collective-permute-start(f32[2,8,512]{2,1,0:T(8,128)S(1)} %get-tuple-element.47.refs_1_.refs_3_), channel_id=1, source_target_pairs={{0,4},{4,0},{8,12},{12,8},{1,5},{5,1},{9,13},{13,9},{2,6},{6,2},{1... | collective-permute-start | bytes 98312 | tf_op jit(solution)/shard_map/ppermute | solution.py:517
  28.4 3.9 %collective-permute-start.14 = (f32[2,8,512]{2,1,0:T(8,128)S(1)}, f32[2,8,512]{2,1,0:T(8,128)S(1)}, u32[]{:S(2)}, u32[]{:S(2)}) collective-permute-start(f32[2,8,512]{2,1,0:T(8,128)S(1)} %get-tuple-element.47.refs_1_.refs_3_), channel_id=1, source_target_pairs={{0,1},{1,0},{2,3},{3,2},{4,5},{5,4},{6,7},{7,6},{8,9},{9,8},{10,11... | collective-permute-start | bytes 98312 | tf_op jit(solution)/shard_map/ppermute | solution.py:516
  32.9 2.1 %collective-permute-start.21 = (bf16[4,2,256,128]{3,2,1,0:T(8,128)(2,1)S(1)}, bf16[4,2,256,128]{3,2,1,0:T(8,128)(2,1)S(1)}, u32[]{:S(2)}, u32[]{:S(2)}) collective-permute-start(bf16[4,2,256,128]{3,2,1,0:T(8,128)(2,1)S(1)} %get-tuple-element.56), channel_id=1, source_target_pairs={{0,1},{1,0},{2,3},{3,2},{4,5},{5,4},{6,7},{7,6},{8,9},{9,8},{10,11... | collective-permute-start | bytes 1572872 | tf_op jit(solution)/shard_map/ppermute | solution.py:516
  33.0 1.9 %collective-permute-start.18 = (f32[2,8,512]{2,1,0:T(8,128)S(1)}, f32[2,8,512]{2,1,0:T(8,128)S(1)}, u32[]{:S(2)}, u32[]{:S(2)}) collective-permute-start(f32[2,8,512]{2,1,0:T(8,128)S(1)} %collective-permute-done.15.refs_5_), channel_id=1, source_target_pairs={{0,1},{1,0},{2,3},{3,2},{4,5},{5,4},{6,7},{7,6},{8,9},{9,8},{10,11... | collective-permute-start | bytes 98312 | tf_op jit(solution)/shard_map/ppermute | solution.py:516
  33.5 1.5 %collective-permute-start.19 = (f32[2,8,512]{2,1,0:T(8,128)S(1)}, f32[2,8,512]{2,1,0:T(8,128)S(1)}, u32[]{:S(2)}, u32[]{:S(2)}) collective-permute-start(f32[2,8,512]{2,1,0:T(8,128)S(1)} %collective-permute-done.16.refs_7_), channel_id=1, source_target_pairs={{0,1},{1,0},{2,3},{3,2},{4,5},{5,4},{6,7},{7,6},{8,9},{9,8},{10,11... | collective-permute-start | bytes 98312 | tf_op jit(solution)/shard_map/ppermute | solution.py:516
  33.5 1.5 %collective-permute-start.20 = (f32[2,8,512]{2,1,0:T(8,128)S(1)}, f32[2,8,512]{2,1,0:T(8,128)S(1)}, u32[]{:S(2)}, u32[]{:S(2)}) collective-permute-start(f32[2,8,512]{2,1,0:T(8,128)S(1)} %collective-permute-done.17.refs_9_), channel_id=1, source_target_pairs={{0,1},{1,0},{2,3},{3,2},{4,5},{5,4},{6,7},{7,6},{8,9},{9,8},{10,11... | collective-permute-start | bytes 98312 | tf_op jit(solution)/shard_map/ppermute | solution.py:516
  35.3 7.8 %collective-permute-start.22 = (bf16[128,256]{1,0:T(8,128)(2,1)S(1)}, bf16[128,256]{1,0:T(8,128)(2,1)S(1)}, u32[]{:S(2)}, u32[]{:S(2)}) collective-permute-start(bf16[128,256]{1,0:T(8,128)(2,1)S(1)} %get-tuple-element.58), channel_id=1, source_target_pairs={{0,12},{4,8},{8,4},{12,0},{1,13},{5,9},{9,5},{13,1},{2,14},{6,10},... | collective-permute-start | bytes 196616 | tf_op jit(solution)/shard_map/ppermute | solution.py:517
  37.2 6.9 %collective-permute-start.23 = (bf16[128,256]{1,0:T(8,128)(2,1)S(1)}, bf16[128,256]{1,0:T(8,128)(2,1)S(1)}, u32[]{:S(2)}, u32[]{:S(2)}) collective-permute-start(bf16[128,256]{1,0:T(8,128)(2,1)S(1)} %get-tuple-element.59), channel_id=1, source_target_pairs={{0,8},{4,12},{8,0},{12,4},{1,9},{5,13},{9,1},{13,5},{2,10},{6,14},... | collective-permute-start | bytes 196616 | tf_op jit(solution)/shard_map/ppermute | solution.py:517
  37.2 6.9 %collective-permute-start.24 = (bf16[128,256]{1,0:T(8,128)(2,1)S(1)}, bf16[128,256]{1,0:T(8,128)(2,1)S(1)}, u32[]{:S(2)}, u32[]{:S(2)}) collective-permute-start(bf16[128,256]{1,0:T(8,128)(2,1)S(1)} %get-tuple-element.60), channel_id=1, source_target_pairs={{0,4},{4,0},{8,12},{12,8},{1,5},{5,1},{9,13},{13,9},{2,6},{6,2},{1... | collective-permute-start | bytes 196616 | tf_op jit(solution)/shard_map/ppermute | solution.py:517
